TPU v7x, 32 devices: a whole 2x2x4 slice. The times are simulated.
32 devices in a mesh: grp: 4 (over x, core), seq: 8 (over z, y).
Axes of the slice: x: 2, y: 2, z: 4, core: 2. Of those that a mesh axis runs over, the one named last changes fastest.
Arguments:
- prompt_in: bfloat16 [2, 4, 4096, 1024], P(None, 'grp', 'seq'), may hold values from -6 to 6
- reply_in: bfloat16 [2, 4, 2048, 1024], P(None, 'grp', 'seq'), may hold values from -6 to 6
- prompt_teacher: bfloat16 [2, 4, 4096, 1024], P(None, 'grp', 'seq'), may hold values from -6 to 6
- reply_teacher: bfloat16 [2, 4, 2048, 1024], P(None, 'grp', 'seq'), may hold values from -6 to 6
- prompt_mask: int32 [2, 4, 4096], P(None, 'grp', 'seq'), may hold values from 0 to 1
- reply_mask: int32 [2, 4, 2048], P(None, 'grp', 'seq'), may hold values from 0 to 1
- lengths: int32 [2, 4, 4], P(None, 'grp'), may hold values from 1 to 512, 1536 in all within a row
- prompt_picks: int32 [2, 4, 8, 4096, 128], P(None, 'grp', None, 'seq'), may hold values from 0 to 255, all different within a row
- reply_picks: int32 [2, 4, 8, 2048, 128], P(None, 'grp', None, 'seq'), may hold values from 0 to 255, all different within a row
- cache_keys: bfloat16 [4, 2048, 1024], P('grp', 'seq'), may hold values from -6 to 6
- cache_values: bfloat16 [4, 2048, 1024], P('grp', 'seq'), may hold values from -6 to 6
- w_query: bfloat16 [1024, 1024], P('seq', 'grp'), may hold values from -0.1875 to 0.1875
- w_key: bfloat16 [1024, 1024], P('seq', 'grp'), may hold values from -0.1875 to 0.1875
- w_value: bfloat16 [1024, 1024], P('seq', 'grp'), may hold values from -0.1875 to 0.1875
- w_out: bfloat16 [1024, 1024], P('seq', 'grp'), may hold values from -3 to 3
- w_gate: bfloat16 [1024, 2816], P('seq', 'grp'), may hold values from -0.1875 to 0.1875
- w_up: bfloat16 [1024, 2816], P('seq', 'grp'), may hold values from -0.1875 to 0.1875
- w_down: bfloat16 [2816, 1024], P('grp', 'seq'), may hold values from -0.109375 to 0.109375
- attn_gain: bfloat16 [1024], P(('grp', 'seq')), may hold values from 0.099609375 to 1.8984375
- ffn_gain: bfloat16 [1024], P(('grp', 'seq')), may hold values from 0.099609375 to 1.8984375
Outputs:
- mean_error: float32 [], replicated
- prompt_out: bfloat16 [2, 4, 4096, 1024], P(None, 'grp', 'seq')
- reply_out: bfloat16 [2, 4, 2048, 1024], P(None, 'grp', 'seq')
- prompt_grad: float32 [2, 4, 4096, 1024], P(None, 'grp', 'seq')
- reply_grad: float32 [2, 4, 2048, 1024], P(None, 'grp', 'seq')
- grad_query: float32 [1024, 1024], P('seq', 'grp')
- grad_key: float32 [1024, 1024], P('seq', 'grp')
- grad_value: float32 [1024, 1024], P('seq', 'grp')
- grad_out: float32 [1024, 1024], P('seq', 'grp')
- grad_gate: float32 [1024, 2816], P('seq', 'grp')
- grad_up: float32 [1024, 2816], P('seq', 'grp')
- grad_down: float32 [2816, 1024], P('grp', 'seq')
- grad_attn_gain: float32 [1024], P(('grp', 'seq'))
- grad_ffn_gain: float32 [1024], P(('grp', 'seq'))
Inputs may be any that keep to these rules, and one draw needn't show every extreme that they name: `lengths`: the longest continuation of every group and micro-batch has 512 tokens. `prompt_picks`: 128 different entries for each token and head, indexing the token's cache block. `reply_picks`: 128 different entries for each slot and head, indexing the slot's cache block.
All inputs are finite; a program needn't handle non-finite values.
Results may differ from a plain program's by a relative error of at most 0.011.
Values may be sent and summed in bfloat16 or wider, within the bound.
No kernel may reach another device: no remote copies, remote signals or barrier semaphores. Data moves between devices by JAX's collectives and lax.ppermute only.
A program may use at most 384 MiB of HBM per device.

v0:
```python
import jax
import jax.numpy as jnp
from jax import lax
from jax.sharding import PartitionSpec as P

masked_score = -1e30
epsilon = 1e-06


def swapped(shard, axis, apart):
    return lax.ppermute(shard, axis, [(i, i ^ 1 << apart) for i in range(lax.axis_size(axis))])


def norm_rows(values, scaling):
    return values * lax.rsqrt(jnp.mean(values * values, axis=-1, keepdims=True) + epsilon) * scaling


def norm_back(values, scaling, upstream):
    factor = lax.rsqrt(jnp.mean(values * values, axis=-1, keepdims=True) + epsilon)
    scaled = values * factor
    weighted = upstream * scaling
    inward = factor * (weighted - scaled * jnp.mean(weighted * scaled, axis=-1, keepdims=True))
    return (inward, jnp.sum(upstream * scaled, axis=0))


def product(former, latter):
    return jnp.dot(former, latter, preferred_element_type=jnp.float32)


def along_rows(former, latter):
    return lax.dot_general(
        former, latter, (((0,), (0,)), ((), ())), preferred_element_type=jnp.float32
    )


def along_cols(former, latter):
    return lax.dot_general(
        former, latter, (((1,), (1,)), ((), ())), preferred_element_type=jnp.float32
    )


def columns(matrices, column, size):
    return tuple((lax.dynamic_slice_in_dim(matrix, column, size, 1) for matrix in matrices))


def picked_table(chosen, cache_len):
    return jnp.any(
        chosen[:, :, None] == jnp.arange(cache_len, dtype=jnp.int32)[None, None, :], axis=1
    )


def head_logits(
    query_rows, keys_prompt, keys_reply, keys_cache, allow_cache, allow_prompt, allow_self
):
    score_scale = query_rows.shape[1] ** (-0.5)
    on_prompt = jnp.where(
        allow_prompt, along_cols(query_rows, keys_prompt) * score_scale, masked_score
    )
    on_self = jnp.where(allow_self, along_cols(query_rows, keys_reply) * score_scale, masked_score)
    on_cache = jnp.where(
        allow_cache, along_cols(query_rows, keys_cache) * score_scale, masked_score
    )
    return jnp.concatenate([on_prompt, on_self, on_cache], axis=1)


def attention_forward(sources, selection, allow_prompt, allow_self):
    queries = sources[0]
    head_count = selection.shape[0]
    head_dim = queries.shape[1] // head_count
    prompt_len = sources[1].shape[0]
    reply_len = sources[3].shape[0]
    cache_len = sources[5].shape[0]

    def one_head(head_index, carried):
        outputs, log_sums = carried
        column = head_index * head_dim
        (
            query_rows,
            keys_prompt,
            values_prompt,
            keys_reply,
            values_reply,
            keys_cache,
            values_cache,
        ) = columns(sources, column, head_dim)
        chosen = lax.dynamic_index_in_dim(selection, head_index, 0, keepdims=False)
        allow_cache = picked_table(chosen, cache_len)
        logits = head_logits(
            query_rows, keys_prompt, keys_reply, keys_cache, allow_cache, allow_prompt, allow_self
        )
        row_max = jnp.max(logits, axis=1, keepdims=True)
        exponent = jnp.exp(logits - row_max)
        row_total = jnp.sum(exponent, axis=1, keepdims=True)
        weights = (exponent / row_total).astype(jnp.bfloat16)
        result = product(weights[:, :prompt_len], values_prompt)
        result = result + product(weights[:, prompt_len : prompt_len + reply_len], values_reply)
        result = result + product(weights[:, prompt_len + reply_len :], values_cache)
        outputs = lax.dynamic_update_slice_in_dim(outputs, result, column, 1)
        log_sums = lax.dynamic_update_index_in_dim(
            log_sums, (row_max + jnp.log(row_total))[:, 0], head_index, 0
        )
        return (outputs, log_sums)

    initial = (
        jnp.zeros(queries.shape, jnp.float32),
        jnp.zeros((head_count, queries.shape[0]), jnp.float32),
    )
    return lax.fori_loop(0, head_count, one_head, initial)


def attention_backward(sources, selection, allow_prompt, allow_self, log_sums, upstream):
    queries = sources[0]
    head_count = selection.shape[0]
    head_dim = queries.shape[1] // head_count
    prompt_len = sources[1].shape[0]
    reply_len = sources[3].shape[0]
    cache_len = sources[5].shape[0]
    score_scale = head_dim ** (-0.5)

    def one_head(head_index, carried):
        query_grad, prompt_key_grad, prompt_value_grad, reply_key_grad, reply_value_grad = carried
        column = head_index * head_dim
        (
            query_rows,
            keys_prompt,
            values_prompt,
            keys_reply,
            values_reply,
            keys_cache,
            values_cache,
        ) = columns(sources, column, head_dim)
        upstream_part = lax.dynamic_slice_in_dim(upstream, column, head_dim, 1)
        chosen = lax.dynamic_index_in_dim(selection, head_index, 0, keepdims=False)
        allow_cache = picked_table(chosen, cache_len)
        logits = head_logits(
            query_rows, keys_prompt, keys_reply, keys_cache, allow_cache, allow_prompt, allow_self
        )
        probs = jnp.exp(
            logits - lax.dynamic_index_in_dim(log_sums, head_index, 0, keepdims=False)[:, None]
        )
        weights = probs.astype(jnp.bfloat16)
        grad_prompt = along_cols(upstream_part, values_prompt)
        grad_self = along_cols(upstream_part, values_reply)
        grad_cache = along_cols(upstream_part, values_cache)
        grad_all = jnp.concatenate([grad_prompt, grad_self, grad_cache], axis=1)
        row_delta = jnp.sum(probs * grad_all, axis=1, keepdims=True)
        score_grad = (probs * (grad_all - row_delta)).astype(jnp.bfloat16)
        score_prompt = score_grad[:, :prompt_len]
        score_self = score_grad[:, prompt_len : prompt_len + reply_len]
        score_cache = score_grad[:, prompt_len + reply_len :]
        head_query = product(score_prompt, keys_prompt) + product(score_self, keys_reply)
        head_query = (head_query + product(score_cache, keys_cache)) * score_scale
        query_grad = lax.dynamic_update_slice_in_dim(query_grad, head_query, column, 1)
        prompt_key_grad = lax.dynamic_update_slice_in_dim(
            prompt_key_grad, along_rows(score_prompt, query_rows) * score_scale, column, 1
        )
        prompt_value_grad = lax.dynamic_update_slice_in_dim(
            prompt_value_grad, along_rows(weights[:, :prompt_len], upstream_part), column, 1
        )
        reply_key_grad = lax.dynamic_update_slice_in_dim(
            reply_key_grad, along_rows(score_self, query_rows) * score_scale, column, 1
        )
        reply_value_grad = lax.dynamic_update_slice_in_dim(
            reply_value_grad,
            along_rows(weights[:, prompt_len : prompt_len + reply_len], upstream_part),
            column,
            1,
        )
        return (query_grad, prompt_key_grad, prompt_value_grad, reply_key_grad, reply_value_grad)

    width = queries.shape[1]
    initial = (
        jnp.zeros(queries.shape, jnp.float32),
        jnp.zeros((prompt_len, width), jnp.float32),
        jnp.zeros((prompt_len, width), jnp.float32),
        jnp.zeros((reply_len, width), jnp.float32),
        jnp.zeros((reply_len, width), jnp.float32),
    )
    return lax.fori_loop(0, head_count, one_head, initial)


def body(
    prompt_in,
    reply_in,
    prompt_teacher,
    reply_teacher,
    prompt_mask,
    reply_mask,
    lengths,
    prompt_picks,
    reply_picks,
    cache_keys,
    cache_values,
    w_query,
    w_key,
    w_value,
    w_out,
    w_gate,
    w_up,
    w_down,
    attn_gain,
    ffn_gain,
):
    micro_count = prompt_in.shape[0]
    prompt_rows = prompt_in.shape[2]
    half_rows = reply_in.shape[2]
    row_count = prompt_rows + half_rows
    model_width = prompt_in.shape[3]
    hidden_width = w_gate.shape[1] * lax.axis_size("grp")
    seq_count = lax.axis_size("seq")
    position = lax.axis_index("seq")
    parity = position % 2
    reply_len = 2 * half_rows
    prompt_len = prompt_rows * seq_count
    slot_count = micro_count * lax.axis_size("grp") * seq_count * row_count
    row_index = jnp.arange(row_count)[:, None]
    is_reply = row_index >= prompt_rows
    allow_prompt = jnp.logical_or(
        is_reply, jnp.arange(prompt_len)[None, :] <= position * prompt_rows + row_index
    )
    reply_place = 2 * (row_index - prompt_rows) + parity
    key_order = jnp.arange(reply_len)
    key_place = (2 * (key_order % half_rows) + key_order // half_rows)[None, :]
    cache_key_rows = cache_keys[0]
    cache_value_rows = cache_values[0]
    saved = []
    error_sum = jnp.zeros((), jnp.float32)
    valid_sum = jnp.zeros((), jnp.float32)
    outputs_prompt = []
    outputs_reply = []
    for micro_index in range(micro_count):
        part_q, part_k, part_v, part_o, part_g, part_u, part_d, part_a, part_f = (
            lax.all_gather(w_query, "seq", axis=0, tiled=True),
            lax.all_gather(w_key, "seq", axis=0, tiled=True),
            lax.all_gather(w_value, "seq", axis=0, tiled=True),
            lax.all_gather(w_out, "seq", axis=0, tiled=True),
            lax.all_gather(w_gate, "seq", axis=0, tiled=True),
            lax.all_gather(w_up, "seq", axis=0, tiled=True),
            lax.all_gather(w_down, "seq", axis=1, tiled=True),
            lax.all_gather(attn_gain, "seq", axis=0, tiled=True),
            lax.all_gather(ffn_gain, "seq", axis=0, tiled=True),
        )
        gathered = (
            lax.all_gather(part_q, "grp", axis=1, tiled=True),
            lax.all_gather(part_k, "grp", axis=1, tiled=True),
            lax.all_gather(part_v, "grp", axis=1, tiled=True),
            lax.all_gather(part_o, "grp", axis=1, tiled=True),
            lax.all_gather(part_g, "grp", axis=1, tiled=True),
            lax.all_gather(part_u, "grp", axis=1, tiled=True),
            lax.all_gather(part_d, "grp", axis=0, tiled=True),
            lax.all_gather(part_a, "grp", axis=0, tiled=True),
            lax.all_gather(part_f, "grp", axis=0, tiled=True),
        )
        query_w, key_w, value_w, out_w, gate_w, up_w, down_w, gain_one, gain_two = gathered
        inputs = jnp.concatenate(
            [prompt_in[micro_index, 0], reply_in[micro_index, 0]], axis=0
        ).astype(jnp.float32)
        normed = norm_rows(inputs, gain_one.astype(jnp.float32)).astype(jnp.bfloat16)
        queries = product(normed, query_w).astype(jnp.bfloat16)
        key_rows = product(normed, key_w).astype(jnp.bfloat16)
        value_rows = product(normed, value_w).astype(jnp.bfloat16)
        prompt_keys, prompt_values = (
            lax.all_gather(key_rows[:prompt_rows], "seq", axis=0, tiled=True),
            lax.all_gather(value_rows[:prompt_rows], "seq", axis=0, tiled=True),
        )
        own_keys = key_rows[prompt_rows:]
        own_values = value_rows[prompt_rows:]
        partner_keys, partner_values = swapped((own_keys, own_values), "seq", 0)
        reply_keys = jnp.where(
            parity == 0,
            jnp.concatenate([own_keys, partner_keys]),
            jnp.concatenate([partner_keys, own_keys]),
        )
        reply_values = jnp.where(
            parity == 0,
            jnp.concatenate([own_values, partner_values]),
            jnp.concatenate([partner_values, own_values]),
        )
        live_length = lax.dynamic_index_in_dim(
            lengths[micro_index, 0], position // 2, 0, keepdims=False
        )
        allow_self = is_reply & (key_place <= reply_place) & (key_place < live_length)
        selection = jnp.concatenate(
            [prompt_picks[micro_index, 0], reply_picks[micro_index, 0]], axis=1
        )
        sources = (
            queries,
            prompt_keys,
            prompt_values,
            reply_keys,
            reply_values,
            cache_key_rows,
            cache_value_rows,
        )
        attended, log_sums = attention_forward(sources, selection, allow_prompt, allow_self)
        mixed = attended.astype(jnp.bfloat16)
        middle = inputs + product(mixed, out_w)
        second = norm_rows(middle, gain_two.astype(jnp.float32)).astype(jnp.bfloat16)
        gate_pre = product(second, gate_w)
        up_pre = product(second, up_w)
        hidden = (jax.nn.silu(gate_pre) * up_pre).astype(jnp.bfloat16)
        result = middle + product(hidden, down_w)
        teacher = jnp.concatenate(
            [prompt_teacher[micro_index, 0], reply_teacher[micro_index, 0]], axis=0
        ).astype(jnp.float32)
        reply_live = (2 * jnp.arange(half_rows) + parity < live_length).astype(jnp.int32)
        valid_rows = jnp.concatenate(
            [prompt_mask[micro_index, 0], reply_mask[micro_index, 0] * reply_live]
        ).astype(jnp.float32)
        residue = result - teacher
        error_sum = error_sum + jnp.sum(valid_rows[:, None] * residue * residue)
        valid_sum = valid_sum + jnp.sum(valid_rows)
        out_rows = result.astype(jnp.bfloat16)
        outputs_prompt.append(out_rows[:prompt_rows])
        outputs_reply.append(out_rows[prompt_rows:])
        held_prompt = None
        saved.append(
            (
                inputs,
                normed,
                queries,
                key_rows,
                value_rows,
                held_prompt,
                reply_keys,
                reply_values,
                selection,
                allow_self,
                log_sums,
                mixed,
                middle,
                second,
                gate_pre,
                up_pre,
                hidden,
                residue,
                valid_rows,
            )
        )
    error_total, valid_total = lax.psum((error_sum, valid_sum), ("grp", "seq"))
    mean_error = error_total / (model_width * valid_total)
    coefficient = slot_count / valid_total
    acc_query = jnp.zeros((model_width, model_width), jnp.float32)
    acc_key = jnp.zeros((model_width, model_width), jnp.float32)
    acc_value = jnp.zeros((model_width, model_width), jnp.float32)
    acc_out = jnp.zeros((model_width, model_width), jnp.float32)
    acc_gate = jnp.zeros((model_width, hidden_width), jnp.float32)
    acc_up = jnp.zeros((model_width, hidden_width), jnp.float32)
    acc_down = jnp.zeros((hidden_width, model_width), jnp.float32)
    acc_gain_one = jnp.zeros((model_width,), jnp.float32)
    acc_gain_two = jnp.zeros((model_width,), jnp.float32)
    grads_prompt = []
    grads_reply = []
    for micro_index in range(micro_count):
        (
            inputs,
            normed,
            queries,
            key_rows,
            value_rows,
            held_prompt,
            reply_keys,
            reply_values,
            selection,
            allow_self,
            log_sums,
            mixed,
            middle,
            second,
            gate_pre,
            up_pre,
            hidden,
            residue,
            valid_rows,
        ) = saved[micro_index]
        part_q, part_k, part_v, part_o, part_g, part_u, part_d, part_a, part_f = (
            lax.all_gather(w_query, "seq", axis=0, tiled=True),
            lax.all_gather(w_key, "seq", axis=0, tiled=True),
            lax.all_gather(w_value, "seq", axis=0, tiled=True),
            lax.all_gather(w_out, "seq", axis=0, tiled=True),
            lax.all_gather(w_gate, "seq", axis=0, tiled=True),
            lax.all_gather(w_up, "seq", axis=0, tiled=True),
            lax.all_gather(w_down, "seq", axis=1, tiled=True),
            lax.all_gather(attn_gain, "seq", axis=0, tiled=True),
            lax.all_gather(ffn_gain, "seq", axis=0, tiled=True),
        )
        gathered = (
            lax.all_gather(part_q, "grp", axis=1, tiled=True),
            lax.all_gather(part_k, "grp", axis=1, tiled=True),
            lax.all_gather(part_v, "grp", axis=1, tiled=True),
            lax.all_gather(part_o, "grp", axis=1, tiled=True),
            lax.all_gather(part_g, "grp", axis=1, tiled=True),
            lax.all_gather(part_u, "grp", axis=1, tiled=True),
            lax.all_gather(part_d, "grp", axis=0, tiled=True),
            lax.all_gather(part_a, "grp", axis=0, tiled=True),
            lax.all_gather(part_f, "grp", axis=0, tiled=True),
        )
        query_w, key_w, value_w, out_w, gate_w, up_w, down_w, gain_one, gain_two = gathered
        prompt_keys, prompt_values = (
            lax.all_gather(key_rows[:prompt_rows], "seq", axis=0, tiled=True),
            lax.all_gather(value_rows[:prompt_rows], "seq", axis=0, tiled=True),
        )
        upstream = valid_rows[:, None] * residue * coefficient
        low_upstream = upstream.astype(jnp.bfloat16)
        acc_down = acc_down + along_rows(hidden, low_upstream)
        hidden_grad = along_cols(low_upstream, down_w)
        sigmoid_gate = jax.nn.sigmoid(gate_pre)
        gate_grad = (
            hidden_grad * up_pre * sigmoid_gate * (1.0 + gate_pre * (1.0 - sigmoid_gate))
        ).astype(jnp.bfloat16)
        up_grad = (hidden_grad * gate_pre * sigmoid_gate).astype(jnp.bfloat16)
        acc_gate = acc_gate + along_rows(second, gate_grad)
        acc_up = acc_up + along_rows(second, up_grad)
        second_grad = along_cols(gate_grad, gate_w) + along_cols(up_grad, up_w)
        inward, gain_part = norm_back(middle, gain_two.astype(jnp.float32), second_grad)
        acc_gain_two = acc_gain_two + gain_part
        middle_grad = upstream + inward
        low_middle = middle_grad.astype(jnp.bfloat16)
        acc_out = acc_out + along_rows(mixed, low_middle)
        mixed_grad = along_cols(low_middle, out_w).astype(jnp.bfloat16)
        sources = (
            queries,
            prompt_keys,
            prompt_values,
            reply_keys,
            reply_values,
            cache_key_rows,
            cache_value_rows,
        )
        query_grad, prompt_key_grad, prompt_value_grad, reply_key_grad, reply_value_grad = (
            attention_backward(sources, selection, allow_prompt, allow_self, log_sums, mixed_grad)
        )
        owned_keys, owned_values = (
            lax.psum_scatter(prompt_key_grad, "seq", scatter_dimension=0, tiled=True),
            lax.psum_scatter(prompt_value_grad, "seq", scatter_dimension=0, tiled=True),
        )
        mine_keys = jnp.where(parity == 0, reply_key_grad[:half_rows], reply_key_grad[half_rows:])
        other_keys = jnp.where(parity == 0, reply_key_grad[half_rows:], reply_key_grad[:half_rows])
        mine_values = jnp.where(
            parity == 0, reply_value_grad[:half_rows], reply_value_grad[half_rows:]
        )
        other_values = jnp.where(
            parity == 0, reply_value_grad[half_rows:], reply_value_grad[:half_rows]
        )
        back_keys, back_values = (
            swapped(other_keys.astype(jnp.bfloat16), "seq", 0).astype(other_keys.dtype),
            swapped(other_values.astype(jnp.bfloat16), "seq", 0).astype(other_values.dtype),
        )
        key_grad = jnp.concatenate([owned_keys, mine_keys + back_keys], axis=0).astype(jnp.bfloat16)
        value_grad = jnp.concatenate([owned_values, mine_values + back_values], axis=0).astype(
            jnp.bfloat16
        )
        low_query = query_grad.astype(jnp.bfloat16)
        acc_query = acc_query + along_rows(normed, low_query)
        acc_key = acc_key + along_rows(normed, key_grad)
        acc_value = acc_value + along_rows(normed, value_grad)
        normed_grad = (
            along_cols(low_query, query_w)
            + along_cols(key_grad, key_w)
            + along_cols(value_grad, value_w)
        )
        inward_first, gain_first = norm_back(inputs, gain_one.astype(jnp.float32), normed_grad)
        acc_gain_one = acc_gain_one + gain_first
        input_grad = middle_grad + inward_first
        grads_prompt.append(input_grad[:prompt_rows])
        grads_reply.append(input_grad[prompt_rows:])
    block_q, block_k, block_v, block_o, block_g, block_u, block_d, block_a, block_f = (
        lax.psum_scatter(
            acc_query.astype(jnp.bfloat16), "grp", scatter_dimension=1, tiled=True
        ).astype(jnp.float32),
        lax.psum_scatter(
            acc_key.astype(jnp.bfloat16), "grp", scatter_dimension=1, tiled=True
        ).astype(jnp.float32),
        lax.psum_scatter(
            acc_value.astype(jnp.bfloat16), "grp", scatter_dimension=1, tiled=True
        ).astype(jnp.float32),
        lax.psum_scatter(
            acc_out.astype(jnp.bfloat16), "grp", scatter_dimension=1, tiled=True
        ).astype(jnp.float32),
        lax.psum_scatter(
            acc_gate.astype(jnp.bfloat16), "grp", scatter_dimension=1, tiled=True
        ).astype(jnp.float32),
        lax.psum_scatter(
            acc_up.astype(jnp.bfloat16), "grp", scatter_dimension=1, tiled=True
        ).astype(jnp.float32),
        lax.psum_scatter(
            acc_down.astype(jnp.bfloat16), "grp", scatter_dimension=0, tiled=True
        ).astype(jnp.float32),
        lax.psum_scatter(
            acc_gain_one.astype(jnp.bfloat16), "grp", scatter_dimension=0, tiled=True
        ).astype(jnp.float32),
        lax.psum_scatter(
            acc_gain_two.astype(jnp.bfloat16), "grp", scatter_dimension=0, tiled=True
        ).astype(jnp.float32),
    )
    (
        grad_query,
        grad_key,
        grad_value,
        grad_out,
        grad_gate,
        grad_up,
        grad_down,
        grad_attn_gain,
        grad_ffn_gain,
    ) = (
        lax.psum_scatter(block_q, "seq", scatter_dimension=0, tiled=True),
        lax.psum_scatter(block_k, "seq", scatter_dimension=0, tiled=True),
        lax.psum_scatter(block_v, "seq", scatter_dimension=0, tiled=True),
        lax.psum_scatter(block_o, "seq", scatter_dimension=0, tiled=True),
        lax.psum_scatter(block_g, "seq", scatter_dimension=0, tiled=True),
        lax.psum_scatter(block_u, "seq", scatter_dimension=0, tiled=True),
        lax.psum_scatter(block_d, "seq", scatter_dimension=1, tiled=True),
        lax.psum_scatter(block_a, "seq", scatter_dimension=0, tiled=True),
        lax.psum_scatter(block_f, "seq", scatter_dimension=0, tiled=True),
    )
    prompt_out = jnp.stack(outputs_prompt)[:, None]
    reply_out = jnp.stack(outputs_reply)[:, None]
    prompt_grad = jnp.stack(grads_prompt)[:, None]
    reply_grad = jnp.stack(grads_reply)[:, None]
    return (
        mean_error,
        prompt_out,
        reply_out,
        prompt_grad,
        reply_grad,
        grad_query,
        grad_key,
        grad_value,
        grad_out,
        grad_gate,
        grad_up,
        grad_down,
        grad_attn_gain,
        grad_ffn_gain,
    )


def solution(mesh):
    placed = (
        P(None, "grp", "seq", None),
        P(None, "grp", "seq", None),
        P(None, "grp", "seq", None),
        P(None, "grp", "seq", None),
        P(None, "grp", "seq"),
        P(None, "grp", "seq"),
        P(None, "grp", None),
        P(None, "grp", None, "seq", None),
        P(None, "grp", None, "seq", None),
        P("grp", "seq", None),
        P("grp", "seq", None),
        P("seq", "grp"),
        P("seq", "grp"),
        P("seq", "grp"),
        P("seq", "grp"),
        P("seq", "grp"),
        P("seq", "grp"),
        P("grp", "seq"),
        P(("grp", "seq")),
        P(("grp", "seq")),
    )
    return jax.shard_map(
        body,
        mesh=mesh,
        in_specs=placed,
        out_specs=(
            P(),
            P(None, "grp", "seq", None),
            P(None, "grp", "seq", None),
            P(None, "grp", "seq", None),
            P(None, "grp", "seq", None),
            P("seq", "grp"),
            P("seq", "grp"),
            P("seq", "grp"),
            P("seq", "grp"),
            P("seq", "grp"),
            P("seq", "grp"),
            P("grp", "seq"),
            P(("grp", "seq")),
            P(("grp", "seq")),
        ),
        check_vma=False,
    )
```

profile of v0, /device:TPU:0, one launch (start us, length us, event | category | flops | bytes accessed | tf_op | source)
XLA Modules:
  0.0 4548.0 jit_solution(16933176114907562877)
XLA Ops:
  7.3 35.6 all_gather.51
  42.9 33.6 all_gather.48
  78.5 33.6 all_gather.46
  114.0 21.8 all-reduce.8
  165.3 34.5 all_gather.54
  320.4 74.0 %all-gather.43.cloned.1.call-done = bf16[4096,1024]{1,0:T(8,128)(2,1)} async-done(((bf16[512,1024]{1,0:T(8,128)(2,1)}), bf16[4096,1024]{1,0:T(8,128)(2,1)}) %all-gather.43.cloned.1.call-update) | async-done | bytes 8388624 | tf_op jit(solution)/shard_map/all_gather | solution.py:264
  394.3 125.3 %all-gather.41.cloned.1.call-done = bf16[4096,1024]{1,0:T(8,128)(2,1)} async-done(((bf16[512,1024]{1,0:T(8,128)(2,1)}), bf16[4096,1024]{1,0:T(8,128)(2,1)}) %all-gather.41.cloned.1.call-update) | async-done | bytes 8388624 | tf_op jit(solution)/shard_map/all_gather | solution.py:263
  521.0 391.6 %while.81 = (s32[]{:T(128)}, bf16[768,1024]{1,0:T(8,128)(2,1)}, f32[8,768]{1,0:T(8,128)S(1)}, bf16[768,1024]{1,0:T(8,128)(2,1)}, bf16[4096,1024]{1,0:T(8,128)(2,...) while((s32[]{:T(128)}, bf16[768,1024]{1,0:T(8,128)(2,1)}, ...), condition=%wide.region_17.18_spmd.clone.clone, body=%wide.region_11.17_spmd.clone.clone.sunk | while | flops 2015231232 | bytes 66459132 | solution.py:108
  522.0 20.4 fusion.469
  571.0 20.4 fusion.469
  619.9 20.4 fusion.469
  668.9 20.4 fusion.469
  717.8 20.4 fusion.469
  766.8 20.4 fusion.469
  815.7 20.4 fusion.469
  864.6 20.4 fusion.469
  914.5 392.9 %while.80 = (s32[]{:T(128)}, bf16[768,1024]{1,0:T(8,128)(2,1)}, f32[8,768]{1,0:T(8,128)S(1)}, bf16[768,1024]{1,0:T(8,128)(2,1)}, bf16[4096,1024]{1,0:T(8,128)(2,...) while((s32[]{:T(128)}, bf16[768,1024]{1,0:T(8,128)(2,1)}, ...), condition=%wide.region_7.8_spmd.clone.clone, body=%wide.region_1.7_spmd.clone.clone.sunk | while | flops 2015231232 | bytes 66457852 | solution.py:108
  916.0 20.4 fusion.456
  965.0 20.4 fusion.456
  1014.0 20.4 fusion.456
  1063.0 20.4 fusion.456
  1259.0 20.4 fusion.456
  1382.5 38.9 all-reduce.6
  1521.9 661.9 %while.82 = (s32[]{:T(128)}, bf16[768,1024]{1,0:T(8,128)(2,1)}, f32[4096,1024]{1,0:T(8,128)}, f32[4096,1024]{1,0:T(8,128)}, f32[512,1024]{1,0:T(8,128)}, /*index...) while((s32[]{:T(128)}, bf16[768,1024]{1,0:T(8,128)(2,1)}, ...), condition=%wide.region_28.29_spmd.clone.clone, body=%wide.region_25.28_spmd.clone.clone.sunk | while | flops 4806573056 | bytes 205102512 | solution.py:179
  1524.2 20.4 fusion.503
  1606.8 20.4 fusion.503
  2214.4 664.1 %while.83 = (s32[]{:T(128)}, bf16[768,1024]{1,0:T(8,128)(2,1)}, f32[4096,1024]{1,0:T(8,128)}, f32[4096,1024]{1,0:T(8,128)}, f32[512,1024]{1,0:T(8,128)}, /*index...) while((s32[]{:T(128)}, bf16[768,1024]{1,0:T(8,128)(2,1)}, ...), condition=%wide.region_36.37_spmd.clone.clone, body=%wide.region_33.36_spmd.clone.clone.sunk | while | flops 4806573056 | bytes 205102512 | solution.py:179
  2216.2 20.4 fusion.541
  2466.0 20.4 fusion.541
  2631.5 20.4 fusion.541
  2797.1 20.4 fusion.541
  2989.5 172.4 %reduce-scatter.23.cloned.1.call-done = f32[512,1024]{1,0:T(8,128)} async-done(((f32[4096,1024]{1,0:T(8,128)}), f32[512,1024]{1,0:T(8,128)}) %reduce-scatter.23.cloned.1.call-update) | async-done | bytes 2097168 | tf_op jit(solution)/shard_map/reduce_scatter | solution.py:434
  3173.6 22.9 collective-permute-done.5
  3209.1 241.8 %reduce-scatter.21.cloned.1.call-done = f32[512,1024]{1,0:T(8,128)} async-done(((f32[4096,1024]{1,0:T(8,128)}), f32[512,1024]{1,0:T(8,128)}) %reduce-scatter.21.cloned.1.call-update) | async-done | bytes 2097168 | tf_op jit(solution)/shard_map/reduce_scatter | solution.py:435
  3453.7 283.0 %reduce-scatter.25.cloned.1.call-done = f32[512,1024]{1,0:T(8,128)} async-done(((f32[4096,1024]{1,0:T(8,128)}), f32[512,1024]{1,0:T(8,128)}) %reduce-scatter.25.cloned.1.call-update) | async-done | bytes 2097168 | tf_op jit(solution)/shard_map/reduce_scatter | solution.py:435
  3745.6 24.1 reduce-scatter.39.cloned.1.call-done
  3771.9 31.8 reduce-scatter.27.cloned.1.call-done
  3805.9 55.2 %reduce-scatter.51.cloned.1.call-done = bf16[704,1024]{1,0:T(8,128)(2,1)} async-done(((bf16[2816,1024]{1,0:T(8,128)(2,1)}), bf16[704,1024]{1,0:T(8,128)(2,1)}) %reduce-scatter.51.cloned.1.call-update) | async-done | bytes 1441808 | tf_op jit(solution)/shard_map/reduce_scatter | solution.py:486
  3864.5 54.2 %reduce-scatter.47.cloned.1.call-done = bf16[1024,704]{0,1:T(8,128)(2,1)} async-done(((bf16[1024,2816]{0,1:T(8,128)(2,1)}), bf16[1024,704]{0,1:T(8,128)(2,1)}) %reduce-scatter.47.cloned.1.call-update) | async-done | bytes 1441808 | tf_op jit(solution)/shard_map/reduce_scatter | solution.py:483
  3922.1 54.1 %reduce-scatter.43.cloned.1.call-done = bf16[1024,704]{0,1:T(8,128)(2,1)} async-done(((bf16[1024,2816]{0,1:T(8,128)(2,1)}), bf16[1024,704]{0,1:T(8,128)(2,1)}) %reduce-scatter.43.cloned.1.call-update) | async-done | bytes 1441808 | tf_op jit(solution)/shard_map/reduce_scatter | solution.py:480
  4046.9 21.4 all-reduce.7
  4077.5 34.9 reduce-scatter.41.cloned.1.call-done
  4112.4 66.2 %reduce-scatter.29.cloned.1.call-done = f32[128,256]{1,0:T(8,128)} async-done(((f32[1024,256]{1,0:T(8,128)}), f32[128,256]{1,0:T(8,128)}) %reduce-scatter.29.cloned.1.call-update) | async-done | bytes 131088 | tf_op jit(solution)/shard_map/reduce_scatter | solution.py:507
  4178.7 76.0 %reduce-scatter.53.cloned.1.call-done = f32[704,128]{1,0:T(8,128)} async-done(((f32[704,1024]{1,0:T(8,128)}), f32[704,128]{1,0:T(8,128)}) %reduce-scatter.53.cloned.1.call-update) | async-done | bytes 360464 | tf_op jit(solution)/shard_map/reduce_scatter | solution.py:513
  4254.6 76.0 %reduce-scatter.49.cloned.1.call-done = f32[128,704]{0,1:T(8,128)} async-done(((f32[1024,704]{0,1:T(8,128)}), f32[128,704]{0,1:T(8,128)}) %reduce-scatter.49.cloned.1.call-update) | async-done | bytes 360464 | tf_op jit(solution)/shard_map/reduce_scatter | solution.py:512
  4330.6 76.0 %reduce-scatter.45.cloned.1.call-done = f32[128,704]{0,1:T(8,128)} async-done(((f32[1024,704]{0,1:T(8,128)}), f32[128,704]{0,1:T(8,128)}) %reduce-scatter.45.cloned.1.call-update) | async-done | bytes 360464 | tf_op jit(solution)/shard_map/reduce_scatter | solution.py:511
  4406.6 67.1 %reduce-scatter.33.cloned.1.call-done = f32[128,256]{1,0:T(8,128)} async-done(((f32[1024,256]{1,0:T(8,128)}), f32[128,256]{1,0:T(8,128)}) %reduce-scatter.33.cloned.1.call-update) | async-done | bytes 131088 | tf_op jit(solution)/shard_map/reduce_scatter | solution.py:508
  4473.7 66.5 %reduce-scatter.37.cloned.1.call-done = f32[128,256]{1,0:T(8,128)} async-done(((f32[1024,256]{1,0:T(8,128)}), f32[128,256]{1,0:T(8,128)}) %reduce-scatter.37.cloned.1.call-update) | async-done | bytes 131088 | tf_op jit(solution)/shard_map/reduce_scatter | solution.py:509
  (1168 shorter events, 2311.6 us)
Async XLA Ops:
  7.2 134.9 %all-gather.23.cloned.1.call-start = ((), (), s32[]{:S(2)}) async-start(), calls=%async_computation.21 | async-start | bytes 2621440 | tf_op jit(solution)/shard_map/all_gather | solution.py:246
  42.9 105.1 %all-gather.19.cloned.1.call-start = ((), (), s32[]{:S(2)}) async-start(), calls=%async_computation.19 | async-start | bytes 2621440 | tf_op jit(solution)/shard_map/all_gather | solution.py:245
  76.5 123.4 %all-gather.29.cloned.1.call-start = ((), (), s32[]{:S(2)}) async-start(), calls=%async_computation.24 | async-start | bytes 1622016 | tf_op jit(solution)/shard_map/all_gather | solution.py:237
  77.2 123.2 %all-gather.33.cloned.1.call-start = ((), (), s32[]{:S(2)}) async-start(), calls=%async_computation.26 | async-start | bytes 1622016 | tf_op jit(solution)/shard_map/all_gather | solution.py:238
  77.8 162.6 %all-gather.37.cloned.1.call-start = ((), (), s32[]{:S(2)}) async-start(), calls=%async_computation.28 | async-start | bytes 1622016 | tf_op jit(solution)/shard_map/all_gather | solution.py:239
  78.4 184.6 %all-gather.17.cloned.1.call-start = ((), (), s32[]{:S(2)}) async-start(), calls=%async_computation.18 | async-start | bytes 2621440 | tf_op jit(solution)/shard_map/all_gather | solution.py:244
  112.1 282.2 %all-gather.43.cloned.1.call-start = ((), (), s32[]{:S(2)}) async-start(), calls=%async_computation.31 | async-start | bytes 9437184 | tf_op jit(solution)/shard_map/all_gather | solution.py:264
  147.9 371.7 %all-gather.41.cloned.1.call-start = ((), (), s32[]{:S(2)}) async-start(), calls=%async_computation.30 | async-start | bytes 9437184 | tf_op jit(solution)/shard_map/all_gather | solution.py:263
  153.6 758.9 %all-gather.25.cloned.1.call-start = ((), (), s32[]{:S(2)}) async-start(), calls=%async_computation.22 | async-start | bytes 9437184 | tf_op jit(solution)/shard_map/all_gather | solution.py:264
  159.5 753.6 %all-gather.21.cloned.1.call-start = ((), (), s32[]{:S(2)}) async-start(), calls=%async_computation.20 | async-start | bytes 9437184 | tf_op jit(solution)/shard_map/all_gather | solution.py:263
  165.3 1142.2 %all-gather.27.cloned.1.call-start = ((), (), s32[]{:S(2)}) async-start(), calls=%async_computation.23 | async-start | bytes 2621440 | tf_op jit(solution)/shard_map/all_gather | solution.py:247
  199.8 1117.0 %all-gather.31.cloned.1.call-start = ((), (), s32[]{:S(2)}) async-start(), calls=%async_computation.25 | async-start | bytes 7208960 | tf_op jit(solution)/shard_map/all_gather | solution.py:248
  200.4 1135.0 %all-gather.35.cloned.1.call-start = ((), (), s32[]{:S(2)}) async-start(), calls=%async_computation.27 | async-start | bytes 7208960 | tf_op jit(solution)/shard_map/all_gather | solution.py:249
  201.2 1160.6 %all-gather.39.cloned.1.call-start = ((), (), s32[]{:S(2)}) async-start(), calls=%async_computation.29 | async-start | bytes 7208960 | tf_op jit(solution)/shard_map/all_gather | solution.py:250
  240.4 2746.2 %reduce-scatter.19.cloned.1.call-start = ((), (), s32[]{:S(2)}) async-start(), calls=%async_computation.32 | async-start | bytes 18874368 | tf_op jit(solution)/shard_map/reduce_scatter | solution.py:434
  258.5 15.2 collective-permute-start.3
  259.9 33.4 collective-permute-start.2
  260.6 46.8 %collective-permute-start.1 = (bf16[256,1024]{1,0:T(8,128)(2,1)}, bf16[256,1024]{1,0:T(8,128)(2,1)}, u32[]{:S(2)}, u32[]{:S(2)}) collective-permute-start(bf16[256,1024]{1,0:T(8,128)(2,1)} %slice.343), channel_id=1, source_target_pairs={{0,1},{1,0},{2,3},{3,2},{4,5},{5,4},{6,7},{7,6},{8,9},{9,8},{10,11... | collective-permute-start | bytes 1572872 | tf_op jit(solution)/shard_map/ppermute | solution.py:11
  262.0 55.3 %collective-permute-start = (bf16[256,1024]{1,0:T(8,128)(2,1)}, bf16[256,1024]{1,0:T(8,128)(2,1)}, u32[]{:S(2)}, u32[]{:S(2)}) collective-permute-start(bf16[256,1024]{1,0:T(8,128)(2,1)} %slice.341), channel_id=1, source_target_pairs={{0,1},{1,0},{2,3},{3,2},{4,5},{5,4},{6,7},{7,6},{8,9},{9,8},{10,11... | collective-permute-start | bytes 1572872 | tf_op jit(solution)/shard_map/ppermute | solution.py:11
  914.5 393.0 %copy-start.15 = (bf16[512,1024]{1,0:T(8,128)(2,1)S(1)}, bf16[512,1024]{1,0:T(8,128)(2,1)}, u32[]{:S(2)}) copy-start(bf16[512,1024]{1,0:T(8,128)(2,1)} %copy-done.14) | copy-start | bytes 3145732
  914.5 393.0 %copy-start.32 = (bf16[256,1024]{1,0:T(8,128)(2,1)S(1)}, bf16[256,1024]{1,0:T(8,128)(2,1)}, u32[]{:S(2)}) copy-start(bf16[256,1024]{1,0:T(8,128)(2,1)} %copy-done.31) | copy-start | bytes 1572868
  1313.9 169.6 %copy-start.10 = (f32[768,1024]{1,0:T(8,128)}, f32[768,1024]{1,0:T(8,128)S(1)}, u32[]{:S(2)}) copy-start(f32[768,1024]{1,0:T(8,128)S(1)} %get-tuple-element.1660) | copy-start | bytes 9437188
  2183.9 978.0 %reduce-scatter.23.cloned.1.call-start = ((), (), s32[]{:S(2)}) async-start(), calls=%async_computation.34 | async-start | bytes 18874368 | tf_op jit(solution)/shard_map/reduce_scatter | solution.py:434
  2878.6 572.4 %reduce-scatter.21.cloned.1.call-start = ((), (), s32[]{:S(2)}) async-start(), calls=%async_computation.33 | async-start | bytes 18874368 | tf_op jit(solution)/shard_map/reduce_scatter | solution.py:435
  2879.2 857.5 %reduce-scatter.25.cloned.1.call-start = ((), (), s32[]{:S(2)}) async-start(), calls=%async_computation.35 | async-start | bytes 18874368 | tf_op jit(solution)/shard_map/reduce_scatter | solution.py:435
  2879.8 889.9 %reduce-scatter.39.cloned.1.call-start = ((), (), s32[]{:S(2)}) async-start(), calls=%async_computation.42 | async-start | bytes 2621440 | tf_op jit(solution)/shard_map/reduce_scatter | solution.py:477
  2887.4 916.2 %reduce-scatter.27.cloned.1.call-start = ((), (), s32[]{:S(2)}) async-start(), calls=%async_computation.36 | async-start | bytes 2621440 | tf_op jit(solution)/shard_map/reduce_scatter | solution.py:468
  2895.1 966.1 %reduce-scatter.51.cloned.1.call-start = ((), (), s32[]{:S(2)}) async-start(), calls=%async_computation.48 | async-start | bytes 7208960 | tf_op jit(solution)/shard_map/reduce_scatter | solution.py:486
  2911.5 1007.2 %reduce-scatter.47.cloned.1.call-start = ((), (), s32[]{:S(2)}) async-start(), calls=%async_computation.46 | async-start | bytes 7208960 | tf_op jit(solution)/shard_map/reduce_scatter | solution.py:483
  2934.4 1041.8 %reduce-scatter.43.cloned.1.call-start = ((), (), s32[]{:S(2)}) async-start(), calls=%async_computation.44 | async-start | bytes 7208960 | tf_op jit(solution)/shard_map/reduce_scatter | solution.py:480
  2956.8 1053.9 %reduce-scatter.31.cloned.1.call-start = ((), (), s32[]{:S(2)}) async-start(), calls=%async_computation.38 | async-start | bytes 2621440 | tf_op jit(solution)/shard_map/reduce_scatter | solution.py:471
  2959.1 16.1 collective-permute-start.4
  2962.1 23.5 collective-permute-start.6
  2986.6 177.2 %copy-start.16 = (bf16[512,1024]{1,0:T(8,128)(2,1)S(1)}, bf16[512,1024]{1,0:T(8,128)(2,1)}, u32[]{:S(2)}) copy-start(bf16[512,1024]{1,0:T(8,128)(2,1)} %copy-done.14) | copy-start | bytes 3145732
  2986.6 177.2 %copy-start.33 = (bf16[256,1024]{1,0:T(8,128)(2,1)S(1)}, bf16[256,1024]{1,0:T(8,128)(2,1)}, u32[]{:S(2)}) copy-start(bf16[256,1024]{1,0:T(8,128)(2,1)} %copy-done.31) | copy-start | bytes 1572868
  2986.6 177.2 %copy-start.79 = (bf16[256,1024]{1,0:T(8,128)(2,1)S(1)}, bf16[256,1024]{1,0:T(8,128)(2,1)}, u32[]{:S(2)}) copy-start(bf16[256,1024]{1,0:T(8,128)(2,1)} %add_convert_fusion.10) | copy-start | bytes 1572868
  3169.4 875.3 %reduce-scatter.35.cloned.1.call-start = ((), (), s32[]{:S(2)}) async-start(), calls=%async_computation.40 | async-start | bytes 2621440 | tf_op jit(solution)/shard_map/reduce_scatter | solution.py:474
  3171.3 25.2 collective-permute-start.5
  3173.0 35.1 collective-permute-start.7
  3209.1 529.4 %copy-start.17 = (bf16[512,1024]{1,0:T(8,128)(2,1)S(1)}, bf16[512,1024]{1,0:T(8,128)(2,1)}, u32[]{:S(2)}) copy-start(bf16[512,1024]{1,0:T(8,128)(2,1)} %copy-done.14) | copy-start | bytes 3145732
  3209.1 529.4 %copy-start.34 = (bf16[256,1024]{1,0:T(8,128)(2,1)S(1)}, bf16[256,1024]{1,0:T(8,128)(2,1)}, u32[]{:S(2)}) copy-start(bf16[256,1024]{1,0:T(8,128)(2,1)} %copy-done.31) | copy-start | bytes 1572868
  3745.6 366.8 %reduce-scatter.41.cloned.1.call-start = ((), (), s32[]{:S(2)}) async-start(), calls=%async_computation.43 | async-start | bytes 1179648 | tf_op jit(solution)/shard_map/reduce_scatter | solution.py:510
  3771.8 406.8 %reduce-scatter.29.cloned.1.call-start = ((), (), s32[]{:S(2)}) async-start(), calls=%async_computation.37 | async-start | bytes 1179648 | tf_op jit(solution)/shard_map/reduce_scatter | solution.py:507
  3805.9 448.7 %reduce-scatter.53.cloned.1.call-start = ((), (), s32[]{:S(2)}) async-start(), calls=%async_computation.49 | async-start | bytes 3244032 | tf_op jit(solution)/shard_map/reduce_scatter | solution.py:513
  3864.4 466.2 %reduce-scatter.49.cloned.1.call-start = ((), (), s32[]{:S(2)}) async-start(), calls=%async_computation.47 | async-start | bytes 3244032 | tf_op jit(solution)/shard_map/reduce_scatter | solution.py:512
  3922.0 484.5 %reduce-scatter.45.cloned.1.call-start = ((), (), s32[]{:S(2)}) async-start(), calls=%async_computation.45 | async-start | bytes 3244032 | tf_op jit(solution)/shard_map/reduce_scatter | solution.py:511
  3979.5 494.2 %reduce-scatter.33.cloned.1.call-start = ((), (), s32[]{:S(2)}) async-start(), calls=%async_computation.39 | async-start | bytes 1179648 | tf_op jit(solution)/shard_map/reduce_scatter | solution.py:508
  4012.9 527.3 %reduce-scatter.37.cloned.1.call-start = ((), (), s32[]{:S(2)}) async-start(), calls=%async_computation.41 | async-start | bytes 1179648 | tf_op jit(solution)/shard_map/reduce_scatter | solution.py:509
  (197 other events, 2837.2 us)
Sparse Core Ops, SparseCore 0:
  43.0 23.8 all-gather.22
  76.6 24.0 all-gather.18
  102.8 43.6 all-gather.28
  148.4 47.2 all-gather.32
  197.6 42.7 all-gather.36
  241.8 21.2 all-gather.16
  265.2 129.1 all-gather.42
  396.5 123.1 all-gather.40
  521.7 123.1 all-gather.24
  646.9 123.0 all-gather.20
  771.6 21.0 all-gather.26
  794.1 43.4 all-gather.30
  839.1 43.4 all-gather.34
  884.0 43.3 all-gather.38
  2184.0 283.3 reduce-scatter.18
  2878.7 283.1 reduce-scatter.22
  3165.6 285.3 reduce-scatter.20
  3455.1 281.5 reduce-scatter.24
  3739.2 30.4 reduce-scatter.38
  3772.2 31.3 reduce-scatter.26
  3806.2 54.8 reduce-scatter.50
  3863.8 54.8 reduce-scatter.46
  3921.3 54.8 reduce-scatter.42
  3979.3 31.3 reduce-scatter.30
  4013.3 31.4 reduce-scatter.34
  4048.9 63.4 reduce-scatter.40
  4116.2 62.3 reduce-scatter.28
  4183.2 71.3 reduce-scatter.52
  4259.2 71.3 reduce-scatter.48
  4335.0 71.5 reduce-scatter.44
  4411.0 62.6 reduce-scatter.32
  4477.6 62.4 reduce-scatter.36
where the time goes:
time: 4570 us; the launch traced here: 4550 us
  waiting for transfers between devices  1720 us (38%)
  other arithmetic  1270 us (28%)
  matrix products  1150 us (25%)
  blocking collectives  235 us (5%)
  local copies, waits for them, and re-layouts  131 us (3%)
    reduce_or x32, other arithmetic, picked_table(): jnp.any(chosen[:, :, None] == jnp.arange(cache_len, dtype=jnp.int32)[None...  654 us
    reduce_scatter x2, waiting for transfers between devices, body(): lax.psum_scatter(prompt_value_grad, 'seq', scatter_dimension=0, tiled=True)  525 us
    dot_general x158, matrix products, along_cols(): lax.dot_general(former, latter, (((1,), (1,)), ((), ())), preferred_eleme...  511 us
    dot_general x110, matrix products, product(): return jnp.dot(former, latter, preferred_element_type=jnp.float32)  354 us
    dot_general x78, matrix products, along_rows(): lax.dot_general(former, latter, (((0,), (0,)), ((), ())), preferred_eleme...  282 us
    convert_element_type x16, other arithmetic, one_head(): weights = probs.astype(jnp.bfloat16)  199 us
    reduce_scatter x2, waiting for transfers between devices, body(): lax.psum_scatter(prompt_key_grad, 'seq', scatter_dimension=0, tiled=True)  172 us
    reduce_sum x16, other arithmetic, one_head(): row_delta = jnp.sum(probs * grad_all, axis=1, keepdims=True)  161 us
  transfers between devices with their start and end apart: 40, of which 29 were waited for; matrix products, arithmetic and copies ran while one was open for 38% of the time, Pallas kernels for 0%

commit v1 on v0

v1 whole, which is shorter than its diff:
```python
import functools

import jax
import jax.numpy as jnp
from jax import lax
from jax.experimental import pallas as pl
from jax.experimental.pallas import tpu as pltpu
from jax.sharding import PartitionSpec as P

epsilon = 1e-06
masked_score = -1e30
log2e = 1.4426950408889634
low = jnp.bfloat16
wide = jnp.float32
lanes = 128
hint = 0.25


def norm_rows(values, scaling):
    return values * lax.rsqrt(jnp.mean(values * values, axis=-1, keepdims=True) + epsilon) * scaling


def norm_back(values, scaling, upstream):
    factor = lax.rsqrt(jnp.mean(values * values, axis=-1, keepdims=True) + epsilon)
    scaled = values * factor
    weighted = upstream * scaling
    inward = factor * (weighted - scaled * jnp.mean(weighted * scaled, axis=-1, keepdims=True))
    return (inward, jnp.sum(upstream * scaled, axis=0))


def contract(former, latter, former_dim, latter_dim):
    return lax.dot_general(
        former,
        latter,
        (((former_dim,), (latter_dim,)), ((), ())),
        preferred_element_type=wide,
    )


def product(former, latter):
    return contract(former, latter, 1, 0)


def along_rows(former, latter):
    return contract(former, latter, 0, 0)


def along_cols(former, latter):
    return contract(former, latter, 1, 1)


def part_list(sizes):
    first = -(-sizes.prompt // lanes)
    return ((0, sizes.prompt, 0), (sizes.prompt, sizes.half, first))


class Sizes:
    def __init__(self, heads, blocks, prompt, half, cache, picks, replies):
        self.heads = heads
        self.blocks = blocks
        self.prompt = prompt
        self.half = half
        self.cache = cache
        self.picks = picks
        self.rows = prompt + half
        self.own_prompt = heads * prompt
        self.all_prompt = self.own_prompt * blocks
        self.all_reply = heads * half
        self.block = 2 * half
        self.queries = self.own_prompt + self.all_reply
        self.keys = self.all_prompt + self.all_reply
        self.replies = replies


def unpack_row(stats, row, size):
    if size < lanes:
        return stats[row : row + 1, :size]
    return jnp.concatenate([stats[row + i : row + i + 1, :] for i in range(size // lanes)], axis=1)


def pack_row(ref, row, values):
    size = values.shape[1]
    if size < lanes:
        values = jnp.concatenate([values, jnp.zeros((1, lanes - size), values.dtype)], axis=1)
        size = lanes
    for i in range(size // lanes):
        ref[row + i : row + i + 1, :] = values[:, i * lanes : (i + 1) * lanes]


def three_parts(stats):
    first = stats.astype(low).astype(wide)
    rest = stats - first
    second = rest.astype(low).astype(wide)
    return [first, second, rest - second]


def three_sum(aux):
    aux = aux.astype(wide)
    return aux[0:8] + aux[8:16] + aux[16:24]


def row_to_column(row):
    return jnp.broadcast_to(row, (lanes, row.shape[1])).T


def slot_place(index, half):
    return 2 * (index % half) + index // half


def self_mask(shape, query_axis, half, live):
    query = slot_place(lax.broadcasted_iota(jnp.int32, shape, query_axis), half)
    key = slot_place(lax.broadcasted_iota(jnp.int32, shape, 1 - query_axis), half)
    return (key <= query) & (key < live)


def causal_mask(shape, query_axis):
    query = lax.broadcasted_iota(jnp.int32, shape, query_axis)
    key = lax.broadcasted_iota(jnp.int32, shape, 1 - query_axis)
    return key <= query


def rows_at(index, size):
    return pl.ds(pl.multiple_of(index * size, size), size)


def copy_tokens(sz, own_block, query_in, pair_in, extra, queries, keys, values, sems):
    pr, hr = sz.prompt, sz.half
    moves = []
    for j in range(sz.heads):
        key_start = pl.multiple_of(own_block * sz.own_prompt + j * pr, pr)
        spots = (
            (0, pr, j * pr, key_start),
            (pr, hr, sz.own_prompt + j * hr, sz.all_prompt + j * hr),
        )
        for row, count, query_at, key_at in spots:
            rows = pl.ds(row, count)
            moves.append((query_in.at[j, rows], queries.at[pl.ds(query_at, count)]))
            for lane, ref in ((0, keys), (1, values)):
                source = pair_in.at[j, rows, pl.ds(lane * lanes, lanes)]
                moves.append((source, ref.at[pl.ds(key_at, count), pl.ds(0, lanes)]))
    for e in range(1, sz.blocks):
        start = pl.multiple_of((own_block ^ e) * sz.own_prompt, sz.own_prompt)
        for lane, ref in ((0, keys), (1, values)):
            source = extra[e - 1].at[:, pl.ds(lane * lanes, lanes)]
            moves.append((source, ref.at[pl.ds(start, sz.own_prompt), pl.ds(0, lanes)]))
    return [pltpu.make_async_copy(*move, sems.at[i]) for i, move in enumerate(moves)]


def token_moves(sz):
    return 6 * sz.heads + 2 * (sz.blocks - 1)


def run_all(copies):
    for copy in copies:
        copy.start()
    for copy in copies:
        copy.wait()


def attend_kernel(sz, meta, *refs):
    n, extras = sz.heads, sz.blocks - 1
    query_in, pair_in, extra = refs[0], refs[1], refs[2 : 2 + extras]
    out, queries, keys, values, scores, total, mixed, sums, packed, aux, sems = refs[2 + extras :]
    own_block = meta[1]
    size = sz.block
    scale = float(lanes**-0.5 * log2e)
    copies = copy_tokens(sz, own_block, query_in, pair_in, extra, queries, keys, values, sems)
    for copy in copies:
        copy.start()
    values[:, lanes:] = jnp.ones_like(values[:, lanes:])
    for copy in copies:
        copy.wait()
    prompt_blocks = sz.all_prompt // size
    own_blocks = sz.own_prompt // size
    offset = own_block * own_blocks

    def widest(tile):
        best = tile[:, 0:lanes]
        for t in range(1, size // lanes):
            best = jnp.maximum(best, tile[:, t * lanes : (t + 1) * lanes])
        return best

    def one(query_index, full_blocks, last_block, mask):
        query = queries[rows_at(query_index, size), :]
        tile = jnp.where(mask, along_cols(query, keys[rows_at(last_block, size), :]), masked_score)
        scores[prompt_blocks] = tile

        def first_pass(index, best):
            tile = along_cols(query, keys[rows_at(index, size), :])
            scores[index] = tile
            return jnp.maximum(best, widest(tile))

        best = lax.fori_loop(0, full_blocks, first_pass, widest(tile))
        best = jnp.max(best, axis=1, keepdims=True) * scale

        def weights(index):
            return jnp.exp2(scores[index] * scale - best).astype(low)

        total[...] = product(weights(prompt_blocks), values[rows_at(last_block, size), :])

        def second_pass(index, carried):
            total[...] += product(weights(index), values[rows_at(index, size), :])
            return carried

        lax.fori_loop(0, full_blocks, second_pass, 0)
        weight = total[:, lanes:]
        mixed[rows_at(query_index, size), :] = (total[:, :lanes] / weight).astype(low)
        sums[:, rows_at(query_index, size)] = (best + jnp.log2(weight)).T[0:8, :]

    @pl.loop(0, own_blocks)
    def _(index):
        one(index, offset + index, offset + index, causal_mask((size, size), 0))

    @pl.loop(0, sz.all_reply // size)
    def _(index):
        live = meta[2 + own_block * (sz.all_reply // size) + index]
        mask = self_mask((size, size), 0, sz.half, live)
        one(own_blocks + index, prompt_blocks, prompt_blocks + index, mask)

    packed[...] = jnp.zeros_like(packed)
    for j in range(n):
        for begin, count, row in (
            (j * sz.prompt, sz.prompt, 0),
            (sz.own_prompt + j * sz.half, sz.half, -(-sz.prompt // lanes)),
        ):
            if count < lanes:
                tile = sums[:, begin // lanes * lanes : begin // lanes * lanes + lanes]
                if begin % lanes:
                    tile = pltpu.roll(tile, lanes - begin % lanes, 1)
                packed[j, row : row + 1, :] = tile[0:1]
            else:
                for i in range(count // lanes):
                    at = begin + i * lanes
                    packed[j, row + i : row + i + 1, :] = sums[0:1, at : at + lanes]
    pr, hr = sz.prompt, sz.half
    copies = []
    for j in range(n):
        parts = three_parts(packed[j])
        aux[j] = jnp.concatenate(parts + [jnp.zeros_like(parts[0])], axis=0).astype(low)
        spots = (
            (mixed.at[pl.ds(j * pr, pr)], 0, pr),
            (mixed.at[pl.ds(sz.own_prompt + j * hr, hr)], pr, hr),
            (aux.at[j], pr + hr, 32),
        )
        for source, row, count in spots:
            copies.append(
                pltpu.make_async_copy(source, out.at[j, pl.ds(row, count)], sems.at[len(copies)])
            )
    run_all(copies)


def cost_hint(flops, exps, moved):
    return pl.CostEstimate(
        flops=int(flops * hint), transcendentals=int(exps * hint), bytes_accessed=int(moved * hint)
    )


def whole_vmem():
    return pl.BlockSpec(memory_space=pltpu.VMEM)


def pair_count(sz):
    prompt = sz.own_prompt * (sz.all_prompt + sz.own_prompt) // 2
    return prompt + sz.all_reply * (sz.all_prompt + sz.block)


def in_place():
    return pl.BlockSpec(memory_space=pl.ANY)


def attend(sz, meta, queries, pairs, extra):
    n = sz.heads
    cost = cost_hint(12 * lanes * pair_count(sz), pair_count(sz), 8 << 20)
    return pl.pallas_call(
        functools.partial(attend_kernel, sz),
        out_shape=jax.ShapeDtypeStruct((n, sz.rows + 32, lanes), low),
        grid_spec=pltpu.PrefetchScalarGridSpec(
            num_scalar_prefetch=1,
            grid=(),
            in_specs=[in_place()] * (2 + len(extra)),
            out_specs=in_place(),
            scratch_shapes=[
                pltpu.VMEM((sz.queries, lanes), low),
                pltpu.VMEM((sz.keys, lanes), low),
                pltpu.VMEM((sz.keys, 2 * lanes), low),
                pltpu.VMEM((sz.all_prompt // sz.block + 1, sz.block, sz.block), wide),
                pltpu.VMEM((sz.block, 2 * lanes), wide),
                pltpu.VMEM((sz.queries, lanes), low),
                pltpu.VMEM((8, sz.queries), wide),
                pltpu.VMEM((n, 8, lanes), wide),
                pltpu.VMEM((n, 32, lanes), low),
                pltpu.SemaphoreType.DMA((token_moves(sz),)),
            ],
        ),
        compiler_params=pltpu.CompilerParams(vmem_limit_bytes=36 << 20),
        cost_estimate=cost,
        name="attend",
    )(meta, queries, pairs, *extra)


def attend_back_kernel(sz, meta, *refs):
    n, extras = sz.heads, sz.blocks - 1
    query_in, pair_in, messages = refs[:3]
    extra, refs = refs[3 : 3 + extras], refs[3 + extras :]
    query_out, pair_out, refs = refs[0], refs[1], refs[2:]
    partial = None
    if extras:
        partial, refs = refs[0], refs[1:]
    queries, keys, values, upstream, aux, stats, *refs = refs
    query_grad, key_grad, value_grad, low_query, low_pair, sems = refs
    own_block = meta[1]
    pr, hr, size = sz.prompt, sz.half, sz.block
    scale = float(lanes**-0.5 * log2e)
    plain_scale = float(lanes**-0.5)
    copies = copy_tokens(sz, own_block, query_in, pair_in, extra, queries, keys, values, sems)
    for j in range(n):
        spots = (
            (upstream.at[pl.ds(j * pr, pr)], 0, pr),
            (upstream.at[pl.ds(sz.own_prompt + j * hr, hr)], pr, hr),
            (aux.at[j], pr + hr, 48),
        )
        for target, row, count in spots:
            source = messages.at[j, pl.ds(row, count)]
            copies.append(pltpu.make_async_copy(source, target, sems.at[len(copies)]))
    for copy in copies:
        copy.start()
    key_grad[...] = jnp.zeros_like(key_grad)
    value_grad[...] = jnp.zeros_like(value_grad)
    query_grad[...] = jnp.zeros_like(query_grad)
    for copy in copies:
        copy.wait()
    first_row = -(-pr // lanes)
    for s in range(2):
        rows = [three_sum(aux[j, 24 * s : 24 * s + 24, :]) for j in range(n)]
        for j in range(n):
            for i in range(hr // lanes):
                start = sz.own_prompt + j * hr + i * lanes
                stats[s : s + 1, start : start + lanes] = rows[j][first_row + i : first_row + i + 1]
            for i in range(pr // lanes):
                start = j * pr + i * lanes
                stats[s : s + 1, start : start + lanes] = rows[j][i : i + 1]
        if pr < lanes:
            group = lanes // pr
            lane = lax.broadcasted_iota(jnp.int32, (8, lanes), 1)
            for t in range(n // group):
                tile = rows[t * group]
                for u in range(1, group):
                    other = pltpu.roll(rows[t * group + u], u * pr, 1)
                    tile = jnp.where(lane >= u * pr, other, tile)
                stats[s : s + 1, t * lanes : (t + 1) * lanes] = tile[0:1]
    prompt_blocks = sz.all_prompt // size
    own_blocks = sz.own_prompt // size
    reply_blocks = sz.all_reply // size
    offset = own_block * own_blocks

    def step(key_index, query_index, mask=None):
        at_key, at_query = rows_at(key_index, size), rows_at(query_index, size)
        key, value = keys[at_key, :], values[at_key, :]
        query, grad = queries[at_query, :], upstream[at_query, :]
        logits = along_cols(key, query) * scale - stats[0:1, at_query]
        if mask is not None:
            logits = jnp.where(mask, logits, masked_score)
        probs = jnp.exp2(logits)
        slope = (probs * (along_cols(value, grad) - stats[1:2, at_query])).astype(low)
        value_grad[at_key, :] += product(probs.astype(low), grad)
        key_grad[at_key, :] += product(slope, query)
        query_grad[at_query, :] += along_rows(slope, key)

    @pl.loop(0, prompt_blocks)
    def _(key_index):
        own = key_index - offset

        @pl.when((own >= 0) & (own < own_blocks))
        def _():
            step(key_index, own, causal_mask((size, size), 1))

        @pl.loop(jnp.clip(own + 1, 0, own_blocks), own_blocks + reply_blocks)
        def _(query_index):
            step(key_index, query_index)

    @pl.loop(0, reply_blocks)
    def _(index):
        live = meta[2 + own_block * reply_blocks + index]
        step(prompt_blocks + index, own_blocks + index, self_mask((size, size), 1, hr, live))

    if extras:
        partial[:, 0:lanes] = key_grad[0 : sz.all_prompt, :] * plain_scale
        partial[:, lanes:] = value_grad[0 : sz.all_prompt, :]
    copies = []
    for j in range(n):
        spots = (
            (0, pr, j * pr, own_block * sz.own_prompt + j * pr),
            (pr, hr, sz.own_prompt + j * hr, sz.all_prompt + j * hr),
        )
        for row, count, query_at, key_at in spots:
            query_at = pl.ds(pl.multiple_of(query_at, count), count)
            key_at = pl.ds(pl.multiple_of(key_at, count), count)
            rows = slice(row, row + count)
            low_query[j, rows, :] = (query_grad[query_at, :] * plain_scale).astype(low)
            low_pair[j, rows, 0:lanes] = (key_grad[key_at, :] * plain_scale).astype(low)
            low_pair[j, rows, lanes:] = value_grad[key_at, :].astype(low)
        for source, target in ((low_query, query_out), (low_pair, pair_out)):
            sem = sems.at[len(copies)]
            copies.append(pltpu.make_async_copy(source.at[j], target.at[j], sem))
            copies[-1].start()
    for copy in copies:
        copy.wait()


def attend_back(sz, meta, queries, pairs, messages, extra):
    n = sz.heads
    out_shape = [jax.ShapeDtypeStruct((n, sz.rows, k * lanes), low) for k in (1, 2)]
    out_specs = [in_place()] * 2
    if extra:
        out_shape.append(jax.ShapeDtypeStruct((sz.all_prompt, 2 * lanes), wide))
        out_specs.append(whole_vmem())
    cost = cost_hint(20 * lanes * pair_count(sz), pair_count(sz), 14 << 20)
    return pl.pallas_call(
        functools.partial(attend_back_kernel, sz),
        out_shape=out_shape,
        grid_spec=pltpu.PrefetchScalarGridSpec(
            num_scalar_prefetch=1,
            grid=(),
            in_specs=[in_place()] * (3 + len(extra)),
            out_specs=out_specs,
            scratch_shapes=[
                pltpu.VMEM((sz.queries, lanes), low),
                pltpu.VMEM((sz.keys, lanes), low),
                pltpu.VMEM((sz.keys, lanes), low),
                pltpu.VMEM((sz.queries, lanes), low),
                pltpu.VMEM((n, 48, lanes), low),
                pltpu.VMEM((8, sz.queries), wide),
                pltpu.VMEM((sz.queries, lanes), wide),
                pltpu.VMEM((sz.keys, lanes), wide),
                pltpu.VMEM((sz.keys, lanes), wide),
                pltpu.VMEM((n, sz.rows, lanes), low),
                pltpu.VMEM((n, sz.rows, 2 * lanes), low),
                pltpu.SemaphoreType.DMA((token_moves(sz) + 3 * n,)),
            ],
        ),
        compiler_params=pltpu.CompilerParams(vmem_limit_bytes=40 << 20),
        cost_estimate=cost,
        name="attend_back",
    )(meta, queries, pairs, messages, *extra)


def fixed(shape):
    return pl.BlockSpec(
        shape, lambda d, meta: (0,) * len(shape), pipeline_mode=pl.Buffered(1)
    )


def per_step(shape):
    return pl.BlockSpec((None,) + shape, lambda d, meta: (d,) + (0,) * len(shape))


def by_head(rows):
    return pl.BlockSpec((rows, lanes), lambda d, meta: (0, d))


def of_micro(micro, rows, width):
    return pl.BlockSpec(
        (None, None, rows, width),
        lambda d, meta: (micro, 0, 0, 0),
        pipeline_mode=pl.Buffered(1),
    )


def query_weights(width, per):
    return pl.BlockSpec((lanes, width), lambda d, meta: (d % per, d // per))


def pair_weights(width, per):
    return pl.BlockSpec((2 * lanes, width), lambda d, meta: (per // 2 + d % per, d // per))


def call(kernel, name, steps, meta, ins, outs, scratch=(), flops=0, exps=0, vmem=32, aliases=None):
    arrays, in_specs = zip(*ins)
    out_shape, out_specs = zip(*outs)
    sized = list(arrays) + list(out_shape)
    return pl.pallas_call(
        kernel,
        out_shape=list(out_shape),
        grid_spec=pltpu.PrefetchScalarGridSpec(
            num_scalar_prefetch=1,
            grid=(steps,),
            in_specs=list(in_specs),
            out_specs=list(out_specs),
            scratch_shapes=list(scratch),
        ),
        input_output_aliases=aliases or {},
        compiler_params=pltpu.CompilerParams(vmem_limit_bytes=vmem << 20),
        cost_estimate=cost_hint(flops, exps, sum(a.size * a.dtype.itemsize for a in sized)),
        name=name,
    )(meta, *arrays)


def shaped(shape, dtype):
    return jax.ShapeDtypeStruct(shape, dtype)


def project_kernel(
    sz, meta, prompt_ref, reply_ref, gain_ref, query_w, pair_w, query_out, pair_out, normed_ref
):
    @pl.when(pl.program_id(0) == 0)
    def _():
        for ref, begin, count in ((prompt_ref, 0, sz.prompt), (reply_ref, sz.prompt, sz.half)):
            values = norm_rows(ref[...].astype(wide), gain_ref[...])
            normed_ref[begin : begin + count, :] = values.astype(low)

    query_out[...] = along_cols(normed_ref[...], query_w[...]).astype(low)
    pair_out[...] = along_cols(normed_ref[...], pair_w[...]).astype(low)


def project(sz, meta, micro, prompt_in, reply_in, gain, weights):
    width = prompt_in.shape[3]
    per = weights.shape[0] // (3 * lanes)
    n = sz.heads
    return call(
        functools.partial(project_kernel, sz),
        "project",
        n,
        meta,
        [
            (prompt_in, of_micro(micro, sz.prompt, width)),
            (reply_in, of_micro(micro, sz.half, width)),
            (gain, fixed((1, width))),
            (weights, query_weights(width, per)),
            (weights, pair_weights(width, per)),
        ],
        [
            (shaped((n, sz.rows, lanes), low), per_step((sz.rows, lanes))),
            (shaped((n, sz.rows, 2 * lanes), low), per_step((sz.rows, 2 * lanes))),
            (shaped((sz.rows, width), low), fixed((sz.rows, width))),
        ],
        flops=6 * sz.rows * width * lanes * n,
    )


def words_kernel(sz, meta, picks_prompt, picks_reply, words_prompt, words_reply):
    for picks, words in ((picks_prompt, words_prompt), (picks_reply, words_reply)):
        chosen = picks[...].T
        place = chosen >> 5
        bit = jnp.left_shift(jnp.ones_like(chosen), chosen & 31)
        for k in range(sz.cache // 32):
            words[k : k + 1, :] = jnp.sum(jnp.where(place == k, bit, 0), axis=0, keepdims=True)


def picks_to_words(sz, meta, micro, picks_prompt, picks_reply):
    n, count = sz.heads, sz.cache // 32

    def spec(rows):
        return pl.BlockSpec((None, None, None, rows, sz.picks), lambda d, meta: (micro, 0, d, 0, 0))

    return pl.pallas_call(
        functools.partial(words_kernel, sz),
        out_shape=[shaped((n, count, sz.prompt), jnp.int32), shaped((n, count, sz.half), jnp.int32)],
        grid_spec=pltpu.PrefetchScalarGridSpec(
            num_scalar_prefetch=1,
            grid=(n,),
            in_specs=[spec(sz.prompt), spec(sz.half)],
            out_specs=[per_step((count, sz.prompt)), per_step((count, sz.half))],
        ),
        cost_estimate=cost_hint(0, 0, 4 * n * sz.rows * sz.picks * 3),
        name="picks_to_words",
    )(meta, picks_prompt, picks_reply)


def word_bits(words, count):
    shape = (32, words.shape[1])
    shifts = lax.broadcasted_iota(jnp.int32, shape, 0)
    tiles = [
        lax.shift_right_logical(jnp.broadcast_to(words[k : k + 1, :], shape), shifts) & 1
        for k in range(count)
    ]
    return jnp.concatenate(tiles, axis=0) == 1


def cache_kernel(sz, meta, chunk, words_prompt, words_reply, cache_key, cache_value, mixed, sums):
    scale = float(lanes**-0.5 * log2e)
    sums[...] = jnp.zeros_like(sums)
    for (begin, count, row), words in zip(part_list(sz), (words_prompt, words_reply)):
        allowed = word_bits(words[...], sz.cache // 32)
        logits = along_cols(cache_key[...], chunk[begin : begin + count, :]) * scale
        logits = jnp.where(allowed, logits, masked_score)
        best = jnp.max(logits, axis=0, keepdims=True)
        exponent = jnp.exp2(logits - best)
        weight = jnp.sum(exponent, axis=0, keepdims=True)
        probs = (exponent / weight).astype(low)
        mixed[begin : begin + count, :] = along_rows(probs, cache_value[...])
        pack_row(sums, row, best + jnp.log2(weight))


def word_ins(sz, words):
    count = sz.cache // 32
    return [(words[0], per_step((count, sz.prompt))), (words[1], per_step((count, sz.half)))]


def queries_of(sz, chunks):
    return (chunks, pl.BlockSpec((None, sz.rows, lanes), lambda d, meta: (d, 0, 0)))


def cache_forward(sz, meta, chunks, words, cache_key, cache_value):
    n = sz.heads
    pairs = n * sz.rows * sz.cache
    return call(
        functools.partial(cache_kernel, sz),
        "cache_forward",
        n,
        meta,
        [queries_of(sz, chunks)]
        + word_ins(sz, words)
        + [(cache_key, by_head(sz.cache)), (cache_value, by_head(sz.cache))],
        [
            (shaped((n, sz.rows, lanes), wide), per_step((sz.rows, lanes))),
            (shaped((n, 8, lanes), wide), per_step((8, lanes))),
        ],
        flops=8 * lanes * pairs,
        exps=pairs,
    )


def merge_kernel(sz, meta, message, cache_mixed, cache_sums, out, sums):
    prompt_sums = three_sum(message[sz.rows : sz.rows + 24, :])
    other_sums = cache_sums[...]
    largest = jnp.maximum(prompt_sums, other_sums)
    joint = largest + jnp.log2(jnp.exp2(prompt_sums - largest) + jnp.exp2(other_sums - largest))
    sums[...] = joint
    one = jnp.exp2(prompt_sums - joint)
    two = jnp.exp2(other_sums - joint)
    for begin, count, row in part_list(sz):
        former = row_to_column(unpack_row(one, row, count))
        latter = row_to_column(unpack_row(two, row, count))
        at = slice(begin, begin + count)
        out[at, :] = (message[at, :].astype(wide) * former + cache_mixed[at, :] * latter).astype(low)


def merge(sz, meta, messages, cache_mixed, cache_sums):
    n = sz.heads
    return call(
        functools.partial(merge_kernel, sz),
        "merge",
        n,
        meta,
        [
            (messages, per_step((sz.rows + 32, lanes))),
            (cache_mixed, per_step((sz.rows, lanes))),
            (cache_sums, per_step((8, lanes))),
        ],
        [
            (shaped((sz.rows, n * lanes), low), by_head(sz.rows)),
            (shaped((n, 8, lanes), wide), per_step((8, lanes))),
        ],
        flops=4 * n * sz.rows * lanes,
    )


def send_kernel(sz, meta, grad, mixed, sums, delta, out):
    prod = grad[...].astype(wide) * mixed[...].astype(wide)
    delta[...] = jnp.zeros_like(delta)
    for begin, count, row in part_list(sz):
        pack_row(delta, row, jnp.sum(prod[begin : begin + count, :].T, axis=0, keepdims=True))
    aux = three_parts(sums[...]) + three_parts(delta[...])
    out[0 : sz.rows, :] = grad[...]
    out[sz.rows :, :] = jnp.concatenate(aux, axis=0).astype(low)


def make_messages(sz, meta, grad, mixed, sums):
    n = sz.heads
    return call(
        functools.partial(send_kernel, sz),
        "make_messages",
        n,
        meta,
        [(grad, by_head(sz.rows)), (mixed, by_head(sz.rows)), (sums, per_step((8, lanes)))],
        [
            (shaped((n, 8, lanes), wide), per_step((8, lanes))),
            (shaped((n, sz.rows + 48, lanes), low), per_step((sz.rows + 48, lanes))),
        ],
        flops=2 * n * sz.rows * lanes,
    )


def cache_back_kernel(
    sz, meta, chunk, words_prompt, words_reply, cache_key, cache_value, grad, sums, delta, out
):
    scale = float(lanes**-0.5 * log2e)
    for (begin, count, row), words in zip(part_list(sz), (words_prompt, words_reply)):
        at = slice(begin, begin + count)
        allowed = word_bits(words[...], sz.cache // 32)
        logits = along_cols(cache_key[...], chunk[at, :]) * scale
        logits = logits - unpack_row(sums[...], row, count)
        probs = jnp.exp2(jnp.where(allowed, logits, masked_score))
        slope = along_cols(cache_value[...], grad[at, :]) - unpack_row(delta[...], row, count)
        slope = (probs * slope).astype(low)
        out[at, :] = along_rows(slope, cache_key[...]) * float(lanes**-0.5)


def cache_backward(sz, meta, chunks, grad, sums, delta, words, cache_key, cache_value):
    n = sz.heads
    pairs = n * sz.rows * sz.cache
    return call(
        functools.partial(cache_back_kernel, sz),
        "cache_backward",
        n,
        meta,
        [queries_of(sz, chunks)]
        + word_ins(sz, words)
        + [(cache_key, by_head(sz.cache)), (cache_value, by_head(sz.cache))]
        + [
            (grad, by_head(sz.rows)),
            (sums, per_step((8, lanes))),
            (delta, per_step((8, lanes))),
        ],
        [(shaped((n, sz.rows, lanes), wide), per_step((sz.rows, lanes)))],
        flops=12 * lanes * pairs,
        exps=pairs,
    )[0]


def tile_rows(rows):
    return 384 if rows % 384 == 0 else rows


def feed_kernel(
    sz,
    groups,
    meta,
    prompt_ref,
    reply_ref,
    prompt_teach,
    reply_teach,
    mixed,
    weight,
    gain,
    out_w,
    gate_w,
    up_w,
    down_w,
    *refs,
):
    (
        prompt_out,
        reply_out,
        middle,
        mixed_grad,
        second,
        low_upstream,
        hidden_out,
        gate_grad,
        up_grad,
        stats,
        total,
        inward,
        gate_slope,
        up_slope,
    ) = refs[-14:]
    step = pl.program_id(0)
    rows, tile = sz.rows, tile_rows(sz.rows)
    width = middle.shape[1]
    part = out_w.shape[0]
    parts = ((0, sz.prompt, prompt_ref, prompt_teach, prompt_out),)
    parts = parts + ((sz.prompt, sz.half, reply_ref, reply_teach, reply_out),)

    @pl.when(step == 0)
    def _():
        stats[...] = jnp.zeros_like(stats)
        for g in range(groups):
            at = slice(g * part, (g + 1) * part)
            moved = along_cols(mixed[...], out_w[:, g * width : (g + 1) * width])
            for begin, count, source, _, _ in parts:
                middle[begin : begin + count, at] = (
                    source[:, at].astype(wide) + moved[begin : begin + count, :]
                )
        second[...] = norm_rows(middle[...], gain[...]).astype(low)

    @pl.when(step < groups)
    def _():
        for begin in range(0, rows, tile):
            at = slice(begin, begin + tile)
            gate = along_cols(second[at, :], gate_w[...])
            up = along_cols(second[at, :], up_w[...])
            sig = jax.nn.sigmoid(gate)
            silu = gate * sig
            hidden = (silu * up).astype(low)
            hidden_out[at, :] = hidden
            up_slope[step, at, :] = silu.astype(low)
            gate_slope[step, at, :] = (up * sig * (1.0 + gate * (1.0 - sig))).astype(low)
            result = product(hidden, down_w[...])

            @pl.when(step == 0)
            def _():
                total[at, :] = result

            @pl.when(step > 0)
            def _():
                total[at, :] += result

    @pl.when(step == groups - 1)
    def _():
        for begin, count, _, teach, out in parts:
            at = slice(begin, begin + count)
            result = total[at, :] + middle[at, :]
            out[...] = result.astype(low)
            residue = result - teach[...].astype(wide)
            stats[0:1, :] += jnp.sum(weight[at, 0:1] * residue * residue, axis=0, keepdims=True)
            upstream = weight[at, 1:2] * residue
            total[at, :] = upstream
            low_upstream[at, :] = upstream.astype(low)

    @pl.when(step >= groups)
    def _():
        group = 2 * groups - 1 - step
        for begin in range(0, rows, tile):
            at = slice(begin, begin + tile)
            hidden_grad = along_cols(low_upstream[at, :], down_w[...])
            low_gate = (hidden_grad * gate_slope[group, at, :].astype(wide)).astype(low)
            low_up = (hidden_grad * up_slope[group, at, :].astype(wide)).astype(low)
            gate_grad[at, :] = low_gate
            up_grad[at, :] = low_up
            back = product(low_gate, gate_w[...]) + product(low_up, up_w[...])

            @pl.when(step == groups)
            def _():
                inward[at, :] = back

            @pl.when(step > groups)
            def _():
                inward[at, :] += back

    @pl.when(step == 2 * groups - 1)
    def _():
        back, gain_part = norm_back(middle[...], gain[...], inward[...])
        stats[1:2, :] = gain_part[None]
        middle[...] = total[...] + back
        for g in range(groups):
            at = slice(g * part, (g + 1) * part)
            piece = product(middle[:, at].astype(low), out_w[:, g * width : (g + 1) * width])
            if g == 0:
                inward[...] = piece
            elif g < groups - 1:
                inward[...] += piece
            else:
                mixed_grad[...] = (inward[...] + piece).astype(low)


def feed_forward(sz, meta, micro, arrays, mixed, weight, gain, weights, prior):
    prompt_in, reply_in, prompt_teach, reply_teach = arrays
    out_w, inner_w, inner = weights
    width = prompt_in.shape[3]
    groups = inner_w.shape[1] // width
    rows = sz.rows

    def weight_spec(k):
        return pl.BlockSpec(
            (inner, width), lambda d, meta: (k, jnp.minimum(d, 2 * groups - 1 - d))
        )

    ins = [
        (prompt_in, of_micro(micro, sz.prompt, width)),
        (reply_in, of_micro(micro, sz.half, width)),
        (prompt_teach, of_micro(micro, sz.prompt, width)),
        (reply_teach, of_micro(micro, sz.half, width)),
        (mixed, fixed((rows, width))),
        (weight, fixed((rows, 2))),
        (gain, fixed((1, width))),
        (out_w, fixed(out_w.shape)),
        (inner_w, weight_spec(0)),
        (inner_w, weight_spec(1)),
        (inner_w, weight_spec(2)),
    ]
    aliases = {}
    for i, array in enumerate(prior):
        aliases[len(ins) + 1] = i
        ins.append((array, in_place()))
    out_tokens = [
        (shaped(prompt_in.shape, low), of_micro(micro, sz.prompt, width)),
        (shaped(reply_in.shape, low), of_micro(micro, sz.half, width)),
    ]
    plain = fixed((rows, width))
    inner_shape = shaped((groups, rows, inner), low)
    early = pl.BlockSpec((None, rows, inner), lambda d, meta: (jnp.minimum(d, groups - 1), 0, 0))
    late = pl.BlockSpec(
        (None, rows, inner),
        lambda d, meta: (jnp.minimum(groups - 1, 2 * groups - 1 - d), 0, 0),
    )
    return call(
        functools.partial(feed_kernel, sz, groups),
        "feed_forward",
        2 * groups,
        meta,
        ins,
        out_tokens
        + [
            (shaped((rows, width), wide), plain),
            (shaped((rows, width), low), plain),
            (shaped((rows, width), low), plain),
            (shaped((rows, width), low), plain),
            (inner_shape, early),
            (inner_shape, late),
            (inner_shape, late),
            (shaped((8, width), wide), fixed((8, width))),
        ],
        scratch=[
            pltpu.VMEM((rows, width), wide),
            pltpu.VMEM((rows, width), wide),
            pltpu.VMEM((groups, rows, inner), low),
            pltpu.VMEM((groups, rows, inner), low),
        ],
        flops=4 * rows * width * (width + 3 * groups * inner),
        vmem=60,
        aliases=aliases,
    )


aways = (3, 1, 2, 0)


def away_of(step, per=1):
    turn = step // per
    return jnp.where(turn == 0, 3, jnp.where(turn == 1, 1, jnp.where(turn == 2, 2, 0)))


def away_outs(width, columns, per=1):
    outs = []
    for turn in range(len(aways)):

        def place(d, meta, turn=turn):
            return (0, jnp.clip(d - turn * per, 0, per - 1))

        spec = pl.BlockSpec((width, columns), place)
        outs.append((shaped((width, columns * per), low), spec))
    return outs


def write_away(outs, per, act):
    for turn, out in enumerate(outs):

        @pl.when(pl.program_id(0) // per == turn)
        def _(out=out):
            act(out)


def weight_grad_kernel(micros, meta, *refs):
    groups_in = [refs[7 * m : 7 * m + 7] for m in range(micros)]
    *outs, buffer, sems = refs[7 * micros :]
    inner = groups_in[0][4].shape[1]
    step = pl.program_id(0)
    stride = -(-inner // lanes) * lanes

    def fill(out):
        def summed(place, pick):
            total = None
            for group in groups_in:
                former, latter = pick(*group)
                part = along_rows(former, latter)
                total = part if total is None else total + part
            out[:, place : place + total.shape[1]] = total.astype(low)

        if stride > inner:
            for i in range(3):
                out[:, i * stride + inner : (i + 1) * stride] = jnp.zeros(
                    (out.shape[0], stride - inner), low
                )
        summed(0, lambda b, dy, o, mid, hid, dg, du: (b[...], dg[...]))
        summed(stride, lambda b, dy, o, mid, hid, dg, du: (b[...], du[...]))
        summed(2 * stride, lambda b, dy, o, mid, hid, dg, du: (dy[...], hid[...]))
        summed(3 * stride, lambda b, dy, o, mid, hid, dg, du: (o[...], mid[...].astype(low)))

    for turn, target in enumerate(outs):
        slot = turn % 2

        @pl.when(step == turn)
        def _(turn=turn, target=target, slot=slot):
            if turn >= 2:
                pltpu.make_async_copy(buffer.at[slot], outs[turn - 2], sems.at[slot]).wait()
            fill(buffer.at[slot])
            pltpu.make_async_copy(buffer.at[slot], target, sems.at[slot]).start()
            if turn == len(outs) - 1:
                for back in (1, 0):
                    spot = (turn - back) % 2
                    pltpu.make_async_copy(buffer.at[spot], outs[turn - back], sems.at[spot]).wait()


def weight_grads(sz, meta, parts):
    groups, rows, inner = parts[0][4].shape
    width = parts[0][0].shape[1]
    piece = width // groups
    ins = []
    block = pl.BlockSpec((None, rows, inner), lambda d, meta: (meta[0] ^ away_of(d), 0, 0))
    for second, low_upstream, mixed, middle_grad, hidden, gate_grad, up_grad in parts:
        for array in (second, low_upstream, mixed):
            ins.append((array, fixed((rows, width))))
        spec = pl.BlockSpec((rows, piece), lambda d, meta: (0, meta[0] ^ away_of(d)))
        ins.append((middle_grad, spec))
        for array in (hidden, gate_grad, up_grad):
            ins.append((array, block))
    columns = 3 * (-(-inner // lanes) * lanes) + piece
    return call(
        functools.partial(weight_grad_kernel, len(parts)),
        "weight_grads",
        groups,
        meta,
        ins,
        [(shaped((width, columns), low), in_place())] * len(aways),
        scratch=[pltpu.VMEM((2, width, columns), low), pltpu.SemaphoreType.DMA((2,))],
        flops=2 * len(parts) * rows * width * (3 * groups * inner + width),
        vmem=60,
    )


def finish_kernel(sz, span, query_side, has_prior, last, per, meta, *refs):
    chunk, weights, normed, *refs = refs
    if query_side:
        extra, carried, middle, prompt_ref, reply_ref, gain, *refs = refs
    prior = None
    if has_prior:
        prior, refs = refs[0], refs[1:]
    if query_side:
        prompt_out, reply_out, stats, *weight_outs, total = refs[-(5 if not last else 8) :]
    else:
        total, *weight_outs = refs[-(2 if not last else 5) :]
    step = pl.program_id(0)
    grads = chunk[...]
    if query_side:
        grads = (grads.astype(wide) + extra[...]).astype(low)
    part = product(grads, weights[...])

    @pl.when(step == 0)
    def _():
        total[...] = part

    @pl.when(step > 0)
    def _():
        total[...] += part

    weight_part = along_rows(normed[...], grads)
    if has_prior:
        weight_part = weight_part + prior[...]

    def put(out):
        out[...] = weight_part.astype(low)

    if last:
        write_away(weight_outs, per, put)
    else:
        weight_outs[0][...] = weight_part
    if query_side:

        @pl.when(step == sz.heads - 1)
        def _():
            stats[...] = jnp.zeros_like(stats)
            for begin, count, source, out in (
                (0, sz.prompt, prompt_ref, prompt_out),
                (sz.prompt, sz.half, reply_ref, reply_out),
            ):
                at = slice(begin, begin + count)
                upstream = carried[at, :] + total[at, :]
                back, gain_part = norm_back(source[...].astype(wide), gain[...], upstream)
                stats[0:1, :] += gain_part[None]
                out[...] = middle[at, :] + back


def finish(sz, meta, micro, chunks, weights, normed, prior, last, tokens=None):
    n, rows = sz.heads, sz.rows
    width = normed.shape[1]
    span = chunks.shape[2]
    per = weights.shape[0] // (3 * lanes)
    groups = n // per
    query_side = tokens is not None

    def head(d, meta):
        return per * (meta[0] ^ away_of(d, per)) + d % per

    if query_side:
        weight_spec = pl.BlockSpec(
            (span, width), lambda d, meta: (head(d, meta) % per, head(d, meta) // per)
        )
    else:
        weight_spec = pl.BlockSpec(
            (span, width), lambda d, meta: (per // 2 + head(d, meta) % per, head(d, meta) // per)
        )
    by_step = pl.BlockSpec((None, rows, span), lambda d, meta: (head(d, meta), 0, 0))
    plain = fixed((rows, width))
    ins = [(chunks, by_step), (weights, weight_spec), (normed, plain)]
    outs = []
    aliases = {}
    scratch = []
    if query_side:
        prompt_in, reply_in, extra, carried, middle, gain, before = tokens
        ins.append((extra, by_step))
        ins.append((carried, plain))
        ins.append((middle, plain))
        ins.append((prompt_in, of_micro(micro, sz.prompt, width)))
        ins.append((reply_in, of_micro(micro, sz.half, width)))
        ins.append((gain, fixed((1, width))))
        outs.append((shaped(prompt_in.shape, wide), of_micro(micro, sz.prompt, width)))
        outs.append((shaped(reply_in.shape, wide), of_micro(micro, sz.half, width)))
        outs.append((shaped((8, width), wide), fixed((8, width))))
        scratch.append(pltpu.VMEM((rows, width), wide))
    else:
        outs.append((shaped((rows, width), wide), plain))
    grad_spec = pl.BlockSpec((None, width, span), lambda d, meta: (head(d, meta), 0, 0))
    if prior is not None:
        ins.append((prior, grad_spec))
    if query_side:
        for i, array in enumerate(before):
            aliases[len(ins) + 1] = i
            ins.append((array, in_place()))
    if last:
        outs.extend(away_outs(width, span, per))
    else:
        outs.append((shaped((n, width, span), wide), grad_spec))
    return call(
        functools.partial(finish_kernel, sz, span, query_side, prior is not None, last, per),
        "finish",
        n,
        meta,
        ins,
        outs,
        scratch=scratch,
        flops=4 * rows * width * span * n,
        vmem=44,
        aliases=aliases,
    )


def subgroups(sz):
    if sz.blocks == 1:
        return None
    return [[b * sz.heads + i for i in range(sz.heads)] for b in range(sz.blocks)]


def exchange(sz, array):
    return lax.all_to_all(array, "seq", 0, 0, axis_index_groups=subgroups(sz))


def other_blocks(sz, pairs):
    if sz.blocks == 1:
        return []
    count = lax.axis_size("seq")
    own = pairs[:, : sz.prompt].reshape(sz.own_prompt, 2 * lanes)
    return [
        lax.ppermute(own, "seq", [(i, i ^ e * sz.heads) for i in range(count)])
        for e in range(1, sz.blocks)
    ]


def settle_blocks(sz, own_block, pairs, partial):
    count = lax.axis_size("seq")
    blocks = partial.reshape(sz.blocks, sz.own_prompt, 2 * lanes)
    total = lax.dynamic_index_in_dim(blocks, own_block, 0, keepdims=False)
    for e in range(1, sz.blocks):
        part = lax.dynamic_index_in_dim(blocks, own_block ^ e, 0, keepdims=False)
        total = total + lax.ppermute(part, "seq", [(i, i ^ e * sz.heads) for i in range(count)])
    total = total.astype(low).reshape(sz.heads, sz.prompt, 2 * lanes)
    return jnp.concatenate([total, pairs[:, sz.prompt :]], axis=1)


def along_grp(array, away):
    count = lax.axis_size("grp")
    return lax.ppermute(array, "grp", [(i, i ^ away) for i in range(count)])


def over_groups(blocks):
    to_core_far, to_core, to_chip, stays = blocks
    handed = to_chip.astype(wide) + along_grp(to_core_far, 1).astype(wide)
    near = along_grp(to_core, 1)
    far = along_grp(handed.astype(low), 2)
    return (stays.astype(wide) + near.astype(wide) + far.astype(wide)).astype(low)


def after(value, *others):
    return lax.optimization_barrier((value,) + others)[0]


def body(
    prompt_in,
    reply_in,
    prompt_teacher,
    reply_teacher,
    prompt_mask,
    reply_mask,
    lengths,
    prompt_picks,
    reply_picks,
    cache_keys,
    cache_values,
    w_query,
    w_key,
    w_value,
    w_out,
    w_gate,
    w_up,
    w_down,
    attn_gain,
    ffn_gain,
):
    micros = range(prompt_in.shape[0])
    model_width = prompt_in.shape[3]
    heads = prompt_picks.shape[2]
    seq_count = lax.axis_size("seq")
    grp_count = lax.axis_size("grp")
    sz = Sizes(
        heads,
        seq_count // heads,
        prompt_in.shape[2],
        reply_in.shape[2],
        cache_keys.shape[1],
        prompt_picks.shape[4],
        lengths.shape[2],
    )
    position = lax.axis_index("seq")
    own_block = position // heads
    parity = position % 2
    slot_count = len(micros) * grp_count * seq_count * sz.rows
    row_part = w_query.shape[0]
    per_grp = w_query.shape[1] // lanes
    everywhere = ("grp", "seq")

    def gathered(part, axis):
        return lax.all_gather(part, everywhere, axis=axis, tiled=True)

    def shared(values):
        count = grp_count * seq_count
        return lax.all_to_all(jnp.broadcast_to(values, (count,) + values.shape), everywhere, 0, 0)

    half_index = jnp.arange(sz.half)
    valids, metas = [], []
    for micro in micros:
        live = lax.dynamic_index_in_dim(lengths[micro, 0], position // 2, 0, keepdims=False)
        reply_live = (2 * half_index + parity < live).astype(jnp.int32)
        valids.append(jnp.concatenate([prompt_mask[micro, 0], reply_mask[micro, 0] * reply_live]))
        metas.append(
            jnp.concatenate(
                [jnp.stack([lax.axis_index("grp"), own_block]).astype(jnp.int32), lengths[micro, 0]]
            )
        )
    own_count = sum(jnp.sum(v) for v in valids)
    share = attn_gain.shape[0]
    counts = jnp.stack([own_count // 256, own_count % 256]).astype(low)
    small = shared(jnp.concatenate([attn_gain, ffn_gain, counts]))
    gain_one = small[:, :share].reshape(1, model_width).astype(wide)
    gain_two = small[:, share : 2 * share].reshape(1, model_width).astype(wide)
    counts = jnp.sum(small[:, 2 * share :].astype(wide), axis=0)
    valid_total = counts[0] * 256.0 + counts[1]
    coefficient = slot_count / valid_total

    query_part = w_query.T
    pair_part = jnp.stack([w.T.reshape(per_grp, lanes, row_part) for w in (w_key, w_value)], axis=1)
    pair_part = pair_part.reshape(per_grp * 2 * lanes, row_part)
    qkv_w = gathered(jnp.concatenate([query_part, pair_part]), 1)
    inner = w_gate.shape[1]
    inner_w = gathered(jnp.concatenate([w_gate.T, w_up.T, w_down, w_out.T]), 1)
    feed_w = (inner_w[3 * inner :], inner_w, inner)
    cache_key_rows, cache_value_rows = cache_keys[0], cache_values[0]
    words = [picks_to_words(sz, metas[m], m, prompt_picks, reply_picks) for m in micros]
    gain_one, words = lax.optimization_barrier((gain_one, words))
    last = len(micros) - 1
    tokens = (prompt_in, reply_in)

    queries, pairs, normed, got_queries, got_pairs = [], [], [], [], []
    for m in micros:
        query, pair, rows = project(sz, metas[m], m, prompt_in, reply_in, gain_one, qkv_w)
        queries.append(query)
        pairs.append(pair)
        normed.append(rows)
    cached = [
        cache_forward(sz, metas[m], queries[m], words[m], cache_key_rows, cache_value_rows)
        for m in micros
    ]
    error_parts, gain_two_parts, gain_one_parts = [], [], []
    outs, grads, parts, arrived, extras = [], [], [], [], []
    middle_grads, mixed_grads, all_sums, deltas = [], [], [], []
    back_queries, back_pairs = [], []
    answers = None
    messages = None

    def run_back(m, feed_grads):
        got = arrived[m] if feed_grads is None else after(arrived[m], feed_grads)
        query, pair, *rest = attend_back(
            sz, metas[m], got_queries[m], got_pairs[m], got, extras[m]
        )
        if sz.blocks > 1:
            pair = settle_blocks(sz, own_block, pair, *rest)
        return query, pair

    pending = None
    feed_grads = None
    got_pairs.append(exchange(sz, pairs[0]))
    for m in micros:
        pair = got_pairs[m]
        query = after(queries[m], pair if answers is None else answers)
        query = exchange(sz, query)
        if m == 0:
            query, cached = lax.optimization_barrier((query, cached))
        if messages is not None:
            query = after(query, messages)
        got_queries.append(query)
        extras.append(other_blocks(sz, pair))
        answers = attend(sz, metas[m], query, pair, extras[m])
        if m < last:
            got_pairs.append(exchange(sz, pairs[m + 1]))
            answers = after(answers, got_pairs[m + 1])
        answers = exchange(sz, answers)
        if m > 0:
            pending = run_back(m - 1, None)
            answers = after(answers, *pending)
            back_pairs.append(exchange(sz, pending[1]))
        mixed, sums = merge(sz, metas[m], answers, *cached[m])
        valid = valids[m].astype(wide)
        weight = jnp.stack([valid, valid * coefficient], axis=1)
        arrays = (prompt_in, reply_in, prompt_teacher, reply_teacher)
        *outs, middle_grad, mixed_grad, second, low_upstream, hidden, gate_grad, up_grad, stats = (
            feed_forward(sz, metas[m], m, arrays, mixed, weight, gain_two, feed_w, outs)
        )
        error_parts.append(stats[0])
        gain_two_parts.append(stats[1])
        delta, messages = make_messages(sz, metas[m], mixed_grad, mixed, sums)
        if m > 0:
            messages = after(messages, back_pairs[m - 1])
        second = after(second, messages)
        parts.append((second, low_upstream, mixed, middle_grad, hidden, gate_grad, up_grad))
        arrived.append(exchange(sz, messages))
        middle_grads.append(middle_grad)
        mixed_grads.append(mixed_grad)
        all_sums.append(sums)
        deltas.append(delta)
        if m > 0:
            back_queries.append(exchange(sz, after(pending[0], arrived[m])))
    feed_grads = weight_grads(sz, metas[0], parts)
    query, pair = run_back(last, feed_grads[0])
    back_pairs.append(exchange(sz, pair))
    late = after(words, pair)
    grad_query = grad_pair = None
    for m in micros:
        cache_grad = cache_backward(
            sz,
            metas[m],
            queries[m],
            mixed_grads[m],
            all_sums[m],
            deltas[m],
            late[m],
            cache_key_rows,
            cache_value_rows,
        )
        carried, *grad_pair = finish(
            sz, metas[m], m, back_pairs[m], qkv_w, normed[m], grad_pair, m == last
        )
        if m == last:
            back_queries.append(exchange(sz, after(query, back_pairs[last], *grads)))
        extra = (cache_grad, carried, middle_grads[m], gain_one, grads)
        prompt_grad, reply_grad, stats, *grad_query = finish(
            sz,
            metas[m],
            m,
            back_queries[m],
            qkv_w,
            normed[m],
            grad_query,
            m == last,
            tokens + extra,
        )
        grads = [prompt_grad, reply_grad]
        gain_one_parts.append(stats[0])
        if m < last:
            grad_pair, grad_query = grad_pair[0], grad_query[0]

    def over_rows(grad):
        grad = grad.reshape(seq_count, row_part, grad.shape[1])
        return jnp.sum(lax.all_to_all(grad, "seq", 0, 0).astype(wide), axis=0)

    feed_grads = over_groups(feed_grads)
    feed_grads = lax.psum_scatter(feed_grads, "seq", scatter_dimension=0, tiled=True).astype(wide)
    stride = -(-inner // lanes) * lanes
    grad_gate, grad_up, grad_down = (
        feed_grads[:, i * stride : i * stride + inner] for i in range(3)
    )
    grad_out = feed_grads[:, 3 * stride :]
    grad_pair = over_rows(over_groups(grad_pair)).reshape(row_part, per_grp, 2, lanes)
    grad_key, grad_value = (
        grad_pair[:, :, i].reshape(row_part, per_grp * lanes) for i in range(2)
    )
    grad_query = over_rows(over_groups(grad_query))
    count = grp_count * seq_count
    tail = jnp.concatenate(
        [
            sum(gain_one_parts).reshape(count, share),
            sum(gain_two_parts).reshape(count, share),
            jnp.broadcast_to(jnp.sum(sum(error_parts)), (count, 1)),
        ],
        axis=1,
    )
    tail = jnp.sum(lax.all_to_all(tail, everywhere, 0, 0), axis=0)
    mean_error = tail[2 * share] / (model_width * valid_total)
    return (
        mean_error,
        *outs,
        *grads,
        grad_query,
        grad_key,
        grad_value,
        grad_out,
        grad_gate,
        grad_up,
        grad_down.T,
        tail[:share],
        tail[share : 2 * share],
    )


def solution(mesh):
    tokens = P(None, "grp", "seq", None)
    rows_first = P("seq", "grp")
    spread = P(("grp", "seq"))
    placed = (
        (tokens,) * 4
        + (P(None, "grp", "seq"),) * 2
        + (P(None, "grp", None),)
        + (P(None, "grp", None, "seq", None),) * 2
        + (P("grp", "seq", None),) * 2
        + (rows_first,) * 6
        + (P("grp", "seq"), spread, spread)
    )
    return jax.shard_map(
        body,
        mesh=mesh,
        in_specs=placed,
        out_specs=(P(),) + (tokens,) * 4 + (rows_first,) * 6 + (P("grp", "seq"), spread, spread),
        check_vma=False,
    )
```

time: 4570 us -> 1220 us (0.27)
  waiting for transfers between devices: 1720 us -> 262 us
  other arithmetic: 1270 us -> 37 us
  matrix products: 1150 us -> 0 us
  Pallas kernels: 0 us -> 605 us
  blocking collectives: 235 us -> 142 us
  local copies, waits for them, and re-layouts: 131 us -> 71.1 us
  starting transfers between devices: 21.8 us -> 72.4 us
    reduce_scatter x18 -> x1, waiting for transfers between devices: 1400 us -> 0.01 us  [body(): lax.psum_scatter(feed_grads, 'seq', scatter_dimension=0, tiled=True)]
    dot_general x346 -> x0, matrix products: 1150 us -> none  [the longest x158 511 us: along_cols(): lax.dot_general(former, latter, (((1,), (1,)), ((), ())), preferred_eleme...]
    reduce_or x32 -> x0, other arithmetic: 654 us -> none  [picked_table(): jnp.any(chosen[:, :, None] == jnp.arange(cache_len, dtype=jnp.int32)[None...]
    pallas_call x0 -> x23, Pallas kernels: none -> 605 us  [the longest x17 339 us: call(): pl.pallas_call(kernel, out_shape=list(out_shape), grid_spec=pltpu.Prefetc...]
    convert_element_type x54 -> x8, other arithmetic: 308 us -> 24.3 us  [the longest x3 14.4 us: over_groups(): (stays.astype(wide) + near.astype(wide) + far.astype(wide)).astype(low)]
    reduce_sum x36 -> x8, other arithmetic: 258 us -> 7.38 us  [the longest x3 4.91 us: body(): own_count = sum((jnp.sum(v) for v in valids))]
    all_to_all x0 -> x14, waiting for transfers between devices: none -> 149 us  [the longest x10 126 us: exchange(): return lax.all_to_all(array, 'seq', 0, 0, axis_index_groups=subgroups(sz))]
    all_gather x6 -> x0, blocking collectives: 147 us -> none  [the longest x1 35.6 us: body(): lax.all_gather(w_value, 'seq', axis=0, tiled=True)]
  transfers between devices with their start and end apart: 40 -> 26, of which waited for: 29 -> 13; matrix products, arithmetic and copies ran while one was open for 38% -> 4% of each run, Pallas kernels for 0% -> 44%
where the time goes in v1:
time: 1220 us; the launch traced here: 1210 us
  Pallas kernels  605 us (50%)
  waiting for transfers between devices  262 us (21%)
  blocking collectives  142 us (12%)
  starting transfers between devices  72.4 us (6%)
  local copies, waits for them, and re-layouts  71.1 us (6%)
  other arithmetic  37 us (3%)
  between operations  21 us (2%)
    pallas_call x17, Pallas kernels, call(): pl.pallas_call(kernel, out_shape=list(out_shape), grid_spec=pltpu.Prefetc...  339 us
    pallas_call x2, Pallas kernels, attend_back(): pl.pallas_call(functools.partial(attend_back_kernel, sz), out_shape=out_s...  145 us
    all_to_all x2, blocking collectives, exchange(): return lax.all_to_all(array, 'seq', 0, 0, axis_index_groups=subgroups(sz))  142 us
    all_to_all x10, waiting for transfers between devices, exchange(): return lax.all_to_all(array, 'seq', 0, 0, axis_index_groups=subgroups(sz))  126 us
    pallas_call x2, Pallas kernels, attend(): pl.pallas_call(functools.partial(attend_kernel, sz), out_shape=jax.ShapeD...  106 us
    all_gather x2, waiting for transfers between devices, gathered(): return lax.all_gather(part, everywhere, axis=axis, tiled=True)  92.1 us
    unnamed x188, local copies, waits for them, and re-layouts  57 us
    all_to_all x10, starting transfers between devices, exchange(): return lax.all_to_all(array, 'seq', 0, 0, axis_index_groups=subgroups(sz))  49.2 us
  transfers between devices with their start and end apart: 26, of which 13 were waited for; matrix products, arithmetic and copies ran while one was open for 4% of the time, Pallas kernels for 44%

profile of v1, /device:TPU:0, one launch (start us, length us, event | category | flops | bytes accessed | tf_op | source)
XLA Modules:
  0.0 1210.2 jit_solution(7521768279961755674)
XLA Ops:
  23.4 7.3 all-to-all-start
  31.3 7.8 picks_to_words.3
  39.1 8.0 picks_to_words.2
  47.9 45.7 %all-gather.3.cloned.1.call-done.query_w.pair_w.refs_1_ = bf16[768,4096]{1,0:T(8,128)(2,1)} async-done(((bf16[768,128]{1,0:T(8,128)(2,1)}), bf16[768,4096]{1,0:T(8,128)(2,1)}) %all-gather.3.cloned.1.call-update) | async-done | bytes 6291472 | tf_op jit(solution)/shard_map/all_gather | solution.py:1222
  96.4 9.8 project.2
  106.2 92.0 %all_to_all.88.refs_1_ = bf16[8,768,256]{2,1,0:T(8,128)(2,1)} all-to-all(bf16[8,768,256]{2,1,0:T(8,128)(2,1)S(1)} %get-tuple-element.113), channel_id=1, replica_groups=mesh['grp'=4,'seq'=8] {'seq'}, dimensions={0} | all-to-all | bytes 6291456 | tf_op jit(solution)/shard_map/all_to_all | solution.py:1135
  198.2 4.3 all-to-all-start.2
  205.3 10.4 project.3
  218.6 27.7 %all-to-all-done.2.refs_0_ = bf16[8,768,128]{2,1,0:T(8,128)(2,1)} async-done(((bf16[8,768,128]{2,1,0:T(8,128)(2,1)}), bf16[8,768,128]{2,1,0:T(8,128)(2,1)}, u32[]{:S(2)}, u32[]{:S(2)}) %all-to-all-start.2) | async-done | bytes 1572896 | tf_op jit(solution)/shard_map/all_to_all | solution.py:1135
  246.4 4.8 all-to-all-start.3
  251.2 6.6 cache_forward.2
  259.4 8.0 cache_forward.3
  269.0 52.1 %attend.2 = bf16[8,800,128]{2,1,0:T(8,128)(2,1)S(1)} custom-call(s32[6]{0:T(128)S(1)} %copy-done.63, bf16[8,768,128]{2,1,0:T(8,128)(2,1)} %all-to-all-done.2.refs_0_, bf16[8,768,256]{2,1,0:T(8,128)(2,1)S(1)} %copy-done.33), custom_call_target="tpu_custom_call" | custom-call | flops 10066329600 | bytes 2097152 | tf_op jit(solution)/shard_map/attend/pallas_call | solution.py:274
  321.1 15.4 %all-to-all-done.3.refs_1_ = bf16[8,768,256]{2,1,0:T(8,128)(2,1)} async-done(((bf16[8,768,256]{2,1,0:T(8,128)(2,1)}), bf16[8,768,256]{2,1,0:T(8,128)(2,1)}, u32[]{:S(2)}, u32[]{:S(2)}) %all-to-all-start.3) | async-done | bytes 3145760 | tf_op jit(solution)/shard_map/all_to_all | solution.py:1135
  336.6 49.7 %all_to_all.89.message = bf16[8,800,128]{2,1,0:T(8,128)(2,1)S(1)} all-to-all(bf16[8,800,128]{2,1,0:T(8,128)(2,1)S(1)} %attend.2), channel_id=1, replica_groups=mesh['grp'=4,'seq'=8] {'seq'}, dimensions={0} | all-to-all | bytes 3276800 | tf_op jit(solution)/shard_map/all_to_all | solution.py:1135
  386.2 4.2 all-to-all-start.6
  401.8 46.4 %all-gather.5.cloned.1.call-done.gate_w.up_w.down_w = bf16[2368,4096]{1,0:T(8,128)(2,1)} async-done(((bf16[2368,128]{1,0:T(8,128)(2,1)}), bf16[2368,4096]{1,0:T(8,128)(2,1)}) %all-gather.5.cloned.1.call-update) | async-done | bytes 19398672 | tf_op jit(solution)/shard_map/all_gather | solution.py:1222
  451.4 62.7 %feed_forward.2 = (bf16[2,1,512,1024]{3,2,1,0:T(8,128)(2,1)}, bf16[2,1,256,1024]{3,2,1,0:T(8,128)(2,1)}, f32[768,1024]{1,0:T(8,128)}, bf16[768,1024]{1,0:T(8,128...) custom-call(s32[6]{0:T(128)} %get-tuple-element.288.meta, ...), custom_call_target="tpu_custom_call" | custom-call | flops 7449083904 | bytes 23046656 | tf_op jit(solution)/shard_map/feed_forward/pallas_call | solution.py:481
  521.5 3.7 all-to-all-start.5
  525.2 53.7 %attend.3 = bf16[8,800,128]{2,1,0:T(8,128)(2,1)S(1)} custom-call(s32[6]{0:T(128)S(1)} %copy-done.66, bf16[8,768,128]{2,1,0:T(8,128)(2,1)S(1)} %copy-done.46, bf16[8,768,256]{2,1,0:T(8,128)(2,1)} %all-to-all-done.3.refs_1_), custom_call_target="tpu_custom_call" | custom-call | flops 10066329600 | bytes 2097152 | tf_op jit(solution)/shard_map/attend/pallas_call | solution.py:274
  580.1 5.9 all-to-all-start.7
  587.9 71.5 %attend_back.2 = (bf16[8,768,128]{2,1,0:T(8,128)(2,1)S(1)}, bf16[8,768,256]{2,1,0:T(8,128)(2,1)S(1)}) custom-call(s32[6]{0:T(128)S(1)} %copy-done.64, bf16[8,768,128]{2,1,0:T(8,128)(2,1)} %all-to-all-done.2.refs_0_, bf16[8,768,256]{2,1,0:T(8,128)(2,1)S(1)} %copy-done.34, bf16[8,816,128]{2,1,0:T(8,128)(2,1)S(1)} %all-to-all-done.5.refs_2_), custom_call_target="tpu_custom_call" | custom-call | flops 16777216000 | bytes 3670016 | tf_op jit(solution)/shard_map/attend_back/pallas_call | solution.py:418
  662.3 6.1 all-to-all-start.8
  675.9 62.4 %feed_forward.3 = (bf16[2,1,512,1024]{3,2,1,0:T(8,128)(2,1)}, bf16[2,1,256,1024]{3,2,1,0:T(8,128)(2,1)}, f32[768,1024]{1,0:T(8,128)}, bf16[768,1024]{1,0:T(8,128...) custom-call(s32[6]{0:T(128)} %get-tuple-element.289.meta, ...), custom_call_target="tpu_custom_call", output_to_operand_aliasing={{0}: (12, {}), {1}: (13, {})} | custom-call | flops 7449083904 | bytes 23833088 | tf_op jit(solution)/shard_map/feed_forward/pallas_call | solution.py:481
  739.7 4.8 make_messages.3
  744.5 70.3 %weight_grads.1 = (bf16[1024,2560]{1,0:T(8,128)(2,1)}, bf16[1024,2560]{1,0:T(8,128)(2,1)}, bf16[1024,2560]{1,0:T(8,128)(2,1)}, bf16[1024,2560]{1,0:T(8,128)(2,1)}) custom-call(s32[6]{0:T(128)} %get-tuple-element.288.meta, bf16[768,1024]{1,0:T(8,128)(2,1)} %get-tuple-element.150.refs_0_, bf16[768,1024]{1,0:T(8,128)(2,1)} %get-tuple-element.151.refs_1_, ...), custom_call_target="tpu_custom_call" | custom-call | flops 7449083904 | bytes 15663104 | tf_op jit(solution)/shard_map/weight_grads/pallas_call | solution.py:481
  814.9 6.0 all-to-all-start.9
  823.9 7.7 add_convert_fusion.1
  831.6 29.0 %all-to-all-done.9.refs_2_ = bf16[8,816,128]{2,1,0:T(8,128)(2,1)S(1)} async-done(((bf16[8,816,128]{2,1,0:T(8,128)(2,1)}), bf16[8,816,128]{2,1,0:T(8,128)(2,1)S(1)}, u32[]{:S(2)}, u32[]{:S(2)}) %all-to-all-start.9) | async-done | bytes 1671200 | tf_op jit(solution)/shard_map/all_to_all | solution.py:1135
  860.6 3.6 all-to-all-start.10
  865.7 73.0 %attend_back.3 = (bf16[8,768,128]{2,1,0:T(8,128)(2,1)S(1)}, bf16[8,768,256]{2,1,0:T(8,128)(2,1)S(1)}) custom-call(s32[6]{0:T(128)S(1)} %copy-done.67, bf16[8,768,128]{2,1,0:T(8,128)(2,1)S(1)} %copy-done.47, bf16[8,768,256]{2,1,0:T(8,128)(2,1)} %all-to-all-done.3.refs_1_, bf16[8,816,128]{2,1,0:T(8,128)(2,1)S(1)} %all-to-all-done.9.refs_2_), custom_call_target="tpu_custom_call" | custom-call | flops 16777216000 | bytes 3670016 | tf_op jit(solution)/shard_map/attend_back/pallas_call | solution.py:418
  942.7 6.0 all-to-all-start.11
  948.7 10.0 add_convert_fusion
  960.2 17.6 %finish.4 = (f32[768,1024]{1,0:T(8,128)S(1)}, f32[8,1024,256]{2,1,0:T(8,128)}) custom-call(s32[6]{0:T(128)S(1)} %copy-done.65, bf16[8,768,256]{2,1,0:T(8,128)(2,1)} %all-to-all-done.8.refs_0_, bf16[768,4096]{1,0:T(8,128)(2,1)} %all-gather.3.cloned.1.call-done.query_w.pair_w.refs_1_, bf16[768,1024]{1,0:T(8,128)(2,1)S(1)} %copy-done.30), custom_call_target="tpu_custom_call" | custom-call | flops 1610612736 | bytes 5636096 | tf_op jit(solution)/shard_map/finish/pallas_call | solution.py:481
  979.4 7.2 cache_backward.2.refs_3_
  986.7 21.1 %finish.5 = (f32[2,1,512,1024]{3,2,1,0:T(8,128)}, f32[2,1,256,1024]{3,2,1,0:T(8,128)}, f32[8,1024]{1,0:T(8,128)S(1)}, f32[8,1024,128]{2,1,0:T(8,128)}) custom-call(s32[6]{0:T(128)S(1)} %copy-done.65, bf16[8,768,128]{2,1,0:T(8,128)(2,1)S(1)} %copy-done.28, bf16[768,4096]{1,0:T(8,128)(2,1)} %all-gather.3.cloned.1.call-done.query_w.pair_w.refs_1_, ...), custom_call_target="tpu_custom_call" | custom-call | flops 805306368 | bytes 8135680 | tf_op jit(solution)/shard_map/finish/pallas_call | solution.py:481
  1007.7 53.5 %all-to-all-done.11.refs_0_ = bf16[8,768,256]{2,1,0:T(8,128)(2,1)} async-done(((bf16[8,768,256]{2,1,0:T(8,128)(2,1)}), bf16[8,768,256]{2,1,0:T(8,128)(2,1)}, u32[]{:S(2)}, u32[]{:S(2)}) %all-to-all-start.11) | async-done | bytes 3145760 | tf_op jit(solution)/shard_map/all_to_all | solution.py:1135
  1061.3 4.5 all-to-all-start.12
  1067.2 18.3 %finish.6 = (f32[768,1024]{1,0:T(8,128)S(1)}, bf16[1024,512]{1,0:T(8,128)(2,1)S(1)}, bf16[1024,512]{1,0:T(8,128)(2,1)}, bf16[1024,512]{1,0:T(8,128)(2,1)S(1)}, bf16[1024,512]{1,0:T(8,128)(2,1)S(1)}) custom-call(s32[6]{0:T(128)S(1)} %copy-done.67, bf16[8,768,256]{2,1,0:T(8,128)(2,1)} %all-to-all-done.11.refs_0_, ...), custom_call_target="tpu_custom_call" | custom-call | flops 1610612736 | bytes 6684672 | tf_op jit(solution)/shard_map/finish/pallas_call | solution.py:481
  1097.6 8.1 cache_backward.3.refs_3_
  1108.9 22.4 %finish.7 = (f32[2,1,512,1024]{3,2,1,0:T(8,128)}, f32[2,1,256,1024]{3,2,1,0:T(8,128)}, f32[8,1024]{1,0:T(8,128)S(1)}, bf16[1024,256]{1,0:T(8,128)(2,1)S(1)}, bf1...) custom-call(s32[6]{0:T(128)S(1)} %copy-done.67, ...), custom_call_target="tpu_custom_call", output_to_operand_aliasing={{0}: (11, {}), {1}: (12, {})} | custom-call | flops 805306368 | bytes 10232832 | tf_op jit(solution)/shard_map/finish/pallas_call | solution.py:481
  1135.2 6.6 all-to-all-start.13
  1145.3 3.6 all-to-all-done.13
  1148.8 3.6 all-to-all-start.15
  1155.2 13.4 %collective-permute-done.2 = bf16[1024,256]{1,0:T(8,128)(2,1)S(1)} collective-permute-done((bf16[1024,256]{1,0:T(8,128)(2,1)S(1)}, bf16[1024,256]{1,0:T(8,128)(2,1)S(1)}, u32[]{:S(2)}, u32[]{:S(2)}) %collective-permute-start.2) | collective-permute-done | bytes 524320 | tf_op jit(solution)/shard_map/ppermute | solution.py:1162
  1169.5 8.8 all-to-all-done.15
  1178.4 3.6 all-to-all-start.14
  1185.7 11.0 all-to-all-done.14
  (269 shorter events, 109.3 us)
Async XLA Ops:
  7.2 86.4 %all-gather.3.cloned.1.call-start = ((), (), s32[]{:S(2)}) async-start(), calls=%async_computation.17 | async-start | bytes 6488064 | tf_op jit(solution)/shard_map/all_gather | solution.py:1222
  10.9 437.4 %all-gather.5.cloned.1.call-start = ((), (), s32[]{:S(2)}) async-start(), calls=%async_computation.18 | async-start | bytes 20004864 | tf_op jit(solution)/shard_map/all_gather | solution.py:1222
  23.4 23.8 %all-to-all-start = ((bf16[32,1,66]{2,1,0:T(2,128)(2,1)}), bf16[32,1,66]{2,1,0:T(2,128)(2,1)S(1)}, u32[]{:S(2)}, u32[]{:S(2)}) async-start(bf16[32,1,66]{2,1,0:T(2,128)(2,1)} %broadcast_in_dim.6), calls=%async_computation | async-start | bytes 32768 | tf_op jit(solution)/shard_map/all_to_all | solution.py:1226
  39.1 54.5 %copy-start.2 = (bf16[2,1,512,1024]{3,2,1,0:T(8,128)(2,1)S(1)}, bf16[2,1,512,1024]{3,2,1,0:T(8,128)(2,1)}, u32[]{:S(2)}) copy-start(bf16[2,1,512,1024]{3,2,1,0:T(8,128)(2,1)} %refs_6_.3) | copy-start | bytes 6291460
  39.1 54.5 %copy-start.4 = (bf16[2,1,256,1024]{3,2,1,0:T(8,128)(2,1)S(1)}, bf16[2,1,256,1024]{3,2,1,0:T(8,128)(2,1)}, u32[]{:S(2)}) copy-start(bf16[2,1,256,1024]{3,2,1,0:T(8,128)(2,1)} %refs_7_.3) | copy-start | bytes 3145732
  39.1 54.5 %copy-start.63 = (s32[6]{0:T(128)S(1)}, s32[6]{0:T(128)}, u32[]{:S(2)}) copy-start(s32[6]{0:T(128)} %get-tuple-element.288.meta) | copy-start | bytes 76
  47.1 59.0 %copy-start.79 = (bf16[32,1,66]{2,0,1:T(8,128)(2,1)}, bf16[32,1,66]{2,0,1:T(8,128)(2,1)S(1)}, u32[]{:S(2)}) copy-start(bf16[32,1,66]{2,0,1:T(8,128)(2,1)S(1)} %copy.86) | copy-start | bytes 12676
  106.2 92.0 %copy-start.8 = (bf16[8,768,128]{2,1,0:T(8,128)(2,1)}, bf16[8,768,128]{2,1,0:T(8,128)(2,1)S(1)}, u32[]{:S(2)}) copy-start(bf16[8,768,128]{2,1,0:T(8,128)(2,1)S(1)} %get-tuple-element.114.chunk) | copy-start | bytes 4718596
  106.2 92.0 %copy-start.29 = (bf16[768,1024]{1,0:T(8,128)(2,1)}, bf16[768,1024]{1,0:T(8,128)(2,1)S(1)}, u32[]{:S(2)}) copy-start(bf16[768,1024]{1,0:T(8,128)(2,1)S(1)} %get-tuple-element.148.refs_2_) | copy-start | bytes 4718596
  198.2 48.1 %all-to-all-start.2 = ((bf16[8,768,128]{2,1,0:T(8,128)(2,1)}), bf16[8,768,128]{2,1,0:T(8,128)(2,1)}, u32[]{:S(2)}, u32[]{:S(2)}) async-start(bf16[8,768,128]{2,1,0:T(8,128)(2,1)} %copy-done.8), calls=%async_computation.2 | async-start | bytes 3145728 | tf_op jit(solution)/shard_map/all_to_all | solution.py:1135
  246.4 90.2 %all-to-all-start.3 = ((bf16[8,768,256]{2,1,0:T(8,128)(2,1)}), bf16[8,768,256]{2,1,0:T(8,128)(2,1)}, u32[]{:S(2)}, u32[]{:S(2)}) async-start(bf16[8,768,256]{2,1,0:T(8,128)(2,1)} %copy-done.41), calls=%async_computation.3 | async-start | bytes 6291456 | tf_op jit(solution)/shard_map/all_to_all | solution.py:1135
  269.0 52.1 %copy-start.72 = (f32[8,8,128]{2,1,0:T(8,128)}, f32[8,8,128]{2,1,0:T(8,128)S(1)}, u32[]{:S(2)}) copy-start(f32[8,8,128]{2,1,0:T(8,128)S(1)} %get-tuple-element.139.cache_sums) | copy-start | bytes 98308
  336.6 53.9 %copy-start.81 = (f32[32,32]{1,0:T(8,128)S(1)}, f32[32,32]{1,0:T(8,128)}, u32[]{:S(2)}) copy-start(f32[32,32]{1,0:T(8,128)} %get-tuple-element.272) | copy-start | bytes 12292
  336.6 54.6 %copy-start.80 = (bf16[32,1,66]{2,0,1:T(8,128)(2,1)S(1)}, bf16[32,1,66]{2,0,1:T(8,128)(2,1)}, u32[]{:S(2)}) copy-start(bf16[32,1,66]{2,0,1:T(8,128)(2,1)} %copy-done.79) | copy-start | bytes 12676
  336.6 56.6 %copy-start.83 = (s32[512,1]{0,1:T(1,128)S(1)}, s32[512,1]{0,1:T(1,128)}, u32[]{:S(2)}) copy-start(s32[512,1]{0,1:T(1,128)} %get-tuple-element.274) | copy-start | bytes 6148
  336.6 56.6 %copy-start.84 = (s32[512,1]{0,1:T(1,128)S(1)}, s32[512,1]{0,1:T(1,128)}, u32[]{:S(2)}) copy-start(s32[512,1]{0,1:T(1,128)} %get-tuple-element.275) | copy-start | bytes 6148
  386.2 134.1 %all-to-all-start.6 = ((bf16[8,768,128]{2,1,0:T(8,128)(2,1)}), bf16[8,768,128]{2,1,0:T(8,128)(2,1)S(1)}, u32[]{:S(2)}, u32[]{:S(2)}) async-start(bf16[8,768,128]{2,1,0:T(8,128)(2,1)} %get-tuple-element.134.chunk), calls=%async_computation.6 | async-start | bytes 3145728 | tf_op jit(solution)/shard_map/all_to_all | solution.py:1135
  401.8 112.3 %copy-start.61 = (f32[8,8,128]{2,1,0:T(8,128)}, f32[8,8,128]{2,1,0:T(8,128)S(1)}, u32[]{:S(2)}) copy-start(f32[8,8,128]{2,1,0:T(8,128)S(1)} %get-tuple-element.131.sums) | copy-start | bytes 98308
  451.4 62.7 %copy-start.12 = (bf16[768,1024]{1,0:T(8,128)(2,1)S(1)}, bf16[768,1024]{1,0:T(8,128)(2,1)}, u32[]{:S(2)}) copy-start(bf16[768,1024]{1,0:T(8,128)(2,1)} %copy-done.11) | copy-start | bytes 4718596
  451.4 62.7 %copy-start.64 = (s32[6]{0:T(128)S(1)}, s32[6]{0:T(128)}, u32[]{:S(2)}) copy-start(s32[6]{0:T(128)} %get-tuple-element.288.meta) | copy-start | bytes 76
  521.5 58.6 %all-to-all-start.5 = ((bf16[8,816,128]{2,1,0:T(8,128)(2,1)}), bf16[8,816,128]{2,1,0:T(8,128)(2,1)S(1)}, u32[]{:S(2)}, u32[]{:S(2)}) async-start(bf16[8,816,128]{2,1,0:T(8,128)(2,1)} %copy-done.43), calls=%async_computation.5 | async-start | bytes 3342336 | tf_op jit(solution)/shard_map/all_to_all | solution.py:1135
  580.1 82.2 %all-to-all-start.7 = ((bf16[8,800,128]{2,1,0:T(8,128)(2,1)}), bf16[8,800,128]{2,1,0:T(8,128)(2,1)S(1)}, u32[]{:S(2)}, u32[]{:S(2)}) async-start(bf16[8,800,128]{2,1,0:T(8,128)(2,1)} %copy-done.44), calls=%async_computation.7 | async-start | bytes 3276800 | tf_op jit(solution)/shard_map/all_to_all | solution.py:1135
  662.3 82.2 %all-to-all-start.8 = ((bf16[8,768,256]{2,1,0:T(8,128)(2,1)}), bf16[8,768,256]{2,1,0:T(8,128)(2,1)}, u32[]{:S(2)}, u32[]{:S(2)}) async-start(bf16[8,768,256]{2,1,0:T(8,128)(2,1)} %copy-done.40), calls=%async_computation.8 | async-start | bytes 6291456 | tf_op jit(solution)/shard_map/all_to_all | solution.py:1135
  675.9 62.4 %copy-start.7 = (bf16[768,1024]{1,0:T(8,128)(2,1)S(1)}, bf16[768,1024]{1,0:T(8,128)(2,1)}, u32[]{:S(2)}) copy-start(bf16[768,1024]{1,0:T(8,128)(2,1)} %copy-done.6) | copy-start | bytes 4718596
  675.9 62.4 %copy-start.67 = (s32[6]{0:T(128)S(1)}, s32[6]{0:T(128)}, u32[]{:S(2)}) copy-start(s32[6]{0:T(128)} %get-tuple-element.289.meta) | copy-start | bytes 76
  744.5 70.3 %copy-start.68 = (f32[8,8,128]{2,1,0:T(8,128)}, f32[8,8,128]{2,1,0:T(8,128)S(1)}, u32[]{:S(2)}) copy-start(f32[8,8,128]{2,1,0:T(8,128)S(1)} %get-tuple-element.178.delta) | copy-start | bytes 98308
  814.8 9.1 collective-permute-start.7
  814.9 45.8 %all-to-all-start.9 = ((bf16[8,816,128]{2,1,0:T(8,128)(2,1)}), bf16[8,816,128]{2,1,0:T(8,128)(2,1)S(1)}, u32[]{:S(2)}, u32[]{:S(2)}) async-start(bf16[8,816,128]{2,1,0:T(8,128)(2,1)} %get-tuple-element.146), calls=%async_computation.9 | async-start | bytes 3342336 | tf_op jit(solution)/shard_map/all_to_all | solution.py:1135
  820.9 127.9 %collective-permute-start.6 = (bf16[1024,2560]{1,0:T(8,128)(2,1)}, bf16[1024,2560]{1,0:T(8,128)(2,1)}, u32[]{:S(2)}, u32[]{:S(2)}) collective-permute-start(bf16[1024,2560]{1,0:T(8,128)(2,1)} %get-tuple-element.198), channel_id=1, source_target_pairs={{0,8},{8,0},{16,24},{24,16},{1,9},{9,1},{17,25},{25,17},{2,10},{10... | collective-permute-start | bytes 15728648 | tf_op jit(solution)/shard_map/ppermute | solution.py:1162
  831.6 117.2 %collective-permute-start.8 = (bf16[1024,2560]{1,0:T(8,128)(2,1)}, bf16[1024,2560]{1,0:T(8,128)(2,1)}, u32[]{:S(2)}, u32[]{:S(2)}) collective-permute-start(bf16[1024,2560]{1,0:T(8,128)(2,1)} %add_convert_fusion.1), channel_id=1, source_target_pairs={{0,16},{8,24},{16,0},{24,8},{1,17},{9,25},{17,1},{25,9},{2,18},{10... | collective-permute-start | bytes 15728648 | tf_op jit(solution)/shard_map/ppermute | solution.py:1162
  860.6 80.9 %all-to-all-start.10 = ((bf16[8,768,128]{2,1,0:T(8,128)(2,1)}), bf16[8,768,128]{2,1,0:T(8,128)(2,1)S(1)}, u32[]{:S(2)}, u32[]{:S(2)}) async-start(bf16[8,768,128]{2,1,0:T(8,128)(2,1)} %copy-done.49), calls=%async_computation.10 | async-start | bytes 3145728 | tf_op jit(solution)/shard_map/all_to_all | solution.py:1135
  942.7 118.6 %all-to-all-start.11 = ((bf16[8,768,256]{2,1,0:T(8,128)(2,1)}), bf16[8,768,256]{2,1,0:T(8,128)(2,1)}, u32[]{:S(2)}, u32[]{:S(2)}) async-start(bf16[8,768,256]{2,1,0:T(8,128)(2,1)} %copy-done.37), calls=%async_computation.11 | async-start | bytes 6291456 | tf_op jit(solution)/shard_map/all_to_all | solution.py:1135
  948.7 248.7 %reduce-scatter.2.cloned.1.call-start = ((), (), s32[]{:S(2)}) async-start(), calls=%async_computation.19 | async-start | bytes 5898240 | tf_op jit(solution)/shard_map/reduce_scatter | solution.py:1375
  960.1 19.2 %copy-start.10 = (bf16[8,768,128]{2,1,0:T(8,128)(2,1)S(1)}, bf16[8,768,128]{2,1,0:T(8,128)(2,1)}, u32[]{:S(2)}) copy-start(bf16[8,768,128]{2,1,0:T(8,128)(2,1)} %copy-done.8) | copy-start | bytes 4718596
  960.1 19.2 %copy-start.15 = (bf16[1,256,1024]{2,1,0:T(8,128)(2,1)S(1)}, bf16[1,256,1024]{2,1,0:T(8,128)(2,1)}, u32[]{:S(2)}) copy-start(bf16[1,256,1024]{2,1,0:T(8,128)(2,1)} %param.29) | copy-start | bytes 1572868
  960.1 19.2 %copy-start.18 = (bf16[1,256,1024]{2,1,0:T(8,128)(2,1)S(1)}, bf16[1,256,1024]{2,1,0:T(8,128)(2,1)}, u32[]{:S(2)}) copy-start(bf16[1,256,1024]{2,1,0:T(8,128)(2,1)} %param.30) | copy-start | bytes 1572868
  960.1 19.2 %copy-start.26 = (bf16[768,1024]{1,0:T(8,128)(2,1)S(1)}, bf16[768,1024]{1,0:T(8,128)(2,1)}, u32[]{:S(2)}) copy-start(bf16[768,1024]{1,0:T(8,128)(2,1)} %get-tuple-element.130.grad) | copy-start | bytes 4718596
  1061.3 46.2 %all-to-all-start.12 = ((bf16[8,768,128]{2,1,0:T(8,128)(2,1)}), bf16[8,768,128]{2,1,0:T(8,128)(2,1)}, u32[]{:S(2)}, u32[]{:S(2)}) async-start(bf16[8,768,128]{2,1,0:T(8,128)(2,1)} %copy-done.48), calls=%async_computation.12 | async-start | bytes 3145728 | tf_op jit(solution)/shard_map/all_to_all | solution.py:1135
  1087.2 3.4 collective-permute-start.4
  1087.3 54.5 %collective-permute-start.3 = (bf16[1024,512]{1,0:T(8,128)(2,1)}, bf16[1024,512]{1,0:T(8,128)(2,1)}, u32[]{:S(2)}, u32[]{:S(2)}) collective-permute-start(bf16[1024,512]{1,0:T(8,128)(2,1)} %get-tuple-element.194), channel_id=1, source_target_pairs={{0,8},{8,0},{16,24},{24,16},{1,9},{9,1},{17,25},{25,17},{2,10},{10... | collective-permute-start | bytes 3145736 | tf_op jit(solution)/shard_map/ppermute | solution.py:1162
  1091.9 49.9 %collective-permute-start.5 = (bf16[1024,512]{1,0:T(8,128)(2,1)}, bf16[1024,512]{1,0:T(8,128)(2,1)}, u32[]{:S(2)}, u32[]{:S(2)}) collective-permute-start(bf16[1024,512]{1,0:T(8,128)(2,1)} %add_convert_fusion.3), channel_id=1, source_target_pairs={{0,16},{8,24},{16,0},{24,8},{1,17},{9,25},{17,1},{25,9},{2,18},{10... | collective-permute-start | bytes 3145736 | tf_op jit(solution)/shard_map/ppermute | solution.py:1162
  1135.2 13.6 %all-to-all-start.13 = ((f32[32,1,65]{2,1,0:T(1,128)}), f32[32,1,65]{2,1,0:T(1,128)S(1)}, u32[]{:S(2)}, u32[]{:S(2)}) async-start(f32[32,1,65]{2,1,0:T(1,128)} %bitcast.26), calls=%async_computation.13 | async-start | bytes 32768 | tf_op jit(solution)/shard_map/all_to_all | solution.py:1395
  1141.8 26.7 %copy-start.57 = (bf16[1024,256]{1,0:T(8,128)(2,1)S(1)}, bf16[1024,256]{1,0:T(8,128)(2,1)}, u32[]{:S(2)}) copy-start(bf16[1024,256]{1,0:T(8,128)(2,1)} %copy-done.56) | copy-start | bytes 1572868
  1148.8 29.5 %all-to-all-start.15 = ((bf16[8,128,512]{2,1,0:T(8,128)(2,1)}), bf16[8,128,512]{2,1,0:T(8,128)(2,1)S(1)}, u32[]{:S(2)}, u32[]{:S(2)}) async-start(bf16[8,128,512]{2,1,0:T(8,128)(2,1)} %bitcast.51), calls=%async_computation.15 | async-start | bytes 2097152 | tf_op jit(solution)/shard_map/all_to_all | solution.py:1372
  1152.4 2.0 collective-permute-start.1
  1152.5 2.7 collective-permute-start
  1154.5 14.0 %collective-permute-start.2 = (bf16[1024,256]{1,0:T(8,128)(2,1)S(1)}, bf16[1024,256]{1,0:T(8,128)(2,1)S(1)}, u32[]{:S(2)}, u32[]{:S(2)}) collective-permute-start(bf16[1024,256]{1,0:T(8,128)(2,1)S(1)} %add_convert_fusion.5), channel_id=1, source_target_pairs={{0,16},{8,24},{16,0},{24,8},{1,17},{9,25},{17,1},{25,9},{2,18},{10... | collective-permute-start | bytes 1572872 | tf_op jit(solution)/shard_map/ppermute | solution.py:1162
  1178.4 18.3 %all-to-all-start.14 = ((bf16[8,128,256]{2,1,0:T(8,128)(2,1)}), bf16[8,128,256]{2,1,0:T(8,128)(2,1)S(1)}, u32[]{:S(2)}, u32[]{:S(2)}) async-start(bf16[8,128,256]{2,1,0:T(8,128)(2,1)} %bitcast.28), calls=%async_computation.14 | async-start | bytes 1048576 | tf_op jit(solution)/shard_map/all_to_all | solution.py:1372
  (68 other events, 326.1 us)
Sparse Core Ops, SparseCore 0:
  11.5 82.0 all-gather.2
  95.6 352.5 all-gather.4
  958.9 165.6 reduce-scatter.1

commit v2 on v1

--- a/solution.py
+++ b/solution.py
@@ -13,7 +13,7 @@
 low = jnp.bfloat16
 wide = jnp.float32
 lanes = 128
-hint = 0.25
+hint = 0.1
 
 
 def norm_rows(values, scaling):
@@ -123,7 +123,7 @@
     return pl.ds(pl.multiple_of(index * size, size), size)
 
 
-def copy_tokens(sz, own_block, query_in, pair_in, extra, queries, keys, values, sems):
+def copy_tokens(sz, own_block, tokens, extra, queries, keys, values, sems):
     pr, hr = sz.prompt, sz.half
     moves = []
     for j in range(sz.heads):
@@ -134,10 +134,9 @@
         )
         for row, count, query_at, key_at in spots:
             rows = pl.ds(row, count)
-            moves.append((query_in.at[j, rows], queries.at[pl.ds(query_at, count)]))
-            for lane, ref in ((0, keys), (1, values)):
-                source = pair_in.at[j, rows, pl.ds(lane * lanes, lanes)]
-                moves.append((source, ref.at[pl.ds(key_at, count), pl.ds(0, lanes)]))
+            for lane, ref, at in ((0, keys, key_at), (1, values, key_at), (2, queries, query_at)):
+                source = tokens.at[j, rows, pl.ds(lane * lanes, lanes)]
+                moves.append((source, ref.at[pl.ds(at, count), pl.ds(0, lanes)]))
     for e in range(1, sz.blocks):
         start = pl.multiple_of((own_block ^ e) * sz.own_prompt, sz.own_prompt)
         for lane, ref in ((0, keys), (1, values)):
@@ -159,12 +158,12 @@
 
 def attend_kernel(sz, meta, *refs):
     n, extras = sz.heads, sz.blocks - 1
-    query_in, pair_in, extra = refs[0], refs[1], refs[2 : 2 + extras]
-    out, queries, keys, values, scores, total, mixed, sums, packed, aux, sems = refs[2 + extras :]
+    tokens, extra = refs[0], refs[1 : 1 + extras]
+    out, queries, keys, values, scores, total, mixed, sums, packed, aux, sems = refs[1 + extras :]
     own_block = meta[1]
     size = sz.block
     scale = float(lanes**-0.5 * log2e)
-    copies = copy_tokens(sz, own_block, query_in, pair_in, extra, queries, keys, values, sems)
+    copies = copy_tokens(sz, own_block, tokens, extra, queries, keys, values, sems)
     for copy in copies:
         copy.start()
     values[:, lanes:] = jnp.ones_like(values[:, lanes:])
@@ -207,15 +206,69 @@
         mixed[rows_at(query_index, size), :] = (total[:, :lanes] / weight).astype(low)
         sums[:, rows_at(query_index, size)] = (best + jnp.log2(weight)).T[0:8, :]
 
-    @pl.loop(0, own_blocks)
-    def _(index):
-        one(index, offset + index, offset + index, causal_mask((size, size), 0))
-
-    @pl.loop(0, sz.all_reply // size)
-    def _(index):
-        live = meta[2 + own_block * (sz.all_reply // size) + index]
-        mask = self_mask((size, size), 0, sz.half, live)
-        one(own_blocks + index, prompt_blocks, prompt_blocks + index, mask)
+    def longest(ref, count):
+        def grow(index, best):
+            rows = ref[rows_at(index, size), 0:lanes].astype(wide)
+            return jnp.maximum(best, jnp.sum(rows * rows, axis=1, keepdims=True))
+
+        return jnp.max(lax.fori_loop(0, count, grow, jnp.zeros((size, 1), wide)))
+
+    bound = longest(queries, sz.queries // size) * longest(keys, sz.keys // size)
+    small = bound * (scale * scale) <= 3600.0
+
+    def quick(query_index, full_blocks, last_block, mask):
+        query = queries[rows_at(query_index, size), :]
+
+        def weighted(start, count, mask=None):
+            rows = pl.ds(pl.multiple_of(start * size, size), count * size)
+            tile = along_cols(query, keys[rows, :]) * scale
+            if mask is not None:
+                tile = jnp.where(mask, tile, masked_score)
+            return product(jnp.exp2(tile).astype(low), values[rows, :])
+
+        total[...] = weighted(last_block, 1, mask)
+        if isinstance(full_blocks, int):
+            done = 0
+            while done < full_blocks:
+                count = min(4, full_blocks - done)
+                total[...] += weighted(done, count)
+                done += count
+        else:
+
+            @pl.loop(0, full_blocks // 4)
+            def _(index):
+                total[...] += weighted(index * 4, 4)
+
+            done = full_blocks // 4 * 4
+            for count in (2, 1):
+
+                @pl.when(full_blocks - done >= count)
+                def _(done=done, count=count):
+                    total[...] += weighted(done, count)
+
+                done = jnp.where(full_blocks - done >= count, done + count, done)
+        weight = total[:, lanes:]
+        mixed[rows_at(query_index, size), :] = (total[:, :lanes] / weight).astype(low)
+        sums[:, rows_at(query_index, size)] = jnp.log2(weight).T[0:8, :]
+
+    def every(run):
+        @pl.loop(0, own_blocks)
+        def _(index):
+            run(index, offset + index, offset + index, causal_mask((size, size), 0))
+
+        @pl.loop(0, sz.all_reply // size)
+        def _(index):
+            live = meta[3 + own_block * (sz.all_reply // size) + index]
+            mask = self_mask((size, size), 0, sz.half, live)
+            run(own_blocks + index, prompt_blocks, prompt_blocks + index, mask)
+
+    @pl.when(small)
+    def _():
+        every(quick)
+
+    @pl.when(jnp.logical_not(small))
+    def _():
+        every(one)
 
     packed[...] = jnp.zeros_like(packed)
     for j in range(n):
@@ -268,7 +321,7 @@
     return pl.BlockSpec(memory_space=pl.ANY)
 
 
-def attend(sz, meta, queries, pairs, extra):
+def attend(sz, meta, tokens, extra):
     n = sz.heads
     cost = cost_hint(12 * lanes * pair_count(sz), pair_count(sz), 8 << 20)
     return pl.pallas_call(
@@ -277,7 +330,7 @@
         grid_spec=pltpu.PrefetchScalarGridSpec(
             num_scalar_prefetch=1,
             grid=(),
-            in_specs=[in_place()] * (2 + len(extra)),
+            in_specs=[in_place()] * (1 + len(extra)),
             out_specs=in_place(),
             scratch_shapes=[
                 pltpu.VMEM((sz.queries, lanes), low),
@@ -295,13 +348,13 @@
         compiler_params=pltpu.CompilerParams(vmem_limit_bytes=36 << 20),
         cost_estimate=cost,
         name="attend",
-    )(meta, queries, pairs, *extra)
+    )(meta, tokens, *extra)
 
 
 def attend_back_kernel(sz, meta, *refs):
     n, extras = sz.heads, sz.blocks - 1
-    query_in, pair_in, messages = refs[:3]
-    extra, refs = refs[3 : 3 + extras], refs[3 + extras :]
+    tokens, messages = refs[:2]
+    extra, refs = refs[2 : 2 + extras], refs[2 + extras :]
     query_out, pair_out, refs = refs[0], refs[1], refs[2:]
     partial = None
     if extras:
@@ -312,7 +365,7 @@
     pr, hr, size = sz.prompt, sz.half, sz.block
     scale = float(lanes**-0.5 * log2e)
     plain_scale = float(lanes**-0.5)
-    copies = copy_tokens(sz, own_block, query_in, pair_in, extra, queries, keys, values, sems)
+    copies = copy_tokens(sz, own_block, tokens, extra, queries, keys, values, sems)
     for j in range(n):
         spots = (
             (upstream.at[pl.ds(j * pr, pr)], 0, pr),
@@ -353,8 +406,9 @@
     reply_blocks = sz.all_reply // size
     offset = own_block * own_blocks
 
-    def step(key_index, query_index, mask=None):
-        at_key, at_query = rows_at(key_index, size), rows_at(query_index, size)
+    def step(key_index, query_index, mask=None, count=1):
+        at_key = rows_at(key_index, size)
+        at_query = pl.ds(pl.multiple_of(query_index * size, size), count * size)
         key, value = keys[at_key, :], values[at_key, :]
         query, grad = queries[at_query, :], upstream[at_query, :]
         logits = along_cols(key, query) * scale - stats[0:1, at_query]
@@ -374,13 +428,25 @@
         def _():
             step(key_index, own, causal_mask((size, size), 1))
 
-        @pl.loop(jnp.clip(own + 1, 0, own_blocks), own_blocks + reply_blocks)
-        def _(query_index):
-            step(key_index, query_index)
+        begin = jnp.clip(own + 1, 0, own_blocks)
+        count = own_blocks + reply_blocks - begin
+
+        @pl.loop(0, count // 4)
+        def _(index):
+            step(key_index, begin + index * 4, count=4)
+
+        done = count // 4 * 4
+        for part in (2, 1):
+
+            @pl.when(count - done >= part)
+            def _(done=done, part=part):
+                step(key_index, begin + done, count=part)
+
+            done = jnp.where(count - done >= part, done + part, done)
 
     @pl.loop(0, reply_blocks)
     def _(index):
-        live = meta[2 + own_block * reply_blocks + index]
+        live = meta[3 + own_block * reply_blocks + index]
         step(prompt_blocks + index, own_blocks + index, self_mask((size, size), 1, hr, live))
 
     if extras:
@@ -407,7 +473,7 @@
         copy.wait()
 
 
-def attend_back(sz, meta, queries, pairs, messages, extra):
+def attend_back(sz, meta, tokens, messages, extra):
     n = sz.heads
     out_shape = [jax.ShapeDtypeStruct((n, sz.rows, k * lanes), low) for k in (1, 2)]
     out_specs = [in_place()] * 2
@@ -421,7 +487,7 @@
         grid_spec=pltpu.PrefetchScalarGridSpec(
             num_scalar_prefetch=1,
             grid=(),
-            in_specs=[in_place()] * (3 + len(extra)),
+            in_specs=[in_place()] * (2 + len(extra)),
             out_specs=out_specs,
             scratch_shapes=[
                 pltpu.VMEM((sz.queries, lanes), low),
@@ -441,7 +507,7 @@
         compiler_params=pltpu.CompilerParams(vmem_limit_bytes=40 << 20),
         cost_estimate=cost,
         name="attend_back",
-    )(meta, queries, pairs, messages, *extra)
+    )(meta, tokens, messages, *extra)
 
 
 def fixed(shape):
@@ -500,7 +566,7 @@
 
 
 def project_kernel(
-    sz, meta, prompt_ref, reply_ref, gain_ref, query_w, pair_w, query_out, pair_out, normed_ref
+    sz, meta, prompt_ref, reply_ref, gain_ref, query_w, pair_w, out, normed_ref
 ):
     @pl.when(pl.program_id(0) == 0)
     def _():
@@ -508,13 +574,13 @@
             values = norm_rows(ref[...].astype(wide), gain_ref[...])
             normed_ref[begin : begin + count, :] = values.astype(low)
 
-    query_out[...] = along_cols(normed_ref[...], query_w[...]).astype(low)
-    pair_out[...] = along_cols(normed_ref[...], pair_w[...]).astype(low)
+    out[:, 0 : 2 * lanes] = along_cols(normed_ref[...], pair_w[...]).astype(low)
+    out[:, 2 * lanes :] = along_cols(normed_ref[...], query_w[...]).astype(low)
 
 
 def project(sz, meta, micro, prompt_in, reply_in, gain, weights):
     width = prompt_in.shape[3]
-    per = weights.shape[0] // (3 * lanes)
+    per = sz.heads // (weights.shape[1] // width)
     n = sz.heads
     return call(
         functools.partial(project_kernel, sz),
@@ -529,8 +595,7 @@
             (weights, pair_weights(width, per)),
         ],
         [
-            (shaped((n, sz.rows, lanes), low), per_step((sz.rows, lanes))),
-            (shaped((n, sz.rows, 2 * lanes), low), per_step((sz.rows, 2 * lanes))),
+            (shaped((n, sz.rows, 3 * lanes), low), per_step((sz.rows, 3 * lanes))),
             (shaped((sz.rows, width), low), fixed((sz.rows, width))),
         ],
         flops=6 * sz.rows * width * lanes * n,
@@ -597,7 +662,7 @@
 
 
 def queries_of(sz, chunks):
-    return (chunks, pl.BlockSpec((None, sz.rows, lanes), lambda d, meta: (d, 0, 0)))
+    return (chunks, pl.BlockSpec((None, sz.rows, lanes), lambda d, meta: (d, 0, 2)))
 
 
 def cache_forward(sz, meta, chunks, words, cache_key, cache_value):
@@ -718,6 +783,17 @@
     )[0]
 
 
+def powers(count):
+    return [1 << i for i in range(count.bit_length() - 1)]
+
+
+def xor_order(count):
+    order = [0]
+    for away in reversed(powers(count)):
+        order = order + [place ^ away for place in order]
+    return order
+
+
 def tile_rows(rows):
     return 384 if rows % 384 == 0 else rows
 
@@ -733,12 +809,9 @@
     mixed,
     weight,
     gain,
-    out_w,
-    gate_w,
-    up_w,
-    down_w,
     *refs,
 ):
+    sources = refs[: 2 * groups]
     (
         prompt_out,
         reply_out,
@@ -754,11 +827,69 @@
         inward,
         gate_slope,
         up_slope,
-    ) = refs[-14:]
+        inner_w,
+        out_w,
+        sems,
+        out_sems,
+    ) = refs[-18:]
     step = pl.program_id(0)
+    seq_place = meta[2]
     rows, tile = sz.rows, tile_rows(sz.rows)
-    width = middle.shape[1]
-    part = out_w.shape[0]
+    part = out_w.shape[1]
+    inner_count = inner_w.shape[2]
+
+    shards, shard = sources[0].shape[0], sources[0].shape[2]
+
+    def copies_from(source, row, count, target, sems):
+        moves = []
+        for j, place in enumerate(xor_order(shards)):
+            start = 0
+            if shards > 1:
+                start = pl.multiple_of((seq_place ^ place) * shard, shard)
+            part_of = source.at[j, pl.ds(row, count), :]
+            moves.append(
+                pltpu.make_async_copy(part_of, target.at[:, pl.ds(start, shard)], sems.at[j])
+            )
+        return moves
+
+    def fetches(d, slot):
+        moves = []
+        for k, (source, row) in enumerate(((0, 0), (0, inner_count), (1, 0))):
+            target = inner_w.at[slot, k]
+            moves += copies_from(sources[2 * d + source], row, inner_count, target, sems.at[slot, k])
+        return moves
+
+    def out_fetches():
+        moves = []
+        for d in range(groups):
+            target = out_w.at[meta[0] ^ d]
+            moves += copies_from(sources[2 * d + 1], inner_count, part, target, out_sems.at[d])
+        return moves
+
+    turns = list(range(groups)) + list(range(groups - 2, -1, -1))
+    fetch_of = [min(i, groups - 1) if i <= groups else i - 1 for i in range(2 * groups)]
+
+    @pl.when(step == 0)
+    def _():
+        for move in out_fetches() + fetches(0, 0):
+            move.start()
+        for move in out_fetches():
+            move.wait()
+
+    for i in range(2 * groups):
+        if i > 0 and fetch_of[i] == fetch_of[i - 1]:
+            continue
+
+        @pl.when(step == i)
+        def _(i=i):
+            for move in fetches(turns[fetch_of[i]], fetch_of[i] % 2):
+                move.wait()
+            if fetch_of[i] + 1 < len(turns):
+                for move in fetches(turns[fetch_of[i] + 1], (fetch_of[i] + 1) % 2):
+                    move.start()
+
+    slot = jnp.where(step > groups - 1, step - 1, step) % 2
+    gate_w, up_w, down_w = (inner_w.at[slot, k] for k in range(3))
     parts = ((0, sz.prompt, prompt_ref, prompt_teach, prompt_out),)
     parts = parts + ((sz.prompt, sz.half, reply_ref, reply_teach, reply_out),)
 
@@ -767,7 +898,7 @@
         stats[...] = jnp.zeros_like(stats)
         for g in range(groups):
             at = slice(g * part, (g + 1) * part)
-            moved = along_cols(mixed[...], out_w[:, g * width : (g + 1) * width])
+            moved = along_cols(mixed[...], out_w[g])
             for begin, count, source, _, _ in parts:
                 middle[begin : begin + count, at] = (
                     source[:, at].astype(wide) + moved[begin : begin + count, :]
@@ -835,7 +966,7 @@
         middle[...] = total[...] + back
         for g in range(groups):
             at = slice(g * part, (g + 1) * part)
-            piece = product(middle[:, at].astype(low), out_w[:, g * width : (g + 1) * width])
+            piece = product(middle[:, at].astype(low), out_w[g])
             if g == 0:
                 inward[...] = piece
             elif g < groups - 1:
@@ -846,16 +977,12 @@
 
 def feed_forward(sz, meta, micro, arrays, mixed, weight, gain, weights, prior):
     prompt_in, reply_in, prompt_teach, reply_teach = arrays
-    out_w, inner_w, inner = weights
+    shares, inner = weights
     width = prompt_in.shape[3]
-    groups = inner_w.shape[1] // width
+    groups = len(shares) // 2
+    piece = shares[1].shape[1] - inner
+    shards = shares[0].shape[0]
     rows = sz.rows
-
-    def weight_spec(k):
-        return pl.BlockSpec(
-            (inner, width), lambda d, meta: (k, jnp.minimum(d, 2 * groups - 1 - d))
-        )
-
     ins = [
         (prompt_in, of_micro(micro, sz.prompt, width)),
         (reply_in, of_micro(micro, sz.half, width)),
@@ -864,11 +991,9 @@
         (mixed, fixed((rows, width))),
         (weight, fixed((rows, 2))),
         (gain, fixed((1, width))),
-        (out_w, fixed(out_w.shape)),
-        (inner_w, weight_spec(0)),
-        (inner_w, weight_spec(1)),
-        (inner_w, weight_spec(2)),
     ]
+    for share in shares:
+        ins.append((share, in_place()))
     aliases = {}
     for i, array in enumerate(prior):
         aliases[len(ins) + 1] = i
@@ -879,10 +1004,12 @@
     ]
     plain = fixed((rows, width))
     inner_shape = shaped((groups, rows, inner), low)
-    early = pl.BlockSpec((None, rows, inner), lambda d, meta: (jnp.minimum(d, groups - 1), 0, 0))
+    early = pl.BlockSpec(
+        (None, rows, inner), lambda d, meta: (meta[0] ^ jnp.minimum(d, groups - 1), 0, 0)
+    )
     late = pl.BlockSpec(
         (None, rows, inner),
-        lambda d, meta: (jnp.minimum(groups - 1, 2 * groups - 1 - d), 0, 0),
+        lambda d, meta: (meta[0] ^ jnp.minimum(groups - 1, 2 * groups - 1 - d), 0, 0),
     )
     return call(
         functools.partial(feed_kernel, sz, groups),
@@ -906,6 +1033,10 @@
             pltpu.VMEM((rows, width), wide),
             pltpu.VMEM((groups, rows, inner), low),
             pltpu.VMEM((groups, rows, inner), low),
+            pltpu.VMEM((2, 3, inner, width), low),
+            pltpu.VMEM((groups, piece, width), low),
+            pltpu.SemaphoreType.DMA((2, 3, shards)),
+            pltpu.SemaphoreType.DMA((groups, shards)),
         ],
         flops=4 * rows * width * (width + 3 * groups * inner),
         vmem=60,
@@ -967,64 +1098,86 @@
         summed(2 * stride, lambda b, dy, o, mid, hid, dg, du: (dy[...], hid[...]))
         summed(3 * stride, lambda b, dy, o, mid, hid, dg, du: (o[...], mid[...].astype(low)))
 
-    for turn, target in enumerate(outs):
-        slot = turn % 2
+    def move(turn):
+        return pltpu.make_async_copy(buffer.at[turn], outs[turn], sems.at[turn])
+
+    fill(buffer.at[step])
+    for turn in range(len(outs)):
 
         @pl.when(step == turn)
-        def _(turn=turn, target=target, slot=slot):
-            if turn >= 2:
-                pltpu.make_async_copy(buffer.at[slot], outs[turn - 2], sems.at[slot]).wait()
-            fill(buffer.at[slot])
-            pltpu.make_async_copy(buffer.at[slot], target, sems.at[slot]).start()
-            if turn == len(outs) - 1:
-                for back in (1, 0):
-                    spot = (turn - back) % 2
-                    pltpu.make_async_copy(buffer.at[spot], outs[turn - back], sems.at[spot]).wait()
-
-
-def weight_grads(sz, meta, parts):
+        def _(turn=turn):
+            move(turn).start()
+
+    @pl.when(step == len(outs) - 1)
+    def _():
+        for turn in range(len(outs)):
+            move(turn).wait()
+
+
+def weight_grads(sz, meta, parts, first):
     groups, rows, inner = parts[0][4].shape
+    turns = groups // 2
     width = parts[0][0].shape[1]
     piece = width // groups
     ins = []
-    block = pl.BlockSpec((None, rows, inner), lambda d, meta: (meta[0] ^ away_of(d), 0, 0))
+    block = pl.BlockSpec((None, rows, inner), lambda d, meta: (meta[0] ^ away_of(d + first), 0, 0))
     for second, low_upstream, mixed, middle_grad, hidden, gate_grad, up_grad in parts:
         for array in (second, low_upstream, mixed):
             ins.append((array, fixed((rows, width))))
-        spec = pl.BlockSpec((rows, piece), lambda d, meta: (0, meta[0] ^ away_of(d)))
+        spec = pl.BlockSpec((rows, piece), lambda d, meta: (0, meta[0] ^ away_of(d + first)))
         ins.append((middle_grad, spec))
         for array in (hidden, gate_grad, up_grad):
             ins.append((array, block))
-    columns = 3 * (-(-inner // lanes) * lanes) + piece
+    stride = -(-inner // lanes) * lanes
+    columns = 3 * stride + piece
     return call(
         functools.partial(weight_grad_kernel, len(parts)),
         "weight_grads",
-        groups,
+        turns,
         meta,
         ins,
-        [(shaped((width, columns), low), in_place())] * len(aways),
-        scratch=[pltpu.VMEM((2, width, columns), low), pltpu.SemaphoreType.DMA((2,))],
-        flops=2 * len(parts) * rows * width * (3 * groups * inner + width),
+        [(shaped((width, columns), low), in_place())] * turns,
+        scratch=[pltpu.VMEM((turns, width, columns), low), pltpu.SemaphoreType.DMA((turns,))],
+        flops=len(parts) * rows * width * (3 * groups * inner + width),
         vmem=60,
     )
 
 
-def finish_kernel(sz, span, query_side, has_prior, last, per, meta, *refs):
-    chunk, weights, normed, *refs = refs
-    if query_side:
-        extra, carried, middle, prompt_ref, reply_ref, gain, *refs = refs
-    prior = None
-    if has_prior:
-        prior, refs = refs[0], refs[1:]
-    if query_side:
-        prompt_out, reply_out, stats, *weight_outs, total = refs[-(5 if not last else 8) :]
-    else:
-        total, *weight_outs = refs[-(2 if not last else 5) :]
+def finish_kernel(sz, sides, has_carried, has_tokens, has_prior, form, per, meta, *refs):
+    refs = list(refs)
+    normed = refs.pop(0)
+    inputs = []
+    for side in sides:
+        chunk, weights = refs.pop(0), refs.pop(0)
+        extra = refs.pop(0) if side == "query" else None
+        inputs.append((chunk, weights, extra, refs.pop(0) if has_prior else None))
+    carried = refs.pop(0) if has_carried else None
+    if has_tokens:
+        middle, prompt_ref, reply_ref, gain = (refs.pop(0) for _ in range(4))
+    count = 4 if form == "away" else 1
+    weight_outs = refs[-1 - count * len(sides) : -1]
+    total = refs[-1]
+    if has_tokens:
+        prompt_out, reply_out, stats = refs[-4 - count * len(sides) : -1 - count * len(sides)]
     step = pl.program_id(0)
-    grads = chunk[...]
-    if query_side:
-        grads = (grads.astype(wide) + extra[...]).astype(low)
-    part = product(grads, weights[...])
+    part = None
+    for i, (chunk, weights, extra, prior) in enumerate(inputs):
+        grads = chunk[...]
+        if extra is not None:
+            grads = (grads.astype(wide) + extra[...]).astype(low)
+        piece = product(grads, weights[...])
+        part = piece if part is None else part + piece
+        weight_part = along_rows(normed[...], grads)
+        if has_prior:
+            weight_part = weight_part + prior[...]
+
+        def put(out, weight_part=weight_part):
+            out[...] = weight_part.astype(low)
+
+        if form == "away":
+            write_away(weight_outs[4 * i : 4 * i + 4], per, put)
+        else:
+            weight_outs[i][...] = weight_part.astype(weight_outs[i].dtype)
 
     @pl.when(step == 0)
     def _():
@@ -1034,62 +1187,65 @@
     def _():
         total[...] += part
 
-    weight_part = along_rows(normed[...], grads)
-    if has_prior:
-        weight_part = weight_part + prior[...]
-
-    def put(out):
-        out[...] = weight_part.astype(low)
-
-    if last:
-        write_away(weight_outs, per, put)
-    else:
-        weight_outs[0][...] = weight_part
-    if query_side:
+    if has_tokens:
 
         @pl.when(step == sz.heads - 1)
         def _():
             stats[...] = jnp.zeros_like(stats)
-            for begin, count, source, out in (
+            for begin, rows, source, out in (
                 (0, sz.prompt, prompt_ref, prompt_out),
                 (sz.prompt, sz.half, reply_ref, reply_out),
             ):
-                at = slice(begin, begin + count)
-                upstream = carried[at, :] + total[at, :]
+                at = slice(begin, begin + rows)
+                upstream = total[at, :]
+                if has_carried:
+                    upstream = upstream + carried[at, :]
                 back, gain_part = norm_back(source[...].astype(wide), gain[...], upstream)
                 stats[0:1, :] += gain_part[None]
                 out[...] = middle[at, :] + back
 
 
-def finish(sz, meta, micro, chunks, weights, normed, prior, last, tokens=None):
+def finish(sz, meta, micro, chunks, weights, normed, prior, form, carried=None, tokens=None):
     n, rows = sz.heads, sz.rows
     width = normed.shape[1]
-    span = chunks.shape[2]
-    per = weights.shape[0] // (3 * lanes)
-    groups = n // per
-    query_side = tokens is not None
+    groups = weights.shape[1] // width
+    per = n // groups
 
     def head(d, meta):
         return per * (meta[0] ^ away_of(d, per)) + d % per
 
-    if query_side:
-        weight_spec = pl.BlockSpec(
-            (span, width), lambda d, meta: (head(d, meta) % per, head(d, meta) // per)
-        )
-    else:
-        weight_spec = pl.BlockSpec(
-            (span, width), lambda d, meta: (per // 2 + head(d, meta) % per, head(d, meta) // per)
-        )
-    by_step = pl.BlockSpec((None, rows, span), lambda d, meta: (head(d, meta), 0, 0))
     plain = fixed((rows, width))
-    ins = [(chunks, by_step), (weights, weight_spec), (normed, plain)]
-    outs = []
-    aliases = {}
-    scratch = []
-    if query_side:
-        prompt_in, reply_in, extra, carried, middle, gain, before = tokens
-        ins.append((extra, by_step))
+    ins = [(normed, plain)]
+    weight_outs = []
+    for side, chunk in chunks.items():
+        base, span = (0, lanes) if side == "query" else (per // 2, 2 * lanes)
+
+        def place(d, meta, base=base):
+            return (base + head(d, meta) % per, head(d, meta) // per)
+
+        by_step = pl.BlockSpec((None, rows, span), lambda d, meta: (head(d, meta), 0, 0))
+        grad_spec = pl.BlockSpec((None, width, span), lambda d, meta: (head(d, meta), 0, 0))
+        if side == "query":
+            ins += [(chunk[0], by_step), (weights, pl.BlockSpec((span, width), place))]
+            ins.append((chunk[1], by_step))
+        else:
+            ins += [(chunk, by_step), (weights, pl.BlockSpec((span, width), place))]
+        if prior is not None:
+            ins.append((prior[side], grad_spec))
+        if form == "away":
+            weight_outs += away_outs(width, span, per)
+        elif form == "whole":
+            whole_spec = pl.BlockSpec(
+                (None, width, span), lambda d, meta: (head(d, meta) // per, 0, head(d, meta) % per)
+            )
+            weight_outs.append((shaped((groups, width, per * span), low), whole_spec))
+        else:
+            weight_outs.append((shaped((n, width, span), wide), grad_spec))
+    if carried is not None:
         ins.append((carried, plain))
+    outs, scratch, aliases = [], [], {}
+    if tokens is not None:
+        prompt_in, reply_in, middle, gain, before = tokens
         ins.append((middle, plain))
         ins.append((prompt_in, of_micro(micro, sz.prompt, width)))
         ins.append((reply_in, of_micro(micro, sz.half, width)))
@@ -1097,30 +1253,33 @@
         outs.append((shaped(prompt_in.shape, wide), of_micro(micro, sz.prompt, width)))
         outs.append((shaped(reply_in.shape, wide), of_micro(micro, sz.half, width)))
         outs.append((shaped((8, width), wide), fixed((8, width))))
+        outs += weight_outs
         scratch.append(pltpu.VMEM((rows, width), wide))
-    else:
-        outs.append((shaped((rows, width), wide), plain))
-    grad_spec = pl.BlockSpec((None, width, span), lambda d, meta: (head(d, meta), 0, 0))
-    if prior is not None:
-        ins.append((prior, grad_spec))
-    if query_side:
         for i, array in enumerate(before):
             aliases[len(ins) + 1] = i
             ins.append((array, in_place()))
-    if last:
-        outs.extend(away_outs(width, span, per))
     else:
-        outs.append((shaped((n, width, span), wide), grad_spec))
+        outs += weight_outs + [(shaped((rows, width), wide), plain)]
+    sides = tuple(chunks)
     return call(
-        functools.partial(finish_kernel, sz, span, query_side, prior is not None, last, per),
+        functools.partial(
+            finish_kernel,
+            sz,
+            sides,
+            carried is not None,
+            tokens is not None,
+            prior is not None,
+            form,
+            per,
+        ),
         "finish",
         n,
         meta,
         ins,
         outs,
         scratch=scratch,
-        flops=4 * rows * width * span * n,
-        vmem=44,
+        flops=4 * rows * width * lanes * n * (2 * len(sides) - 1),
+        vmem=52,
         aliases=aliases,
     )
 
@@ -1139,7 +1298,7 @@
     if sz.blocks == 1:
         return []
     count = lax.axis_size("seq")
-    own = pairs[:, : sz.prompt].reshape(sz.own_prompt, 2 * lanes)
+    own = pairs[:, : sz.prompt, : 2 * lanes].reshape(sz.own_prompt, 2 * lanes)
     return [
         lax.ppermute(own, "seq", [(i, i ^ e * sz.heads) for i in range(count)])
         for e in range(1, sz.blocks)
@@ -1162,12 +1321,21 @@
     return lax.ppermute(array, "grp", [(i, i ^ away) for i in range(count)])
 
 
-def over_groups(blocks):
-    to_core_far, to_core, to_chip, stays = blocks
-    handed = to_chip.astype(wide) + along_grp(to_core_far, 1).astype(wide)
+def along_seq(array, away):
+    count = lax.axis_size("seq")
+    return lax.ppermute(array, "seq", [(i, i ^ away) for i in range(count)])
+
+
+def hand_over(blocks):
+    return (blocks[2].astype(wide) + along_grp(blocks[0], 1).astype(wide)).astype(low)
+
+
+def over_groups(blocks, far=None):
+    _, to_core, _, stays = blocks
     near = along_grp(to_core, 1)
-    far = along_grp(handed.astype(low), 2)
-    return (stays.astype(wide) + near.astype(wide) + far.astype(wide)).astype(low)
+    if far is None:
+        far = along_grp(hand_over(blocks), 2)
+    return stays.astype(wide) + near.astype(wide) + far.astype(wide)
 
 
 def after(value, *others):
@@ -1218,13 +1386,6 @@
     per_grp = w_query.shape[1] // lanes
     everywhere = ("grp", "seq")
 
-    def gathered(part, axis):
-        return lax.all_gather(part, everywhere, axis=axis, tiled=True)
-
-    def shared(values):
-        count = grp_count * seq_count
-        return lax.all_to_all(jnp.broadcast_to(values, (count,) + values.shape), everywhere, 0, 0)
-
     half_index = jnp.arange(sz.half)
     valids, metas = [], []
     for micro in micros:
@@ -1233,81 +1394,96 @@
         valids.append(jnp.concatenate([prompt_mask[micro, 0], reply_mask[micro, 0] * reply_live]))
         metas.append(
             jnp.concatenate(
-                [jnp.stack([lax.axis_index("grp"), own_block]).astype(jnp.int32), lengths[micro, 0]]
+                [
+                    jnp.stack([lax.axis_index("grp"), own_block, position]).astype(jnp.int32),
+                    lengths[micro, 0],
+                ]
             )
         )
     own_count = sum(jnp.sum(v) for v in valids)
     share = attn_gain.shape[0]
     counts = jnp.stack([own_count // 256, own_count % 256]).astype(low)
-    small = shared(jnp.concatenate([attn_gain, ffn_gain, counts]))
-    gain_one = small[:, :share].reshape(1, model_width).astype(wide)
-    gain_two = small[:, share : 2 * share].reshape(1, model_width).astype(wide)
-    counts = jnp.sum(small[:, 2 * share :].astype(wide), axis=0)
-    valid_total = counts[0] * 256.0 + counts[1]
-    coefficient = slot_count / valid_total
-
+    small = jnp.concatenate([attn_gain, ffn_gain, counts])
+    lines = -(-small.shape[0] // row_part)
+    small = jnp.pad(small, (0, lines * row_part - small.shape[0])).reshape(lines, row_part)
+    small = jnp.pad(small, ((0, -lines % 16), (0, 0)))
     query_part = w_query.T
     pair_part = jnp.stack([w.T.reshape(per_grp, lanes, row_part) for w in (w_key, w_value)], axis=1)
     pair_part = pair_part.reshape(per_grp * 2 * lanes, row_part)
-    qkv_w = gathered(jnp.concatenate([query_part, pair_part]), 1)
+    qkv_w = lax.all_gather(
+        jnp.concatenate([query_part, pair_part, small]), everywhere, axis=1, tiled=True
+    )
+    small = qkv_w[per_grp * 3 * lanes :][:lines].reshape(lines, -1, row_part)
+    small = jnp.swapaxes(small, 0, 1).reshape(-1, lines * row_part)
+    gain_one = small[:, :share].reshape(1, model_width).astype(wide)
+    gain_two = small[:, share : 2 * share].reshape(1, model_width).astype(wide)
+    counts = jnp.sum(small[:, 2 * share : 2 * share + 2].astype(wide), axis=0)
+    valid_total = counts[0] * 256.0 + counts[1]
+    coefficient = slot_count / valid_total
     inner = w_gate.shape[1]
-    inner_w = gathered(jnp.concatenate([w_gate.T, w_up.T, w_down, w_out.T]), 1)
-    feed_w = (inner_w[3 * inner :], inner_w, inner)
+    words = [picks_to_words(sz, metas[m], m, prompt_picks, reply_picks) for m in micros]
+    shares = [jnp.concatenate([w_gate.T, w_up.T])[None], jnp.concatenate([w_down, w_out.T])[None]]
+    nearest = [gain_one] * 2
+    if row_part % lanes:
+        shares = [lax.all_gather(share, "seq", axis=2, tiled=True) for share in shares]
+    else:
+        for away in reversed(powers(seq_count)):
+            if away == 1:
+                gain_one, *shares = lax.optimization_barrier((gain_one, *shares))
+            nearest = [along_seq(share, away) for share in shares]
+            if away * 2 < seq_count and away > 1:
+                nearest = list(lax.optimization_barrier((*nearest, words)))[:-1]
+            shares = [jnp.concatenate(pair) for pair in zip(shares, nearest)]
+    far = [along_grp(share, 2) for share in shares]
+    feed_w = (
+        shares
+        + [along_grp(share, 1) for share in shares]
+        + far
+        + [along_grp(share, 1) for share in far],
+        inner,
+    )
     cache_key_rows, cache_value_rows = cache_keys[0], cache_values[0]
-    words = [picks_to_words(sz, metas[m], m, prompt_picks, reply_picks) for m in micros]
     gain_one, words = lax.optimization_barrier((gain_one, words))
     last = len(micros) - 1
-    tokens = (prompt_in, reply_in)
-
-    queries, pairs, normed, got_queries, got_pairs = [], [], [], [], []
+
+    own, normed = [], []
     for m in micros:
-        query, pair, rows = project(sz, metas[m], m, prompt_in, reply_in, gain_one, qkv_w)
-        queries.append(query)
-        pairs.append(pair)
+        chunks, rows = project(sz, metas[m], m, prompt_in, reply_in, gain_one, qkv_w)
+        own.append(chunks)
         normed.append(rows)
     cached = [
-        cache_forward(sz, metas[m], queries[m], words[m], cache_key_rows, cache_value_rows)
+        cache_forward(sz, metas[m], own[m], words[m], cache_key_rows, cache_value_rows)
         for m in micros
     ]
     error_parts, gain_two_parts, gain_one_parts = [], [], []
     outs, grads, parts, arrived, extras = [], [], [], [], []
-    middle_grads, mixed_grads, all_sums, deltas = [], [], [], []
+    received, middle_grads, mixed_grads, all_sums, deltas = [], [], [], [], []
     back_queries, back_pairs = [], []
-    answers = None
-    messages = None
-
-    def run_back(m, feed_grads):
-        got = arrived[m] if feed_grads is None else after(arrived[m], feed_grads)
-        query, pair, *rest = attend_back(
-            sz, metas[m], got_queries[m], got_pairs[m], got, extras[m]
-        )
+    answers = messages = pending = None
+
+    def run_back(m, got):
+        query, pair, *rest = attend_back(sz, metas[m], received[m], got, extras[m])
         if sz.blocks > 1:
             pair = settle_blocks(sz, own_block, pair, *rest)
         return query, pair
 
-    pending = None
-    feed_grads = None
-    got_pairs.append(exchange(sz, pairs[0]))
     for m in micros:
-        pair = got_pairs[m]
-        query = after(queries[m], pair if answers is None else answers)
-        query = exchange(sz, query)
+        chunks = exchange(sz, after(own[m], nearest[0] if answers is None else answers))
         if m == 0:
-            query, cached = lax.optimization_barrier((query, cached))
+            chunks, cached, _ = lax.optimization_barrier((chunks, cached, far[0]))
         if messages is not None:
-            query = after(query, messages)
-        got_queries.append(query)
-        extras.append(other_blocks(sz, pair))
-        answers = attend(sz, metas[m], query, pair, extras[m])
-        if m < last:
-            got_pairs.append(exchange(sz, pairs[m + 1]))
-            answers = after(answers, got_pairs[m + 1])
+            chunks = after(chunks, messages)
+        received.append(chunks)
+        extras.append(other_blocks(sz, chunks))
+        answers = attend(sz, metas[m], chunks, extras[m])
+        answers = after(answers, arrived[m - 1] if m > 0 else far[1])
         answers = exchange(sz, answers)
+        arrived_answers = answers
         if m > 0:
-            pending = run_back(m - 1, None)
-            answers = after(answers, *pending)
-            back_pairs.append(exchange(sz, pending[1]))
-        mixed, sums = merge(sz, metas[m], answers, *cached[m])
+            pending = run_back(m - 1, arrived[m - 1])
+            arrived_answers = after(answers, *pending)
+            back_pairs.append(exchange(sz, after(pending[1], answers)))
+        mixed, sums = merge(sz, metas[m], arrived_answers, *cached[m])
         valid = valids[m].astype(wide)
         weight = jnp.stack([valid, valid * coefficient], axis=1)
         arrays = (prompt_in, reply_in, prompt_teacher, reply_teacher)
@@ -1328,50 +1504,53 @@
         deltas.append(delta)
         if m > 0:
             back_queries.append(exchange(sz, after(pending[0], arrived[m])))
-    feed_grads = weight_grads(sz, metas[0], parts)
-    query, pair = run_back(last, feed_grads[0])
-    back_pairs.append(exchange(sz, pair))
+    feed_grads = weight_grads(sz, metas[0], parts, 0) + weight_grads(sz, metas[0], parts, 2)
+    handed = hand_over(feed_grads)
+    query, pair = run_back(last, after(arrived[last], handed))
+    across = along_grp(handed, 2)
+    back_pairs.append(exchange(sz, after(pair, *back_queries)))
     late = after(words, pair)
-    grad_query = grad_pair = None
+
+    prior = None
     for m in micros:
         cache_grad = cache_backward(
             sz,
             metas[m],
-            queries[m],
+            own[m],
             mixed_grads[m],
             all_sums[m],
             deltas[m],
-            late[m],
+            late[m] if m == last else words[m],
             cache_key_rows,
             cache_value_rows,
         )
-        carried, *grad_pair = finish(
-            sz, metas[m], m, back_pairs[m], qkv_w, normed[m], grad_pair, m == last
-        )
-        if m == last:
-            back_queries.append(exchange(sz, after(query, back_pairs[last], *grads)))
-        extra = (cache_grad, carried, middle_grads[m], gain_one, grads)
-        prompt_grad, reply_grad, stats, *grad_query = finish(
-            sz,
-            metas[m],
-            m,
-            back_queries[m],
-            qkv_w,
-            normed[m],
-            grad_query,
-            m == last,
-            tokens + extra,
-        )
+        tokens = (prompt_in, reply_in, middle_grads[m], gain_one, grads)
+        if m < last:
+            sides = {"pair": back_pairs[m], "query": (back_queries[m], cache_grad)}
+            prompt_grad, reply_grad, stats, *prior_list = finish(
+                sz, metas[m], m, sides, qkv_w, normed[m], prior, "carry", None, tokens
+            )
+            prior = dict(zip(sides, prior_list))
+        else:
+            back_pair = after(back_pairs[m], cache_grad, *grads)
+            back_queries.append(exchange(sz, after(query, back_pair)))
+            *grad_pair, carried = finish(
+                sz, metas[m], m, {"pair": back_pair}, qkv_w, normed[m], prior, "away"
+            )
+            sides = {"query": (back_queries[m], cache_grad)}
+            prompt_grad, reply_grad, stats, grad_query = finish(
+                sz, metas[m], m, sides, qkv_w, normed[m], prior, "whole", carried, tokens
+            )
         grads = [prompt_grad, reply_grad]
+        if m == 0:
+            early_grads = grads
         gain_one_parts.append(stats[0])
-        if m < last:
-            grad_pair, grad_query = grad_pair[0], grad_query[0]
 
     def over_rows(grad):
-        grad = grad.reshape(seq_count, row_part, grad.shape[1])
+        grad = grad.astype(low).reshape(seq_count, row_part, grad.shape[1])
         return jnp.sum(lax.all_to_all(grad, "seq", 0, 0).astype(wide), axis=0)
 
-    feed_grads = over_groups(feed_grads)
+    feed_grads = over_groups(feed_grads, after(across, *early_grads)).astype(low)
     feed_grads = lax.psum_scatter(feed_grads, "seq", scatter_dimension=0, tiled=True).astype(wide)
     stride = -(-inner // lanes) * lanes
     grad_gate, grad_up, grad_down = (
@@ -1382,7 +1561,8 @@
     grad_key, grad_value = (
         grad_pair[:, :, i].reshape(row_part, per_grp * lanes) for i in range(2)
     )
-    grad_query = over_rows(over_groups(grad_query))
+    grad_query = grad_query.reshape(grp_count * seq_count, row_part, per_grp * lanes)
+    grad_query = jnp.sum(lax.all_to_all(grad_query, everywhere, 0, 0).astype(wide), axis=0)
     count = grp_count * seq_count
     tail = jnp.concatenate(
         [
@@ -1392,6 +1572,7 @@
         ],
         axis=1,
     )
+    tail = after(tail, grad_query)
     tail = jnp.sum(lax.all_to_all(tail, everywhere, 0, 0), axis=0)
     mean_error = tail[2 * share] / (model_width * valid_total)
     return (

time: 1220 us -> 1100 us (0.902)
  blocking collectives: 142 us -> 41.6 us
  Pallas kernels: 605 us -> 528 us
  waiting for transfers between devices: 262 us -> 320 us
    ppermute x0 -> x6, waiting for transfers between devices: none -> 140 us  [along_seq(): return lax.ppermute(array, 'seq', [(i, i ^ away) for i in range(count)])]
    all_to_all x2 -> x1, blocking collectives: 142 us -> 41.6 us  [exchange(): return lax.all_to_all(array, 'seq', 0, 0, axis_index_groups=subgroups(sz))]
    all_gather x2 -> x1, waiting for transfers between devices: 92.1 us -> 6.93 us  [body(): lax.all_gather(jnp.concatenate([query_part, pair_part, small]), everywher...]
    all_to_all x10 -> x9, waiting for transfers between devices: 126 us -> 63 us  [exchange(): return lax.all_to_all(array, 'seq', 0, 0, axis_index_groups=subgroups(sz))]
    all_to_all x1, waiting for transfers between devices: 0.01 us -> 46.8 us  [body(): lax.all_to_all(grad_query, everywhere, 0, 0).astype(wide)]
    pallas_call x2, Pallas kernels: 106 us -> 75.5 us  [attend(): pl.pallas_call(functools.partial(attend_kernel, sz), out_shape=jax.ShapeD...]
    pallas_call x17, Pallas kernels: 339 us -> 309 us  [call(): pl.pallas_call(kernel, out_shape=list(out_shape), grid_spec=pltpu.Prefetc...]
    pallas_call x2, Pallas kernels: 145 us -> 128 us  [attend_back(): pl.pallas_call(functools.partial(attend_back_kernel, sz), out_shape=out_s...]
  transfers between devices with their start and end apart: 26 -> 32, of which waited for: 13 -> 18; matrix products, arithmetic and copies ran while one was open for 4% -> 4% of each run, Pallas kernels for 44% -> 46%
where the time goes in v2:
time: 1100 us; the launch traced here: 1090 us
  Pallas kernels  528 us (48%)
  waiting for transfers between devices  320 us (29%)
  starting transfers between devices  78.4 us (7%)
  local copies, waits for them, and re-layouts  63.5 us (6%)
  other arithmetic  41.7 us (4%)
  blocking collectives  41.6 us (4%)
  between operations  20.9 us (2%)
    pallas_call x17, Pallas kernels, call(): pl.pallas_call(kernel, out_shape=list(out_shape), grid_spec=pltpu.Prefetc...  309 us
    ppermute x6, waiting for transfers between devices, along_seq(): return lax.ppermute(array, 'seq', [(i, i ^ away) for i in range(count)])  140 us
    pallas_call x2, Pallas kernels, attend_back(): pl.pallas_call(functools.partial(attend_back_kernel, sz), out_shape=out_s...  128 us
    pallas_call x2, Pallas kernels, attend(): pl.pallas_call(functools.partial(attend_kernel, sz), out_shape=jax.ShapeD...  75.5 us
    all_to_all x9, waiting for transfers between devices, exchange(): return lax.all_to_all(array, 'seq', 0, 0, axis_index_groups=subgroups(sz))  63 us
    unnamed x135, local copies, waits for them, and re-layouts  48.2 us
    all_to_all x1, waiting for transfers between devices, body(): lax.all_to_all(grad_query, everywhere, 0, 0).astype(wide)  46.8 us
    all_to_all x9, starting transfers between devices, exchange(): return lax.all_to_all(array, 'seq', 0, 0, axis_index_groups=subgroups(sz))  46.7 us
  transfers between devices with their start and end apart: 32, of which 18 were waited for; matrix products, arithmetic and copies ran while one was open for 4% of the time, Pallas kernels for 46%

profile of v2, /device:TPU:0, one launch (start us, length us, event | category | flops | bytes accessed | tf_op | source)
XLA Modules:
  0.0 1094.1 jit_solution(10360953723422203579)
XLA Ops:
  23.5 4.1 collective-permute-start
  29.6 20.4 %collective-permute-done = bf16[1,1408,128]{2,1,0:T(8,128)(2,1)S(1)} collective-permute-done((bf16[1,1408,128]{2,1,0:T(8,128)(2,1)S(1)}, bf16[1,1408,128]{2,1,0:T(8,128)(2,1)S(1)}, u32[]{:S(2)}, u32[]{:S(2)}) %collective-permute-start) | collective-permute-done | bytes 360480 | tf_op jit(solution)/shard_map/ppermute | solution.py:1326
  54.0 8.1 collective-permute-done.2
  65.8 7.8 picks_to_words.3
  73.5 7.8 picks_to_words.2
  81.3 29.7 %collective-permute-done.3 = bf16[2,960,128]{2,1,0:T(8,128)(2,1)} collective-permute-done((bf16[2,960,128]{2,1,0:T(8,128)(2,1)}, bf16[2,960,128]{2,1,0:T(8,128)(2,1)}, u32[]{:S(2)}, u32[]{:S(2)}) %collective-permute-start.3) | collective-permute-done | bytes 491552 | tf_op jit(solution)/shard_map/ppermute | solution.py:1326
  115.7 6.9 all-gather.2.cloned.1.call-done.query_w.pair_w.refs_2_.refs_4_
  127.9 10.0 project.2
  141.2 16.6 %collective-permute-done.4 = bf16[4,1408,128]{2,1,0:T(8,128)(2,1)} collective-permute-done((bf16[4,1408,128]{2,1,0:T(8,128)(2,1)}, bf16[4,1408,128]{2,1,0:T(8,128)(2,1)}, u32[]{:S(2)}, u32[]{:S(2)}) %collective-permute-start.4) | collective-permute-done | bytes 1441824 | tf_op jit(solution)/shard_map/ppermute | solution.py:1326
  157.8 5.4 all-to-all-start
  171.1 65.7 %collective-permute-done.6 = bf16[4,960,128]{2,1,0:T(8,128)(2,1)S(1)} collective-permute-done((bf16[4,960,128]{2,1,0:T(8,128)(2,1)S(1)}, bf16[4,960,128]{2,1,0:T(8,128)(2,1)S(1)}, u32[]{:S(2)}, u32[]{:S(2)}) %collective-permute-start.6) | collective-permute-done | bytes 983072 | tf_op jit(solution)/shard_map/ppermute | solution.py:1326
  241.6 6.8 cache_forward.2
  250.3 10.0 project.3
  261.4 6.9 cache_forward.3
  270.0 37.9 %attend.2 = bf16[8,800,128]{2,1,0:T(8,128)(2,1)S(1)} custom-call(s32[7]{0:T(128)S(1)} %copy-done.40, bf16[8,768,384]{2,1,0:T(8,128)(2,1)} %all-to-all-done.refs_0_), custom_call_target="tpu_custom_call" | custom-call | flops 4026531840 | bytes 838860 | tf_op jit(solution)/shard_map/attend/pallas_call | solution.py:327
  307.8 41.6 %all_to_all.69.message = bf16[8,800,128]{2,1,0:T(8,128)(2,1)S(1)} all-to-all(bf16[8,800,128]{2,1,0:T(8,128)(2,1)S(1)} %attend.2), channel_id=1, replica_groups=mesh['grp'=4,'seq'=8] {'seq'}, dimensions={0} | all-to-all | bytes 3276800 | tf_op jit(solution)/shard_map/all_to_all | solution.py:1294
  349.5 4.6 all-to-all-start.3
  369.5 64.5 %feed_forward.2 = (bf16[2,1,512,1024]{3,2,1,0:T(8,128)(2,1)}, bf16[2,1,256,1024]{3,2,1,0:T(8,128)(2,1)}, f32[768,1024]{1,0:T(8,128)}, bf16[768,1024]{1,0:T(8,128...) custom-call(s32[7]{0:T(128)} %get-tuple-element.256.meta, ...), custom_call_target="tpu_custom_call" | custom-call | flops 2979633664 | bytes 5129216 | tf_op jit(solution)/shard_map/feed_forward/pallas_call | solution.py:547
  439.6 17.2 %all-to-all-done.3.refs_0_ = bf16[8,768,384]{2,1,0:T(8,128)(2,1)} async-done(((bf16[8,768,384]{2,1,0:T(8,128)(2,1)}), bf16[8,768,384]{2,1,0:T(8,128)(2,1)}, u32[]{:S(2)}, u32[]{:S(2)}) %all-to-all-start.3) | async-done | bytes 4718624 | tf_op jit(solution)/shard_map/all_to_all | solution.py:1294
  456.8 3.6 all-to-all-start.2
  460.4 37.6 %attend.3 = bf16[8,800,128]{2,1,0:T(8,128)(2,1)S(1)} custom-call(s32[7]{0:T(128)S(1)} %copy-done.43, bf16[8,768,384]{2,1,0:T(8,128)(2,1)} %all-to-all-done.3.refs_0_), custom_call_target="tpu_custom_call" | custom-call | flops 4026531840 | bytes 838860 | tf_op jit(solution)/shard_map/attend/pallas_call | solution.py:327
  499.7 5.8 all-to-all-start.4
  505.5 63.4 %attend_back.2 = (bf16[8,768,128]{2,1,0:T(8,128)(2,1)}, bf16[8,768,256]{2,1,0:T(8,128)(2,1)S(1)}) custom-call(s32[7]{0:T(128)S(1)} %copy-done.41, bf16[8,768,384]{2,1,0:T(8,128)(2,1)} %all-to-all-done.refs_0_, bf16[8,816,128]{2,1,0:T(8,128)(2,1)S(1)} %all-to-all-done.2.refs_1_), custom_call_target="tpu_custom_call" | custom-call | flops 6710886400 | bytes 1468006 | tf_op jit(solution)/shard_map/attend_back/pallas_call | solution.py:484
  570.6 6.1 all-to-all-start.5
  584.1 64.6 %feed_forward.3 = (bf16[2,1,512,1024]{3,2,1,0:T(8,128)(2,1)}, bf16[2,1,256,1024]{3,2,1,0:T(8,128)(2,1)}, f32[768,1024]{1,0:T(8,128)}, bf16[768,1024]{1,0:T(8,128...) custom-call(s32[7]{0:T(128)} %pad_add_fusion.2.meta, ...), custom_call_target="tpu_custom_call", output_to_operand_aliasing={{0}: (16, {}), {1}: (17, {})} | custom-call | flops 2979633664 | bytes 5443788 | tf_op jit(solution)/shard_map/feed_forward/pallas_call | solution.py:547
  650.2 4.8 make_messages.3
  655.0 27.2 %weight_grads.3 = (bf16[1024,2560]{1,0:T(8,128)(2,1)}, bf16[1024,2560]{1,0:T(8,128)(2,1)}) custom-call(s32[7]{0:T(128)} %get-tuple-element.256.meta, bf16[768,1024]{1,0:T(8,128)(2,1)} %get-tuple-element.162.refs_0_, bf16[768,1024]{1,0:T(8,128)(2,1)} %get-tuple-element.163.refs_1_, bf16[768,1024]{1,0:T(8,128)(2,1)} %copy-done.11, ...), custom_call_target="tpu_custom_call" | custom-call | flops 1489816832 | bytes 5216665 | tf_op jit(solution)/shard_map/weight_grads/pallas_call | solution.py:547
  682.3 6.0 all-to-all-start.6
  688.3 27.5 %weight_grads.2 = (bf16[1024,2560]{1,0:T(8,128)(2,1)}, bf16[1024,2560]{1,0:T(8,128)(2,1)}) custom-call(s32[7]{0:T(128)} %get-tuple-element.256.meta, bf16[768,1024]{1,0:T(8,128)(2,1)} %get-tuple-element.162.refs_0_, bf16[768,1024]{1,0:T(8,128)(2,1)} %get-tuple-element.163.refs_1_, bf16[768,1024]{1,0:T(8,128)(2,1)} %copy-done.11, ...), custom_call_target="tpu_custom_call" | custom-call | flops 1489816832 | bytes 5216665 | tf_op jit(solution)/shard_map/weight_grads/pallas_call | solution.py:547
  715.8 12.2 %all-to-all-done.6.refs_1_ = bf16[8,816,128]{2,1,0:T(8,128)(2,1)S(1)} async-done(((bf16[8,816,128]{2,1,0:T(8,128)(2,1)}), bf16[8,816,128]{2,1,0:T(8,128)(2,1)S(1)}, u32[]{:S(2)}, u32[]{:S(2)}) %all-to-all-start.6) | async-done | bytes 1671200 | tf_op jit(solution)/shard_map/all_to_all | solution.py:1294
  728.0 4.7 all-to-all-start.7
  732.7 7.7 add_convert_fusion.1
  741.1 64.9 %attend_back.3 = (bf16[8,768,128]{2,1,0:T(8,128)(2,1)S(1)}, bf16[8,768,256]{2,1,0:T(8,128)(2,1)S(1)}) custom-call(s32[7]{0:T(128)S(1)} %copy-done.44, bf16[8,768,384]{2,1,0:T(8,128)(2,1)} %all-to-all-done.3.refs_0_, bf16[8,816,128]{2,1,0:T(8,128)(2,1)S(1)} %all-to-all-done.6.refs_1_), custom_call_target="tpu_custom_call" | custom-call | flops 6710886400 | bytes 1468006 | tf_op jit(solution)/shard_map/attend_back/pallas_call | solution.py:484
  808.8 6.1 all-to-all-start.8
  818.7 7.6 cache_backward.2.refs_5_
  828.1 25.7 %finish.3 = (f32[2,1,512,1024]{3,2,1,0:T(8,128)}, f32[2,1,256,1024]{3,2,1,0:T(8,128)}, f32[8,1024]{1,0:T(8,128)S(1)}, f32[8,1024,256]{2,1,0:T(8,128)}, f32[8,1024,128]{2,1,0:T(8,128)}) custom-call(s32[7]{0:T(128)S(1)} %copy-done.42, bf16[768,1024]{1,0:T(8,128)(2,1)} %copy-done.33, bf16[8,768,256]{2,1,0:T(8,128)(2,1)} %all-to-all-done.5.refs_1_, ...), custom_call_target="tpu_custom_call" | custom-call | flops 966367616 | bytes 4748492 | tf_op jit(solution)/shard_map/finish/pallas_call | solution.py:547
  855.1 9.9 add_convert_fusion
  868.8 7.5 cache_backward.3.refs_3_
  878.0 33.1 %all-to-all-done.8.refs_1_ = bf16[8,768,256]{2,1,0:T(8,128)(2,1)} async-done(((bf16[8,768,256]{2,1,0:T(8,128)(2,1)}), bf16[8,768,256]{2,1,0:T(8,128)(2,1)}, u32[]{:S(2)}, u32[]{:S(2)}) %all-to-all-start.8) | async-done | bytes 3145760 | tf_op jit(solution)/shard_map/all_to_all | solution.py:1294
  911.0 4.3 all-to-all-start.9
  915.4 16.9 %finish.4 = (bf16[1024,512]{1,0:T(8,128)(2,1)S(1)}, bf16[1024,512]{1,0:T(8,128)(2,1)}, bf16[1024,512]{1,0:T(8,128)(2,1)}, bf16[1024,512]{1,0:T(8,128)(2,1)}, f32[768,1024]{1,0:T(8,128)}) custom-call(s32[7]{0:T(128)S(1)} %copy-done.44, bf16[768,1024]{1,0:T(8,128)(2,1)} %copy-done.19, bf16[8,768,256]{2,1,0:T(8,128)(2,1)} %all-to-all-done.8.refs_1_, ...), custom_call_target="tpu_custom_call" | custom-call | flops 322122560 | bytes 2686976 | tf_op jit(solution)/shard_map/finish/pallas_call | solution.py:547
  938.7 23.8 %collective-permute-done.15 = bf16[1024,512]{1,0:T(8,128)(2,1)S(1)} collective-permute-done((bf16[1024,512]{1,0:T(8,128)(2,1)S(1)}, bf16[1024,512]{1,0:T(8,128)(2,1)S(1)}, u32[]{:S(2)}, u32[]{:S(2)}) %collective-permute-start.15) | collective-permute-done | bytes 1048608 | tf_op jit(solution)/shard_map/ppermute | solution.py:1321
  964.0 6.1 all-to-all-start.12
  970.1 19.3 %finish.5 = (f32[2,1,512,1024]{3,2,1,0:T(8,128)}, f32[2,1,256,1024]{3,2,1,0:T(8,128)}, f32[8,1024]{1,0:T(8,128)S(1)}, bf16[4,1024,256]{2,1,0:T(8,128)(2,1)}) custom-call(s32[7]{0:T(128)S(1)} %copy-done.44, bf16[768,1024]{1,0:T(8,128)(2,1)} %copy-done.19, ...), custom_call_target="tpu_custom_call", output_to_operand_aliasing={{0}: (11, {}), {1}: (12, {})} | custom-call | flops 322122560 | bytes 4106240 | tf_op jit(solution)/shard_map/finish/pallas_call | solution.py:547
  989.4 25.3 %all-to-all-done.12 = bf16[8,128,512]{2,1,0:T(8,128)(2,1)S(1)} async-done(((bf16[8,128,512]{2,1,0:T(8,128)(2,1)}), bf16[8,128,512]{2,1,0:T(8,128)(2,1)S(1)}, u32[]{:S(2)}, u32[]{:S(2)}) %all-to-all-start.12) | async-done | bytes 1048608 | tf_op jit(solution)/shard_map/all_to_all | solution.py:1551
  1014.7 4.0 all-to-all-start.10
  1022.0 46.8 %all-to-all-done.10 = bf16[32,128,256]{2,1,0:T(8,128)(2,1)S(1)} async-done(((bf16[32,128,256]{2,1,0:T(8,128)(2,1)}), bf16[32,128,256]{2,1,0:T(8,128)(2,1)S(1)}, u32[]{:S(2)}, u32[]{:S(2)}) %all-to-all-start.10) | async-done | bytes 2097184 | tf_op jit(solution)/shard_map/all_to_all | solution.py:1565
  1073.8 5.5 all-to-all-done.11
  (232 shorter events, 123.2 us)
Async XLA Ops:
  7.2 115.5 %all-gather.2.cloned.1.call-start = ((), (), s32[]{:S(2)}) async-start(), calls=%async_computation.14 | async-start | bytes 6623232 | tf_op jit(solution)/shard_map/all_gather | solution.py:1413
  23.5 26.5 %collective-permute-start = (bf16[1,1408,128]{2,1,0:T(8,128)(2,1)S(1)}, bf16[1,1408,128]{2,1,0:T(8,128)(2,1)S(1)}, u32[]{:S(2)}, u32[]{:S(2)}) collective-permute-start(bf16[1,1408,128]{2,1,0:T(8,128)(2,1)S(1)} %maximum_bitcast_fusion), channel_id=1, source_target_pairs={{0,4},{1,5},{2,6},{3,7},{4,0},{5,1},{6,2},{7,3},{8,12},{9,13},{10,... | collective-permute-start | bytes 1081352 | tf_op jit(solution)/shard_map/ppermute | solution.py:1326
  29.5 32.7 %collective-permute-start.2 = (bf16[1,960,128]{2,1,0:T(8,128)(2,1)S(1)}, bf16[1,960,128]{2,1,0:T(8,128)(2,1)S(1)}, u32[]{:S(2)}, u32[]{:S(2)}) collective-permute-start(bf16[1,960,128]{2,1,0:T(8,128)(2,1)S(1)} %maximum_bitcast_fusion.1), channel_id=1, source_target_pairs={{0,4},{1,5},{2,6},{3,7},{4,0},{5,1},{6,2},{7,3},{8,12},{9,13},{10,... | collective-permute-start | bytes 737288 | tf_op jit(solution)/shard_map/ppermute | solution.py:1326
  50.9 60.1 %collective-permute-start.1 = (bf16[2,1408,128]{2,1,0:T(8,128)(2,1)}, bf16[2,1408,128]{2,1,0:T(8,128)(2,1)}, u32[]{:S(2)}, u32[]{:S(2)}) collective-permute-start(bf16[2,1408,128]{2,1,0:T(8,128)(2,1)} %pad_maximum_fusion.2), channel_id=1, source_target_pairs={{0,2},{1,3},{2,0},{3,1},{4,6},{5,7},{6,4},{7,5},{8,10},{9,11},{10,... | collective-permute-start | bytes 2162696 | tf_op jit(solution)/shard_map/ppermute | solution.py:1326
  63.0 48.0 %collective-permute-start.3 = (bf16[2,960,128]{2,1,0:T(8,128)(2,1)}, bf16[2,960,128]{2,1,0:T(8,128)(2,1)}, u32[]{:S(2)}, u32[]{:S(2)}) collective-permute-start(bf16[2,960,128]{2,1,0:T(8,128)(2,1)} %pad_maximum_fusion.3), channel_id=1, source_target_pairs={{0,2},{1,3},{2,0},{3,1},{4,6},{5,7},{6,4},{7,5},{8,10},{9,11},{10,... | collective-permute-start | bytes 1474568 | tf_op jit(solution)/shard_map/ppermute | solution.py:1326
  81.3 43.8 %copy-start.1 = (bf16[2,1,512,1024]{3,2,1,0:T(8,128)(2,1)S(1)}, bf16[2,1,512,1024]{3,2,1,0:T(8,128)(2,1)}, u32[]{:S(2)}) copy-start(bf16[2,1,512,1024]{3,2,1,0:T(8,128)(2,1)} %refs_7_.3) | copy-start | bytes 6291460
  81.3 43.8 %copy-start.7 = (bf16[2,1,256,1024]{3,2,1,0:T(8,128)(2,1)S(1)}, bf16[2,1,256,1024]{3,2,1,0:T(8,128)(2,1)}, u32[]{:S(2)}) copy-start(bf16[2,1,256,1024]{3,2,1,0:T(8,128)(2,1)} %refs_8_.3) | copy-start | bytes 3145732
  81.3 43.8 %copy-start.40 = (s32[7]{0:T(128)S(1)}, s32[7]{0:T(128)}, u32[]{:S(2)}) copy-start(s32[7]{0:T(128)} %get-tuple-element.256.meta) | copy-start | bytes 88
  123.7 34.1 %collective-permute-start.4 = (bf16[4,1408,128]{2,1,0:T(8,128)(2,1)}, bf16[4,1408,128]{2,1,0:T(8,128)(2,1)}, u32[]{:S(2)}, u32[]{:S(2)}) collective-permute-start(bf16[4,1408,128]{2,1,0:T(8,128)(2,1)} %pad_maximum_fusion), channel_id=1, source_target_pairs={{0,1},{1,0},{2,3},{3,2},{4,5},{5,4},{6,7},{7,6},{8,9},{9,8},{10,11... | collective-permute-start | bytes 4325384 | tf_op jit(solution)/shard_map/ppermute | solution.py:1326
  157.8 112.2 %all-to-all-start = ((bf16[8,768,384]{2,1,0:T(8,128)(2,1)}), bf16[8,768,384]{2,1,0:T(8,128)(2,1)}, u32[]{:S(2)}, u32[]{:S(2)}) async-start(bf16[8,768,384]{2,1,0:T(8,128)(2,1)} %copy-done.4), calls=%async_computation | async-start | bytes 9437184 | tf_op jit(solution)/shard_map/all_to_all | solution.py:1294
  163.2 76.1 %copy-start.17 = (bf16[1,256,1024]{2,1,0:T(8,128)(2,1)S(1)}, bf16[1,256,1024]{2,1,0:T(8,128)(2,1)}, u32[]{:S(2)}) copy-start(bf16[1,256,1024]{2,1,0:T(8,128)(2,1)} %param.30) | copy-start | bytes 1572868
  163.2 76.1 %copy-start.38 = (s32[8,8,256]{2,1,0:T(8,128)S(1)}, s32[8,8,256]{2,1,0:T(8,128)}, u32[]{:S(2)}) copy-start(s32[8,8,256]{2,1,0:T(8,128)} %get-tuple-element.123.words_reply) | copy-start | bytes 196612
  164.8 74.5 %copy-start.15 = (bf16[1,256,1024]{2,1,0:T(8,128)(2,1)S(1)}, bf16[1,256,1024]{2,1,0:T(8,128)(2,1)}, u32[]{:S(2)}) copy-start(bf16[1,256,1024]{2,1,0:T(8,128)(2,1)} %param.29) | copy-start | bytes 1572868
  164.8 74.5 %copy-start.35 = (s32[8,8,512]{2,1,0:T(8,128)S(1)}, s32[8,8,512]{2,1,0:T(8,128)}, u32[]{:S(2)}) copy-start(s32[8,8,512]{2,1,0:T(8,128)} %get-tuple-element.122.words_prompt) | copy-start | bytes 393220
  164.8 85.4 %slice-start = ((s8[6422528]{0:T(1024)(128)(4,1)}), s8[4194304]{0:T(1024)(128)(4,1)S(1)}, s32[]{:S(2)}) async-start(s8[6422528]{0:T(1024)(128)(4,1)} %bitcast.48), calls=%async_computation.16 | async-start | bytes 8388608
  166.6 81.9 %copy-start.49 = (bf16[8,1408,128]{2,1,0:T(8,128)(2,1)}, bf16[8,1408,128]{2,1,0:T(8,128)(2,1)S(1)}, u32[]{:S(2)}) copy-start(bf16[8,1408,128]{2,1,0:T(8,128)(2,1)S(1)} %constant_dynamic-update-slice_fusion.refs_0_) | copy-start | bytes 8650756
  166.6 103.4 %collective-permute-start.5 = (bf16[8,1408,128]{2,1,0:T(8,128)(2,1)S(1)}, bf16[8,1408,128]{2,1,0:T(8,128)(2,1)}, u32[]{:S(2)}, u32[]{:S(2)}) collective-permute-start(bf16[8,1408,128]{2,1,0:T(8,128)(2,1)S(1)} %constant_dynamic-update-slice_fusion.refs_0_), channel_id=1, source_target_pairs={{0,16},{8,24},{16,0},{24,8},{1,17},{9,25},{17,1},{25,9},{2,18},{10... | collective-permute-start | bytes 8650760 | tf_op jit(solution)/shard_map/ppermute | solution.py:1321
  168.1 68.7 %collective-permute-start.6 = (bf16[4,960,128]{2,1,0:T(8,128)(2,1)S(1)}, bf16[4,960,128]{2,1,0:T(8,128)(2,1)S(1)}, u32[]{:S(2)}, u32[]{:S(2)}) collective-permute-start(bf16[4,960,128]{2,1,0:T(8,128)(2,1)S(1)} %copy-done.50), channel_id=1, source_target_pairs={{0,1},{1,0},{2,3},{3,2},{4,5},{5,4},{6,7},{7,6},{8,9},{9,8},{10,11... | collective-permute-start | bytes 2949128 | tf_op jit(solution)/shard_map/ppermute | solution.py:1326
  171.1 79.1 %slice-start.1 = ((s8[6422528]{0:T(1024)(128)(4,1)}), s8[2228224]{0:T(1024)(128)(4,1)S(1)}, s32[]{:S(2)}) async-start(s8[6422528]{0:T(1024)(128)(4,1)} %bitcast.48), calls=%async_computation.17 | async-start | bytes 4456448
  237.8 70.0 %collective-permute-start.7 = (bf16[8,960,128]{2,1,0:T(8,128)(2,1)}, bf16[8,960,128]{2,1,0:T(8,128)(2,1)}, u32[]{:S(2)}, u32[]{:S(2)}) collective-permute-start(bf16[8,960,128]{2,1,0:T(8,128)(2,1)} %constant_dynamic-update-slice_fusion.2.refs_1_), channel_id=1, source_target_pairs={{0,16},{8,24},{16,0},{24,8},{1,17},{9,25},{17,1},{25,9},{2,18},{10... | collective-permute-start | bytes 5898248 | tf_op jit(solution)/shard_map/ppermute | solution.py:1321
  269.9 37.9 %copy-start.47 = (f32[8,8,128]{2,1,0:T(8,128)}, f32[8,8,128]{2,1,0:T(8,128)S(1)}, u32[]{:S(2)}) copy-start(f32[8,8,128]{2,1,0:T(8,128)S(1)} %get-tuple-element.148.cache_sums) | copy-start | bytes 98308
  349.5 107.4 %all-to-all-start.3 = ((bf16[8,768,384]{2,1,0:T(8,128)(2,1)}), bf16[8,768,384]{2,1,0:T(8,128)(2,1)}, u32[]{:S(2)}, u32[]{:S(2)}) async-start(bf16[8,768,384]{2,1,0:T(8,128)(2,1)} %copy-done.2), calls=%async_computation.3 | async-start | bytes 9437184 | tf_op jit(solution)/shard_map/all_to_all | solution.py:1294
  354.1 12.6 %collective-permute-start.8 = (bf16[8,1408,128]{2,1,0:T(8,128)(2,1)}, bf16[8,1408,128]{2,1,0:T(8,128)(2,1)}, u32[]{:S(2)}, u32[]{:S(2)}) collective-permute-start(bf16[8,1408,128]{2,1,0:T(8,128)(2,1)} %copy-done.49), channel_id=1, source_target_pairs={{0,8},{8,0},{16,24},{24,16},{1,9},{9,1},{17,25},{25,17},{2,10},{10... | collective-permute-start | bytes 8650760 | tf_op jit(solution)/shard_map/ppermute | solution.py:1321
  354.2 15.4 %collective-permute-start.10 = (bf16[8,1408,128]{2,1,0:T(8,128)(2,1)}, bf16[8,1408,128]{2,1,0:T(8,128)(2,1)}, u32[]{:S(2)}, u32[]{:S(2)}) collective-permute-start(bf16[8,1408,128]{2,1,0:T(8,128)(2,1)} %collective-permute-done.5.refs_4_), channel_id=1, source_target_pairs={{0,8},{8,0},{16,24},{24,16},{1,9},{9,1},{17,25},{25,17},{2,10},{10... | collective-permute-start | bytes 8650760 | tf_op jit(solution)/shard_map/ppermute | solution.py:1321
  354.7 12.1 %collective-permute-start.9 = (bf16[8,960,128]{2,1,0:T(8,128)(2,1)}, bf16[8,960,128]{2,1,0:T(8,128)(2,1)}, u32[]{:S(2)}, u32[]{:S(2)}) collective-permute-start(bf16[8,960,128]{2,1,0:T(8,128)(2,1)} %constant_dynamic-update-slice_fusion.2.refs_1_), channel_id=1, source_target_pairs={{0,8},{8,0},{16,24},{24,16},{1,9},{9,1},{17,25},{25,17},{2,10},{10... | collective-permute-start | bytes 5898248 | tf_op jit(solution)/shard_map/ppermute | solution.py:1321
  354.7 14.8 %collective-permute-start.11 = (bf16[8,960,128]{2,1,0:T(8,128)(2,1)}, bf16[8,960,128]{2,1,0:T(8,128)(2,1)}, u32[]{:S(2)}, u32[]{:S(2)}) collective-permute-start(bf16[8,960,128]{2,1,0:T(8,128)(2,1)} %collective-permute-done.7.refs_5_), channel_id=1, source_target_pairs={{0,8},{8,0},{16,24},{24,16},{1,9},{9,1},{17,25},{25,17},{2,10},{10... | collective-permute-start | bytes 5898248 | tf_op jit(solution)/shard_map/ppermute | solution.py:1321
  369.5 64.5 %copy-start.12 = (bf16[768,1024]{1,0:T(8,128)(2,1)S(1)}, bf16[768,1024]{1,0:T(8,128)(2,1)}, u32[]{:S(2)}) copy-start(bf16[768,1024]{1,0:T(8,128)(2,1)} %copy-done.11) | copy-start | bytes 4718596
  369.5 64.5 %copy-start.41 = (s32[7]{0:T(128)S(1)}, s32[7]{0:T(128)}, u32[]{:S(2)}) copy-start(s32[7]{0:T(128)} %get-tuple-element.256.meta) | copy-start | bytes 88
  439.6 58.5 %copy-start.45 = (f32[8,8,128]{2,1,0:T(8,128)}, f32[8,8,128]{2,1,0:T(8,128)S(1)}, u32[]{:S(2)}) copy-start(f32[8,8,128]{2,1,0:T(8,128)S(1)} %get-tuple-element.157.delta) | copy-start | bytes 98308
  456.8 42.9 %all-to-all-start.2 = ((bf16[8,816,128]{2,1,0:T(8,128)(2,1)}), bf16[8,816,128]{2,1,0:T(8,128)(2,1)S(1)}, u32[]{:S(2)}, u32[]{:S(2)}) async-start(bf16[8,816,128]{2,1,0:T(8,128)(2,1)} %copy-done.30), calls=%async_computation.2 | async-start | bytes 3342336 | tf_op jit(solution)/shard_map/all_to_all | solution.py:1294
  499.7 70.9 %all-to-all-start.4 = ((bf16[8,800,128]{2,1,0:T(8,128)(2,1)}), bf16[8,800,128]{2,1,0:T(8,128)(2,1)S(1)}, u32[]{:S(2)}, u32[]{:S(2)}) async-start(bf16[8,800,128]{2,1,0:T(8,128)(2,1)} %copy-done.31), calls=%async_computation.4 | async-start | bytes 3276800 | tf_op jit(solution)/shard_map/all_to_all | solution.py:1294
  570.6 84.4 %all-to-all-start.5 = ((bf16[8,768,256]{2,1,0:T(8,128)(2,1)}), bf16[8,768,256]{2,1,0:T(8,128)(2,1)}, u32[]{:S(2)}, u32[]{:S(2)}) async-start(bf16[8,768,256]{2,1,0:T(8,128)(2,1)} %copy-done.29), calls=%async_computation.5 | async-start | bytes 6291456 | tf_op jit(solution)/shard_map/all_to_all | solution.py:1294
  584.1 64.7 %copy-start.10 = (bf16[768,1024]{1,0:T(8,128)(2,1)S(1)}, bf16[768,1024]{1,0:T(8,128)(2,1)}, u32[]{:S(2)}) copy-start(bf16[768,1024]{1,0:T(8,128)(2,1)} %copy-done.9) | copy-start | bytes 4718596
  584.1 64.7 %copy-start.44 = (s32[7]{0:T(128)S(1)}, s32[7]{0:T(128)}, u32[]{:S(2)}) copy-start(s32[7]{0:T(128)} %pad_add_fusion.2.meta) | copy-start | bytes 88
  682.2 50.5 %collective-permute-start.12 = (bf16[1024,2560]{1,0:T(8,128)(2,1)}, bf16[1024,2560]{1,0:T(8,128)(2,1)}, u32[]{:S(2)}, u32[]{:S(2)}) collective-permute-start(bf16[1024,2560]{1,0:T(8,128)(2,1)} %get-tuple-element.175), channel_id=1, source_target_pairs={{0,8},{8,0},{16,24},{24,16},{1,9},{9,1},{17,25},{25,17},{2,10},{10... | collective-permute-start | bytes 15728648 | tf_op jit(solution)/shard_map/ppermute | solution.py:1321
  682.3 45.7 %all-to-all-start.6 = ((bf16[8,816,128]{2,1,0:T(8,128)(2,1)}), bf16[8,816,128]{2,1,0:T(8,128)(2,1)S(1)}, u32[]{:S(2)}, u32[]{:S(2)}) async-start(bf16[8,816,128]{2,1,0:T(8,128)(2,1)} %get-tuple-element.155), calls=%async_computation.6 | async-start | bytes 3342336 | tf_op jit(solution)/shard_map/all_to_all | solution.py:1294
  728.0 80.7 %all-to-all-start.7 = ((bf16[8,768,128]{2,1,0:T(8,128)(2,1)}), bf16[8,768,128]{2,1,0:T(8,128)(2,1)}, u32[]{:S(2)}, u32[]{:S(2)}) async-start(bf16[8,768,128]{2,1,0:T(8,128)(2,1)} %get-tuple-element.156), calls=%async_computation.7 | async-start | bytes 3145728 | tf_op jit(solution)/shard_map/all_to_all | solution.py:1294
  740.5 114.6 %collective-permute-start.17 = (bf16[1024,2560]{1,0:T(8,128)(2,1)}, bf16[1024,2560]{1,0:T(8,128)(2,1)}, u32[]{:S(2)}, u32[]{:S(2)}) collective-permute-start(bf16[1024,2560]{1,0:T(8,128)(2,1)} %add_convert_fusion.1), channel_id=1, source_target_pairs={{0,16},{8,24},{16,0},{24,8},{1,17},{9,25},{17,1},{25,9},{2,18},{10... | collective-permute-start | bytes 15728648 | tf_op jit(solution)/shard_map/ppermute | solution.py:1321
  741.1 114.0 %collective-permute-start.16 = (bf16[1024,2560]{1,0:T(8,128)(2,1)}, bf16[1024,2560]{1,0:T(8,128)(2,1)}, u32[]{:S(2)}, u32[]{:S(2)}) collective-permute-start(bf16[1024,2560]{1,0:T(8,128)(2,1)} %get-tuple-element.204), channel_id=1, source_target_pairs={{0,8},{8,0},{16,24},{24,16},{1,9},{9,1},{17,25},{25,17},{2,10},{10... | collective-permute-start | bytes 15728648 | tf_op jit(solution)/shard_map/ppermute | solution.py:1321
  808.8 102.3 %all-to-all-start.8 = ((bf16[8,768,256]{2,1,0:T(8,128)(2,1)}), bf16[8,768,256]{2,1,0:T(8,128)(2,1)}, u32[]{:S(2)}, u32[]{:S(2)}) async-start(bf16[8,768,256]{2,1,0:T(8,128)(2,1)} %copy-done.28), calls=%async_computation.8 | async-start | bytes 6291456 | tf_op jit(solution)/shard_map/all_to_all | solution.py:1294
  814.9 266.3 %reduce-scatter.2.cloned.1.call-start = ((), (), s32[]{:S(2)}) async-start(), calls=%async_computation.15 | async-start | bytes 5898240 | tf_op jit(solution)/shard_map/reduce_scatter | solution.py:1554
  911.0 52.9 %all-to-all-start.9 = ((bf16[8,768,128]{2,1,0:T(8,128)(2,1)}), bf16[8,768,128]{2,1,0:T(8,128)(2,1)}, u32[]{:S(2)}, u32[]{:S(2)}) async-start(bf16[8,768,128]{2,1,0:T(8,128)(2,1)} %copy-done.32), calls=%async_computation.9 | async-start | bytes 3145728 | tf_op jit(solution)/shard_map/all_to_all | solution.py:1294
  932.3 3.4 collective-permute-start.14
  932.4 6.4 collective-permute-start.13
  937.2 25.3 %collective-permute-start.15 = (bf16[1024,512]{1,0:T(8,128)(2,1)S(1)}, bf16[1024,512]{1,0:T(8,128)(2,1)S(1)}, u32[]{:S(2)}, u32[]{:S(2)}) collective-permute-start(bf16[1024,512]{1,0:T(8,128)(2,1)S(1)} %add_convert_fusion.3), channel_id=1, source_target_pairs={{0,16},{8,24},{16,0},{24,8},{1,17},{9,25},{17,1},{25,9},{2,18},{10... | collective-permute-start | bytes 3145736 | tf_op jit(solution)/shard_map/ppermute | solution.py:1321
  964.0 50.7 %all-to-all-start.12 = ((bf16[8,128,512]{2,1,0:T(8,128)(2,1)}), bf16[8,128,512]{2,1,0:T(8,128)(2,1)S(1)}, u32[]{:S(2)}, u32[]{:S(2)}) async-start(bf16[8,128,512]{2,1,0:T(8,128)(2,1)} %bitcast.33), calls=%async_computation.12 | async-start | bytes 2097152 | tf_op jit(solution)/shard_map/all_to_all | solution.py:1551
  1014.7 54.1 %all-to-all-start.10 = ((bf16[32,128,256]{2,1,0:T(8,128)(2,1)}), bf16[32,128,256]{2,1,0:T(8,128)(2,1)S(1)}, u32[]{:S(2)}, u32[]{:S(2)}) async-start(bf16[32,128,256]{2,1,0:T(8,128)(2,1)} %bitcast.58), calls=%async_computation.10 | async-start | bytes 4194304 | tf_op jit(solution)/shard_map/all_to_all | solution.py:1565
  1069.7 9.6 all-to-all-start.11
  (47 other events, 276.6 us)
Sparse Core Ops, SparseCore 0:
  22.6 100.0 all-gather.1
  865.1 152.6 reduce-scatter.1

commit v3 on v2

--- a/solution.py
+++ b/solution.py
@@ -13,7 +13,7 @@
 low = jnp.bfloat16
 wide = jnp.float32
 lanes = 128
-hint = 0.1
+hint = 0.3
 
 
 def norm_rows(values, scaling):
@@ -1098,10 +1098,18 @@
         summed(2 * stride, lambda b, dy, o, mid, hid, dg, du: (dy[...], hid[...]))
         summed(3 * stride, lambda b, dy, o, mid, hid, dg, du: (o[...], mid[...].astype(low)))
 
+    slot = step % 2
+
     def move(turn):
-        return pltpu.make_async_copy(buffer.at[turn], outs[turn], sems.at[turn])
-
-    fill(buffer.at[step])
+        return pltpu.make_async_copy(buffer.at[turn % 2], outs[turn], sems.at[turn % 2])
+
+    for turn in range(2, len(outs)):
+
+        @pl.when(step == turn)
+        def _(turn=turn):
+            move(turn - 2).wait()
+
+    fill(buffer.at[slot])
     for turn in range(len(outs)):
 
         @pl.when(step == turn)
@@ -1110,8 +1118,8 @@
 
     @pl.when(step == len(outs) - 1)
     def _():
-        for turn in range(len(outs)):
-            move(turn).wait()
+        move(len(outs) - 2).wait()
+        move(len(outs) - 1).wait()
 
 
 def weight_grads(sz, meta, parts, first):
@@ -1128,8 +1136,7 @@
         ins.append((middle_grad, spec))
         for array in (hidden, gate_grad, up_grad):
             ins.append((array, block))
-    stride = -(-inner // lanes) * lanes
-    columns = 3 * stride + piece
+    columns = 3 * (-(-inner // lanes) * lanes) + piece
     return call(
         functools.partial(weight_grad_kernel, len(parts)),
         "weight_grads",
@@ -1137,13 +1144,13 @@
         meta,
         ins,
         [(shaped((width, columns), low), in_place())] * turns,
-        scratch=[pltpu.VMEM((turns, width, columns), low), pltpu.SemaphoreType.DMA((turns,))],
+        scratch=[pltpu.VMEM((2, width, columns), low), pltpu.SemaphoreType.DMA((2,))],
         flops=len(parts) * rows * width * (3 * groups * inner + width),
         vmem=60,
     )
 
 
-def finish_kernel(sz, sides, has_carried, has_tokens, has_prior, form, per, meta, *refs):
+def finish_kernel(sz, sides, has_carried, has_tokens, has_prior, last, per, meta, *refs):
     refs = list(refs)
     normed = refs.pop(0)
     inputs = []
@@ -1154,7 +1161,7 @@
     carried = refs.pop(0) if has_carried else None
     if has_tokens:
         middle, prompt_ref, reply_ref, gain = (refs.pop(0) for _ in range(4))
-    count = 4 if form == "away" else 1
+    count = 4 if last else 1
     weight_outs = refs[-1 - count * len(sides) : -1]
     total = refs[-1]
     if has_tokens:
@@ -1174,10 +1181,10 @@
         def put(out, weight_part=weight_part):
             out[...] = weight_part.astype(low)
 
-        if form == "away":
+        if last:
             write_away(weight_outs[4 * i : 4 * i + 4], per, put)
         else:
-            weight_outs[i][...] = weight_part.astype(weight_outs[i].dtype)
+            weight_outs[i][...] = weight_part
 
     @pl.when(step == 0)
     def _():
@@ -1205,7 +1212,7 @@
                 out[...] = middle[at, :] + back
 
 
-def finish(sz, meta, micro, chunks, weights, normed, prior, form, carried=None, tokens=None):
+def finish(sz, meta, micro, chunks, weights, normed, prior, last, carried=None, tokens=None):
     n, rows = sz.heads, sz.rows
     width = normed.shape[1]
     groups = weights.shape[1] // width
@@ -1232,13 +1239,8 @@
             ins += [(chunk, by_step), (weights, pl.BlockSpec((span, width), place))]
         if prior is not None:
             ins.append((prior[side], grad_spec))
-        if form == "away":
+        if last:
             weight_outs += away_outs(width, span, per)
-        elif form == "whole":
-            whole_spec = pl.BlockSpec(
-                (None, width, span), lambda d, meta: (head(d, meta) // per, 0, head(d, meta) % per)
-            )
-            weight_outs.append((shaped((groups, width, per * span), low), whole_spec))
         else:
             weight_outs.append((shaped((n, width, span), wide), grad_spec))
     if carried is not None:
@@ -1269,7 +1271,7 @@
             carried is not None,
             tokens is not None,
             prior is not None,
-            form,
+            last,
             per,
         ),
         "finish",
@@ -1330,12 +1332,24 @@
     return (blocks[2].astype(wide) + along_grp(blocks[0], 1).astype(wide)).astype(low)
 
 
-def over_groups(blocks, far=None):
+def over_groups(blocks, handed=None, wait=()):
     _, to_core, _, stays = blocks
     near = along_grp(to_core, 1)
-    if far is None:
-        far = along_grp(hand_over(blocks), 2)
+    far = after(along_grp(hand_over(blocks) if handed is None else handed, 2), *wait)
     return stays.astype(wide) + near.astype(wide) + far.astype(wide)
+
+
+def over_rows_by_halves(total, row_part, wait=()):
+    place = lax.axis_index("seq")
+    total = total.reshape(-1, row_part, total.shape[1])
+    for away in powers(lax.axis_size("seq")):
+        total = total.reshape(total.shape[0] // 2, 2, row_part, total.shape[2])
+        mine = jnp.where((place & away) == 0, 0, 1)
+        sent = lax.dynamic_index_in_dim(total, 1 - mine, 1, keepdims=False).astype(low)
+        kept = lax.dynamic_index_in_dim(total, mine, 1, keepdims=False)
+        got = along_seq(sent, away)
+        total = kept + (after(got, *wait) if away == 1 else got).astype(wide)
+    return total[0]
 
 
 def after(value, *others):
@@ -1421,7 +1435,6 @@
     valid_total = counts[0] * 256.0 + counts[1]
     coefficient = slot_count / valid_total
     inner = w_gate.shape[1]
-    words = [picks_to_words(sz, metas[m], m, prompt_picks, reply_picks) for m in micros]
     shares = [jnp.concatenate([w_gate.T, w_up.T])[None], jnp.concatenate([w_down, w_out.T])[None]]
     nearest = [gain_one] * 2
     if row_part % lanes:
@@ -1431,8 +1444,6 @@
             if away == 1:
                 gain_one, *shares = lax.optimization_barrier((gain_one, *shares))
             nearest = [along_seq(share, away) for share in shares]
-            if away * 2 < seq_count and away > 1:
-                nearest = list(lax.optimization_barrier((*nearest, words)))[:-1]
             shares = [jnp.concatenate(pair) for pair in zip(shares, nearest)]
     far = [along_grp(share, 2) for share in shares]
     feed_w = (
@@ -1443,6 +1454,7 @@
         inner,
     )
     cache_key_rows, cache_value_rows = cache_keys[0], cache_values[0]
+    words = [picks_to_words(sz, metas[m], m, prompt_picks, reply_picks) for m in micros]
     gain_one, words = lax.optimization_barrier((gain_one, words))
     last = len(micros) - 1
 
@@ -1507,7 +1519,6 @@
     feed_grads = weight_grads(sz, metas[0], parts, 0) + weight_grads(sz, metas[0], parts, 2)
     handed = hand_over(feed_grads)
     query, pair = run_back(last, after(arrived[last], handed))
-    across = along_grp(handed, 2)
     back_pairs.append(exchange(sz, after(pair, *back_queries)))
     late = after(words, pair)
 
@@ -1520,7 +1531,7 @@
             mixed_grads[m],
             all_sums[m],
             deltas[m],
-            late[m] if m == last else words[m],
+            late[m],
             cache_key_rows,
             cache_value_rows,
         )
@@ -1528,18 +1539,18 @@
         if m < last:
             sides = {"pair": back_pairs[m], "query": (back_queries[m], cache_grad)}
             prompt_grad, reply_grad, stats, *prior_list = finish(
-                sz, metas[m], m, sides, qkv_w, normed[m], prior, "carry", None, tokens
+                sz, metas[m], m, sides, qkv_w, normed[m], prior, False, None, tokens
             )
             prior = dict(zip(sides, prior_list))
         else:
             back_pair = after(back_pairs[m], cache_grad, *grads)
             back_queries.append(exchange(sz, after(query, back_pair)))
             *grad_pair, carried = finish(
-                sz, metas[m], m, {"pair": back_pair}, qkv_w, normed[m], prior, "away"
+                sz, metas[m], m, {"pair": back_pair}, qkv_w, normed[m], prior, True
             )
             sides = {"query": (back_queries[m], cache_grad)}
-            prompt_grad, reply_grad, stats, grad_query = finish(
-                sz, metas[m], m, sides, qkv_w, normed[m], prior, "whole", carried, tokens
+            prompt_grad, reply_grad, stats, *grad_query = finish(
+                sz, metas[m], m, sides, qkv_w, normed[m], prior, True, carried, tokens
             )
         grads = [prompt_grad, reply_grad]
         if m == 0:
@@ -1550,19 +1561,17 @@
         grad = grad.astype(low).reshape(seq_count, row_part, grad.shape[1])
         return jnp.sum(lax.all_to_all(grad, "seq", 0, 0).astype(wide), axis=0)
 
-    feed_grads = over_groups(feed_grads, after(across, *early_grads)).astype(low)
-    feed_grads = lax.psum_scatter(feed_grads, "seq", scatter_dimension=0, tiled=True).astype(wide)
+    feed_grads = over_rows_by_halves(over_groups(feed_grads, handed, early_grads), row_part, (stats,))
     stride = -(-inner // lanes) * lanes
     grad_gate, grad_up, grad_down = (
         feed_grads[:, i * stride : i * stride + inner] for i in range(3)
     )
     grad_out = feed_grads[:, 3 * stride :]
-    grad_pair = over_rows(over_groups(grad_pair)).reshape(row_part, per_grp, 2, lanes)
+    grad_pair = over_rows(over_groups(grad_pair, None, (stats,))).reshape(row_part, per_grp, 2, lanes)
     grad_key, grad_value = (
         grad_pair[:, :, i].reshape(row_part, per_grp * lanes) for i in range(2)
     )
-    grad_query = grad_query.reshape(grp_count * seq_count, row_part, per_grp * lanes)
-    grad_query = jnp.sum(lax.all_to_all(grad_query, everywhere, 0, 0).astype(wide), axis=0)
+    grad_query = over_rows(over_groups(grad_query))
     count = grp_count * seq_count
     tail = jnp.concatenate(
         [

time: 1100 us -> 1090 us (level)
  waiting for transfers between devices: 320 us -> 279 us
  local copies, waits for them, and re-layouts: 63.5 us -> 76.2 us
  other arithmetic: 41.7 us -> 53.3 us
    ppermute x6 -> x9, waiting for transfers between devices: 140 us -> 209 us  [along_seq(): return lax.ppermute(array, 'seq', [(i, i ^ away) for i in range(count)])]
    all_to_all x1 -> x0, waiting for transfers between devices: 46.8 us -> none  [body(): lax.all_to_all(grad_query, everywhere, 0, 0).astype(wide)]
    ppermute x12 -> x15, waiting for transfers between devices: 31.7 us -> 7.64 us  [along_grp(): return lax.ppermute(array, 'grp', [(i, i ^ away) for i in range(count)])]
    all_to_all x1 -> x2, waiting for transfers between devices: 25.3 us -> 3.12 us  [over_rows(): return jnp.sum(lax.all_to_all(grad, 'seq', 0, 0).astype(wide), axis=0)]
    add x0 -> x3, other arithmetic: none -> 18.1 us  [the longest x1 11.5 us: over_groups(): return stays.astype(wide) + near.astype(wide) + far.astype(wide)]
    all_to_all x9, waiting for transfers between devices: 63 us -> 47.2 us  [exchange(): return lax.all_to_all(array, 'seq', 0, 0, axis_index_groups=subgroups(sz))]
    unnamed x135 -> x139, local copies, waits for them, and re-layouts: 48.2 us -> 52.8 us
  transfers between devices with their start and end apart: 32 -> 37, of which waited for: 18 -> 20; matrix products, arithmetic and copies ran while one was open for 4% -> 7% of each run, Pallas kernels for 46% -> 46%
where the time goes in v3:
time: 1090 us; the launch traced here: 1080 us
  Pallas kernels  527 us (48%)
  waiting for transfers between devices  279 us (26%)
  starting transfers between devices  85 us (8%)
  local copies, waits for them, and re-layouts  76.2 us (7%)
  other arithmetic  53.3 us (5%)
  blocking collectives  42.9 us (4%)
  between operations  20.9 us (2%)
    pallas_call x17, Pallas kernels, call(): pl.pallas_call(kernel, out_shape=list(out_shape), grid_spec=pltpu.Prefetc...  308 us
    ppermute x9, waiting for transfers between devices, along_seq(): return lax.ppermute(array, 'seq', [(i, i ^ away) for i in range(count)])  209 us
    pallas_call x2, Pallas kernels, attend_back(): pl.pallas_call(functools.partial(attend_back_kernel, sz), out_shape=out_s...  128 us
    pallas_call x2, Pallas kernels, attend(): pl.pallas_call(functools.partial(attend_kernel, sz), out_shape=jax.ShapeD...  75.5 us
    unnamed x139, local copies, waits for them, and re-layouts  52.8 us
    all_to_all x9, waiting for transfers between devices, exchange(): return lax.all_to_all(array, 'seq', 0, 0, axis_index_groups=subgroups(sz))  47.2 us
    all_to_all x9, starting transfers between devices, exchange(): return lax.all_to_all(array, 'seq', 0, 0, axis_index_groups=subgroups(sz))  46 us
    all_to_all x1, blocking collectives, exchange(): return lax.all_to_all(array, 'seq', 0, 0, axis_index_groups=subgroups(sz))  42.9 us
  transfers between devices with their start and end apart: 37, of which 20 were waited for; matrix products, arithmetic and copies ran while one was open for 7% of the time, Pallas kernels for 46%

profile of v3, /device:TPU:0, one launch (start us, length us, event | category | flops | bytes accessed | tf_op | source)
XLA Modules:
  0.0 1084.3 jit_solution(17192106732682316153)
XLA Ops:
  22.2 4.1 collective-permute-start
  28.3 20.4 %collective-permute-done = bf16[1,1408,128]{2,1,0:T(8,128)(2,1)S(1)} collective-permute-done((bf16[1,1408,128]{2,1,0:T(8,128)(2,1)S(1)}, bf16[1,1408,128]{2,1,0:T(8,128)(2,1)S(1)}, u32[]{:S(2)}, u32[]{:S(2)}) %collective-permute-start) | collective-permute-done | bytes 360480 | tf_op jit(solution)/shard_map/ppermute | solution.py:1328
  52.0 8.8 collective-permute-done.2
  62.6 46.7 %collective-permute-done.3 = bf16[2,960,128]{2,1,0:T(8,128)(2,1)S(1)} collective-permute-done((bf16[2,960,128]{2,1,0:T(8,128)(2,1)S(1)}, bf16[2,960,128]{2,1,0:T(8,128)(2,1)S(1)}, u32[]{:S(2)}, u32[]{:S(2)}) %collective-permute-start.3) | collective-permute-done | bytes 491552 | tf_op jit(solution)/shard_map/ppermute | solution.py:1328
  111.6 10.1 all-gather.2.cloned.1.call-done.query_w.pair_w.refs_2_.refs_4_
  126.1 7.8 picks_to_words.3
  133.9 7.9 picks_to_words.2
  145.8 10.0 project.2
  159.3 4.8 all-to-all-start
  173.2 65.1 %collective-permute-done.6 = bf16[4,960,128]{2,1,0:T(8,128)(2,1)S(1)} collective-permute-done((bf16[4,960,128]{2,1,0:T(8,128)(2,1)}, bf16[4,960,128]{2,1,0:T(8,128)(2,1)S(1)}, u32[]{:S(2)}, u32[]{:S(2)}) %collective-permute-start.6) | collective-permute-done | bytes 983072 | tf_op jit(solution)/shard_map/ppermute | solution.py:1328
  240.9 6.9 cache_forward.2
  250.0 10.0 project.3
  261.2 6.9 cache_forward.3
  269.9 37.9 %attend.2 = bf16[8,800,128]{2,1,0:T(8,128)(2,1)S(1)} custom-call(s32[7]{0:T(128)S(1)} %copy-done.39, bf16[8,768,384]{2,1,0:T(8,128)(2,1)} %all-to-all-done.refs_0_), custom_call_target="tpu_custom_call" | custom-call | flops 12079595520 | bytes 2516582 | tf_op jit(solution)/shard_map/attend/pallas_call | solution.py:327
  307.8 42.9 %all_to_all.69.message = bf16[8,800,128]{2,1,0:T(8,128)(2,1)S(1)} all-to-all(bf16[8,800,128]{2,1,0:T(8,128)(2,1)S(1)} %attend.2), channel_id=1, replica_groups=mesh['grp'=4,'seq'=8] {'seq'}, dimensions={0} | all-to-all | bytes 3276800 | tf_op jit(solution)/shard_map/all_to_all | solution.py:1296
  350.7 4.8 all-to-all-start.3
  370.9 64.5 %feed_forward.2 = (bf16[2,1,512,1024]{3,2,1,0:T(8,128)(2,1)}, bf16[2,1,256,1024]{3,2,1,0:T(8,128)(2,1)}, f32[768,1024]{1,0:T(8,128)}, bf16[768,1024]{1,0:T(8,128...) custom-call(s32[7]{0:T(128)} %get-tuple-element.266.meta, ...), custom_call_target="tpu_custom_call" | custom-call | flops 8938900480 | bytes 15387648 | tf_op jit(solution)/shard_map/feed_forward/pallas_call | solution.py:547
  441.0 17.8 %all-to-all-done.3.refs_0_ = bf16[8,768,384]{2,1,0:T(8,128)(2,1)} async-done(((bf16[8,768,384]{2,1,0:T(8,128)(2,1)}), bf16[8,768,384]{2,1,0:T(8,128)(2,1)}, u32[]{:S(2)}, u32[]{:S(2)}) %all-to-all-start.3) | async-done | bytes 4718624 | tf_op jit(solution)/shard_map/all_to_all | solution.py:1296
  462.5 37.6 %attend.3 = bf16[8,800,128]{2,1,0:T(8,128)(2,1)S(1)} custom-call(s32[7]{0:T(128)S(1)} %copy-done.44, bf16[8,768,384]{2,1,0:T(8,128)(2,1)} %all-to-all-done.3.refs_0_), custom_call_target="tpu_custom_call" | custom-call | flops 12079595520 | bytes 2516582 | tf_op jit(solution)/shard_map/attend/pallas_call | solution.py:327
  503.0 5.8 all-to-all-start.4
  510.3 64.9 %attend_back.2 = (bf16[8,768,128]{2,1,0:T(8,128)(2,1)S(1)}, bf16[8,768,256]{2,1,0:T(8,128)(2,1)S(1)}) custom-call(s32[7]{0:T(128)S(1)} %copy-done.40, bf16[8,768,384]{2,1,0:T(8,128)(2,1)} %all-to-all-done.refs_0_, bf16[8,816,128]{2,1,0:T(8,128)(2,1)S(1)} %copy-done.30), custom_call_target="tpu_custom_call" | custom-call | flops 20132659200 | bytes 4404019 | tf_op jit(solution)/shard_map/attend_back/pallas_call | solution.py:484
  578.1 6.1 all-to-all-start.5
  591.6 64.6 %feed_forward.3 = (bf16[2,1,512,1024]{3,2,1,0:T(8,128)(2,1)}, bf16[2,1,256,1024]{3,2,1,0:T(8,128)(2,1)}, f32[768,1024]{1,0:T(8,128)}, bf16[768,1024]{1,0:T(8,128...) custom-call(s32[7]{0:T(128)} %pad_add_fusion.2.meta, ...), custom_call_target="tpu_custom_call", output_to_operand_aliasing={{0}: (16, {}), {1}: (17, {})} | custom-call | flops 8938900480 | bytes 16331366 | tf_op jit(solution)/shard_map/feed_forward/pallas_call | solution.py:547
  661.7 27.3 %weight_grads.3 = (bf16[1024,2560]{1,0:T(8,128)(2,1)}, bf16[1024,2560]{1,0:T(8,128)(2,1)}) custom-call(s32[7]{0:T(128)} %get-tuple-element.266.meta, bf16[768,1024]{1,0:T(8,128)(2,1)} %get-tuple-element.161.refs_0_, bf16[768,1024]{1,0:T(8,128)(2,1)} %get-tuple-element.162.refs_1_, bf16[768,1024]{1,0:T(8,128)(2,1)} %copy-done.8, ...), custom_call_target="tpu_custom_call" | custom-call | flops 4469450240 | bytes 15649996 | tf_op jit(solution)/shard_map/weight_grads/pallas_call | solution.py:547
  689.1 6.0 all-to-all-start.6
  695.3 27.3 %weight_grads.2 = (bf16[1024,2560]{1,0:T(8,128)(2,1)}, bf16[1024,2560]{1,0:T(8,128)(2,1)}) custom-call(s32[7]{0:T(128)} %get-tuple-element.266.meta, bf16[768,1024]{1,0:T(8,128)(2,1)} %get-tuple-element.161.refs_0_, bf16[768,1024]{1,0:T(8,128)(2,1)} %get-tuple-element.162.refs_1_, bf16[768,1024]{1,0:T(8,128)(2,1)} %copy-done.8, ...), custom_call_target="tpu_custom_call" | custom-call | flops 4469450240 | bytes 15649996 | tf_op jit(solution)/shard_map/weight_grads/pallas_call | solution.py:547
  722.6 12.2 %all-to-all-done.6.refs_1_ = bf16[8,816,128]{2,1,0:T(8,128)(2,1)S(1)} async-done(((bf16[8,816,128]{2,1,0:T(8,128)(2,1)}), bf16[8,816,128]{2,1,0:T(8,128)(2,1)S(1)}, u32[]{:S(2)}, u32[]{:S(2)}) %all-to-all-start.6) | async-done | bytes 1671200 | tf_op jit(solution)/shard_map/all_to_all | solution.py:1296
  734.8 4.5 all-to-all-start.7
  739.4 7.8 add_convert_fusion
  747.8 63.4 %attend_back.3 = (bf16[8,768,128]{2,1,0:T(8,128)(2,1)}, bf16[8,768,256]{2,1,0:T(8,128)(2,1)S(1)}) custom-call(s32[7]{0:T(128)S(1)} %copy-done.45, bf16[8,768,384]{2,1,0:T(8,128)(2,1)} %all-to-all-done.3.refs_0_, bf16[8,816,128]{2,1,0:T(8,128)(2,1)S(1)} %all-to-all-done.6.refs_1_), custom_call_target="tpu_custom_call" | custom-call | flops 20132659200 | bytes 4404019 | tf_op jit(solution)/shard_map/attend_back/pallas_call | solution.py:484
  812.8 6.6 all-to-all-start.8
  823.2 7.5 cache_backward.3.refs_3_
  832.3 7.5 cache_backward.2.refs_5_
  841.5 25.7 %finish.3 = (f32[2,1,512,1024]{3,2,1,0:T(8,128)}, f32[2,1,256,1024]{3,2,1,0:T(8,128)}, f32[8,1024]{1,0:T(8,128)S(1)}, f32[8,1024,256]{2,1,0:T(8,128)}, f32[8,1024,128]{2,1,0:T(8,128)}) custom-call(s32[7]{0:T(128)S(1)} %copy-done.41, bf16[768,1024]{1,0:T(8,128)(2,1)} %copy-done.34, bf16[8,768,256]{2,1,0:T(8,128)(2,1)} %all-to-all-done.5.refs_1_, ...), custom_call_target="tpu_custom_call" | custom-call | flops 2899102976 | bytes 14245478 | tf_op jit(solution)/shard_map/finish/pallas_call | solution.py:547
  867.2 11.5 %convert_add_fusion = f32[1024,2560]{1,0:T(8,128)} fusion(bf16[1024,2560]{1,0:T(8,128)(2,1)} %collective-permute-done.20, bf16[1024,2560]{1,0:T(8,128)(2,1)} %collective-permute-done.19, bf16[1024,2560]{1,0:T(8,128)(2,1)} %get-tuple-element.212), kind=kLoop, calls=%fused_computation | loop fusion | flops 13107200 | bytes 26214400 | tf_op jit(solution)/shard_map/add | solution.py:1339
  878.8 10.3 all-to-all-done.8.refs_1_
  889.1 3.8 all-to-all-start.9
  893.0 4.3 fusion
  899.3 16.9 %finish.4 = (bf16[1024,512]{1,0:T(8,128)(2,1)S(1)}, bf16[1024,512]{1,0:T(8,128)(2,1)}, bf16[1024,512]{1,0:T(8,128)(2,1)}, bf16[1024,512]{1,0:T(8,128)(2,1)}, f32[768,1024]{1,0:T(8,128)}) custom-call(s32[7]{0:T(128)S(1)} %copy-done.45, bf16[768,1024]{1,0:T(8,128)(2,1)} %copy-done.17, bf16[8,768,256]{2,1,0:T(8,128)(2,1)} %all-to-all-done.8.refs_1_, ...), custom_call_target="tpu_custom_call" | custom-call | flops 966367616 | bytes 8060928 | tf_op jit(solution)/shard_map/finish/pallas_call | solution.py:547
  923.9 6.2 all-to-all-done.9.refs_1_
  931.4 20.0 %finish.5 = (f32[2,1,512,1024]{3,2,1,0:T(8,128)}, f32[2,1,256,1024]{3,2,1,0:T(8,128)}, f32[8,1024]{1,0:T(8,128)S(1)}, bf16[1024,256]{1,0:T(8,128)(2,1)S(1)}, bf1...) custom-call(s32[7]{0:T(128)S(1)} %copy-done.45, ...), custom_call_target="tpu_custom_call", output_to_operand_aliasing={{0}: (11, {}), {1}: (12, {})} | custom-call | flops 966367616 | bytes 12318720 | tf_op jit(solution)/shard_map/finish/pallas_call | solution.py:547
  951.4 17.2 %collective-permute-done.21 = bf16[4,128,2560]{2,1,0:T(8,128)(2,1)} collective-permute-done((bf16[4,128,2560]{2,1,0:T(8,128)(2,1)}, bf16[4,128,2560]{2,1,0:T(8,128)(2,1)}, u32[]{:S(2)}, u32[]{:S(2)}) %collective-permute-start.21) | collective-permute-done | bytes 2621472 | tf_op jit(solution)/shard_map/ppermute | solution.py:1328
  968.6 4.1 bitcast_add_fusion
  981.6 4.2 all-to-all-start.12
  989.4 26.5 %collective-permute-done.22 = bf16[2,128,2560]{2,1,0:T(8,128)(2,1)} collective-permute-done((bf16[2,128,2560]{2,1,0:T(8,128)(2,1)S(1)}, bf16[2,128,2560]{2,1,0:T(8,128)(2,1)}, u32[]{:S(2)}, u32[]{:S(2)}) %collective-permute-start.22) | collective-permute-done | bytes 1310752 | tf_op jit(solution)/shard_map/ppermute | solution.py:1328
  1019.3 3.8 collective-permute-start.23
  1025.3 3.9 all-to-all-start.10
  1034.0 24.5 %collective-permute-done.23 = bf16[1,128,2560]{2,1,0:T(8,128)(2,1)} collective-permute-done((bf16[1,128,2560]{2,1,0:T(8,128)(2,1)}, bf16[1,128,2560]{2,1,0:T(8,128)(2,1)}, u32[]{:S(2)}, u32[]{:S(2)}) %collective-permute-start.23) | collective-permute-done | bytes 655392 | tf_op jit(solution)/shard_map/ppermute | solution.py:1328
  (253 shorter events, 153.8 us)
Async XLA Ops:
  7.2 114.6 %all-gather.2.cloned.1.call-start = ((), (), s32[]{:S(2)}) async-start(), calls=%async_computation.13 | async-start | bytes 6623232 | tf_op jit(solution)/shard_map/all_gather | solution.py:1427
  22.2 26.5 %collective-permute-start = (bf16[1,1408,128]{2,1,0:T(8,128)(2,1)S(1)}, bf16[1,1408,128]{2,1,0:T(8,128)(2,1)S(1)}, u32[]{:S(2)}, u32[]{:S(2)}) collective-permute-start(bf16[1,1408,128]{2,1,0:T(8,128)(2,1)S(1)} %maximum_bitcast_fusion), channel_id=1, source_target_pairs={{0,4},{1,5},{2,6},{3,7},{4,0},{5,1},{6,2},{7,3},{8,12},{9,13},{10,... | collective-permute-start | bytes 1081352 | tf_op jit(solution)/shard_map/ppermute | solution.py:1328
  28.3 32.6 %collective-permute-start.2 = (bf16[1,960,128]{2,1,0:T(8,128)(2,1)S(1)}, bf16[1,960,128]{2,1,0:T(8,128)(2,1)S(1)}, u32[]{:S(2)}, u32[]{:S(2)}) collective-permute-start(bf16[1,960,128]{2,1,0:T(8,128)(2,1)S(1)} %maximum_bitcast_fusion.1), channel_id=1, source_target_pairs={{0,4},{1,5},{2,6},{3,7},{4,0},{5,1},{6,2},{7,3},{8,12},{9,13},{10,... | collective-permute-start | bytes 737288 | tf_op jit(solution)/shard_map/ppermute | solution.py:1328
  48.8 61.6 %collective-permute-start.1 = (bf16[2,1408,128]{2,1,0:T(8,128)(2,1)S(1)}, bf16[2,1408,128]{2,1,0:T(8,128)(2,1)S(1)}, u32[]{:S(2)}, u32[]{:S(2)}) collective-permute-start(bf16[2,1408,128]{2,1,0:T(8,128)(2,1)S(1)} %pad_maximum_fusion.2), channel_id=1, source_target_pairs={{0,2},{1,3},{2,0},{3,1},{4,6},{5,7},{6,4},{7,5},{8,10},{9,11},{10,... | collective-permute-start | bytes 2162696 | tf_op jit(solution)/shard_map/ppermute | solution.py:1328
  60.9 48.5 %collective-permute-start.3 = (bf16[2,960,128]{2,1,0:T(8,128)(2,1)S(1)}, bf16[2,960,128]{2,1,0:T(8,128)(2,1)S(1)}, u32[]{:S(2)}, u32[]{:S(2)}) collective-permute-start(bf16[2,960,128]{2,1,0:T(8,128)(2,1)S(1)} %pad_maximum_fusion.3), channel_id=1, source_target_pairs={{0,2},{1,3},{2,0},{3,1},{4,6},{5,7},{6,4},{7,5},{8,10},{9,11},{10,... | collective-permute-start | bytes 1474568 | tf_op jit(solution)/shard_map/ppermute | solution.py:1328
  123.4 35.9 %collective-permute-start.4 = (bf16[4,1408,128]{2,1,0:T(8,128)(2,1)}, bf16[4,1408,128]{2,1,0:T(8,128)(2,1)}, u32[]{:S(2)}, u32[]{:S(2)}) collective-permute-start(bf16[4,1408,128]{2,1,0:T(8,128)(2,1)} %pad_maximum_fusion), channel_id=1, source_target_pairs={{0,1},{1,0},{2,3},{3,2},{4,5},{5,4},{6,7},{7,6},{8,9},{9,8},{10,11... | collective-permute-start | bytes 4325384 | tf_op jit(solution)/shard_map/ppermute | solution.py:1328
  159.3 81.5 %slice-start.2 = ((s8[4718592]{0:T(1024)(128)(4,1)}), s8[524288]{0:T(1024)(128)(4,1)S(1)}, s32[]{:S(2)}) async-start(s8[4718592]{0:T(1024)(128)(4,1)} %bitcast.66), calls=%async_computation.16 | async-start | bytes 1048576
  159.3 110.6 %all-to-all-start = ((bf16[8,768,384]{2,1,0:T(8,128)(2,1)}), bf16[8,768,384]{2,1,0:T(8,128)(2,1)}, u32[]{:S(2)}, u32[]{:S(2)}) async-start(bf16[8,768,384]{2,1,0:T(8,128)(2,1)} %copy-done.1), calls=%async_computation | async-start | bytes 9437184 | tf_op jit(solution)/shard_map/all_to_all | solution.py:1296
  164.1 76.7 %slice-start.3 = ((s8[4718592]{0:T(1024)(128)(4,1)}), s8[4194304]{0:T(1024)(128)(4,1)S(1)}, s32[]{:S(2)}) async-start(s8[4718592]{0:T(1024)(128)(4,1)} %bitcast.66), calls=%async_computation.17 | async-start | bytes 8388608
  165.7 84.3 %slice-start = ((s8[6422528]{0:T(1024)(128)(4,1)}), s8[4194304]{0:T(1024)(128)(4,1)S(1)}, s32[]{:S(2)}) async-start(s8[6422528]{0:T(1024)(128)(4,1)} %bitcast.64), calls=%async_computation.14 | async-start | bytes 8388608
  167.4 80.3 %copy-start.50 = (bf16[8,1408,128]{2,1,0:T(8,128)(2,1)}, bf16[8,1408,128]{2,1,0:T(8,128)(2,1)S(1)}, u32[]{:S(2)}) copy-start(bf16[8,1408,128]{2,1,0:T(8,128)(2,1)S(1)} %constant_dynamic-update-slice_fusion.refs_0_) | copy-start | bytes 8650756
  167.4 73.4 %copy-start.14 = (bf16[1,256,1024]{2,1,0:T(8,128)(2,1)S(1)}, bf16[1,256,1024]{2,1,0:T(8,128)(2,1)}, u32[]{:S(2)}) copy-start(bf16[1,256,1024]{2,1,0:T(8,128)(2,1)} %param.29) | copy-start | bytes 1572868
  167.4 73.4 %copy-start.15 = (bf16[1,256,1024]{2,1,0:T(8,128)(2,1)S(1)}, bf16[1,256,1024]{2,1,0:T(8,128)(2,1)}, u32[]{:S(2)}) copy-start(bf16[1,256,1024]{2,1,0:T(8,128)(2,1)} %param.30) | copy-start | bytes 1572868
  167.5 73.4 %copy-start.35 = (s32[8,8,512]{2,1,0:T(8,128)S(1)}, s32[8,8,512]{2,1,0:T(8,128)}, u32[]{:S(2)}) copy-start(s32[8,8,512]{2,1,0:T(8,128)} %get-tuple-element.178.words_prompt) | copy-start | bytes 393220
  167.5 73.4 %copy-start.37 = (s32[8,8,256]{2,1,0:T(8,128)S(1)}, s32[8,8,256]{2,1,0:T(8,128)}, u32[]{:S(2)}) copy-start(s32[8,8,256]{2,1,0:T(8,128)} %get-tuple-element.179.words_reply) | copy-start | bytes 196612
  167.5 102.3 %collective-permute-start.5 = (bf16[8,1408,128]{2,1,0:T(8,128)(2,1)S(1)}, bf16[8,1408,128]{2,1,0:T(8,128)(2,1)}, u32[]{:S(2)}, u32[]{:S(2)}) collective-permute-start(bf16[8,1408,128]{2,1,0:T(8,128)(2,1)S(1)} %constant_dynamic-update-slice_fusion.refs_0_), channel_id=1, source_target_pairs={{0,16},{8,24},{16,0},{24,8},{1,17},{9,25},{17,1},{25,9},{2,18},{10... | collective-permute-start | bytes 8650760 | tf_op jit(solution)/shard_map/ppermute | solution.py:1323
  169.0 69.4 %collective-permute-start.6 = (bf16[4,960,128]{2,1,0:T(8,128)(2,1)}, bf16[4,960,128]{2,1,0:T(8,128)(2,1)S(1)}, u32[]{:S(2)}, u32[]{:S(2)}) collective-permute-start(bf16[4,960,128]{2,1,0:T(8,128)(2,1)} %pad_maximum_fusion.1), channel_id=1, source_target_pairs={{0,1},{1,0},{2,3},{3,2},{4,5},{5,4},{6,7},{7,6},{8,9},{9,8},{10,11... | collective-permute-start | bytes 2949128 | tf_op jit(solution)/shard_map/ppermute | solution.py:1328
  173.2 76.8 %slice-start.1 = ((s8[6422528]{0:T(1024)(128)(4,1)}), s8[2228224]{0:T(1024)(128)(4,1)S(1)}, s32[]{:S(2)}) async-start(s8[6422528]{0:T(1024)(128)(4,1)} %bitcast.64), calls=%async_computation.15 | async-start | bytes 4456448
  239.4 68.4 %collective-permute-start.7 = (bf16[8,960,128]{2,1,0:T(8,128)(2,1)}, bf16[8,960,128]{2,1,0:T(8,128)(2,1)}, u32[]{:S(2)}, u32[]{:S(2)}) collective-permute-start(bf16[8,960,128]{2,1,0:T(8,128)(2,1)} %constant_dynamic-update-slice_fusion.2.refs_1_), channel_id=1, source_target_pairs={{0,16},{8,24},{16,0},{24,8},{1,17},{9,25},{17,1},{25,9},{2,18},{10... | collective-permute-start | bytes 5898248 | tf_op jit(solution)/shard_map/ppermute | solution.py:1323
  350.7 108.2 %all-to-all-start.3 = ((bf16[8,768,384]{2,1,0:T(8,128)(2,1)}), bf16[8,768,384]{2,1,0:T(8,128)(2,1)}, u32[]{:S(2)}, u32[]{:S(2)}) async-start(bf16[8,768,384]{2,1,0:T(8,128)(2,1)} %copy-done.2), calls=%async_computation.3 | async-start | bytes 9437184 | tf_op jit(solution)/shard_map/all_to_all | solution.py:1296
  355.5 12.6 %collective-permute-start.8 = (bf16[8,1408,128]{2,1,0:T(8,128)(2,1)}, bf16[8,1408,128]{2,1,0:T(8,128)(2,1)}, u32[]{:S(2)}, u32[]{:S(2)}) collective-permute-start(bf16[8,1408,128]{2,1,0:T(8,128)(2,1)} %copy-done.50), channel_id=1, source_target_pairs={{0,8},{8,0},{16,24},{24,16},{1,9},{9,1},{17,25},{25,17},{2,10},{10... | collective-permute-start | bytes 8650760 | tf_op jit(solution)/shard_map/ppermute | solution.py:1323
  355.6 15.4 %collective-permute-start.10 = (bf16[8,1408,128]{2,1,0:T(8,128)(2,1)}, bf16[8,1408,128]{2,1,0:T(8,128)(2,1)}, u32[]{:S(2)}, u32[]{:S(2)}) collective-permute-start(bf16[8,1408,128]{2,1,0:T(8,128)(2,1)} %collective-permute-done.5.refs_4_), channel_id=1, source_target_pairs={{0,8},{8,0},{16,24},{24,16},{1,9},{9,1},{17,25},{25,17},{2,10},{10... | collective-permute-start | bytes 8650760 | tf_op jit(solution)/shard_map/ppermute | solution.py:1323
  356.1 12.1 %collective-permute-start.9 = (bf16[8,960,128]{2,1,0:T(8,128)(2,1)}, bf16[8,960,128]{2,1,0:T(8,128)(2,1)}, u32[]{:S(2)}, u32[]{:S(2)}) collective-permute-start(bf16[8,960,128]{2,1,0:T(8,128)(2,1)} %constant_dynamic-update-slice_fusion.2.refs_1_), channel_id=1, source_target_pairs={{0,8},{8,0},{16,24},{24,16},{1,9},{9,1},{17,25},{25,17},{2,10},{10... | collective-permute-start | bytes 5898248 | tf_op jit(solution)/shard_map/ppermute | solution.py:1323
  356.1 14.8 %collective-permute-start.11 = (bf16[8,960,128]{2,1,0:T(8,128)(2,1)}, bf16[8,960,128]{2,1,0:T(8,128)(2,1)}, u32[]{:S(2)}, u32[]{:S(2)}) collective-permute-start(bf16[8,960,128]{2,1,0:T(8,128)(2,1)} %collective-permute-done.7.refs_5_), channel_id=1, source_target_pairs={{0,8},{8,0},{16,24},{24,16},{1,9},{9,1},{17,25},{25,17},{2,10},{10... | collective-permute-start | bytes 5898248 | tf_op jit(solution)/shard_map/ppermute | solution.py:1323
  458.9 42.9 %all-to-all-start.2 = ((bf16[8,816,128]{2,1,0:T(8,128)(2,1)}), bf16[8,816,128]{2,1,0:T(8,128)(2,1)S(1)}, u32[]{:S(2)}, u32[]{:S(2)}) async-start(bf16[8,816,128]{2,1,0:T(8,128)(2,1)} %copy-done.31), calls=%async_computation.2 | async-start | bytes 3342336 | tf_op jit(solution)/shard_map/all_to_all | solution.py:1296
  503.0 75.1 %all-to-all-start.4 = ((bf16[8,800,128]{2,1,0:T(8,128)(2,1)}), bf16[8,800,128]{2,1,0:T(8,128)(2,1)S(1)}, u32[]{:S(2)}, u32[]{:S(2)}) async-start(bf16[8,800,128]{2,1,0:T(8,128)(2,1)} %copy-done.32), calls=%async_computation.4 | async-start | bytes 3276800 | tf_op jit(solution)/shard_map/all_to_all | solution.py:1296
  578.1 83.6 %all-to-all-start.5 = ((bf16[8,768,256]{2,1,0:T(8,128)(2,1)}), bf16[8,768,256]{2,1,0:T(8,128)(2,1)}, u32[]{:S(2)}, u32[]{:S(2)}) async-start(bf16[8,768,256]{2,1,0:T(8,128)(2,1)} %copy-done.27), calls=%async_computation.5 | async-start | bytes 6291456 | tf_op jit(solution)/shard_map/all_to_all | solution.py:1296
  591.6 64.6 %copy-start.11 = (bf16[768,1024]{1,0:T(8,128)(2,1)S(1)}, bf16[768,1024]{1,0:T(8,128)(2,1)}, u32[]{:S(2)}) copy-start(bf16[768,1024]{1,0:T(8,128)(2,1)} %copy-done.10) | copy-start | bytes 4718596
  591.6 64.6 %copy-start.45 = (s32[7]{0:T(128)S(1)}, s32[7]{0:T(128)}, u32[]{:S(2)}) copy-start(s32[7]{0:T(128)} %pad_add_fusion.2.meta) | copy-start | bytes 88
  689.0 50.3 %collective-permute-start.12 = (bf16[1024,2560]{1,0:T(8,128)(2,1)}, bf16[1024,2560]{1,0:T(8,128)(2,1)}, u32[]{:S(2)}, u32[]{:S(2)}) collective-permute-start(bf16[1024,2560]{1,0:T(8,128)(2,1)} %get-tuple-element.175), channel_id=1, source_target_pairs={{0,8},{8,0},{16,24},{24,16},{1,9},{9,1},{17,25},{25,17},{2,10},{10... | collective-permute-start | bytes 15728648 | tf_op jit(solution)/shard_map/ppermute | solution.py:1323
  689.1 45.7 %all-to-all-start.6 = ((bf16[8,816,128]{2,1,0:T(8,128)(2,1)}), bf16[8,816,128]{2,1,0:T(8,128)(2,1)S(1)}, u32[]{:S(2)}, u32[]{:S(2)}) async-start(bf16[8,816,128]{2,1,0:T(8,128)(2,1)} %copy-done.28), calls=%async_computation.6 | async-start | bytes 3342336 | tf_op jit(solution)/shard_map/all_to_all | solution.py:1296
  695.1 172.2 %collective-permute-start.19 = (bf16[1024,2560]{1,0:T(8,128)(2,1)}, bf16[1024,2560]{1,0:T(8,128)(2,1)}, u32[]{:S(2)}, u32[]{:S(2)}) collective-permute-start(bf16[1024,2560]{1,0:T(8,128)(2,1)} %get-tuple-element.213), channel_id=1, source_target_pairs={{0,8},{8,0},{16,24},{24,16},{1,9},{9,1},{17,25},{25,17},{2,10},{10... | collective-permute-start | bytes 15728648 | tf_op jit(solution)/shard_map/ppermute | solution.py:1323
  734.8 78.0 %all-to-all-start.7 = ((bf16[8,768,128]{2,1,0:T(8,128)(2,1)}), bf16[8,768,128]{2,1,0:T(8,128)(2,1)}, u32[]{:S(2)}, u32[]{:S(2)}) async-start(bf16[8,768,128]{2,1,0:T(8,128)(2,1)} %copy-done.33), calls=%async_computation.7 | async-start | bytes 3145728 | tf_op jit(solution)/shard_map/all_to_all | solution.py:1296
  747.1 120.1 %collective-permute-start.20 = (bf16[1024,2560]{1,0:T(8,128)(2,1)}, bf16[1024,2560]{1,0:T(8,128)(2,1)}, u32[]{:S(2)}, u32[]{:S(2)}) collective-permute-start(bf16[1024,2560]{1,0:T(8,128)(2,1)} %add_convert_fusion), channel_id=1, source_target_pairs={{0,16},{8,24},{16,0},{24,8},{1,17},{9,25},{17,1},{25,9},{2,18},{10... | collective-permute-start | bytes 15728648 | tf_op jit(solution)/shard_map/ppermute | solution.py:1323
  812.8 76.3 %all-to-all-start.8 = ((bf16[8,768,256]{2,1,0:T(8,128)(2,1)}), bf16[8,768,256]{2,1,0:T(8,128)(2,1)}, u32[]{:S(2)}, u32[]{:S(2)}) async-start(bf16[8,768,256]{2,1,0:T(8,128)(2,1)} %copy-done.26), calls=%async_computation.8 | async-start | bytes 6291456 | tf_op jit(solution)/shard_map/all_to_all | solution.py:1296
  889.1 41.0 %all-to-all-start.9 = ((bf16[8,768,128]{2,1,0:T(8,128)(2,1)}), bf16[8,768,128]{2,1,0:T(8,128)(2,1)S(1)}, u32[]{:S(2)}, u32[]{:S(2)}) async-start(bf16[8,768,128]{2,1,0:T(8,128)(2,1)} %get-tuple-element.191), calls=%async_computation.9 | async-start | bytes 3145728 | tf_op jit(solution)/shard_map/all_to_all | solution.py:1296
  897.2 71.4 %collective-permute-start.21 = (bf16[4,128,2560]{2,1,0:T(8,128)(2,1)}, bf16[4,128,2560]{2,1,0:T(8,128)(2,1)}, u32[]{:S(2)}, u32[]{:S(2)}) collective-permute-start(bf16[4,128,2560]{2,1,0:T(8,128)(2,1)} %fusion), channel_id=1, source_target_pairs={{0,1},{1,0},{2,3},{3,2},{4,5},{5,4},{6,7},{7,6},{8,9},{9,8},{10,11... | collective-permute-start | bytes 7864328 | tf_op jit(solution)/shard_map/ppermute | solution.py:1328
  916.2 3.5 collective-permute-start.17
  916.3 62.1 %collective-permute-start.16 = (bf16[1024,512]{1,0:T(8,128)(2,1)}, bf16[1024,512]{1,0:T(8,128)(2,1)}, u32[]{:S(2)}, u32[]{:S(2)}) collective-permute-start(bf16[1024,512]{1,0:T(8,128)(2,1)} %get-tuple-element.208), channel_id=1, source_target_pairs={{0,8},{8,0},{16,24},{24,16},{1,9},{9,1},{17,25},{25,17},{2,10},{10... | collective-permute-start | bytes 3145736 | tf_op jit(solution)/shard_map/ppermute | solution.py:1323
  922.5 54.2 %collective-permute-start.18 = (bf16[1024,512]{1,0:T(8,128)(2,1)}, bf16[1024,512]{1,0:T(8,128)(2,1)}, u32[]{:S(2)}, u32[]{:S(2)}) collective-permute-start(bf16[1024,512]{1,0:T(8,128)(2,1)} %add_convert_fusion.2), channel_id=1, source_target_pairs={{0,16},{8,24},{16,0},{24,8},{1,17},{9,25},{17,1},{25,9},{2,18},{10... | collective-permute-start | bytes 3145736 | tf_op jit(solution)/shard_map/ppermute | solution.py:1323
  951.4 25.4 %collective-permute-start.14 = (bf16[1024,256]{1,0:T(8,128)(2,1)S(1)}, bf16[1024,256]{1,0:T(8,128)(2,1)S(1)}, u32[]{:S(2)}, u32[]{:S(2)}) collective-permute-start(bf16[1024,256]{1,0:T(8,128)(2,1)S(1)} %get-tuple-element.201), channel_id=1, source_target_pairs={{0,8},{8,0},{16,24},{24,16},{1,9},{9,1},{17,25},{25,17},{2,10},{10... | collective-permute-start | bytes 1572872 | tf_op jit(solution)/shard_map/ppermute | solution.py:1323
  975.2 40.6 %collective-permute-start.22 = (bf16[2,128,2560]{2,1,0:T(8,128)(2,1)S(1)}, bf16[2,128,2560]{2,1,0:T(8,128)(2,1)}, u32[]{:S(2)}, u32[]{:S(2)}) collective-permute-start(bf16[2,128,2560]{2,1,0:T(8,128)(2,1)S(1)} %fusion.1), channel_id=1, source_target_pairs={{0,2},{1,3},{2,0},{3,1},{4,6},{5,7},{6,4},{7,5},{8,10},{9,11},{10,... | collective-permute-start | bytes 3932168 | tf_op jit(solution)/shard_map/ppermute | solution.py:1328
  976.9 12.5 %collective-permute-start.15 = (bf16[1024,256]{1,0:T(8,128)(2,1)S(1)}, bf16[1024,256]{1,0:T(8,128)(2,1)S(1)}, u32[]{:S(2)}, u32[]{:S(2)}) collective-permute-start(bf16[1024,256]{1,0:T(8,128)(2,1)S(1)} %add_convert_fusion.4), channel_id=1, source_target_pairs={{0,16},{8,24},{16,0},{24,8},{1,17},{9,25},{17,1},{25,9},{2,18},{10... | collective-permute-start | bytes 1572872 | tf_op jit(solution)/shard_map/ppermute | solution.py:1323
  981.6 43.7 %all-to-all-start.12 = ((bf16[8,128,512]{2,1,0:T(8,128)(2,1)}), bf16[8,128,512]{2,1,0:T(8,128)(2,1)}, u32[]{:S(2)}, u32[]{:S(2)}) async-start(bf16[8,128,512]{2,1,0:T(8,128)(2,1)} %bitcast.33), calls=%async_computation.12 | async-start | bytes 2097152 | tf_op jit(solution)/shard_map/all_to_all | solution.py:1562
  988.2 34.9 %collective-permute-start.13 = (bf16[1024,256]{1,0:T(8,128)(2,1)S(1)}, bf16[1024,256]{1,0:T(8,128)(2,1)S(1)}, u32[]{:S(2)}, u32[]{:S(2)}) collective-permute-start(bf16[1024,256]{1,0:T(8,128)(2,1)S(1)} %get-tuple-element.199), channel_id=1, source_target_pairs={{0,8},{8,0},{16,24},{24,16},{1,9},{9,1},{17,25},{25,17},{2,10},{10... | collective-permute-start | bytes 1572872 | tf_op jit(solution)/shard_map/ppermute | solution.py:1323
  1019.3 39.2 %collective-permute-start.23 = (bf16[1,128,2560]{2,1,0:T(8,128)(2,1)}, bf16[1,128,2560]{2,1,0:T(8,128)(2,1)}, u32[]{:S(2)}, u32[]{:S(2)}) collective-permute-start(bf16[1,128,2560]{2,1,0:T(8,128)(2,1)} %dynamic-slice_convert_fusion.1), channel_id=1, source_target_pairs={{0,4},{1,5},{2,6},{3,7},{4,0},{5,1},{6,2},{7,3},{8,12},{9,13},{10,... | collective-permute-start | bytes 1966088 | tf_op jit(solution)/shard_map/ppermute | solution.py:1328
  1025.3 38.6 %all-to-all-start.10 = ((bf16[8,128,256]{2,1,0:T(8,128)(2,1)}), bf16[8,128,256]{2,1,0:T(8,128)(2,1)S(1)}, u32[]{:S(2)}, u32[]{:S(2)}) async-start(bf16[8,128,256]{2,1,0:T(8,128)(2,1)} %bitcast.82), calls=%async_computation.10 | async-start | bytes 1048576 | tf_op jit(solution)/shard_map/all_to_all | solution.py:1562
  1064.6 9.6 all-to-all-start.11
  (54 other events, 447.2 us)
Sparse Core Ops, SparseCore 0:
  21.3 100.3 all-gather.1

commit v4 on v3

--- a/solution.py
+++ b/solution.py
@@ -1480,15 +1480,15 @@
         return query, pair
 
     for m in micros:
-        chunks = exchange(sz, after(own[m], nearest[0] if answers is None else answers))
+        chunks = exchange(sz, own[m] if answers is None else after(own[m], answers, far[1]))
         if m == 0:
-            chunks, cached, _ = lax.optimization_barrier((chunks, cached, far[0]))
+            chunks, cached, _ = lax.optimization_barrier((chunks, cached, nearest[1]))
         if messages is not None:
             chunks = after(chunks, messages)
         received.append(chunks)
         extras.append(other_blocks(sz, chunks))
         answers = attend(sz, metas[m], chunks, extras[m])
-        answers = after(answers, arrived[m - 1] if m > 0 else far[1])
+        answers = after(answers, arrived[m - 1] if m > 0 else far[0])
         answers = exchange(sz, answers)
         arrived_answers = answers
         if m > 0:

time: 1090 us -> 1090 us (level)
  blocking collectives: 42.9 us -> 0 us
  waiting for transfers between devices: 279 us -> 313 us
    all_to_all x1 -> x0, blocking collectives: 42.9 us -> none  [exchange(): return lax.all_to_all(array, 'seq', 0, 0, axis_index_groups=subgroups(sz))]
    ppermute x15, waiting for transfers between devices: 7.64 us -> 49.6 us  [along_grp(): return lax.ppermute(array, 'grp', [(i, i ^ away) for i in range(count)])]
    all_to_all x9 -> x10, starting transfers between devices: 46 us -> 54.1 us  [exchange(): return lax.all_to_all(array, 'seq', 0, 0, axis_index_groups=subgroups(sz))]
    unnamed x139 -> x145, local copies, waits for them, and re-layouts: 52.8 us -> 48.7 us
    all_to_all x9 -> x10, waiting for transfers between devices: 47.2 us -> 45.5 us  [exchange(): return lax.all_to_all(array, 'seq', 0, 0, axis_index_groups=subgroups(sz))]
  transfers between devices with their start and end apart: 37 -> 38, of which waited for: 20 -> 20; matrix products, arithmetic and copies ran while one was open for 7% -> 7% of each run, Pallas kernels for 46% -> 45%
where the time goes in v4:
time: 1090 us; the launch traced here: 1080 us
  Pallas kernels  526 us (48%)
  waiting for transfers between devices  313 us (29%)
  starting transfers between devices  90.5 us (8%)
  local copies, waits for them, and re-layouts  71.8 us (7%)
  other arithmetic  56.2 us (5%)
  between operations  21 us (2%)
    pallas_call x17, Pallas kernels, call(): pl.pallas_call(kernel, out_shape=list(out_shape), grid_spec=pltpu.Prefetc...  309 us
    ppermute x9, waiting for transfers between devices, along_seq(): return lax.ppermute(array, 'seq', [(i, i ^ away) for i in range(count)])  206 us
    pallas_call x2, Pallas kernels, attend_back(): pl.pallas_call(functools.partial(attend_back_kernel, sz), out_shape=out_s...  127 us
    pallas_call x2, Pallas kernels, attend(): pl.pallas_call(functools.partial(attend_kernel, sz), out_shape=jax.ShapeD...  74.5 us
    all_to_all x10, starting transfers between devices, exchange(): return lax.all_to_all(array, 'seq', 0, 0, axis_index_groups=subgroups(sz))  54.1 us
    ppermute x15, waiting for transfers between devices, along_grp(): return lax.ppermute(array, 'grp', [(i, i ^ away) for i in range(count)])  49.6 us
    unnamed x145, local copies, waits for them, and re-layouts  48.7 us
    all_to_all x10, waiting for transfers between devices, exchange(): return lax.all_to_all(array, 'seq', 0, 0, axis_index_groups=subgroups(sz))  45.5 us
  transfers between devices with their start and end apart: 38, of which 20 were waited for; matrix products, arithmetic and copies ran while one was open for 7% of the time, Pallas kernels for 45%

profile of v4, /device:TPU:0, one launch (start us, length us, event | category | flops | bytes accessed | tf_op | source)
XLA Modules:
  0.0 1078.8 jit_solution(6680927337079548769)
XLA Ops:
  22.3 4.1 collective-permute-start
  28.4 20.3 %collective-permute-done = bf16[1,1408,128]{2,1,0:T(8,128)(2,1)S(1)} collective-permute-done((bf16[1,1408,128]{2,1,0:T(8,128)(2,1)S(1)}, bf16[1,1408,128]{2,1,0:T(8,128)(2,1)S(1)}, u32[]{:S(2)}, u32[]{:S(2)}) %collective-permute-start) | collective-permute-done | bytes 360480 | tf_op jit(solution)/shard_map/ppermute | solution.py:1328
  52.9 8.1 collective-permute-done.2
  64.5 7.8 picks_to_words.3
  72.3 7.8 picks_to_words.2
  80.1 29.7 %collective-permute-done.3 = bf16[2,960,128]{2,1,0:T(8,128)(2,1)} collective-permute-done((bf16[2,960,128]{2,1,0:T(8,128)(2,1)}, bf16[2,960,128]{2,1,0:T(8,128)(2,1)}, u32[]{:S(2)}, u32[]{:S(2)}) %collective-permute-start.3) | collective-permute-done | bytes 491552 | tf_op jit(solution)/shard_map/ppermute | solution.py:1328
  114.4 7.0 all-gather.2.cloned.1.call-done.query_w.pair_w.refs_2_.refs_4_
  125.9 10.0 project.2
  139.4 5.7 all-to-all-start
  149.8 79.5 %collective-permute-done.5 = bf16[4,1408,128]{2,1,0:T(8,128)(2,1)S(1)} collective-permute-done((bf16[4,1408,128]{2,1,0:T(8,128)(2,1)}, bf16[4,1408,128]{2,1,0:T(8,128)(2,1)S(1)}, u32[]{:S(2)}, u32[]{:S(2)}) %collective-permute-start.5) | collective-permute-done | bytes 1441824 | tf_op jit(solution)/shard_map/ppermute | solution.py:1328
  234.4 6.8 cache_forward.2
  242.9 10.0 project.3
  254.1 6.8 cache_forward.3
  262.6 36.8 %attend.2 = bf16[8,800,128]{2,1,0:T(8,128)(2,1)} custom-call(s32[7]{0:T(128)S(1)} %copy-done.39, bf16[8,768,384]{2,1,0:T(8,128)(2,1)} %all-to-all-done.refs_0_), custom_call_target="tpu_custom_call" | custom-call | flops 12079595520 | bytes 2516582 | tf_op jit(solution)/shard_map/attend/pallas_call | solution.py:327
  299.5 6.1 all-to-all-start.1
  308.3 42.1 %collective-permute-done.9.refs_5_ = bf16[8,960,128]{2,1,0:T(8,128)(2,1)} collective-permute-done((bf16[8,960,128]{2,1,0:T(8,128)(2,1)S(1)}, bf16[8,960,128]{2,1,0:T(8,128)(2,1)}, u32[]{:S(2)}, u32[]{:S(2)}) %collective-permute-start.9) | collective-permute-done | bytes 1966112 | tf_op jit(solution)/shard_map/ppermute | solution.py:1323
  350.4 5.7 all-to-all-start.3
  371.5 64.5 %feed_forward.2 = (bf16[2,1,512,1024]{3,2,1,0:T(8,128)(2,1)}, bf16[2,1,256,1024]{3,2,1,0:T(8,128)(2,1)}, f32[768,1024]{1,0:T(8,128)}, bf16[768,1024]{1,0:T(8,128...) custom-call(s32[7]{0:T(128)} %get-tuple-element.264.meta, ...), custom_call_target="tpu_custom_call" | custom-call | flops 8938900480 | bytes 15387648 | tf_op jit(solution)/shard_map/feed_forward/pallas_call | solution.py:547
  441.5 16.4 %all-to-all-done.3.refs_0_ = bf16[8,768,384]{2,1,0:T(8,128)(2,1)} async-done(((bf16[8,768,384]{2,1,0:T(8,128)(2,1)}), bf16[8,768,384]{2,1,0:T(8,128)(2,1)}, u32[]{:S(2)}, u32[]{:S(2)}) %all-to-all-start.3) | async-done | bytes 4718624 | tf_op jit(solution)/shard_map/all_to_all | solution.py:1296
  461.6 37.6 %attend.3 = bf16[8,800,128]{2,1,0:T(8,128)(2,1)S(1)} custom-call(s32[7]{0:T(128)S(1)} %copy-done.46, bf16[8,768,384]{2,1,0:T(8,128)(2,1)} %all-to-all-done.3.refs_0_), custom_call_target="tpu_custom_call" | custom-call | flops 12079595520 | bytes 2516582 | tf_op jit(solution)/shard_map/attend/pallas_call | solution.py:327
  500.9 5.9 all-to-all-start.4
  506.7 63.4 %attend_back.2 = (bf16[8,768,128]{2,1,0:T(8,128)(2,1)}, bf16[8,768,256]{2,1,0:T(8,128)(2,1)S(1)}) custom-call(s32[7]{0:T(128)S(1)} %copy-done.40, bf16[8,768,384]{2,1,0:T(8,128)(2,1)} %all-to-all-done.refs_0_, bf16[8,816,128]{2,1,0:T(8,128)(2,1)S(1)} %all-to-all-done.2.refs_1_), custom_call_target="tpu_custom_call" | custom-call | flops 20132659200 | bytes 4404019 | tf_op jit(solution)/shard_map/attend_back/pallas_call | solution.py:484
  571.9 6.1 all-to-all-start.5
  585.4 64.5 %feed_forward.3 = (bf16[2,1,512,1024]{3,2,1,0:T(8,128)(2,1)}, bf16[2,1,256,1024]{3,2,1,0:T(8,128)(2,1)}, f32[768,1024]{1,0:T(8,128)}, bf16[768,1024]{1,0:T(8,128...) custom-call(s32[7]{0:T(128)} %pad_add_fusion.2.meta, ...), custom_call_target="tpu_custom_call", output_to_operand_aliasing={{0}: (16, {}), {1}: (17, {})} | custom-call | flops 8938900480 | bytes 16331366 | tf_op jit(solution)/shard_map/feed_forward/pallas_call | solution.py:547
  651.4 4.8 make_messages.3
  656.2 27.3 %weight_grads.3 = (bf16[1024,2560]{1,0:T(8,128)(2,1)}, bf16[1024,2560]{1,0:T(8,128)(2,1)}) custom-call(s32[7]{0:T(128)} %get-tuple-element.264.meta, bf16[768,1024]{1,0:T(8,128)(2,1)} %get-tuple-element.159.refs_0_, bf16[768,1024]{1,0:T(8,128)(2,1)} %get-tuple-element.160.refs_1_, bf16[768,1024]{1,0:T(8,128)(2,1)} %copy-done.9, ...), custom_call_target="tpu_custom_call" | custom-call | flops 4469450240 | bytes 15649996 | tf_op jit(solution)/shard_map/weight_grads/pallas_call | solution.py:547
  683.6 6.0 all-to-all-start.6
  689.8 27.3 %weight_grads.2 = (bf16[1024,2560]{1,0:T(8,128)(2,1)}, bf16[1024,2560]{1,0:T(8,128)(2,1)}) custom-call(s32[7]{0:T(128)} %get-tuple-element.264.meta, bf16[768,1024]{1,0:T(8,128)(2,1)} %get-tuple-element.159.refs_0_, bf16[768,1024]{1,0:T(8,128)(2,1)} %get-tuple-element.160.refs_1_, bf16[768,1024]{1,0:T(8,128)(2,1)} %copy-done.9, ...), custom_call_target="tpu_custom_call" | custom-call | flops 4469450240 | bytes 15649996 | tf_op jit(solution)/shard_map/weight_grads/pallas_call | solution.py:547
  717.1 12.2 %all-to-all-done.6.refs_1_ = bf16[8,816,128]{2,1,0:T(8,128)(2,1)S(1)} async-done(((bf16[8,816,128]{2,1,0:T(8,128)(2,1)}), bf16[8,816,128]{2,1,0:T(8,128)(2,1)S(1)}, u32[]{:S(2)}, u32[]{:S(2)}) %all-to-all-start.6) | async-done | bytes 1671200 | tf_op jit(solution)/shard_map/all_to_all | solution.py:1296
  729.3 4.5 all-to-all-start.7
  733.9 7.7 add_convert_fusion
  742.2 63.4 %attend_back.3 = (bf16[8,768,128]{2,1,0:T(8,128)(2,1)}, bf16[8,768,256]{2,1,0:T(8,128)(2,1)S(1)}) custom-call(s32[7]{0:T(128)S(1)} %copy-done.47, bf16[8,768,384]{2,1,0:T(8,128)(2,1)} %all-to-all-done.3.refs_0_, bf16[8,816,128]{2,1,0:T(8,128)(2,1)S(1)} %all-to-all-done.6.refs_1_), custom_call_target="tpu_custom_call" | custom-call | flops 20132659200 | bytes 4404019 | tf_op jit(solution)/shard_map/attend_back/pallas_call | solution.py:484
  807.3 6.6 all-to-all-start.8
  817.7 7.5 cache_backward.3.refs_3_
  826.9 7.5 cache_backward.2.refs_5_
  836.0 25.7 %finish.3 = (f32[2,1,512,1024]{3,2,1,0:T(8,128)}, f32[2,1,256,1024]{3,2,1,0:T(8,128)}, f32[8,1024]{1,0:T(8,128)S(1)}, f32[8,1024,256]{2,1,0:T(8,128)}, f32[8,1024,128]{2,1,0:T(8,128)}) custom-call(s32[7]{0:T(128)S(1)} %copy-done.41, bf16[768,1024]{1,0:T(8,128)(2,1)} %copy-done.32, bf16[8,768,256]{2,1,0:T(8,128)(2,1)} %all-to-all-done.5.refs_1_, ...), custom_call_target="tpu_custom_call" | custom-call | flops 2899102976 | bytes 14245478 | tf_op jit(solution)/shard_map/finish/pallas_call | solution.py:547
  861.8 11.5 %convert_add_fusion = f32[1024,2560]{1,0:T(8,128)} fusion(bf16[1024,2560]{1,0:T(8,128)(2,1)} %collective-permute-done.20, bf16[1024,2560]{1,0:T(8,128)(2,1)} %collective-permute-done.19, bf16[1024,2560]{1,0:T(8,128)(2,1)} %get-tuple-element.210), kind=kLoop, calls=%fused_computation | loop fusion | flops 13107200 | bytes 26214400 | tf_op jit(solution)/shard_map/add | solution.py:1339
  873.3 10.3 all-to-all-done.8.refs_1_
  887.4 4.3 fusion
  893.7 16.9 %finish.4 = (bf16[1024,512]{1,0:T(8,128)(2,1)S(1)}, bf16[1024,512]{1,0:T(8,128)(2,1)}, bf16[1024,512]{1,0:T(8,128)(2,1)}, bf16[1024,512]{1,0:T(8,128)(2,1)}, f32[768,1024]{1,0:T(8,128)}) custom-call(s32[7]{0:T(128)S(1)} %copy-done.47, bf16[768,1024]{1,0:T(8,128)(2,1)} %copy-done.19, bf16[8,768,256]{2,1,0:T(8,128)(2,1)} %all-to-all-done.8.refs_1_, ...), custom_call_target="tpu_custom_call" | custom-call | flops 966367616 | bytes 8060928 | tf_op jit(solution)/shard_map/finish/pallas_call | solution.py:547
  918.5 6.2 all-to-all-done.9.refs_1_
  925.8 20.0 %finish.5 = (f32[2,1,512,1024]{3,2,1,0:T(8,128)}, f32[2,1,256,1024]{3,2,1,0:T(8,128)}, f32[8,1024]{1,0:T(8,128)S(1)}, bf16[1024,256]{1,0:T(8,128)(2,1)S(1)}, bf1...) custom-call(s32[7]{0:T(128)S(1)} %copy-done.47, ...), custom_call_target="tpu_custom_call", output_to_operand_aliasing={{0}: (11, {}), {1}: (12, {})} | custom-call | flops 966367616 | bytes 12318720 | tf_op jit(solution)/shard_map/finish/pallas_call | solution.py:547
  945.8 17.2 %collective-permute-done.21 = bf16[4,128,2560]{2,1,0:T(8,128)(2,1)} collective-permute-done((bf16[4,128,2560]{2,1,0:T(8,128)(2,1)}, bf16[4,128,2560]{2,1,0:T(8,128)(2,1)}, u32[]{:S(2)}, u32[]{:S(2)}) %collective-permute-start.21) | collective-permute-done | bytes 2621472 | tf_op jit(solution)/shard_map/ppermute | solution.py:1328
  963.1 4.1 bitcast_add_fusion
  976.2 4.3 all-to-all-start.12
  984.6 25.7 %collective-permute-done.22 = bf16[2,128,2560]{2,1,0:T(8,128)(2,1)} collective-permute-done((bf16[2,128,2560]{2,1,0:T(8,128)(2,1)S(1)}, bf16[2,128,2560]{2,1,0:T(8,128)(2,1)}, u32[]{:S(2)}, u32[]{:S(2)}) %collective-permute-start.22) | collective-permute-done | bytes 1310752 | tf_op jit(solution)/shard_map/ppermute | solution.py:1328
  1018.5 3.9 all-to-all-start.10
  1027.1 25.8 %collective-permute-done.23 = bf16[1,128,2560]{2,1,0:T(8,128)(2,1)} collective-permute-done((bf16[1,128,2560]{2,1,0:T(8,128)(2,1)}, bf16[1,128,2560]{2,1,0:T(8,128)(2,1)}, u32[]{:S(2)}, u32[]{:S(2)}) %collective-permute-start.23) | collective-permute-done | bytes 655392 | tf_op jit(solution)/shard_map/ppermute | solution.py:1328
  (259 shorter events, 154.3 us)
Async XLA Ops:
  7.2 114.2 %all-gather.2.cloned.1.call-start = ((), (), s32[]{:S(2)}) async-start(), calls=%async_computation.13 | async-start | bytes 6623232 | tf_op jit(solution)/shard_map/all_gather | solution.py:1427
  22.3 26.5 %collective-permute-start = (bf16[1,1408,128]{2,1,0:T(8,128)(2,1)S(1)}, bf16[1,1408,128]{2,1,0:T(8,128)(2,1)S(1)}, u32[]{:S(2)}, u32[]{:S(2)}) collective-permute-start(bf16[1,1408,128]{2,1,0:T(8,128)(2,1)S(1)} %maximum_bitcast_fusion), channel_id=1, source_target_pairs={{0,4},{1,5},{2,6},{3,7},{4,0},{5,1},{6,2},{7,3},{8,12},{9,13},{10,... | collective-permute-start | bytes 1081352 | tf_op jit(solution)/shard_map/ppermute | solution.py:1328
  28.3 32.7 %collective-permute-start.2 = (bf16[1,960,128]{2,1,0:T(8,128)(2,1)S(1)}, bf16[1,960,128]{2,1,0:T(8,128)(2,1)S(1)}, u32[]{:S(2)}, u32[]{:S(2)}) collective-permute-start(bf16[1,960,128]{2,1,0:T(8,128)(2,1)S(1)} %maximum_bitcast_fusion.1), channel_id=1, source_target_pairs={{0,4},{1,5},{2,6},{3,7},{4,0},{5,1},{6,2},{7,3},{8,12},{9,13},{10,... | collective-permute-start | bytes 737288 | tf_op jit(solution)/shard_map/ppermute | solution.py:1328
  49.7 62.2 %collective-permute-start.1 = (bf16[2,1408,128]{2,1,0:T(8,128)(2,1)}, bf16[2,1408,128]{2,1,0:T(8,128)(2,1)}, u32[]{:S(2)}, u32[]{:S(2)}) collective-permute-start(bf16[2,1408,128]{2,1,0:T(8,128)(2,1)} %pad_maximum_fusion.2), channel_id=1, source_target_pairs={{0,2},{1,3},{2,0},{3,1},{4,6},{5,7},{6,4},{7,5},{8,10},{9,11},{10,... | collective-permute-start | bytes 2162696 | tf_op jit(solution)/shard_map/ppermute | solution.py:1328
  61.8 47.9 %collective-permute-start.3 = (bf16[2,960,128]{2,1,0:T(8,128)(2,1)}, bf16[2,960,128]{2,1,0:T(8,128)(2,1)}, u32[]{:S(2)}, u32[]{:S(2)}) collective-permute-start(bf16[2,960,128]{2,1,0:T(8,128)(2,1)} %pad_maximum_fusion.3), channel_id=1, source_target_pairs={{0,2},{1,3},{2,0},{3,1},{4,6},{5,7},{6,4},{7,5},{8,10},{9,11},{10,... | collective-permute-start | bytes 1474568 | tf_op jit(solution)/shard_map/ppermute | solution.py:1328
  139.4 103.5 %slice-start = ((s8[6422528]{0:T(1024)(128)(4,1)}), s8[2228224]{0:T(1024)(128)(4,1)S(1)}, s32[]{:S(2)}) async-start(s8[6422528]{0:T(1024)(128)(4,1)} %bitcast.64), calls=%async_computation.14 | async-start | bytes 4456448
  139.4 123.2 %all-to-all-start = ((bf16[8,768,384]{2,1,0:T(8,128)(2,1)}), bf16[8,768,384]{2,1,0:T(8,128)(2,1)}, u32[]{:S(2)}, u32[]{:S(2)}) async-start(bf16[8,768,384]{2,1,0:T(8,128)(2,1)} %copy-done.1), calls=%async_computation | async-start | bytes 9437184 | tf_op jit(solution)/shard_map/all_to_all | solution.py:1296
  145.1 86.9 %copy-start.15 = (bf16[1,256,1024]{2,1,0:T(8,128)(2,1)S(1)}, bf16[1,256,1024]{2,1,0:T(8,128)(2,1)}, u32[]{:S(2)}) copy-start(bf16[1,256,1024]{2,1,0:T(8,128)(2,1)} %param.29) | copy-start | bytes 1572868
  145.1 86.9 %copy-start.17 = (bf16[1,256,1024]{2,1,0:T(8,128)(2,1)S(1)}, bf16[1,256,1024]{2,1,0:T(8,128)(2,1)}, u32[]{:S(2)}) copy-start(bf16[1,256,1024]{2,1,0:T(8,128)(2,1)} %param.30) | copy-start | bytes 1572868
  145.1 86.9 %copy-start.33 = (s32[8,8,512]{2,1,0:T(8,128)S(1)}, s32[8,8,512]{2,1,0:T(8,128)}, u32[]{:S(2)}) copy-start(s32[8,8,512]{2,1,0:T(8,128)} %get-tuple-element.176.words_prompt) | copy-start | bytes 393220
  145.1 86.9 %copy-start.36 = (s32[8,8,256]{2,1,0:T(8,128)S(1)}, s32[8,8,256]{2,1,0:T(8,128)}, u32[]{:S(2)}) copy-start(s32[8,8,256]{2,1,0:T(8,128)} %get-tuple-element.177.words_reply) | copy-start | bytes 196612
  145.1 97.7 %slice-start.1 = ((s8[6422528]{0:T(1024)(128)(4,1)}), s8[4194304]{0:T(1024)(128)(4,1)S(1)}, s32[]{:S(2)}) async-start(s8[6422528]{0:T(1024)(128)(4,1)} %bitcast.64), calls=%async_computation.15 | async-start | bytes 8388608
  145.1 84.2 %collective-permute-start.5 = (bf16[4,1408,128]{2,1,0:T(8,128)(2,1)}, bf16[4,1408,128]{2,1,0:T(8,128)(2,1)S(1)}, u32[]{:S(2)}, u32[]{:S(2)}) collective-permute-start(bf16[4,1408,128]{2,1,0:T(8,128)(2,1)} %pad_maximum_fusion), channel_id=1, source_target_pairs={{0,1},{1,0},{2,3},{3,2},{4,5},{5,4},{6,7},{7,6},{8,9},{9,8},{10,11... | collective-permute-start | bytes 4325384 | tf_op jit(solution)/shard_map/ppermute | solution.py:1328
  230.5 69.0 %collective-permute-start.6 = (bf16[8,1408,128]{2,1,0:T(8,128)(2,1)}, bf16[8,1408,128]{2,1,0:T(8,128)(2,1)}, u32[]{:S(2)}, u32[]{:S(2)}) collective-permute-start(bf16[8,1408,128]{2,1,0:T(8,128)(2,1)} %constant_dynamic-update-slice_fusion.refs_0_), channel_id=1, source_target_pairs={{0,16},{8,24},{16,0},{24,8},{1,17},{9,25},{17,1},{25,9},{2,18},{10... | collective-permute-start | bytes 8650760 | tf_op jit(solution)/shard_map/ppermute | solution.py:1323
  232.0 30.6 %collective-permute-start.4 = (bf16[4,960,128]{2,1,0:T(8,128)(2,1)}, bf16[4,960,128]{2,1,0:T(8,128)(2,1)}, u32[]{:S(2)}, u32[]{:S(2)}) collective-permute-start(bf16[4,960,128]{2,1,0:T(8,128)(2,1)} %pad_maximum_fusion.1), channel_id=1, source_target_pairs={{0,1},{1,0},{2,3},{3,2},{4,5},{5,4},{6,7},{7,6},{8,9},{9,8},{10,11... | collective-permute-start | bytes 2949128 | tf_op jit(solution)/shard_map/ppermute | solution.py:1328
  299.5 50.9 %all-to-all-start.1 = ((bf16[8,800,128]{2,1,0:T(8,128)(2,1)}), bf16[8,800,128]{2,1,0:T(8,128)(2,1)S(1)}, u32[]{:S(2)}, u32[]{:S(2)}) async-start(bf16[8,800,128]{2,1,0:T(8,128)(2,1)} %attend.2), calls=%async_computation.1 | async-start | bytes 3276800 | tf_op jit(solution)/shard_map/all_to_all | solution.py:1296
  307.1 43.3 %collective-permute-start.9 = (bf16[8,960,128]{2,1,0:T(8,128)(2,1)S(1)}, bf16[8,960,128]{2,1,0:T(8,128)(2,1)}, u32[]{:S(2)}, u32[]{:S(2)}) collective-permute-start(bf16[8,960,128]{2,1,0:T(8,128)(2,1)S(1)} %constant_dynamic-update-slice_fusion.2.refs_1_), channel_id=1, source_target_pairs={{0,16},{8,24},{16,0},{24,8},{1,17},{9,25},{17,1},{25,9},{2,18},{10... | collective-permute-start | bytes 5898248 | tf_op jit(solution)/shard_map/ppermute | solution.py:1323
  350.4 107.6 %all-to-all-start.3 = ((bf16[8,768,384]{2,1,0:T(8,128)(2,1)}), bf16[8,768,384]{2,1,0:T(8,128)(2,1)}, u32[]{:S(2)}, u32[]{:S(2)}) async-start(bf16[8,768,384]{2,1,0:T(8,128)(2,1)} %copy-done.3), calls=%async_computation.3 | async-start | bytes 9437184 | tf_op jit(solution)/shard_map/all_to_all | solution.py:1296
  356.1 12.6 %collective-permute-start.7 = (bf16[8,1408,128]{2,1,0:T(8,128)(2,1)}, bf16[8,1408,128]{2,1,0:T(8,128)(2,1)}, u32[]{:S(2)}, u32[]{:S(2)}) collective-permute-start(bf16[8,1408,128]{2,1,0:T(8,128)(2,1)} %constant_dynamic-update-slice_fusion.refs_0_), channel_id=1, source_target_pairs={{0,8},{8,0},{16,24},{24,16},{1,9},{9,1},{17,25},{25,17},{2,10},{10... | collective-permute-start | bytes 8650760 | tf_op jit(solution)/shard_map/ppermute | solution.py:1323
  356.1 15.4 %collective-permute-start.10 = (bf16[8,1408,128]{2,1,0:T(8,128)(2,1)}, bf16[8,1408,128]{2,1,0:T(8,128)(2,1)}, u32[]{:S(2)}, u32[]{:S(2)}) collective-permute-start(bf16[8,1408,128]{2,1,0:T(8,128)(2,1)} %collective-permute-done.6.refs_4_), channel_id=1, source_target_pairs={{0,8},{8,0},{16,24},{24,16},{1,9},{9,1},{17,25},{25,17},{2,10},{10... | collective-permute-start | bytes 8650760 | tf_op jit(solution)/shard_map/ppermute | solution.py:1323
  356.6 12.1 %collective-permute-start.8 = (bf16[8,960,128]{2,1,0:T(8,128)(2,1)}, bf16[8,960,128]{2,1,0:T(8,128)(2,1)}, u32[]{:S(2)}, u32[]{:S(2)}) collective-permute-start(bf16[8,960,128]{2,1,0:T(8,128)(2,1)} %copy-done.57), channel_id=1, source_target_pairs={{0,8},{8,0},{16,24},{24,16},{1,9},{9,1},{17,25},{25,17},{2,10},{10... | collective-permute-start | bytes 5898248 | tf_op jit(solution)/shard_map/ppermute | solution.py:1323
  356.7 14.8 %collective-permute-start.11 = (bf16[8,960,128]{2,1,0:T(8,128)(2,1)}, bf16[8,960,128]{2,1,0:T(8,128)(2,1)}, u32[]{:S(2)}, u32[]{:S(2)}) collective-permute-start(bf16[8,960,128]{2,1,0:T(8,128)(2,1)} %collective-permute-done.9.refs_5_), channel_id=1, source_target_pairs={{0,8},{8,0},{16,24},{24,16},{1,9},{9,1},{17,25},{25,17},{2,10},{10... | collective-permute-start | bytes 5898248 | tf_op jit(solution)/shard_map/ppermute | solution.py:1323
  371.5 64.5 %copy-start.10 = (bf16[768,1024]{1,0:T(8,128)(2,1)S(1)}, bf16[768,1024]{1,0:T(8,128)(2,1)}, u32[]{:S(2)}) copy-start(bf16[768,1024]{1,0:T(8,128)(2,1)} %copy-done.9) | copy-start | bytes 4718596
  371.5 64.5 %copy-start.40 = (s32[7]{0:T(128)S(1)}, s32[7]{0:T(128)}, u32[]{:S(2)}) copy-start(s32[7]{0:T(128)} %get-tuple-element.264.meta) | copy-start | bytes 88
  457.9 42.9 %all-to-all-start.2 = ((bf16[8,816,128]{2,1,0:T(8,128)(2,1)}), bf16[8,816,128]{2,1,0:T(8,128)(2,1)S(1)}, u32[]{:S(2)}, u32[]{:S(2)}) async-start(bf16[8,816,128]{2,1,0:T(8,128)(2,1)} %copy-done.30), calls=%async_computation.2 | async-start | bytes 3342336 | tf_op jit(solution)/shard_map/all_to_all | solution.py:1296
  500.9 71.1 %all-to-all-start.4 = ((bf16[8,800,128]{2,1,0:T(8,128)(2,1)}), bf16[8,800,128]{2,1,0:T(8,128)(2,1)S(1)}, u32[]{:S(2)}, u32[]{:S(2)}) async-start(bf16[8,800,128]{2,1,0:T(8,128)(2,1)} %copy-done.31), calls=%async_computation.4 | async-start | bytes 3276800 | tf_op jit(solution)/shard_map/all_to_all | solution.py:1296
  571.9 84.3 %all-to-all-start.5 = ((bf16[8,768,256]{2,1,0:T(8,128)(2,1)}), bf16[8,768,256]{2,1,0:T(8,128)(2,1)}, u32[]{:S(2)}, u32[]{:S(2)}) async-start(bf16[8,768,256]{2,1,0:T(8,128)(2,1)} %copy-done.29), calls=%async_computation.5 | async-start | bytes 6291456 | tf_op jit(solution)/shard_map/all_to_all | solution.py:1296
  585.4 64.6 %copy-start.12 = (bf16[768,1024]{1,0:T(8,128)(2,1)S(1)}, bf16[768,1024]{1,0:T(8,128)(2,1)}, u32[]{:S(2)}) copy-start(bf16[768,1024]{1,0:T(8,128)(2,1)} %copy-done.11) | copy-start | bytes 4718596
  585.4 64.6 %copy-start.47 = (s32[7]{0:T(128)S(1)}, s32[7]{0:T(128)}, u32[]{:S(2)}) copy-start(s32[7]{0:T(128)} %pad_add_fusion.2.meta) | copy-start | bytes 88
  683.5 50.3 %collective-permute-start.12 = (bf16[1024,2560]{1,0:T(8,128)(2,1)}, bf16[1024,2560]{1,0:T(8,128)(2,1)}, u32[]{:S(2)}, u32[]{:S(2)}) collective-permute-start(bf16[1024,2560]{1,0:T(8,128)(2,1)} %get-tuple-element.173), channel_id=1, source_target_pairs={{0,8},{8,0},{16,24},{24,16},{1,9},{9,1},{17,25},{25,17},{2,10},{10... | collective-permute-start | bytes 15728648 | tf_op jit(solution)/shard_map/ppermute | solution.py:1323
  683.6 45.7 %all-to-all-start.6 = ((bf16[8,816,128]{2,1,0:T(8,128)(2,1)}), bf16[8,816,128]{2,1,0:T(8,128)(2,1)S(1)}, u32[]{:S(2)}, u32[]{:S(2)}) async-start(bf16[8,816,128]{2,1,0:T(8,128)(2,1)} %get-tuple-element.156), calls=%async_computation.6 | async-start | bytes 3342336 | tf_op jit(solution)/shard_map/all_to_all | solution.py:1296
  689.6 172.2 %collective-permute-start.19 = (bf16[1024,2560]{1,0:T(8,128)(2,1)}, bf16[1024,2560]{1,0:T(8,128)(2,1)}, u32[]{:S(2)}, u32[]{:S(2)}) collective-permute-start(bf16[1024,2560]{1,0:T(8,128)(2,1)} %get-tuple-element.211), channel_id=1, source_target_pairs={{0,8},{8,0},{16,24},{24,16},{1,9},{9,1},{17,25},{25,17},{2,10},{10... | collective-permute-start | bytes 15728648 | tf_op jit(solution)/shard_map/ppermute | solution.py:1323
  729.3 77.9 %all-to-all-start.7 = ((bf16[8,768,128]{2,1,0:T(8,128)(2,1)}), bf16[8,768,128]{2,1,0:T(8,128)(2,1)}, u32[]{:S(2)}, u32[]{:S(2)}) async-start(bf16[8,768,128]{2,1,0:T(8,128)(2,1)} %get-tuple-element.157), calls=%async_computation.7 | async-start | bytes 3145728 | tf_op jit(solution)/shard_map/all_to_all | solution.py:1296
  741.6 120.1 %collective-permute-start.20 = (bf16[1024,2560]{1,0:T(8,128)(2,1)}, bf16[1024,2560]{1,0:T(8,128)(2,1)}, u32[]{:S(2)}, u32[]{:S(2)}) collective-permute-start(bf16[1024,2560]{1,0:T(8,128)(2,1)} %add_convert_fusion), channel_id=1, source_target_pairs={{0,16},{8,24},{16,0},{24,8},{1,17},{9,25},{17,1},{25,9},{2,18},{10... | collective-permute-start | bytes 15728648 | tf_op jit(solution)/shard_map/ppermute | solution.py:1323
  807.3 76.3 %all-to-all-start.8 = ((bf16[8,768,256]{2,1,0:T(8,128)(2,1)}), bf16[8,768,256]{2,1,0:T(8,128)(2,1)}, u32[]{:S(2)}, u32[]{:S(2)}) async-start(bf16[8,768,256]{2,1,0:T(8,128)(2,1)} %copy-done.28), calls=%async_computation.8 | async-start | bytes 6291456 | tf_op jit(solution)/shard_map/all_to_all | solution.py:1296
  883.6 41.0 %all-to-all-start.9 = ((bf16[8,768,128]{2,1,0:T(8,128)(2,1)}), bf16[8,768,128]{2,1,0:T(8,128)(2,1)S(1)}, u32[]{:S(2)}, u32[]{:S(2)}) async-start(bf16[8,768,128]{2,1,0:T(8,128)(2,1)} %get-tuple-element.189), calls=%async_computation.9 | async-start | bytes 3145728 | tf_op jit(solution)/shard_map/all_to_all | solution.py:1296
  891.7 71.4 %collective-permute-start.21 = (bf16[4,128,2560]{2,1,0:T(8,128)(2,1)}, bf16[4,128,2560]{2,1,0:T(8,128)(2,1)}, u32[]{:S(2)}, u32[]{:S(2)}) collective-permute-start(bf16[4,128,2560]{2,1,0:T(8,128)(2,1)} %fusion), channel_id=1, source_target_pairs={{0,1},{1,0},{2,3},{3,2},{4,5},{5,4},{6,7},{7,6},{8,9},{9,8},{10,11... | collective-permute-start | bytes 7864328 | tf_op jit(solution)/shard_map/ppermute | solution.py:1328
  910.7 3.5 collective-permute-start.17
  910.7 62.1 %collective-permute-start.16 = (bf16[1024,512]{1,0:T(8,128)(2,1)}, bf16[1024,512]{1,0:T(8,128)(2,1)}, u32[]{:S(2)}, u32[]{:S(2)}) collective-permute-start(bf16[1024,512]{1,0:T(8,128)(2,1)} %get-tuple-element.206), channel_id=1, source_target_pairs={{0,8},{8,0},{16,24},{24,16},{1,9},{9,1},{17,25},{25,17},{2,10},{10... | collective-permute-start | bytes 3145736 | tf_op jit(solution)/shard_map/ppermute | solution.py:1323
  917.0 54.2 %collective-permute-start.18 = (bf16[1024,512]{1,0:T(8,128)(2,1)}, bf16[1024,512]{1,0:T(8,128)(2,1)}, u32[]{:S(2)}, u32[]{:S(2)}) collective-permute-start(bf16[1024,512]{1,0:T(8,128)(2,1)} %add_convert_fusion.2), channel_id=1, source_target_pairs={{0,16},{8,24},{16,0},{24,8},{1,17},{9,25},{17,1},{25,9},{2,18},{10... | collective-permute-start | bytes 3145736 | tf_op jit(solution)/shard_map/ppermute | solution.py:1323
  945.8 25.4 %collective-permute-start.14 = (bf16[1024,256]{1,0:T(8,128)(2,1)S(1)}, bf16[1024,256]{1,0:T(8,128)(2,1)S(1)}, u32[]{:S(2)}, u32[]{:S(2)}) collective-permute-start(bf16[1024,256]{1,0:T(8,128)(2,1)S(1)} %get-tuple-element.199), channel_id=1, source_target_pairs={{0,8},{8,0},{16,24},{24,16},{1,9},{9,1},{17,25},{25,17},{2,10},{10... | collective-permute-start | bytes 1572872 | tf_op jit(solution)/shard_map/ppermute | solution.py:1323
  969.7 40.6 %collective-permute-start.22 = (bf16[2,128,2560]{2,1,0:T(8,128)(2,1)S(1)}, bf16[2,128,2560]{2,1,0:T(8,128)(2,1)}, u32[]{:S(2)}, u32[]{:S(2)}) collective-permute-start(bf16[2,128,2560]{2,1,0:T(8,128)(2,1)S(1)} %fusion.1), channel_id=1, source_target_pairs={{0,2},{1,3},{2,0},{3,1},{4,6},{5,7},{6,4},{7,5},{8,10},{9,11},{10,... | collective-permute-start | bytes 3932168 | tf_op jit(solution)/shard_map/ppermute | solution.py:1328
  971.4 12.5 %collective-permute-start.15 = (bf16[1024,256]{1,0:T(8,128)(2,1)S(1)}, bf16[1024,256]{1,0:T(8,128)(2,1)S(1)}, u32[]{:S(2)}, u32[]{:S(2)}) collective-permute-start(bf16[1024,256]{1,0:T(8,128)(2,1)S(1)} %add_convert_fusion.4), channel_id=1, source_target_pairs={{0,16},{8,24},{16,0},{24,8},{1,17},{9,25},{17,1},{25,9},{2,18},{10... | collective-permute-start | bytes 1572872 | tf_op jit(solution)/shard_map/ppermute | solution.py:1323
  976.2 42.4 %all-to-all-start.12 = ((bf16[8,128,512]{2,1,0:T(8,128)(2,1)}), bf16[8,128,512]{2,1,0:T(8,128)(2,1)}, u32[]{:S(2)}, u32[]{:S(2)}) async-start(bf16[8,128,512]{2,1,0:T(8,128)(2,1)} %bitcast.33), calls=%async_computation.12 | async-start | bytes 2097152 | tf_op jit(solution)/shard_map/all_to_all | solution.py:1562
  982.8 34.7 %collective-permute-start.13 = (bf16[1024,256]{1,0:T(8,128)(2,1)S(1)}, bf16[1024,256]{1,0:T(8,128)(2,1)S(1)}, u32[]{:S(2)}, u32[]{:S(2)}) collective-permute-start(bf16[1024,256]{1,0:T(8,128)(2,1)S(1)} %get-tuple-element.197), channel_id=1, source_target_pairs={{0,8},{8,0},{16,24},{24,16},{1,9},{9,1},{17,25},{25,17},{2,10},{10... | collective-permute-start | bytes 1572872 | tf_op jit(solution)/shard_map/ppermute | solution.py:1323
  1013.7 39.2 %collective-permute-start.23 = (bf16[1,128,2560]{2,1,0:T(8,128)(2,1)}, bf16[1,128,2560]{2,1,0:T(8,128)(2,1)}, u32[]{:S(2)}, u32[]{:S(2)}) collective-permute-start(bf16[1,128,2560]{2,1,0:T(8,128)(2,1)} %dynamic-slice_convert_fusion.1), channel_id=1, source_target_pairs={{0,4},{1,5},{2,6},{3,7},{4,0},{5,1},{6,2},{7,3},{8,12},{9,13},{10,... | collective-permute-start | bytes 1966088 | tf_op jit(solution)/shard_map/ppermute | solution.py:1328
  1018.5 39.9 %all-to-all-start.10 = ((bf16[8,128,256]{2,1,0:T(8,128)(2,1)}), bf16[8,128,256]{2,1,0:T(8,128)(2,1)S(1)}, u32[]{:S(2)}, u32[]{:S(2)}) async-start(bf16[8,128,256]{2,1,0:T(8,128)(2,1)} %bitcast.80), calls=%async_computation.10 | async-start | bytes 1048576 | tf_op jit(solution)/shard_map/all_to_all | solution.py:1562
  1059.1 9.6 all-to-all-start.11
  (58 other events, 767.7 us)
Sparse Core Ops, SparseCore 0:
  21.3 100.0 all-gather.1

commit v5 on v4

--- a/solution.py
+++ b/solution.py
@@ -1445,14 +1445,6 @@
                 gain_one, *shares = lax.optimization_barrier((gain_one, *shares))
             nearest = [along_seq(share, away) for share in shares]
             shares = [jnp.concatenate(pair) for pair in zip(shares, nearest)]
-    far = [along_grp(share, 2) for share in shares]
-    feed_w = (
-        shares
-        + [along_grp(share, 1) for share in shares]
-        + far
-        + [along_grp(share, 1) for share in far],
-        inner,
-    )
     cache_key_rows, cache_value_rows = cache_keys[0], cache_values[0]
     words = [picks_to_words(sz, metas[m], m, prompt_picks, reply_picks) for m in micros]
     gain_one, words = lax.optimization_barrier((gain_one, words))
@@ -1467,6 +1459,17 @@
         cache_forward(sz, metas[m], own[m], words[m], cache_key_rows, cache_value_rows)
         for m in micros
     ]
+    shares[0] = after(shares[0], cached)
+    nearest[1] = after(nearest[1], shares[0])
+    shares[1] = after(shares[1], shares[0])
+    far = [along_grp(share, 2) for share in shares]
+    feed_w = (
+        shares
+        + [along_grp(share, 1) for share in shares]
+        + far
+        + [along_grp(share, 1) for share in far],
+        inner,
+    )
     error_parts, gain_two_parts, gain_one_parts = [], [], []
     outs, grads, parts, arrived, extras = [], [], [], [], []
     received, middle_grads, mixed_grads, all_sums, deltas = [], [], [], [], []
@@ -1482,7 +1485,7 @@
     for m in micros:
         chunks = exchange(sz, own[m] if answers is None else after(own[m], answers, far[1]))
         if m == 0:
-            chunks, cached, _ = lax.optimization_barrier((chunks, cached, nearest[1]))
+            chunks, cached = lax.optimization_barrier((chunks, cached))
         if messages is not None:
             chunks = after(chunks, messages)
         received.append(chunks)

time: 1090 us -> 1090 us (level)
    ppermute x9, waiting for transfers between devices: 206 us -> 176 us  [along_seq(): return lax.ppermute(array, 'seq', [(i, i ^ away) for i in range(count)])]
    all_to_all x10, waiting for transfers between devices: 45.5 us -> 63.5 us  [exchange(): return lax.all_to_all(array, 'seq', 0, 0, axis_index_groups=subgroups(sz))]
    unnamed x145 -> x137, local copies, waits for them, and re-layouts: 48.7 us -> 53.6 us
  transfers between devices with their start and end apart: 38 -> 38, of which waited for: 20 -> 22; matrix products, arithmetic and copies ran while one was open for 7% -> 7% of each run, Pallas kernels for 45% -> 45%
where the time goes in v5:
time: 1090 us; the launch traced here: 1080 us
  Pallas kernels  527 us (48%)
  waiting for transfers between devices  308 us (28%)
  starting transfers between devices  88.9 us (8%)
  local copies, waits for them, and re-layouts  74.4 us (7%)
  other arithmetic  60.5 us (6%)
  between operations  20.8 us (2%)
    pallas_call x17, Pallas kernels, call(): pl.pallas_call(kernel, out_shape=list(out_shape), grid_spec=pltpu.Prefetc...  308 us
    ppermute x9, waiting for transfers between devices, along_seq(): return lax.ppermute(array, 'seq', [(i, i ^ away) for i in range(count)])  176 us
    pallas_call x2, Pallas kernels, attend_back(): pl.pallas_call(functools.partial(attend_back_kernel, sz), out_shape=out_s...  128 us
    pallas_call x2, Pallas kernels, attend(): pl.pallas_call(functools.partial(attend_kernel, sz), out_shape=jax.ShapeD...  75.5 us
    all_to_all x10, waiting for transfers between devices, exchange(): return lax.all_to_all(array, 'seq', 0, 0, axis_index_groups=subgroups(sz))  63.5 us
    ppermute x15, waiting for transfers between devices, along_grp(): return lax.ppermute(array, 'grp', [(i, i ^ away) for i in range(count)])  55.8 us
    unnamed x137, local copies, waits for them, and re-layouts  53.6 us
    all_to_all x10, starting transfers between devices, exchange(): return lax.all_to_all(array, 'seq', 0, 0, axis_index_groups=subgroups(sz))  52.5 us
  transfers between devices with their start and end apart: 38, of which 22 were waited for; matrix products, arithmetic and copies ran while one was open for 7% of the time, Pallas kernels for 45%

profile of v5, /device:TPU:0, one launch (start us, length us, event | category | flops | bytes accessed | tf_op | source)
XLA Modules:
  0.0 1078.9 jit_solution(11389117831666194443)
XLA Ops:
  22.3 4.1 collective-permute-start
  28.3 20.4 %collective-permute-done = bf16[1,1408,128]{2,1,0:T(8,128)(2,1)S(1)} collective-permute-done((bf16[1,1408,128]{2,1,0:T(8,128)(2,1)S(1)}, bf16[1,1408,128]{2,1,0:T(8,128)(2,1)S(1)}, u32[]{:S(2)}, u32[]{:S(2)}) %collective-permute-start) | collective-permute-done | bytes 360480 | tf_op jit(solution)/shard_map/ppermute | solution.py:1328
  52.8 8.2 collective-permute-done.2
  64.4 7.8 picks_to_words.3
  72.2 7.8 picks_to_words.2
  80.0 29.8 %collective-permute-done.3 = bf16[2,960,128]{2,1,0:T(8,128)(2,1)} collective-permute-done((bf16[2,960,128]{2,1,0:T(8,128)(2,1)}, bf16[2,960,128]{2,1,0:T(8,128)(2,1)}, u32[]{:S(2)}, u32[]{:S(2)}) %collective-permute-start.3) | collective-permute-done | bytes 491552 | tf_op jit(solution)/shard_map/ppermute | solution.py:1328
  114.2 7.1 all-gather.2.cloned.1.call-done.query_w.pair_w.refs_2_.refs_4_
  127.0 10.0 project.2
  140.6 5.7 all-to-all-start
  150.6 6.9 cache_forward.2
  162.6 10.0 project.3
  173.7 6.9 cache_forward.3
  180.6 49.9 %collective-permute-done.4 = bf16[4,1408,128]{2,1,0:T(8,128)(2,1)S(1)} collective-permute-done((bf16[4,1408,128]{2,1,0:T(8,128)(2,1)}, bf16[4,1408,128]{2,1,0:T(8,128)(2,1)S(1)}, u32[]{:S(2)}, u32[]{:S(2)}) %collective-permute-start.4) | collective-permute-done | bytes 1441824 | tf_op jit(solution)/shard_map/ppermute | solution.py:1328
  233.8 17.4 %all-to-all-done.refs_0_ = bf16[8,768,384]{2,1,0:T(8,128)(2,1)} async-done(((bf16[8,768,384]{2,1,0:T(8,128)(2,1)}), bf16[8,768,384]{2,1,0:T(8,128)(2,1)}, u32[]{:S(2)}, u32[]{:S(2)}) %all-to-all-start) | async-done | bytes 4718624 | tf_op jit(solution)/shard_map/all_to_all | solution.py:1296
  251.2 37.9 %attend.2 = bf16[8,800,128]{2,1,0:T(8,128)(2,1)S(1)} custom-call(s32[7]{0:T(128)S(1)} %copy-done.42, bf16[8,768,384]{2,1,0:T(8,128)(2,1)} %all-to-all-done.refs_0_), custom_call_target="tpu_custom_call" | custom-call | flops 12079595520 | bytes 2516582 | tf_op jit(solution)/shard_map/attend/pallas_call | solution.py:327
  290.3 5.9 collective-permute-done.5.refs_4_
  296.2 4.6 all-to-all-start.1
  304.1 41.4 %collective-permute-done.9.refs_5_ = bf16[8,960,128]{2,1,0:T(8,128)(2,1)} collective-permute-done((bf16[8,960,128]{2,1,0:T(8,128)(2,1)S(1)}, bf16[8,960,128]{2,1,0:T(8,128)(2,1)}, u32[]{:S(2)}, u32[]{:S(2)}) %collective-permute-start.9) | collective-permute-done | bytes 1966112 | tf_op jit(solution)/shard_map/ppermute | solution.py:1323
  345.5 5.7 all-to-all-start.3
  366.6 64.5 %feed_forward.2 = (bf16[2,1,512,1024]{3,2,1,0:T(8,128)(2,1)}, bf16[2,1,256,1024]{3,2,1,0:T(8,128)(2,1)}, f32[768,1024]{1,0:T(8,128)}, bf16[768,1024]{1,0:T(8,128...) custom-call(s32[7]{0:T(128)} %get-tuple-element.268.meta, ...), custom_call_target="tpu_custom_call" | custom-call | flops 8938900480 | bytes 15387648 | tf_op jit(solution)/shard_map/feed_forward/pallas_call | solution.py:547
  436.7 16.0 %all-to-all-done.3.refs_0_ = bf16[8,768,384]{2,1,0:T(8,128)(2,1)} async-done(((bf16[8,768,384]{2,1,0:T(8,128)(2,1)}), bf16[8,768,384]{2,1,0:T(8,128)(2,1)}, u32[]{:S(2)}, u32[]{:S(2)}) %all-to-all-start.3) | async-done | bytes 4718624 | tf_op jit(solution)/shard_map/all_to_all | solution.py:1296
  456.4 37.6 %attend.3 = bf16[8,800,128]{2,1,0:T(8,128)(2,1)S(1)} custom-call(s32[7]{0:T(128)S(1)} %copy-done.47, bf16[8,768,384]{2,1,0:T(8,128)(2,1)} %all-to-all-done.3.refs_0_), custom_call_target="tpu_custom_call" | custom-call | flops 12079595520 | bytes 2516582 | tf_op jit(solution)/shard_map/attend/pallas_call | solution.py:327
  496.9 5.8 all-to-all-start.4
  504.1 64.9 %attend_back.2 = (bf16[8,768,128]{2,1,0:T(8,128)(2,1)S(1)}, bf16[8,768,256]{2,1,0:T(8,128)(2,1)S(1)}) custom-call(s32[7]{0:T(128)S(1)} %copy-done.43, bf16[8,768,384]{2,1,0:T(8,128)(2,1)} %all-to-all-done.refs_0_, bf16[8,816,128]{2,1,0:T(8,128)(2,1)S(1)} %copy-done.32), custom_call_target="tpu_custom_call" | custom-call | flops 20132659200 | bytes 4404019 | tf_op jit(solution)/shard_map/attend_back/pallas_call | solution.py:484
  571.9 6.1 all-to-all-start.5
  585.4 64.5 %feed_forward.3 = (bf16[2,1,512,1024]{3,2,1,0:T(8,128)(2,1)}, bf16[2,1,256,1024]{3,2,1,0:T(8,128)(2,1)}, f32[768,1024]{1,0:T(8,128)}, bf16[768,1024]{1,0:T(8,128...) custom-call(s32[7]{0:T(128)} %pad_add_fusion.2.meta, ...), custom_call_target="tpu_custom_call", output_to_operand_aliasing={{0}: (16, {}), {1}: (17, {})} | custom-call | flops 8938900480 | bytes 16331366 | tf_op jit(solution)/shard_map/feed_forward/pallas_call | solution.py:547
  655.5 27.3 %weight_grads.3 = (bf16[1024,2560]{1,0:T(8,128)(2,1)}, bf16[1024,2560]{1,0:T(8,128)(2,1)}) custom-call(s32[7]{0:T(128)} %get-tuple-element.268.meta, bf16[768,1024]{1,0:T(8,128)(2,1)} %get-tuple-element.163.refs_0_, bf16[768,1024]{1,0:T(8,128)(2,1)} %get-tuple-element.164.refs_1_, bf16[768,1024]{1,0:T(8,128)(2,1)} %copy-done.10, ...), custom_call_target="tpu_custom_call" | custom-call | flops 4469450240 | bytes 15649996 | tf_op jit(solution)/shard_map/weight_grads/pallas_call | solution.py:547
  682.9 6.0 all-to-all-start.6
  689.1 27.3 %weight_grads.2 = (bf16[1024,2560]{1,0:T(8,128)(2,1)}, bf16[1024,2560]{1,0:T(8,128)(2,1)}) custom-call(s32[7]{0:T(128)} %get-tuple-element.268.meta, bf16[768,1024]{1,0:T(8,128)(2,1)} %get-tuple-element.163.refs_0_, bf16[768,1024]{1,0:T(8,128)(2,1)} %get-tuple-element.164.refs_1_, bf16[768,1024]{1,0:T(8,128)(2,1)} %copy-done.10, ...), custom_call_target="tpu_custom_call" | custom-call | flops 4469450240 | bytes 15649996 | tf_op jit(solution)/shard_map/weight_grads/pallas_call | solution.py:547
  716.5 12.2 %all-to-all-done.6.refs_1_ = bf16[8,816,128]{2,1,0:T(8,128)(2,1)S(1)} async-done(((bf16[8,816,128]{2,1,0:T(8,128)(2,1)}), bf16[8,816,128]{2,1,0:T(8,128)(2,1)S(1)}, u32[]{:S(2)}, u32[]{:S(2)}) %all-to-all-start.6) | async-done | bytes 1671200 | tf_op jit(solution)/shard_map/all_to_all | solution.py:1296
  728.7 4.5 all-to-all-start.7
  733.2 7.7 add_convert_fusion
  742.4 63.4 %attend_back.3 = (bf16[8,768,128]{2,1,0:T(8,128)(2,1)}, bf16[8,768,256]{2,1,0:T(8,128)(2,1)S(1)}) custom-call(s32[7]{0:T(128)S(1)} %copy-done.48, bf16[8,768,384]{2,1,0:T(8,128)(2,1)} %all-to-all-done.3.refs_0_, bf16[8,816,128]{2,1,0:T(8,128)(2,1)S(1)} %all-to-all-done.6.refs_1_), custom_call_target="tpu_custom_call" | custom-call | flops 20132659200 | bytes 4404019 | tf_op jit(solution)/shard_map/attend_back/pallas_call | solution.py:484
  807.5 6.6 all-to-all-start.8
  817.8 7.5 cache_backward.3.refs_3_
  827.0 7.5 cache_backward.2.refs_5_
  836.1 25.7 %finish.3 = (f32[2,1,512,1024]{3,2,1,0:T(8,128)}, f32[2,1,256,1024]{3,2,1,0:T(8,128)}, f32[8,1024]{1,0:T(8,128)S(1)}, f32[8,1024,256]{2,1,0:T(8,128)}, f32[8,1024,128]{2,1,0:T(8,128)}) custom-call(s32[7]{0:T(128)S(1)} %copy-done.44, bf16[768,1024]{1,0:T(8,128)(2,1)} %copy-done.37, bf16[8,768,256]{2,1,0:T(8,128)(2,1)} %all-to-all-done.5.refs_1_, ...), custom_call_target="tpu_custom_call" | custom-call | flops 2899102976 | bytes 14245478 | tf_op jit(solution)/shard_map/finish/pallas_call | solution.py:547
  861.8 11.5 %convert_add_fusion = f32[1024,2560]{1,0:T(8,128)} fusion(bf16[1024,2560]{1,0:T(8,128)(2,1)} %collective-permute-done.20, bf16[1024,2560]{1,0:T(8,128)(2,1)} %collective-permute-done.19, bf16[1024,2560]{1,0:T(8,128)(2,1)} %get-tuple-element.214), kind=kLoop, calls=%fused_computation | loop fusion | flops 13107200 | bytes 26214400 | tf_op jit(solution)/shard_map/add | solution.py:1339
  873.4 10.4 all-to-all-done.8.refs_1_
  887.6 4.3 fusion
  893.9 16.9 %finish.4 = (bf16[1024,512]{1,0:T(8,128)(2,1)S(1)}, bf16[1024,512]{1,0:T(8,128)(2,1)}, bf16[1024,512]{1,0:T(8,128)(2,1)}, bf16[1024,512]{1,0:T(8,128)(2,1)}, f32[768,1024]{1,0:T(8,128)}) custom-call(s32[7]{0:T(128)S(1)} %copy-done.48, bf16[768,1024]{1,0:T(8,128)(2,1)} %copy-done.19, bf16[8,768,256]{2,1,0:T(8,128)(2,1)} %all-to-all-done.8.refs_1_, ...), custom_call_target="tpu_custom_call" | custom-call | flops 966367616 | bytes 8060928 | tf_op jit(solution)/shard_map/finish/pallas_call | solution.py:547
  917.8 7.0 all-to-all-done.9.refs_1_
  926.0 20.0 %finish.5 = (f32[2,1,512,1024]{3,2,1,0:T(8,128)}, f32[2,1,256,1024]{3,2,1,0:T(8,128)}, f32[8,1024]{1,0:T(8,128)S(1)}, bf16[1024,256]{1,0:T(8,128)(2,1)S(1)}, bf1...) custom-call(s32[7]{0:T(128)S(1)} %copy-done.48, ...), custom_call_target="tpu_custom_call", output_to_operand_aliasing={{0}: (11, {}), {1}: (12, {})} | custom-call | flops 966367616 | bytes 12318720 | tf_op jit(solution)/shard_map/finish/pallas_call | solution.py:547
  946.0 17.2 %collective-permute-done.21 = bf16[4,128,2560]{2,1,0:T(8,128)(2,1)} collective-permute-done((bf16[4,128,2560]{2,1,0:T(8,128)(2,1)}, bf16[4,128,2560]{2,1,0:T(8,128)(2,1)}, u32[]{:S(2)}, u32[]{:S(2)}) %collective-permute-start.21) | collective-permute-done | bytes 2621472 | tf_op jit(solution)/shard_map/ppermute | solution.py:1328
  963.3 4.1 bitcast_add_fusion
  975.4 4.2 all-to-all-start.12
  984.0 26.5 %collective-permute-done.22 = bf16[2,128,2560]{2,1,0:T(8,128)(2,1)} collective-permute-done((bf16[2,128,2560]{2,1,0:T(8,128)(2,1)S(1)}, bf16[2,128,2560]{2,1,0:T(8,128)(2,1)}, u32[]{:S(2)}, u32[]{:S(2)}) %collective-permute-start.22) | collective-permute-done | bytes 1310752 | tf_op jit(solution)/shard_map/ppermute | solution.py:1328
  1028.6 24.5 %collective-permute-done.23 = bf16[1,128,2560]{2,1,0:T(8,128)(2,1)} collective-permute-done((bf16[1,128,2560]{2,1,0:T(8,128)(2,1)}, bf16[1,128,2560]{2,1,0:T(8,128)(2,1)}, u32[]{:S(2)}, u32[]{:S(2)}) %collective-permute-start.23) | collective-permute-done | bytes 655392 | tf_op jit(solution)/shard_map/ppermute | solution.py:1328
  (250 shorter events, 168.8 us)
Async XLA Ops:
  7.2 114.2 %all-gather.2.cloned.1.call-start = ((), (), s32[]{:S(2)}) async-start(), calls=%async_computation.13 | async-start | bytes 6623232 | tf_op jit(solution)/shard_map/all_gather | solution.py:1427
  22.3 26.5 %collective-permute-start = (bf16[1,1408,128]{2,1,0:T(8,128)(2,1)S(1)}, bf16[1,1408,128]{2,1,0:T(8,128)(2,1)S(1)}, u32[]{:S(2)}, u32[]{:S(2)}) collective-permute-start(bf16[1,1408,128]{2,1,0:T(8,128)(2,1)S(1)} %maximum_bitcast_fusion), channel_id=1, source_target_pairs={{0,4},{1,5},{2,6},{3,7},{4,0},{5,1},{6,2},{7,3},{8,12},{9,13},{10,... | collective-permute-start | bytes 1081352 | tf_op jit(solution)/shard_map/ppermute | solution.py:1328
  28.3 32.7 %collective-permute-start.2 = (bf16[1,960,128]{2,1,0:T(8,128)(2,1)S(1)}, bf16[1,960,128]{2,1,0:T(8,128)(2,1)S(1)}, u32[]{:S(2)}, u32[]{:S(2)}) collective-permute-start(bf16[1,960,128]{2,1,0:T(8,128)(2,1)S(1)} %maximum_bitcast_fusion.1), channel_id=1, source_target_pairs={{0,4},{1,5},{2,6},{3,7},{4,0},{5,1},{6,2},{7,3},{8,12},{9,13},{10,... | collective-permute-start | bytes 737288 | tf_op jit(solution)/shard_map/ppermute | solution.py:1328
  49.6 62.2 %collective-permute-start.1 = (bf16[2,1408,128]{2,1,0:T(8,128)(2,1)}, bf16[2,1408,128]{2,1,0:T(8,128)(2,1)}, u32[]{:S(2)}, u32[]{:S(2)}) collective-permute-start(bf16[2,1408,128]{2,1,0:T(8,128)(2,1)} %pad_maximum_fusion.4), channel_id=1, source_target_pairs={{0,2},{1,3},{2,0},{3,1},{4,6},{5,7},{6,4},{7,5},{8,10},{9,11},{10,... | collective-permute-start | bytes 2162696 | tf_op jit(solution)/shard_map/ppermute | solution.py:1328
  61.8 48.0 %collective-permute-start.3 = (bf16[2,960,128]{2,1,0:T(8,128)(2,1)}, bf16[2,960,128]{2,1,0:T(8,128)(2,1)}, u32[]{:S(2)}, u32[]{:S(2)}) collective-permute-start(bf16[2,960,128]{2,1,0:T(8,128)(2,1)} %pad_maximum_fusion.5), channel_id=1, source_target_pairs={{0,2},{1,3},{2,0},{3,1},{4,6},{5,7},{6,4},{7,5},{8,10},{9,11},{10,... | collective-permute-start | bytes 1474568 | tf_op jit(solution)/shard_map/ppermute | solution.py:1328
  140.6 110.7 %all-to-all-start = ((bf16[8,768,384]{2,1,0:T(8,128)(2,1)}), bf16[8,768,384]{2,1,0:T(8,128)(2,1)}, u32[]{:S(2)}, u32[]{:S(2)}) async-start(bf16[8,768,384]{2,1,0:T(8,128)(2,1)} %copy-done.2), calls=%async_computation | async-start | bytes 9437184 | tf_op jit(solution)/shard_map/all_to_all | solution.py:1296
  146.2 84.2 %collective-permute-start.4 = (bf16[4,1408,128]{2,1,0:T(8,128)(2,1)}, bf16[4,1408,128]{2,1,0:T(8,128)(2,1)S(1)}, u32[]{:S(2)}, u32[]{:S(2)}) collective-permute-start(bf16[4,1408,128]{2,1,0:T(8,128)(2,1)} %pad_maximum_fusion.2), channel_id=1, source_target_pairs={{0,1},{1,0},{2,3},{3,2},{4,5},{5,4},{6,7},{7,6},{8,9},{9,8},{10,11... | collective-permute-start | bytes 4325384 | tf_op jit(solution)/shard_map/ppermute | solution.py:1328
  173.7 56.7 %copy-start.53 = (bf16[4,1408,128]{2,1,0:T(8,128)(2,1)S(1)}, bf16[4,1408,128]{2,1,0:T(8,128)(2,1)}, u32[]{:S(2)}) copy-start(bf16[4,1408,128]{2,1,0:T(8,128)(2,1)} %pad_maximum_fusion.2) | copy-start | bytes 4325380
  180.6 51.7 %copy-start.24 = (f32[8,768,128]{2,1,0:T(8,128)}, f32[8,768,128]{2,1,0:T(8,128)S(1)}, u32[]{:S(2)}) copy-start(f32[8,768,128]{2,1,0:T(8,128)S(1)} %get-tuple-element.152.cache_mixed) | copy-start | bytes 9437188
  232.4 63.8 %collective-permute-start.5 = (bf16[8,1408,128]{2,1,0:T(8,128)(2,1)}, bf16[8,1408,128]{2,1,0:T(8,128)(2,1)}, u32[]{:S(2)}, u32[]{:S(2)}) collective-permute-start(bf16[8,1408,128]{2,1,0:T(8,128)(2,1)} %pad_maximum_fusion.refs_0_), channel_id=1, source_target_pairs={{0,16},{8,24},{16,0},{24,8},{1,17},{9,25},{17,1},{25,9},{2,18},{10... | collective-permute-start | bytes 8650760 | tf_op jit(solution)/shard_map/ppermute | solution.py:1323
  233.8 67.0 %collective-permute-start.6 = (bf16[4,960,128]{2,1,0:T(8,128)(2,1)}, bf16[4,960,128]{2,1,0:T(8,128)(2,1)}, u32[]{:S(2)}, u32[]{:S(2)}) collective-permute-start(bf16[4,960,128]{2,1,0:T(8,128)(2,1)} %pad_maximum_fusion.3), channel_id=1, source_target_pairs={{0,1},{1,0},{2,3},{3,2},{4,5},{5,4},{6,7},{7,6},{8,9},{9,8},{10,11... | collective-permute-start | bytes 2949128 | tf_op jit(solution)/shard_map/ppermute | solution.py:1328
  296.2 49.3 %all-to-all-start.1 = ((bf16[8,800,128]{2,1,0:T(8,128)(2,1)}), bf16[8,800,128]{2,1,0:T(8,128)(2,1)S(1)}, u32[]{:S(2)}, u32[]{:S(2)}) async-start(bf16[8,800,128]{2,1,0:T(8,128)(2,1)} %copy-done.34), calls=%async_computation.1 | async-start | bytes 3276800 | tf_op jit(solution)/shard_map/all_to_all | solution.py:1296
  302.5 50.4 %copy-start.58 = (bf16[4096]{0:T(1024)(128)(2,1)S(1)}, bf16[4096]{0:T(1024)(128)(2,1)}, u32[]{:S(2)}) copy-start(bf16[4096]{0:T(1024)(128)(2,1)} %copy-done.57) | copy-start | bytes 24580
  302.6 52.4 %copy-start.60 = (s32[512,1]{0,1:T(1,128)S(1)}, s32[512,1]{0,1:T(1,128)}, u32[]{:S(2)}) copy-start(s32[512,1]{0,1:T(1,128)} %get-tuple-element.282) | copy-start | bytes 6148
  302.6 52.4 %copy-start.62 = (s32[256]{0:T(256)S(1)}, s32[256]{0:T(256)}, u32[]{:S(2)}) copy-start(s32[256]{0:T(256)} %get-tuple-element.294) | copy-start | bytes 3076
  302.6 53.4 %copy-start.46 = (f32[8,8,128]{2,1,0:T(8,128)S(1)}, f32[8,8,128]{2,1,0:T(8,128)}, u32[]{:S(2)}) copy-start(f32[8,8,128]{2,1,0:T(8,128)} %copy-done.45) | copy-start | bytes 98308
  302.6 42.9 %collective-permute-start.9 = (bf16[8,960,128]{2,1,0:T(8,128)(2,1)S(1)}, bf16[8,960,128]{2,1,0:T(8,128)(2,1)}, u32[]{:S(2)}, u32[]{:S(2)}) collective-permute-start(bf16[8,960,128]{2,1,0:T(8,128)(2,1)S(1)} %pad_maximum_fusion.1.refs_1_), channel_id=1, source_target_pairs={{0,16},{8,24},{16,0},{24,8},{1,17},{9,25},{17,1},{25,9},{2,18},{10... | collective-permute-start | bytes 5898248 | tf_op jit(solution)/shard_map/ppermute | solution.py:1323
  345.5 107.2 %all-to-all-start.3 = ((bf16[8,768,384]{2,1,0:T(8,128)(2,1)}), bf16[8,768,384]{2,1,0:T(8,128)(2,1)}, u32[]{:S(2)}, u32[]{:S(2)}) async-start(bf16[8,768,384]{2,1,0:T(8,128)(2,1)} %copy-done.4), calls=%async_computation.3 | async-start | bytes 9437184 | tf_op jit(solution)/shard_map/all_to_all | solution.py:1296
  351.2 12.6 %collective-permute-start.7 = (bf16[8,1408,128]{2,1,0:T(8,128)(2,1)}, bf16[8,1408,128]{2,1,0:T(8,128)(2,1)}, u32[]{:S(2)}, u32[]{:S(2)}) collective-permute-start(bf16[8,1408,128]{2,1,0:T(8,128)(2,1)} %pad_maximum_fusion.refs_0_), channel_id=1, source_target_pairs={{0,8},{8,0},{16,24},{24,16},{1,9},{9,1},{17,25},{25,17},{2,10},{10... | collective-permute-start | bytes 8650760 | tf_op jit(solution)/shard_map/ppermute | solution.py:1323
  351.2 15.4 %collective-permute-start.10 = (bf16[8,1408,128]{2,1,0:T(8,128)(2,1)}, bf16[8,1408,128]{2,1,0:T(8,128)(2,1)}, u32[]{:S(2)}, u32[]{:S(2)}) collective-permute-start(bf16[8,1408,128]{2,1,0:T(8,128)(2,1)} %collective-permute-done.5.refs_4_), channel_id=1, source_target_pairs={{0,8},{8,0},{16,24},{24,16},{1,9},{9,1},{17,25},{25,17},{2,10},{10... | collective-permute-start | bytes 8650760 | tf_op jit(solution)/shard_map/ppermute | solution.py:1323
  351.7 12.1 %collective-permute-start.8 = (bf16[8,960,128]{2,1,0:T(8,128)(2,1)}, bf16[8,960,128]{2,1,0:T(8,128)(2,1)}, u32[]{:S(2)}, u32[]{:S(2)}) collective-permute-start(bf16[8,960,128]{2,1,0:T(8,128)(2,1)} %copy-done.54), channel_id=1, source_target_pairs={{0,8},{8,0},{16,24},{24,16},{1,9},{9,1},{17,25},{25,17},{2,10},{10... | collective-permute-start | bytes 5898248 | tf_op jit(solution)/shard_map/ppermute | solution.py:1323
  351.8 14.8 %collective-permute-start.11 = (bf16[8,960,128]{2,1,0:T(8,128)(2,1)}, bf16[8,960,128]{2,1,0:T(8,128)(2,1)}, u32[]{:S(2)}, u32[]{:S(2)}) collective-permute-start(bf16[8,960,128]{2,1,0:T(8,128)(2,1)} %collective-permute-done.9.refs_5_), channel_id=1, source_target_pairs={{0,8},{8,0},{16,24},{24,16},{1,9},{9,1},{17,25},{25,17},{2,10},{10... | collective-permute-start | bytes 5898248 | tf_op jit(solution)/shard_map/ppermute | solution.py:1323
  366.6 64.5 %copy-start.11 = (bf16[768,1024]{1,0:T(8,128)(2,1)S(1)}, bf16[768,1024]{1,0:T(8,128)(2,1)}, u32[]{:S(2)}) copy-start(bf16[768,1024]{1,0:T(8,128)(2,1)} %copy-done.10) | copy-start | bytes 4718596
  366.6 64.5 %copy-start.43 = (s32[7]{0:T(128)S(1)}, s32[7]{0:T(128)}, u32[]{:S(2)}) copy-start(s32[7]{0:T(128)} %get-tuple-element.268.meta) | copy-start | bytes 88
  452.7 42.9 %all-to-all-start.2 = ((bf16[8,816,128]{2,1,0:T(8,128)(2,1)}), bf16[8,816,128]{2,1,0:T(8,128)(2,1)S(1)}, u32[]{:S(2)}, u32[]{:S(2)}) async-start(bf16[8,816,128]{2,1,0:T(8,128)(2,1)} %copy-done.33), calls=%async_computation.2 | async-start | bytes 3342336 | tf_op jit(solution)/shard_map/all_to_all | solution.py:1296
  496.9 75.0 %all-to-all-start.4 = ((bf16[8,800,128]{2,1,0:T(8,128)(2,1)}), bf16[8,800,128]{2,1,0:T(8,128)(2,1)S(1)}, u32[]{:S(2)}, u32[]{:S(2)}) async-start(bf16[8,800,128]{2,1,0:T(8,128)(2,1)} %copy-done.35), calls=%async_computation.4 | async-start | bytes 3276800 | tf_op jit(solution)/shard_map/all_to_all | solution.py:1296
  571.9 83.6 %all-to-all-start.5 = ((bf16[8,768,256]{2,1,0:T(8,128)(2,1)}), bf16[8,768,256]{2,1,0:T(8,128)(2,1)}, u32[]{:S(2)}, u32[]{:S(2)}) async-start(bf16[8,768,256]{2,1,0:T(8,128)(2,1)} %copy-done.29), calls=%async_computation.5 | async-start | bytes 6291456 | tf_op jit(solution)/shard_map/all_to_all | solution.py:1296
  585.4 64.6 %copy-start.13 = (bf16[768,1024]{1,0:T(8,128)(2,1)S(1)}, bf16[768,1024]{1,0:T(8,128)(2,1)}, u32[]{:S(2)}) copy-start(bf16[768,1024]{1,0:T(8,128)(2,1)} %copy-done.12) | copy-start | bytes 4718596
  585.4 64.6 %copy-start.48 = (s32[7]{0:T(128)S(1)}, s32[7]{0:T(128)}, u32[]{:S(2)}) copy-start(s32[7]{0:T(128)} %pad_add_fusion.2.meta) | copy-start | bytes 88
  682.9 50.3 %collective-permute-start.12 = (bf16[1024,2560]{1,0:T(8,128)(2,1)}, bf16[1024,2560]{1,0:T(8,128)(2,1)}, u32[]{:S(2)}, u32[]{:S(2)}) collective-permute-start(bf16[1024,2560]{1,0:T(8,128)(2,1)} %get-tuple-element.177), channel_id=1, source_target_pairs={{0,8},{8,0},{16,24},{24,16},{1,9},{9,1},{17,25},{25,17},{2,10},{10... | collective-permute-start | bytes 15728648 | tf_op jit(solution)/shard_map/ppermute | solution.py:1323
  682.9 45.7 %all-to-all-start.6 = ((bf16[8,816,128]{2,1,0:T(8,128)(2,1)}), bf16[8,816,128]{2,1,0:T(8,128)(2,1)S(1)}, u32[]{:S(2)}, u32[]{:S(2)}) async-start(bf16[8,816,128]{2,1,0:T(8,128)(2,1)} %copy-done.30), calls=%async_computation.6 | async-start | bytes 3342336 | tf_op jit(solution)/shard_map/all_to_all | solution.py:1296
  688.9 172.9 %collective-permute-start.19 = (bf16[1024,2560]{1,0:T(8,128)(2,1)}, bf16[1024,2560]{1,0:T(8,128)(2,1)}, u32[]{:S(2)}, u32[]{:S(2)}) collective-permute-start(bf16[1024,2560]{1,0:T(8,128)(2,1)} %get-tuple-element.215), channel_id=1, source_target_pairs={{0,8},{8,0},{16,24},{24,16},{1,9},{9,1},{17,25},{25,17},{2,10},{10... | collective-permute-start | bytes 15728648 | tf_op jit(solution)/shard_map/ppermute | solution.py:1323
  728.7 78.8 %all-to-all-start.7 = ((bf16[8,768,128]{2,1,0:T(8,128)(2,1)}), bf16[8,768,128]{2,1,0:T(8,128)(2,1)}, u32[]{:S(2)}, u32[]{:S(2)}) async-start(bf16[8,768,128]{2,1,0:T(8,128)(2,1)} %copy-done.36), calls=%async_computation.7 | async-start | bytes 3145728 | tf_op jit(solution)/shard_map/all_to_all | solution.py:1296
  740.9 120.9 %collective-permute-start.20 = (bf16[1024,2560]{1,0:T(8,128)(2,1)}, bf16[1024,2560]{1,0:T(8,128)(2,1)}, u32[]{:S(2)}, u32[]{:S(2)}) collective-permute-start(bf16[1024,2560]{1,0:T(8,128)(2,1)} %add_convert_fusion), channel_id=1, source_target_pairs={{0,16},{8,24},{16,0},{24,8},{1,17},{9,25},{17,1},{25,9},{2,18},{10... | collective-permute-start | bytes 15728648 | tf_op jit(solution)/shard_map/ppermute | solution.py:1323
  807.5 76.3 %all-to-all-start.8 = ((bf16[8,768,256]{2,1,0:T(8,128)(2,1)}), bf16[8,768,256]{2,1,0:T(8,128)(2,1)}, u32[]{:S(2)}, u32[]{:S(2)}) async-start(bf16[8,768,256]{2,1,0:T(8,128)(2,1)} %copy-done.28), calls=%async_computation.8 | async-start | bytes 6291456 | tf_op jit(solution)/shard_map/all_to_all | solution.py:1296
  883.8 41.0 %all-to-all-start.9 = ((bf16[8,768,128]{2,1,0:T(8,128)(2,1)}), bf16[8,768,128]{2,1,0:T(8,128)(2,1)S(1)}, u32[]{:S(2)}, u32[]{:S(2)}) async-start(bf16[8,768,128]{2,1,0:T(8,128)(2,1)} %get-tuple-element.193), calls=%async_computation.9 | async-start | bytes 3145728 | tf_op jit(solution)/shard_map/all_to_all | solution.py:1296
  891.9 71.4 %collective-permute-start.21 = (bf16[4,128,2560]{2,1,0:T(8,128)(2,1)}, bf16[4,128,2560]{2,1,0:T(8,128)(2,1)}, u32[]{:S(2)}, u32[]{:S(2)}) collective-permute-start(bf16[4,128,2560]{2,1,0:T(8,128)(2,1)} %fusion), channel_id=1, source_target_pairs={{0,1},{1,0},{2,3},{3,2},{4,5},{5,4},{6,7},{7,6},{8,9},{9,8},{10,11... | collective-permute-start | bytes 7864328 | tf_op jit(solution)/shard_map/ppermute | solution.py:1328
  910.9 3.5 collective-permute-start.17
  910.9 61.2 %collective-permute-start.16 = (bf16[1024,512]{1,0:T(8,128)(2,1)}, bf16[1024,512]{1,0:T(8,128)(2,1)}, u32[]{:S(2)}, u32[]{:S(2)}) collective-permute-start(bf16[1024,512]{1,0:T(8,128)(2,1)} %get-tuple-element.210), channel_id=1, source_target_pairs={{0,8},{8,0},{16,24},{24,16},{1,9},{9,1},{17,25},{25,17},{2,10},{10... | collective-permute-start | bytes 3145736 | tf_op jit(solution)/shard_map/ppermute | solution.py:1323
  917.2 54.2 %collective-permute-start.18 = (bf16[1024,512]{1,0:T(8,128)(2,1)}, bf16[1024,512]{1,0:T(8,128)(2,1)}, u32[]{:S(2)}, u32[]{:S(2)}) collective-permute-start(bf16[1024,512]{1,0:T(8,128)(2,1)} %add_convert_fusion.2), channel_id=1, source_target_pairs={{0,16},{8,24},{16,0},{24,8},{1,17},{9,25},{17,1},{25,9},{2,18},{10... | collective-permute-start | bytes 3145736 | tf_op jit(solution)/shard_map/ppermute | solution.py:1323
  946.0 25.4 %collective-permute-start.14 = (bf16[1024,256]{1,0:T(8,128)(2,1)S(1)}, bf16[1024,256]{1,0:T(8,128)(2,1)S(1)}, u32[]{:S(2)}, u32[]{:S(2)}) collective-permute-start(bf16[1024,256]{1,0:T(8,128)(2,1)S(1)} %get-tuple-element.203), channel_id=1, source_target_pairs={{0,8},{8,0},{16,24},{24,16},{1,9},{9,1},{17,25},{25,17},{2,10},{10... | collective-permute-start | bytes 1572872 | tf_op jit(solution)/shard_map/ppermute | solution.py:1323
  969.9 40.6 %collective-permute-start.22 = (bf16[2,128,2560]{2,1,0:T(8,128)(2,1)S(1)}, bf16[2,128,2560]{2,1,0:T(8,128)(2,1)}, u32[]{:S(2)}, u32[]{:S(2)}) collective-permute-start(bf16[2,128,2560]{2,1,0:T(8,128)(2,1)S(1)} %fusion.1), channel_id=1, source_target_pairs={{0,2},{1,3},{2,0},{3,1},{4,6},{5,7},{6,4},{7,5},{8,10},{9,11},{10,... | collective-permute-start | bytes 3932168 | tf_op jit(solution)/shard_map/ppermute | solution.py:1328
  971.5 12.5 %collective-permute-start.15 = (bf16[1024,256]{1,0:T(8,128)(2,1)S(1)}, bf16[1024,256]{1,0:T(8,128)(2,1)S(1)}, u32[]{:S(2)}, u32[]{:S(2)}) collective-permute-start(bf16[1024,256]{1,0:T(8,128)(2,1)S(1)} %add_convert_fusion.4), channel_id=1, source_target_pairs={{0,16},{8,24},{16,0},{24,8},{1,17},{9,25},{17,1},{25,9},{2,18},{10... | collective-permute-start | bytes 1572872 | tf_op jit(solution)/shard_map/ppermute | solution.py:1323
  975.4 44.5 %all-to-all-start.12 = ((bf16[8,128,512]{2,1,0:T(8,128)(2,1)}), bf16[8,128,512]{2,1,0:T(8,128)(2,1)}, u32[]{:S(2)}, u32[]{:S(2)}) async-start(bf16[8,128,512]{2,1,0:T(8,128)(2,1)} %bitcast.33), calls=%async_computation.12 | async-start | bytes 2097152 | tf_op jit(solution)/shard_map/all_to_all | solution.py:1565
  982.0 35.7 %collective-permute-start.13 = (bf16[1024,256]{1,0:T(8,128)(2,1)S(1)}, bf16[1024,256]{1,0:T(8,128)(2,1)S(1)}, u32[]{:S(2)}, u32[]{:S(2)}) collective-permute-start(bf16[1024,256]{1,0:T(8,128)(2,1)S(1)} %get-tuple-element.201), channel_id=1, source_target_pairs={{0,8},{8,0},{16,24},{24,16},{1,9},{9,1},{17,25},{25,17},{2,10},{10... | collective-permute-start | bytes 1572872 | tf_op jit(solution)/shard_map/ppermute | solution.py:1323
  1014.0 39.2 %collective-permute-start.23 = (bf16[1,128,2560]{2,1,0:T(8,128)(2,1)}, bf16[1,128,2560]{2,1,0:T(8,128)(2,1)}, u32[]{:S(2)}, u32[]{:S(2)}) collective-permute-start(bf16[1,128,2560]{2,1,0:T(8,128)(2,1)} %dynamic-slice_convert_fusion.1), channel_id=1, source_target_pairs={{0,4},{1,5},{2,6},{3,7},{4,0},{5,1},{6,2},{7,3},{8,12},{9,13},{10,... | collective-permute-start | bytes 1966088 | tf_op jit(solution)/shard_map/ppermute | solution.py:1328
  1020.0 38.6 %all-to-all-start.10 = ((bf16[8,128,256]{2,1,0:T(8,128)(2,1)}), bf16[8,128,256]{2,1,0:T(8,128)(2,1)S(1)}, u32[]{:S(2)}, u32[]{:S(2)}) async-start(bf16[8,128,256]{2,1,0:T(8,128)(2,1)} %bitcast.78), calls=%async_computation.10 | async-start | bytes 1048576 | tf_op jit(solution)/shard_map/all_to_all | solution.py:1565
  1059.3 9.6 all-to-all-start.11
  (55 other events, 451.0 us)
Sparse Core Ops, SparseCore 0:
  21.3 99.9 all-gather.1

commit v6 on v5

--- a/solution.py
+++ b/solution.py
@@ -1118,13 +1118,12 @@
 
     @pl.when(step == len(outs) - 1)
     def _():
-        move(len(outs) - 2).wait()
-        move(len(outs) - 1).wait()
-
-
-def weight_grads(sz, meta, parts, first):
+        for turn in range(max(len(outs) - 2, 0), len(outs)):
+            move(turn).wait()
+
+
+def weight_grads(sz, meta, parts, first, turns):
     groups, rows, inner = parts[0][4].shape
-    turns = groups // 2
     width = parts[0][0].shape[1]
     piece = width // groups
     ins = []
@@ -1519,7 +1518,7 @@
         deltas.append(delta)
         if m > 0:
             back_queries.append(exchange(sz, after(pending[0], arrived[m])))
-    feed_grads = weight_grads(sz, metas[0], parts, 0) + weight_grads(sz, metas[0], parts, 2)
+    feed_grads = weight_grads(sz, metas[0], parts, 0, 1) + weight_grads(sz, metas[0], parts, 1, 3)
     handed = hand_over(feed_grads)
     query, pair = run_back(last, after(arrived[last], handed))
     back_pairs.append(exchange(sz, after(pair, *back_queries)))

time: 1090 us -> 1080 us (level)
    unnamed x137 -> x139, local copies, waits for them, and re-layouts: 53.6 us -> 53.5 us
  transfers between devices with their start and end apart: 38 -> 38, of which waited for: 22 -> 22; matrix products, arithmetic and copies ran while one was open for 7% -> 7% of each run, Pallas kernels for 45% -> 47%
where the time goes in v6:
time: 1080 us; the launch traced here: 1070 us
  Pallas kernels  526 us (49%)
  waiting for transfers between devices  299 us (28%)
  starting transfers between devices  88.7 us (8%)
  local copies, waits for them, and re-layouts  75.4 us (7%)
  other arithmetic  60.1 us (6%)
  between operations  20.9 us (2%)
    pallas_call x17, Pallas kernels, call(): pl.pallas_call(kernel, out_shape=list(out_shape), grid_spec=pltpu.Prefetc...  306 us
    ppermute x9, waiting for transfers between devices, along_seq(): return lax.ppermute(array, 'seq', [(i, i ^ away) for i in range(count)])  177 us
    pallas_call x2, Pallas kernels, attend_back(): pl.pallas_call(functools.partial(attend_back_kernel, sz), out_shape=out_s...  128 us
    pallas_call x2, Pallas kernels, attend(): pl.pallas_call(functools.partial(attend_kernel, sz), out_shape=jax.ShapeD...  75.5 us
    ppermute x15, waiting for transfers between devices, along_grp(): return lax.ppermute(array, 'grp', [(i, i ^ away) for i in range(count)])  55.9 us
    all_to_all x10, waiting for transfers between devices, exchange(): return lax.all_to_all(array, 'seq', 0, 0, axis_index_groups=subgroups(sz))  55.1 us
    unnamed x139, local copies, waits for them, and re-layouts  53.5 us
    all_to_all x10, starting transfers between devices, exchange(): return lax.all_to_all(array, 'seq', 0, 0, axis_index_groups=subgroups(sz))  52.4 us
  transfers between devices with their start and end apart: 38, of which 22 were waited for; matrix products, arithmetic and copies ran while one was open for 7% of the time, Pallas kernels for 47%

profile of v6, /device:TPU:0, one launch (start us, length us, event | category | flops | bytes accessed | tf_op | source)
XLA Modules:
  0.0 1070.3 jit_solution(16940753545135976908)
XLA Ops:
  22.2 4.1 collective-permute-start
  28.3 20.4 %collective-permute-done = bf16[1,1408,128]{2,1,0:T(8,128)(2,1)S(1)} collective-permute-done((bf16[1,1408,128]{2,1,0:T(8,128)(2,1)S(1)}, bf16[1,1408,128]{2,1,0:T(8,128)(2,1)S(1)}, u32[]{:S(2)}, u32[]{:S(2)}) %collective-permute-start) | collective-permute-done | bytes 360480 | tf_op jit(solution)/shard_map/ppermute | solution.py:1327
  52.8 8.2 collective-permute-done.2
  64.5 7.8 picks_to_words.3
  72.3 7.8 picks_to_words.2
  80.0 29.8 %collective-permute-done.3 = bf16[2,960,128]{2,1,0:T(8,128)(2,1)} collective-permute-done((bf16[2,960,128]{2,1,0:T(8,128)(2,1)}, bf16[2,960,128]{2,1,0:T(8,128)(2,1)}, u32[]{:S(2)}, u32[]{:S(2)}) %collective-permute-start.3) | collective-permute-done | bytes 491552 | tf_op jit(solution)/shard_map/ppermute | solution.py:1327
  114.3 7.1 all-gather.2.cloned.1.call-done.query_w.pair_w.refs_2_.refs_4_
  127.1 10.0 project.2
  140.6 5.6 all-to-all-start
  150.5 6.9 cache_forward.2
  162.5 10.0 project.3
  173.6 6.9 cache_forward.3
  180.5 49.9 %collective-permute-done.4 = bf16[4,1408,128]{2,1,0:T(8,128)(2,1)S(1)} collective-permute-done((bf16[4,1408,128]{2,1,0:T(8,128)(2,1)}, bf16[4,1408,128]{2,1,0:T(8,128)(2,1)S(1)}, u32[]{:S(2)}, u32[]{:S(2)}) %collective-permute-start.4) | collective-permute-done | bytes 1441824 | tf_op jit(solution)/shard_map/ppermute | solution.py:1327
  233.7 17.5 %all-to-all-done.refs_0_ = bf16[8,768,384]{2,1,0:T(8,128)(2,1)} async-done(((bf16[8,768,384]{2,1,0:T(8,128)(2,1)}), bf16[8,768,384]{2,1,0:T(8,128)(2,1)}, u32[]{:S(2)}, u32[]{:S(2)}) %all-to-all-start) | async-done | bytes 4718624 | tf_op jit(solution)/shard_map/all_to_all | solution.py:1295
  251.1 37.9 %attend.2 = bf16[8,800,128]{2,1,0:T(8,128)(2,1)S(1)} custom-call(s32[7]{0:T(128)S(1)} %copy-done.42, bf16[8,768,384]{2,1,0:T(8,128)(2,1)} %all-to-all-done.refs_0_), custom_call_target="tpu_custom_call" | custom-call | flops 12079595520 | bytes 2516582 | tf_op jit(solution)/shard_map/attend/pallas_call | solution.py:327
  290.2 5.8 collective-permute-done.5.refs_4_
  296.0 4.6 all-to-all-start.1
  303.9 41.3 %collective-permute-done.9.refs_5_ = bf16[8,960,128]{2,1,0:T(8,128)(2,1)} collective-permute-done((bf16[8,960,128]{2,1,0:T(8,128)(2,1)S(1)}, bf16[8,960,128]{2,1,0:T(8,128)(2,1)}, u32[]{:S(2)}, u32[]{:S(2)}) %collective-permute-start.9) | collective-permute-done | bytes 1966112 | tf_op jit(solution)/shard_map/ppermute | solution.py:1322
  345.3 5.7 all-to-all-start.3
  366.4 64.5 %feed_forward.2 = (bf16[2,1,512,1024]{3,2,1,0:T(8,128)(2,1)}, bf16[2,1,256,1024]{3,2,1,0:T(8,128)(2,1)}, f32[768,1024]{1,0:T(8,128)}, bf16[768,1024]{1,0:T(8,128...) custom-call(s32[7]{0:T(128)} %get-tuple-element.266.meta, ...), custom_call_target="tpu_custom_call" | custom-call | flops 8938900480 | bytes 15387648 | tf_op jit(solution)/shard_map/feed_forward/pallas_call | solution.py:547
  436.4 16.1 %all-to-all-done.3.refs_0_ = bf16[8,768,384]{2,1,0:T(8,128)(2,1)} async-done(((bf16[8,768,384]{2,1,0:T(8,128)(2,1)}), bf16[8,768,384]{2,1,0:T(8,128)(2,1)}, u32[]{:S(2)}, u32[]{:S(2)}) %all-to-all-start.3) | async-done | bytes 4718624 | tf_op jit(solution)/shard_map/all_to_all | solution.py:1295
  456.1 37.6 %attend.3 = bf16[8,800,128]{2,1,0:T(8,128)(2,1)S(1)} custom-call(s32[7]{0:T(128)S(1)} %copy-done.47, bf16[8,768,384]{2,1,0:T(8,128)(2,1)} %all-to-all-done.3.refs_0_), custom_call_target="tpu_custom_call" | custom-call | flops 12079595520 | bytes 2516582 | tf_op jit(solution)/shard_map/attend/pallas_call | solution.py:327
  496.6 5.8 all-to-all-start.4
  503.8 64.9 %attend_back.2 = (bf16[8,768,128]{2,1,0:T(8,128)(2,1)S(1)}, bf16[8,768,256]{2,1,0:T(8,128)(2,1)S(1)}) custom-call(s32[7]{0:T(128)S(1)} %copy-done.43, bf16[8,768,384]{2,1,0:T(8,128)(2,1)} %all-to-all-done.refs_0_, bf16[8,816,128]{2,1,0:T(8,128)(2,1)S(1)} %copy-done.32), custom_call_target="tpu_custom_call" | custom-call | flops 20132659200 | bytes 4404019 | tf_op jit(solution)/shard_map/attend_back/pallas_call | solution.py:484
  571.6 6.1 all-to-all-start.5
  585.1 64.6 %feed_forward.3 = (bf16[2,1,512,1024]{3,2,1,0:T(8,128)(2,1)}, bf16[2,1,256,1024]{3,2,1,0:T(8,128)(2,1)}, f32[768,1024]{1,0:T(8,128)}, bf16[768,1024]{1,0:T(8,128...) custom-call(s32[7]{0:T(128)} %pad_add_fusion.2.meta, ...), custom_call_target="tpu_custom_call", output_to_operand_aliasing={{0}: (16, {}), {1}: (17, {})} | custom-call | flops 8938900480 | bytes 16331366 | tf_op jit(solution)/shard_map/feed_forward/pallas_call | solution.py:547
  655.3 17.6 %weight_grads.3 = bf16[1024,2560]{1,0:T(8,128)(2,1)} custom-call(s32[7]{0:T(128)} %get-tuple-element.266.meta, bf16[768,1024]{1,0:T(8,128)(2,1)} %get-tuple-element.162.refs_0_, bf16[768,1024]{1,0:T(8,128)(2,1)} %get-tuple-element.163.refs_1_, bf16[768,1024]{1,0:T(8,128)(2,1)} %copy-done.10, f32[768,1024]{1,0:T(8,128)} %get-tuple-element.164.refs_3_.refs_6_, ...), custom_call_target="tpu_custom_call" | custom-call | flops 4469450240 | bytes 14077132 | tf_op jit(solution)/shard_map/weight_grads/pallas_call | solution.py:547
  673.0 6.0 all-to-all-start.6
  678.9 35.9 %weight_grads.2 = (bf16[1024,2560]{1,0:T(8,128)(2,1)}, bf16[1024,2560]{1,0:T(8,128)(2,1)}, bf16[1024,2560]{1,0:T(8,128)(2,1)}) custom-call(s32[7]{0:T(128)} %get-tuple-element.266.meta, bf16[768,1024]{1,0:T(8,128)(2,1)} %get-tuple-element.162.refs_0_, bf16[768,1024]{1,0:T(8,128)(2,1)} %get-tuple-element.163.refs_1_, bf16[768,1024]{1,0:T(8,128)(2,1)} %copy-done.10, ...), custom_call_target="tpu_custom_call" | custom-call | flops 4469450240 | bytes 17222860 | tf_op jit(solution)/shard_map/weight_grads/pallas_call | solution.py:547
  718.7 4.5 all-to-all-start.7
  723.2 7.7 add_convert_fusion
  732.5 63.4 %attend_back.3 = (bf16[8,768,128]{2,1,0:T(8,128)(2,1)}, bf16[8,768,256]{2,1,0:T(8,128)(2,1)S(1)}) custom-call(s32[7]{0:T(128)S(1)} %copy-done.48, bf16[8,768,384]{2,1,0:T(8,128)(2,1)} %all-to-all-done.3.refs_0_, bf16[8,816,128]{2,1,0:T(8,128)(2,1)S(1)} %all-to-all-done.6.refs_1_), custom_call_target="tpu_custom_call" | custom-call | flops 20132659200 | bytes 4404019 | tf_op jit(solution)/shard_map/attend_back/pallas_call | solution.py:484
  797.6 6.6 all-to-all-start.8
  807.9 7.5 cache_backward.3.refs_3_
  817.1 7.5 cache_backward.2.refs_5_
  826.3 25.7 %finish.3 = (f32[2,1,512,1024]{3,2,1,0:T(8,128)}, f32[2,1,256,1024]{3,2,1,0:T(8,128)}, f32[8,1024]{1,0:T(8,128)S(1)}, f32[8,1024,256]{2,1,0:T(8,128)}, f32[8,1024,128]{2,1,0:T(8,128)}) custom-call(s32[7]{0:T(128)S(1)} %copy-done.44, bf16[768,1024]{1,0:T(8,128)(2,1)} %copy-done.37, bf16[8,768,256]{2,1,0:T(8,128)(2,1)} %all-to-all-done.5.refs_1_, ...), custom_call_target="tpu_custom_call" | custom-call | flops 2899102976 | bytes 14245478 | tf_op jit(solution)/shard_map/finish/pallas_call | solution.py:547
  852.0 11.5 %convert_add_fusion = f32[1024,2560]{1,0:T(8,128)} fusion(bf16[1024,2560]{1,0:T(8,128)(2,1)} %collective-permute-done.20, bf16[1024,2560]{1,0:T(8,128)(2,1)} %collective-permute-done.19, bf16[1024,2560]{1,0:T(8,128)(2,1)} %get-tuple-element.212), kind=kLoop, calls=%fused_computation | loop fusion | flops 13107200 | bytes 26214400 | tf_op jit(solution)/shard_map/add | solution.py:1338
  863.5 10.4 all-to-all-done.8.refs_1_
  877.7 4.3 fusion
  884.0 16.9 %finish.4 = (bf16[1024,512]{1,0:T(8,128)(2,1)S(1)}, bf16[1024,512]{1,0:T(8,128)(2,1)}, bf16[1024,512]{1,0:T(8,128)(2,1)}, bf16[1024,512]{1,0:T(8,128)(2,1)}, f32[768,1024]{1,0:T(8,128)}) custom-call(s32[7]{0:T(128)S(1)} %copy-done.48, bf16[768,1024]{1,0:T(8,128)(2,1)} %copy-done.19, bf16[8,768,256]{2,1,0:T(8,128)(2,1)} %all-to-all-done.8.refs_1_, ...), custom_call_target="tpu_custom_call" | custom-call | flops 966367616 | bytes 8060928 | tf_op jit(solution)/shard_map/finish/pallas_call | solution.py:547
  907.8 7.1 all-to-all-done.9.refs_1_
  916.1 20.0 %finish.5 = (f32[2,1,512,1024]{3,2,1,0:T(8,128)}, f32[2,1,256,1024]{3,2,1,0:T(8,128)}, f32[8,1024]{1,0:T(8,128)S(1)}, bf16[1024,256]{1,0:T(8,128)(2,1)S(1)}, bf1...) custom-call(s32[7]{0:T(128)S(1)} %copy-done.48, ...), custom_call_target="tpu_custom_call", output_to_operand_aliasing={{0}: (11, {}), {1}: (12, {})} | custom-call | flops 966367616 | bytes 12318720 | tf_op jit(solution)/shard_map/finish/pallas_call | solution.py:547
  936.1 17.2 %collective-permute-done.21 = bf16[4,128,2560]{2,1,0:T(8,128)(2,1)} collective-permute-done((bf16[4,128,2560]{2,1,0:T(8,128)(2,1)}, bf16[4,128,2560]{2,1,0:T(8,128)(2,1)}, u32[]{:S(2)}, u32[]{:S(2)}) %collective-permute-start.21) | collective-permute-done | bytes 2621472 | tf_op jit(solution)/shard_map/ppermute | solution.py:1327
  953.3 4.1 bitcast_add_fusion
  966.3 4.3 all-to-all-start.12
  975.2 26.6 %collective-permute-done.22 = bf16[2,128,2560]{2,1,0:T(8,128)(2,1)} collective-permute-done((bf16[2,128,2560]{2,1,0:T(8,128)(2,1)}, bf16[2,128,2560]{2,1,0:T(8,128)(2,1)}, u32[]{:S(2)}, u32[]{:S(2)}) %collective-permute-start.22) | collective-permute-done | bytes 1310752 | tf_op jit(solution)/shard_map/ppermute | solution.py:1327
  1005.4 3.9 collective-permute-start.23
  1020.0 24.5 %collective-permute-done.23 = bf16[1,128,2560]{2,1,0:T(8,128)(2,1)} collective-permute-done((bf16[1,128,2560]{2,1,0:T(8,128)(2,1)}, bf16[1,128,2560]{2,1,0:T(8,128)(2,1)}, u32[]{:S(2)}, u32[]{:S(2)}) %collective-permute-start.23) | collective-permute-done | bytes 655392 | tf_op jit(solution)/shard_map/ppermute | solution.py:1327
  (252 shorter events, 169.5 us)
Async XLA Ops:
  7.2 114.2 %all-gather.2.cloned.1.call-start = ((), (), s32[]{:S(2)}) async-start(), calls=%async_computation.13 | async-start | bytes 6623232 | tf_op jit(solution)/shard_map/all_gather | solution.py:1426
  22.2 26.5 %collective-permute-start = (bf16[1,1408,128]{2,1,0:T(8,128)(2,1)S(1)}, bf16[1,1408,128]{2,1,0:T(8,128)(2,1)S(1)}, u32[]{:S(2)}, u32[]{:S(2)}) collective-permute-start(bf16[1,1408,128]{2,1,0:T(8,128)(2,1)S(1)} %maximum_bitcast_fusion), channel_id=1, source_target_pairs={{0,4},{1,5},{2,6},{3,7},{4,0},{5,1},{6,2},{7,3},{8,12},{9,13},{10,... | collective-permute-start | bytes 1081352 | tf_op jit(solution)/shard_map/ppermute | solution.py:1327
  28.3 32.7 %collective-permute-start.2 = (bf16[1,960,128]{2,1,0:T(8,128)(2,1)S(1)}, bf16[1,960,128]{2,1,0:T(8,128)(2,1)S(1)}, u32[]{:S(2)}, u32[]{:S(2)}) collective-permute-start(bf16[1,960,128]{2,1,0:T(8,128)(2,1)S(1)} %maximum_bitcast_fusion.1), channel_id=1, source_target_pairs={{0,4},{1,5},{2,6},{3,7},{4,0},{5,1},{6,2},{7,3},{8,12},{9,13},{10,... | collective-permute-start | bytes 737288 | tf_op jit(solution)/shard_map/ppermute | solution.py:1327
  49.6 62.3 %collective-permute-start.1 = (bf16[2,1408,128]{2,1,0:T(8,128)(2,1)}, bf16[2,1408,128]{2,1,0:T(8,128)(2,1)}, u32[]{:S(2)}, u32[]{:S(2)}) collective-permute-start(bf16[2,1408,128]{2,1,0:T(8,128)(2,1)} %pad_maximum_fusion.4), channel_id=1, source_target_pairs={{0,2},{1,3},{2,0},{3,1},{4,6},{5,7},{6,4},{7,5},{8,10},{9,11},{10,... | collective-permute-start | bytes 2162696 | tf_op jit(solution)/shard_map/ppermute | solution.py:1327
  61.8 48.0 %collective-permute-start.3 = (bf16[2,960,128]{2,1,0:T(8,128)(2,1)}, bf16[2,960,128]{2,1,0:T(8,128)(2,1)}, u32[]{:S(2)}, u32[]{:S(2)}) collective-permute-start(bf16[2,960,128]{2,1,0:T(8,128)(2,1)} %pad_maximum_fusion.5), channel_id=1, source_target_pairs={{0,2},{1,3},{2,0},{3,1},{4,6},{5,7},{6,4},{7,5},{8,10},{9,11},{10,... | collective-permute-start | bytes 1474568 | tf_op jit(solution)/shard_map/ppermute | solution.py:1327
  140.6 110.6 %all-to-all-start = ((bf16[8,768,384]{2,1,0:T(8,128)(2,1)}), bf16[8,768,384]{2,1,0:T(8,128)(2,1)}, u32[]{:S(2)}, u32[]{:S(2)}) async-start(bf16[8,768,384]{2,1,0:T(8,128)(2,1)} %copy-done.2), calls=%async_computation | async-start | bytes 9437184 | tf_op jit(solution)/shard_map/all_to_all | solution.py:1295
  146.2 84.2 %collective-permute-start.4 = (bf16[4,1408,128]{2,1,0:T(8,128)(2,1)}, bf16[4,1408,128]{2,1,0:T(8,128)(2,1)S(1)}, u32[]{:S(2)}, u32[]{:S(2)}) collective-permute-start(bf16[4,1408,128]{2,1,0:T(8,128)(2,1)} %pad_maximum_fusion.2), channel_id=1, source_target_pairs={{0,1},{1,0},{2,3},{3,2},{4,5},{5,4},{6,7},{7,6},{8,9},{9,8},{10,11... | collective-permute-start | bytes 4325384 | tf_op jit(solution)/shard_map/ppermute | solution.py:1327
  173.6 56.8 %copy-start.53 = (bf16[4,1408,128]{2,1,0:T(8,128)(2,1)S(1)}, bf16[4,1408,128]{2,1,0:T(8,128)(2,1)}, u32[]{:S(2)}) copy-start(bf16[4,1408,128]{2,1,0:T(8,128)(2,1)} %pad_maximum_fusion.2) | copy-start | bytes 4325380
  180.5 51.7 %copy-start.24 = (f32[8,768,128]{2,1,0:T(8,128)}, f32[8,768,128]{2,1,0:T(8,128)S(1)}, u32[]{:S(2)}) copy-start(f32[8,768,128]{2,1,0:T(8,128)S(1)} %get-tuple-element.151.cache_mixed) | copy-start | bytes 9437188
  232.2 63.8 %collective-permute-start.5 = (bf16[8,1408,128]{2,1,0:T(8,128)(2,1)}, bf16[8,1408,128]{2,1,0:T(8,128)(2,1)}, u32[]{:S(2)}, u32[]{:S(2)}) collective-permute-start(bf16[8,1408,128]{2,1,0:T(8,128)(2,1)} %pad_maximum_fusion.refs_0_), channel_id=1, source_target_pairs={{0,16},{8,24},{16,0},{24,8},{1,17},{9,25},{17,1},{25,9},{2,18},{10... | collective-permute-start | bytes 8650760 | tf_op jit(solution)/shard_map/ppermute | solution.py:1322
  233.7 67.0 %collective-permute-start.6 = (bf16[4,960,128]{2,1,0:T(8,128)(2,1)}, bf16[4,960,128]{2,1,0:T(8,128)(2,1)}, u32[]{:S(2)}, u32[]{:S(2)}) collective-permute-start(bf16[4,960,128]{2,1,0:T(8,128)(2,1)} %pad_maximum_fusion.3), channel_id=1, source_target_pairs={{0,1},{1,0},{2,3},{3,2},{4,5},{5,4},{6,7},{7,6},{8,9},{9,8},{10,11... | collective-permute-start | bytes 2949128 | tf_op jit(solution)/shard_map/ppermute | solution.py:1327
  296.0 49.3 %all-to-all-start.1 = ((bf16[8,800,128]{2,1,0:T(8,128)(2,1)}), bf16[8,800,128]{2,1,0:T(8,128)(2,1)S(1)}, u32[]{:S(2)}, u32[]{:S(2)}) async-start(bf16[8,800,128]{2,1,0:T(8,128)(2,1)} %copy-done.34), calls=%async_computation.1 | async-start | bytes 3276800 | tf_op jit(solution)/shard_map/all_to_all | solution.py:1295
  302.3 50.4 %copy-start.59 = (bf16[4096]{0:T(1024)(128)(2,1)S(1)}, bf16[4096]{0:T(1024)(128)(2,1)}, u32[]{:S(2)}) copy-start(bf16[4096]{0:T(1024)(128)(2,1)} %copy-done.58) | copy-start | bytes 24580
  302.4 52.4 %copy-start.61 = (s32[512,1]{0,1:T(1,128)S(1)}, s32[512,1]{0,1:T(1,128)}, u32[]{:S(2)}) copy-start(s32[512,1]{0,1:T(1,128)} %get-tuple-element.280) | copy-start | bytes 6148
  302.4 52.4 %copy-start.63 = (s32[256]{0:T(256)S(1)}, s32[256]{0:T(256)}, u32[]{:S(2)}) copy-start(s32[256]{0:T(256)} %get-tuple-element.292) | copy-start | bytes 3076
  302.4 53.4 %copy-start.46 = (f32[8,8,128]{2,1,0:T(8,128)S(1)}, f32[8,8,128]{2,1,0:T(8,128)}, u32[]{:S(2)}) copy-start(f32[8,8,128]{2,1,0:T(8,128)} %copy-done.45) | copy-start | bytes 98308
  302.4 42.9 %collective-permute-start.9 = (bf16[8,960,128]{2,1,0:T(8,128)(2,1)S(1)}, bf16[8,960,128]{2,1,0:T(8,128)(2,1)}, u32[]{:S(2)}, u32[]{:S(2)}) collective-permute-start(bf16[8,960,128]{2,1,0:T(8,128)(2,1)S(1)} %pad_maximum_fusion.1.refs_1_), channel_id=1, source_target_pairs={{0,16},{8,24},{16,0},{24,8},{1,17},{9,25},{17,1},{25,9},{2,18},{10... | collective-permute-start | bytes 5898248 | tf_op jit(solution)/shard_map/ppermute | solution.py:1322
  345.3 107.2 %all-to-all-start.3 = ((bf16[8,768,384]{2,1,0:T(8,128)(2,1)}), bf16[8,768,384]{2,1,0:T(8,128)(2,1)}, u32[]{:S(2)}, u32[]{:S(2)}) async-start(bf16[8,768,384]{2,1,0:T(8,128)(2,1)} %copy-done.4), calls=%async_computation.3 | async-start | bytes 9437184 | tf_op jit(solution)/shard_map/all_to_all | solution.py:1295
  351.0 12.6 %collective-permute-start.7 = (bf16[8,1408,128]{2,1,0:T(8,128)(2,1)}, bf16[8,1408,128]{2,1,0:T(8,128)(2,1)}, u32[]{:S(2)}, u32[]{:S(2)}) collective-permute-start(bf16[8,1408,128]{2,1,0:T(8,128)(2,1)} %pad_maximum_fusion.refs_0_), channel_id=1, source_target_pairs={{0,8},{8,0},{16,24},{24,16},{1,9},{9,1},{17,25},{25,17},{2,10},{10... | collective-permute-start | bytes 8650760 | tf_op jit(solution)/shard_map/ppermute | solution.py:1322
  351.0 15.4 %collective-permute-start.10 = (bf16[8,1408,128]{2,1,0:T(8,128)(2,1)}, bf16[8,1408,128]{2,1,0:T(8,128)(2,1)}, u32[]{:S(2)}, u32[]{:S(2)}) collective-permute-start(bf16[8,1408,128]{2,1,0:T(8,128)(2,1)} %collective-permute-done.5.refs_4_), channel_id=1, source_target_pairs={{0,8},{8,0},{16,24},{24,16},{1,9},{9,1},{17,25},{25,17},{2,10},{10... | collective-permute-start | bytes 8650760 | tf_op jit(solution)/shard_map/ppermute | solution.py:1322
  351.5 12.1 %collective-permute-start.8 = (bf16[8,960,128]{2,1,0:T(8,128)(2,1)}, bf16[8,960,128]{2,1,0:T(8,128)(2,1)}, u32[]{:S(2)}, u32[]{:S(2)}) collective-permute-start(bf16[8,960,128]{2,1,0:T(8,128)(2,1)} %copy-done.54), channel_id=1, source_target_pairs={{0,8},{8,0},{16,24},{24,16},{1,9},{9,1},{17,25},{25,17},{2,10},{10... | collective-permute-start | bytes 5898248 | tf_op jit(solution)/shard_map/ppermute | solution.py:1322
  351.6 14.8 %collective-permute-start.11 = (bf16[8,960,128]{2,1,0:T(8,128)(2,1)}, bf16[8,960,128]{2,1,0:T(8,128)(2,1)}, u32[]{:S(2)}, u32[]{:S(2)}) collective-permute-start(bf16[8,960,128]{2,1,0:T(8,128)(2,1)} %collective-permute-done.9.refs_5_), channel_id=1, source_target_pairs={{0,8},{8,0},{16,24},{24,16},{1,9},{9,1},{17,25},{25,17},{2,10},{10... | collective-permute-start | bytes 5898248 | tf_op jit(solution)/shard_map/ppermute | solution.py:1322
  366.4 64.5 %copy-start.11 = (bf16[768,1024]{1,0:T(8,128)(2,1)S(1)}, bf16[768,1024]{1,0:T(8,128)(2,1)}, u32[]{:S(2)}) copy-start(bf16[768,1024]{1,0:T(8,128)(2,1)} %copy-done.10) | copy-start | bytes 4718596
  366.4 64.5 %copy-start.43 = (s32[7]{0:T(128)S(1)}, s32[7]{0:T(128)}, u32[]{:S(2)}) copy-start(s32[7]{0:T(128)} %get-tuple-element.266.meta) | copy-start | bytes 88
  452.5 42.9 %all-to-all-start.2 = ((bf16[8,816,128]{2,1,0:T(8,128)(2,1)}), bf16[8,816,128]{2,1,0:T(8,128)(2,1)S(1)}, u32[]{:S(2)}, u32[]{:S(2)}) async-start(bf16[8,816,128]{2,1,0:T(8,128)(2,1)} %copy-done.33), calls=%async_computation.2 | async-start | bytes 3342336 | tf_op jit(solution)/shard_map/all_to_all | solution.py:1295
  496.6 75.0 %all-to-all-start.4 = ((bf16[8,800,128]{2,1,0:T(8,128)(2,1)}), bf16[8,800,128]{2,1,0:T(8,128)(2,1)S(1)}, u32[]{:S(2)}, u32[]{:S(2)}) async-start(bf16[8,800,128]{2,1,0:T(8,128)(2,1)} %copy-done.35), calls=%async_computation.4 | async-start | bytes 3276800 | tf_op jit(solution)/shard_map/all_to_all | solution.py:1295
  571.6 83.7 %all-to-all-start.5 = ((bf16[8,768,256]{2,1,0:T(8,128)(2,1)}), bf16[8,768,256]{2,1,0:T(8,128)(2,1)}, u32[]{:S(2)}, u32[]{:S(2)}) async-start(bf16[8,768,256]{2,1,0:T(8,128)(2,1)} %copy-done.29), calls=%async_computation.5 | async-start | bytes 6291456 | tf_op jit(solution)/shard_map/all_to_all | solution.py:1295
  585.1 64.6 %copy-start.13 = (bf16[768,1024]{1,0:T(8,128)(2,1)S(1)}, bf16[768,1024]{1,0:T(8,128)(2,1)}, u32[]{:S(2)}) copy-start(bf16[768,1024]{1,0:T(8,128)(2,1)} %copy-done.12) | copy-start | bytes 4718596
  585.1 64.6 %copy-start.48 = (s32[7]{0:T(128)S(1)}, s32[7]{0:T(128)}, u32[]{:S(2)}) copy-start(s32[7]{0:T(128)} %pad_add_fusion.2.meta) | copy-start | bytes 88
  672.9 50.3 %collective-permute-start.12 = (bf16[1024,2560]{1,0:T(8,128)(2,1)}, bf16[1024,2560]{1,0:T(8,128)(2,1)}, u32[]{:S(2)}, u32[]{:S(2)}) collective-permute-start(bf16[1024,2560]{1,0:T(8,128)(2,1)} %weight_grads.3), channel_id=1, source_target_pairs={{0,8},{8,0},{16,24},{24,16},{1,9},{9,1},{17,25},{25,17},{2,10},{10... | collective-permute-start | bytes 15728648 | tf_op jit(solution)/shard_map/ppermute | solution.py:1322
  673.0 45.7 %all-to-all-start.6 = ((bf16[8,816,128]{2,1,0:T(8,128)(2,1)}), bf16[8,816,128]{2,1,0:T(8,128)(2,1)S(1)}, u32[]{:S(2)}, u32[]{:S(2)}) async-start(bf16[8,816,128]{2,1,0:T(8,128)(2,1)} %copy-done.30), calls=%async_computation.6 | async-start | bytes 3342336 | tf_op jit(solution)/shard_map/all_to_all | solution.py:1295
  714.8 137.1 %collective-permute-start.19 = (bf16[1024,2560]{1,0:T(8,128)(2,1)}, bf16[1024,2560]{1,0:T(8,128)(2,1)}, u32[]{:S(2)}, u32[]{:S(2)}) collective-permute-start(bf16[1024,2560]{1,0:T(8,128)(2,1)} %get-tuple-element.213), channel_id=1, source_target_pairs={{0,8},{8,0},{16,24},{24,16},{1,9},{9,1},{17,25},{25,17},{2,10},{10... | collective-permute-start | bytes 15728648 | tf_op jit(solution)/shard_map/ppermute | solution.py:1322
  718.7 78.9 %all-to-all-start.7 = ((bf16[8,768,128]{2,1,0:T(8,128)(2,1)}), bf16[8,768,128]{2,1,0:T(8,128)(2,1)}, u32[]{:S(2)}, u32[]{:S(2)}) async-start(bf16[8,768,128]{2,1,0:T(8,128)(2,1)} %copy-done.36), calls=%async_computation.7 | async-start | bytes 3145728 | tf_op jit(solution)/shard_map/all_to_all | solution.py:1295
  731.0 121.0 %collective-permute-start.20 = (bf16[1024,2560]{1,0:T(8,128)(2,1)}, bf16[1024,2560]{1,0:T(8,128)(2,1)}, u32[]{:S(2)}, u32[]{:S(2)}) collective-permute-start(bf16[1024,2560]{1,0:T(8,128)(2,1)} %add_convert_fusion), channel_id=1, source_target_pairs={{0,16},{8,24},{16,0},{24,8},{1,17},{9,25},{17,1},{25,9},{2,18},{10... | collective-permute-start | bytes 15728648 | tf_op jit(solution)/shard_map/ppermute | solution.py:1322
  797.6 76.3 %all-to-all-start.8 = ((bf16[8,768,256]{2,1,0:T(8,128)(2,1)}), bf16[8,768,256]{2,1,0:T(8,128)(2,1)}, u32[]{:S(2)}, u32[]{:S(2)}) async-start(bf16[8,768,256]{2,1,0:T(8,128)(2,1)} %copy-done.28), calls=%async_computation.8 | async-start | bytes 6291456 | tf_op jit(solution)/shard_map/all_to_all | solution.py:1295
  873.9 41.0 %all-to-all-start.9 = ((bf16[8,768,128]{2,1,0:T(8,128)(2,1)}), bf16[8,768,128]{2,1,0:T(8,128)(2,1)S(1)}, u32[]{:S(2)}, u32[]{:S(2)}) async-start(bf16[8,768,128]{2,1,0:T(8,128)(2,1)} %get-tuple-element.191), calls=%async_computation.9 | async-start | bytes 3145728 | tf_op jit(solution)/shard_map/all_to_all | solution.py:1295
  882.0 71.4 %collective-permute-start.21 = (bf16[4,128,2560]{2,1,0:T(8,128)(2,1)}, bf16[4,128,2560]{2,1,0:T(8,128)(2,1)}, u32[]{:S(2)}, u32[]{:S(2)}) collective-permute-start(bf16[4,128,2560]{2,1,0:T(8,128)(2,1)} %fusion), channel_id=1, source_target_pairs={{0,1},{1,0},{2,3},{3,2},{4,5},{5,4},{6,7},{7,6},{8,9},{9,8},{10,11... | collective-permute-start | bytes 7864328 | tf_op jit(solution)/shard_map/ppermute | solution.py:1327
  901.0 3.5 collective-permute-start.17
  901.1 62.3 %collective-permute-start.16 = (bf16[1024,512]{1,0:T(8,128)(2,1)}, bf16[1024,512]{1,0:T(8,128)(2,1)}, u32[]{:S(2)}, u32[]{:S(2)}) collective-permute-start(bf16[1024,512]{1,0:T(8,128)(2,1)} %get-tuple-element.208), channel_id=1, source_target_pairs={{0,8},{8,0},{16,24},{24,16},{1,9},{9,1},{17,25},{25,17},{2,10},{10... | collective-permute-start | bytes 3145736 | tf_op jit(solution)/shard_map/ppermute | solution.py:1322
  907.3 55.3 %collective-permute-start.18 = (bf16[1024,512]{1,0:T(8,128)(2,1)}, bf16[1024,512]{1,0:T(8,128)(2,1)}, u32[]{:S(2)}, u32[]{:S(2)}) collective-permute-start(bf16[1024,512]{1,0:T(8,128)(2,1)} %add_convert_fusion.2), channel_id=1, source_target_pairs={{0,16},{8,24},{16,0},{24,8},{1,17},{9,25},{17,1},{25,9},{2,18},{10... | collective-permute-start | bytes 3145736 | tf_op jit(solution)/shard_map/ppermute | solution.py:1322
  936.1 26.5 %collective-permute-start.14 = (bf16[1024,256]{1,0:T(8,128)(2,1)S(1)}, bf16[1024,256]{1,0:T(8,128)(2,1)S(1)}, u32[]{:S(2)}, u32[]{:S(2)}) collective-permute-start(bf16[1024,256]{1,0:T(8,128)(2,1)S(1)} %get-tuple-element.201), channel_id=1, source_target_pairs={{0,8},{8,0},{16,24},{24,16},{1,9},{9,1},{17,25},{25,17},{2,10},{10... | collective-permute-start | bytes 1572872 | tf_op jit(solution)/shard_map/ppermute | solution.py:1322
  961.1 40.7 %collective-permute-start.22 = (bf16[2,128,2560]{2,1,0:T(8,128)(2,1)}, bf16[2,128,2560]{2,1,0:T(8,128)(2,1)}, u32[]{:S(2)}, u32[]{:S(2)}) collective-permute-start(bf16[2,128,2560]{2,1,0:T(8,128)(2,1)} %fusion.1), channel_id=1, source_target_pairs={{0,2},{1,3},{2,0},{3,1},{4,6},{5,7},{6,4},{7,5},{8,10},{9,11},{10,... | collective-permute-start | bytes 3932168 | tf_op jit(solution)/shard_map/ppermute | solution.py:1327
  962.7 12.5 %collective-permute-start.15 = (bf16[1024,256]{1,0:T(8,128)(2,1)S(1)}, bf16[1024,256]{1,0:T(8,128)(2,1)S(1)}, u32[]{:S(2)}, u32[]{:S(2)}) collective-permute-start(bf16[1024,256]{1,0:T(8,128)(2,1)S(1)} %add_convert_fusion.4), channel_id=1, source_target_pairs={{0,16},{8,24},{16,0},{24,8},{1,17},{9,25},{17,1},{25,9},{2,18},{10... | collective-permute-start | bytes 1572872 | tf_op jit(solution)/shard_map/ppermute | solution.py:1322
  966.3 45.2 %all-to-all-start.12 = ((bf16[8,128,512]{2,1,0:T(8,128)(2,1)}), bf16[8,128,512]{2,1,0:T(8,128)(2,1)}, u32[]{:S(2)}, u32[]{:S(2)}) async-start(bf16[8,128,512]{2,1,0:T(8,128)(2,1)} %bitcast.33), calls=%async_computation.12 | async-start | bytes 2097152 | tf_op jit(solution)/shard_map/all_to_all | solution.py:1564
  972.9 36.3 %collective-permute-start.13 = (bf16[1024,256]{1,0:T(8,128)(2,1)S(1)}, bf16[1024,256]{1,0:T(8,128)(2,1)S(1)}, u32[]{:S(2)}, u32[]{:S(2)}) collective-permute-start(bf16[1024,256]{1,0:T(8,128)(2,1)S(1)} %get-tuple-element.199), channel_id=1, source_target_pairs={{0,8},{8,0},{16,24},{24,16},{1,9},{9,1},{17,25},{25,17},{2,10},{10... | collective-permute-start | bytes 1572872 | tf_op jit(solution)/shard_map/ppermute | solution.py:1322
  1005.4 39.2 %collective-permute-start.23 = (bf16[1,128,2560]{2,1,0:T(8,128)(2,1)}, bf16[1,128,2560]{2,1,0:T(8,128)(2,1)}, u32[]{:S(2)}, u32[]{:S(2)}) collective-permute-start(bf16[1,128,2560]{2,1,0:T(8,128)(2,1)} %dynamic-slice_convert_fusion.1), channel_id=1, source_target_pairs={{0,4},{1,5},{2,6},{3,7},{4,0},{5,1},{6,2},{7,3},{8,12},{9,13},{10,... | collective-permute-start | bytes 1966088 | tf_op jit(solution)/shard_map/ppermute | solution.py:1327
  1011.5 38.5 %all-to-all-start.10 = ((bf16[8,128,256]{2,1,0:T(8,128)(2,1)}), bf16[8,128,256]{2,1,0:T(8,128)(2,1)S(1)}, u32[]{:S(2)}, u32[]{:S(2)}) async-start(bf16[8,128,256]{2,1,0:T(8,128)(2,1)} %bitcast.78), calls=%async_computation.10 | async-start | bytes 1048576 | tf_op jit(solution)/shard_map/all_to_all | solution.py:1564
  1050.7 9.6 all-to-all-start.11
  (56 other events, 457.3 us)
Sparse Core Ops, SparseCore 0:
  21.3 99.9 all-gather.1
